TPU v7x, 32 devices: a whole 2x2x4 slice. The times are simulated.
32 devices in a mesh: crops: 2 (over y), xy: 4 (over z), gz: 2 (over x), lab: 2 (over core).
Axes of the slice: x: 2, y: 2, z: 4, core: 2. Of those that a mesh axis runs over, the one named last changes fastest.
Arguments:
- image: bfloat16 [16, 32, 64, 128], P('lab', ('crops', 'xy'), 'gz'), parts along dimension 1, may hold values from -6 to 6
- filt: bfloat16 [3, 16, 3, 3, 3], replicated, may hold values from -0.3125 to 0.3125
- planted_colours: int32 [32, 64, 128], P(('crops', 'xy'), 'gz'), parts along dimension 0, may hold values from 0 to 63
- likelihoods: float32 [8, 32, 64, 128], P('lab', ('crops', 'xy'), 'gz'), parts along dimension 1, may hold values from 0 to 1
- loss_slope: float32 [8, 32, 64, 128], P('lab', ('crops', 'xy'), 'gz'), parts along dimension 1, may hold values from -5.25 to 5.25
Outputs:
- grad_image: bfloat16 [16, 32, 64, 128], P('lab', ('crops', 'xy'), 'gz'), parts along dimension 1
- grad_filter: float32 [6, 16, 3, 3, 3], P('crops', 'lab'), parts along dimension 0
There are 2 independent parts, one for each index of `crops`. A program takes and returns all parts, laid end to end along the dimension named above; an argument that names none is the same for every part. Nothing has to cross between parts.
Inputs may be any that keep to these rules, and one draw needn't show every extreme that they name: `planted_colours`: A value below 8 marks a seed of that colour; any other value marks an unseeded cell.
All inputs are finite; a program needn't handle non-finite values.
Results may differ from a plain program's by a relative error of at most 0.015.
Values may be sent and summed in bfloat16 or wider, within the bound.
No kernel may reach another device: no remote copies, remote signals or barrier semaphores. Data moves between devices by JAX's collectives and lax.ppermute only.
A program may use at most 64 MiB of HBM per device.

v0:
```python
import jax
import jax.numpy as jnp
from jax import lax
from jax.sharding import PartitionSpec as P

ITERS = 3


def with_halo(cells, sides, width):
    for axis, dim in sides:
        count = lax.axis_size(axis)
        ends = count - 1
        head = lax.slice_in_dim(cells, 0, width, axis=dim)
        tail = lax.slice_in_dim(cells, cells.shape[dim] - width, cells.shape[dim], axis=dim)
        cells = jnp.concatenate(
            [
                lax.ppermute(tail, axis, [(i, (i + 1) % count) for i in range(ends)]),
                cells,
                lax.ppermute(head, axis, [((i + 1) % count, i) for i in range(ends)]),
            ],
            axis=dim,
        )
    return cells


def passed_along(block, axis, distance):
    devices = range(lax.axis_size(axis))
    route = [(i - distance, i) for i in devices if i - distance in devices]
    return lax.ppermute(block, axis, route)


def offsets():
    return [
        (first, second, third) for first in range(3) for second in range(3) for third in range(3)
    ]


def correlate(weights, wide, rows_x, rows_z, rows_y):
    grand_quantity = jnp.zeros((weights.shape[0], rows_x, rows_z, rows_y), jnp.float32)
    for first, second, third in offsets():
        window = wide[:, first : first + rows_x, second : second + rows_z, third : third + rows_y]
        grand_quantity = grand_quantity + jnp.einsum(
            "dc,cxzy->dxzy",
            weights[:, :, first, second, third],
            window,
            preferred_element_type=jnp.float32,
        )
    return grand_quantity


def squares(remainder_grid):
    return lax.psum(jnp.sum(remainder_grid * remainder_grid, axis=(1, 2, 3)), ("xy", "gz"))[
        :, None, None, None
    ]


def local(image, filt, planted_colours, likelihoods, loss_slope):
    channels_here = image.shape[0]
    labels_here = likelihoods.shape[0]
    rows_x, rows_z, rows_y = (likelihoods.shape[1], likelihoods.shape[2], likelihoods.shape[3])
    lab_index = lax.axis_index("lab")
    own_filt = lax.dynamic_slice_in_dim(filt, lab_index * channels_here, channels_here, 1)
    image_edge = with_halo(image, (("xy", 1), ("gz", 2)), 1)
    own_wide = jnp.pad(image_edge, ((0, 0), (0, 0), (0, 0), (1, 1)))
    logits = lax.psum(
        correlate(own_filt, own_wide, rows_x, rows_z, rows_y).astype(jnp.bfloat16), "lab"
    ).astype(jnp.float32)
    xy_index = lax.axis_index("xy")
    gz_index = lax.axis_index("gz")
    xy_count = lax.axis_size("xy")
    gz_count = lax.axis_size("gz")
    shape = (rows_x, rows_z, rows_y)
    along_x = jnp.arange(rows_x, dtype=jnp.int32) + xy_index * rows_x < rows_x * xy_count - 1
    along_z = jnp.arange(rows_z, dtype=jnp.int32) + gz_index * rows_z < rows_z * gz_count - 1
    along_y = jnp.arange(rows_y, dtype=jnp.int32) < rows_y - 1
    edge_valid = jnp.stack(
        [
            jnp.broadcast_to(along_x[:, None, None], shape),
            jnp.broadcast_to(along_z[None, :, None], shape),
            jnp.broadcast_to(along_y[None, None, :], shape),
        ]
    ).astype(jnp.float32)
    squashed = jax.nn.sigmoid(logits)
    weight = (0.05 + squashed) * edge_valid
    below_x = passed_along(weight[0, -1:], "xy", 1)
    lower_x = jnp.concatenate([below_x, weight[0, :-1]], axis=0)
    below_z = passed_along(weight[1, :, -1:], "gz", 1)
    lower_z = jnp.concatenate([below_z, weight[1, :, :-1]], axis=1)
    lower_y = jnp.concatenate(
        [jnp.zeros((rows_x, rows_z, 1), jnp.float32), weight[2, :, :, :-1]], axis=2
    )
    class_count_overall = labels_here * lax.axis_size("lab")
    free_cell_flags = (planted_colours >= class_count_overall).astype(jnp.float32)[None]
    colours = lab_index * labels_here + jnp.arange(labels_here, dtype=jnp.int32)
    class_membership = (planted_colours[None] == colours[:, None, None, None]).astype(jnp.float32)
    entire_grid_state = free_cell_flags * likelihoods + class_membership
    adjoint = jnp.zeros_like(likelihoods)
    remainder_grid = free_cell_flags * loss_slope
    direction = remainder_grid
    norm_now = squares(remainder_grid)
    for count in range(ITERS):
        extended = with_halo(direction.astype(jnp.bfloat16), (("xy", 1), ("gz", 2)), 1).astype(
            direction.dtype
        )
        zeros_y = jnp.zeros(direction.shape[:3] + (1,), jnp.float32)
        upper_y = jnp.concatenate([direction[..., 1:], zeros_y], axis=3)
        under_y = jnp.concatenate([zeros_y, direction[..., :-1]], axis=3)
        grand_quantity = weight[0] * (direction - extended[:, 2:, 1:-1]) + lower_x * (
            direction - extended[:, :-2, 1:-1]
        )
        grand_quantity = (
            grand_quantity
            + weight[1] * (direction - extended[:, 1:-1, 2:])
            + lower_z * (direction - extended[:, 1:-1, :-2])
        )
        grand_quantity = (
            grand_quantity + weight[2] * (direction - upper_y) + lower_y * (direction - under_y)
        )
        picture_pixels_flat = free_cell_flags * grand_quantity
        curve = lax.psum(jnp.sum(direction * picture_pixels_flat, axis=(1, 2, 3)), ("xy", "gz"))
        alpha = norm_now / curve[:, None, None, None]
        adjoint = adjoint + alpha * direction
        remainder_grid = remainder_grid - alpha * picture_pixels_flat
        norm_next = squares(remainder_grid)
        direction = remainder_grid + norm_next / norm_now * direction
        norm_now = norm_next
    field_pair = jnp.concatenate([adjoint, entire_grid_state], axis=0)
    above_x = passed_along(field_pair[:, :1].astype(jnp.bfloat16), "xy", -1).astype(jnp.float32)
    next_x = jnp.concatenate([field_pair[:, 1:], above_x], axis=1)
    above_z = passed_along(field_pair[:, :, :1], "gz", -1)
    next_z = jnp.concatenate([field_pair[:, :, 1:], above_z], axis=2)
    next_y = jnp.concatenate(
        [field_pair[..., 1:], jnp.zeros(field_pair.shape[:3] + (1,), jnp.float32)], axis=3
    )
    partial_grads = []
    for neighbour in (next_x, next_z, next_y):
        change = field_pair - neighbour
        partial_grads.append(-jnp.sum(change[:labels_here] * change[labels_here:], axis=0))
    edge_grad = lax.psum(jnp.stack(partial_grads), "lab")
    logit_grad = (edge_grad * squashed * (1.0 - squashed) * edge_valid).astype(jnp.bfloat16)
    grad_edge = with_halo(logit_grad, (("xy", 1), ("gz", 2)), 1)
    grad_wide = jnp.pad(grad_edge, ((0, 0), (0, 0), (0, 0), (1, 1)))
    grad_image = jnp.zeros((channels_here, rows_x, rows_z, rows_y), jnp.float32)
    filter_terms = []
    for first, second, third in offsets():
        window = grad_wide[
            :,
            2 - first : 2 - first + rows_x,
            2 - second : 2 - second + rows_z,
            2 - third : 2 - third + rows_y,
        ]
        grad_image = grad_image + jnp.einsum(
            "dc,dxzy->cxzy",
            own_filt[:, :, first, second, third],
            window,
            preferred_element_type=jnp.float32,
        )
        image_window = own_wide[
            :, first : first + rows_x, second : second + rows_z, third : third + rows_y
        ]
        filter_terms.append(
            jnp.einsum(
                "dxzy,cxzy->dc", logit_grad, image_window, preferred_element_type=jnp.float32
            )
        )
    filter_part = jnp.stack(filter_terms, axis=-1).reshape(3, channels_here, 3, 3, 3)
    grad_filter = lax.psum(filter_part, ("xy", "gz"))
    return (grad_image.astype(jnp.bfloat16), grad_filter)


def solution(mesh):
    return jax.shard_map(
        local,
        mesh=mesh,
        in_specs=(
            P("lab", ("crops", "xy"), "gz", None),
            P(),
            P(("crops", "xy"), "gz", None),
            P("lab", ("crops", "xy"), "gz", None),
            P("lab", ("crops", "xy"), "gz", None),
        ),
        out_specs=(P("lab", ("crops", "xy"), "gz", None), P("crops", "lab", None, None, None)),
        check_vma=False,
    )
```

profile of v0, /device:TPU:0, one launch (start us, length us, event | category | flops | bytes accessed | tf_op | source)
XLA Modules:
  0.0 312.0 jit_solution(1046695100650287679)
XLA Ops:
  9.7 5.6 %collective-permute-start = (bf16[8,1,32,128]{3,0,2,1:T(8,128)(2,1)S(1)}, bf16[8,1,32,128]{3,0,2,1:T(8,128)(2,1)S(1)}, u32[]{:S(2)}, u32[]{:S(2)}) collective-permute-start(bf16[8,1,32,128]{3,0,2,1:T(8,128)(2,1)S(1)} %get-tuple-element.42), channel_id=1, source_target_pairs={{0,4},{4,8},{8,12},{1,5},{5,9},{9,13},{2,6},{6,10},{10,14},{3,7},{... | collective-permute-start | bytes 196616 | tf_op jit(solution)/shard_map/ppermute | solution.py:17
  16.2 4.1 %collective-permute-start.4 = (bf16[4,1,32,128]{3,2,1,0:T(8,128)(2,1)S(1)}, bf16[4,1,32,128]{3,2,1,0:T(8,128)(2,1)S(1)}, u32[]{:S(2)}, u32[]{:S(2)}) collective-permute-start(bf16[4,1,32,128]{3,2,1,0:T(8,128)(2,1)S(1)} %get-tuple-element.59), channel_id=1, source_target_pairs={{0,4},{4,8},{8,12},{1,5},{5,9},{9,13},{2,6},{6,10},{10,14},{3,7},{... | collective-permute-start | bytes 98312 | tf_op jit(solution)/shard_map/ppermute | solution.py:17
  23.1 3.4 %collective-permute-start.2 = (bf16[8,6,1,128]{3,0,2,1:T(8,128)(2,1)S(1)}, bf16[8,6,1,128]{3,0,2,1:T(8,128)(2,1)S(1)}, u32[]{:S(2)}, u32[]{:S(2)}) collective-permute-start(bf16[8,6,1,128]{3,0,2,1:T(8,128)(2,1)S(1)} %get-tuple-element.30), channel_id=1, source_target_pairs={{0,2},{1,3},{4,6},{5,7},{8,10},{9,11},{12,14},{13,15},{16,18},{17,... | collective-permute-start | bytes 36872 | tf_op jit(solution)/shard_map/ppermute | solution.py:17
  27.8 4.5 %collective-permute-start.6 = (bf16[4,6,1,128]{3,2,1,0:T(2,128)(2,1)S(1)}, bf16[4,6,1,128]{3,2,1,0:T(2,128)(2,1)S(1)}, u32[]{:S(2)}, u32[]{:S(2)}) collective-permute-start(bf16[4,6,1,128]{3,2,1,0:T(2,128)(2,1)S(1)} %get-tuple-element.51), channel_id=1, source_target_pairs={{0,2},{1,3},{4,6},{5,7},{8,10},{9,11},{12,14},{13,15},{16,18},{17,... | collective-permute-start | bytes 18440 | tf_op jit(solution)/shard_map/ppermute | solution.py:17
  42.4 20.3 %all-reduce.14.cloned.1.call-done = bf16[3,4,32,128]{3,0,2,1:T(4,128)(2,1)} async-done(((bf16[3,4,32,128]{3,0,2,1:T(4,128)(2,1)}), bf16[3,4,32,128]{3,0,2,1:T(4,128)(2,1)}) %all-reduce.14.cloned.1.call-update) | async-done | bytes 98320 | tf_op jit(solution)/shard_map/psum | solution.py:65
  64.4 3.6 %collective-permute-start.9 = (f32[4,1,128]{2,0,1:T(4,128)S(1)}, f32[4,1,128]{2,0,1:T(4,128)S(1)}, u32[]{:S(2)}, u32[]{:S(2)}) collective-permute-start(f32[4,1,128]{2,0,1:T(4,128)S(1)} %bitcast.468), channel_id=1, source_target_pairs={{0,2},{1,3},{4,6},{5,7},{8,10},{9,11},{12,14},{13,15},{16,18},{17,... | collective-permute-start | bytes 6152 | tf_op jit(solution)/shard_map/ppermute | solution.py:29
  68.4 3.4 %collective-permute-start.8 = (f32[1,32,128]{2,1,0:T(8,128)S(1)}, f32[1,32,128]{2,1,0:T(8,128)S(1)}, u32[]{:S(2)}, u32[]{:S(2)}) collective-permute-start(f32[1,32,128]{2,1,0:T(8,128)S(1)} %bitcast.466), channel_id=1, source_target_pairs={{0,4},{4,8},{8,12},{1,5},{5,9},{9,13},{2,6},{6,10},{10,14},{3,7},{... | collective-permute-start | bytes 49160 | tf_op jit(solution)/shard_map/ppermute | solution.py:29
  73.8 20.1 %all-reduce.10 = (f32[4]{0:T(128)S(1)}, f32[4]{0:T(128)S(1)}) all-reduce(f32[4]{0:T(128)S(1)} %get-tuple-element.13, f32[4]{0:T(128)S(1)} %get-tuple-element.12), channel_id=1, replica_groups=mesh['crops'=2,'xy'=4,'gz'=2,'lab'=2] {'xy','gz'}, use_global_device_ids=true, to_apply=%region_1.2 | all-reduce | flops 8 | bytes 64 | tf_op jit(solution)/shard_map/psum | solution.py:52
  94.1 17.2 %psum.66 = f32[4]{0:T(128)S(1)} all-reduce(f32[4]{0:T(128)S(1)} %get-tuple-element.22), channel_id=1, replica_groups=mesh['crops'=2,'xy'=4,'gz'=2,'lab'=2] {'xy','gz'}, use_global_device_ids=true, to_apply=%region_6.7 | all-reduce | flops 4 | bytes 32 | tf_op jit(solution)/shard_map/psum | solution.py:52
  114.9 4.2 %collective-permute-done.11 = bf16[4,1,32,128]{3,2,1,0:T(8,128)(2,1)S(1)} collective-permute-done((bf16[4,1,32,128]{3,2,1,0:T(8,128)(2,1)S(1)}, bf16[4,1,32,128]{3,2,1,0:T(8,128)(2,1)S(1)}, u32[]{:S(2)}, u32[]{:S(2)}) %collective-permute-start.11) | collective-permute-done | bytes 32800 | tf_op jit(solution)/shard_map/ppermute | solution.py:19
  119.1 3.8 %collective-permute-start.12 = (bf16[4,6,1,128]{3,2,1,0:T(2,128)(2,1)S(1)}, bf16[4,6,1,128]{3,2,1,0:T(2,128)(2,1)S(1)}, u32[]{:S(2)}, u32[]{:S(2)}) collective-permute-start(bf16[4,6,1,128]{3,2,1,0:T(2,128)(2,1)S(1)} %get-tuple-element.49), channel_id=1, source_target_pairs={{0,2},{1,3},{4,6},{5,7},{8,10},{9,11},{12,14},{13,15},{16,18},{17,... | collective-permute-start | bytes 18440 | tf_op jit(solution)/shard_map/ppermute | solution.py:17
  124.4 4.1 %collective-permute-done.13 = bf16[4,6,1,128]{3,2,1,0:T(2,128)(2,1)S(1)} collective-permute-done((bf16[4,6,1,128]{3,2,1,0:T(2,128)(2,1)S(1)}, bf16[4,6,1,128]{3,2,1,0:T(2,128)(2,1)S(1)}, u32[]{:S(2)}, u32[]{:S(2)}) %collective-permute-start.13) | collective-permute-done | bytes 6176 | tf_op jit(solution)/shard_map/ppermute | solution.py:19
  129.6 17.3 %psum.67 = f32[4]{0:T(128)S(1)} all-reduce(f32[4]{0:T(128)} %get-tuple-element.18), channel_id=1, replica_groups=mesh['crops'=2,'xy'=4,'gz'=2,'lab'=2] {'xy','gz'}, use_global_device_ids=true, to_apply=%region_8.9 | all-reduce | flops 4 | bytes 32 | tf_op jit(solution)/shard_map/psum | solution.py:120
  147.7 19.1 %psum.68 = f32[4]{0:T(128)S(1)} all-reduce(f32[4]{0:T(128)S(1)} %multiply_reduce_fusion), channel_id=1, replica_groups=mesh['crops'=2,'xy'=4,'gz'=2,'lab'=2] {'xy','gz'}, use_global_device_ids=true, to_apply=%region_10.11 | all-reduce | flops 4 | bytes 32 | tf_op jit(solution)/shard_map/psum | solution.py:52
  171.7 4.2 %collective-permute-done.15 = bf16[4,1,32,128]{3,2,1,0:T(8,128)(2,1)S(1)} collective-permute-done((bf16[4,1,32,128]{3,2,1,0:T(8,128)(2,1)S(1)}, bf16[4,1,32,128]{3,2,1,0:T(8,128)(2,1)S(1)}, u32[]{:S(2)}, u32[]{:S(2)}) %collective-permute-start.15) | collective-permute-done | bytes 32800 | tf_op jit(solution)/shard_map/ppermute | solution.py:19
  176.0 2.0 collective-permute-start.16
  179.4 4.1 %collective-permute-done.17 = bf16[4,6,1,128]{3,2,1,0:T(2,128)(2,1)S(1)} collective-permute-done((bf16[4,6,1,128]{3,2,1,0:T(2,128)(2,1)S(1)}, bf16[4,6,1,128]{3,2,1,0:T(2,128)(2,1)S(1)}, u32[]{:S(2)}, u32[]{:S(2)}) %collective-permute-start.17) | collective-permute-done | bytes 6176 | tf_op jit(solution)/shard_map/ppermute | solution.py:19
  184.1 17.2 %psum.69 = f32[4]{0:T(128)S(1)} all-reduce(f32[4]{0:T(128)S(1)} %fusion.71), channel_id=1, replica_groups=mesh['crops'=2,'xy'=4,'gz'=2,'lab'=2] {'xy','gz'}, use_global_device_ids=true, to_apply=%region_12.13 | all-reduce | flops 4 | bytes 32 | tf_op jit(solution)/shard_map/psum | solution.py:120
  204.5 4.6 %collective-permute-done.18 = bf16[8,1,32,128]{3,2,1,0:T(8,128)(2,1)S(1)} collective-permute-done((bf16[8,1,32,128]{3,2,1,0:T(8,128)(2,1)S(1)}, bf16[8,1,32,128]{3,2,1,0:T(8,128)(2,1)S(1)}, u32[]{:S(2)}, u32[]{:S(2)}) %collective-permute-start.18) | collective-permute-done | bytes 65568 | tf_op jit(solution)/shard_map/ppermute | solution.py:29
  210.6 17.7 %all-reduce.16.cloned.1.call-done = f32[3,4,32,128]{3,0,2,1:T(4,128)} async-done(((f32[3,4,32,128]{3,0,2,1:T(4,128)}), f32[3,4,32,128]{3,0,2,1:T(4,128)}) %all-reduce.16.cloned.1.call-update) | async-done | bytes 196624 | tf_op jit(solution)/shard_map/psum | solution.py:139
  237.9 3.7 %collective-permute-start.20 = (bf16[3,1,32,128]{3,0,2,1:T(4,128)(2,1)S(1)}, bf16[3,1,32,128]{3,0,2,1:T(4,128)(2,1)S(1)}, u32[]{:S(2)}, u32[]{:S(2)}) collective-permute-start(bf16[3,1,32,128]{3,0,2,1:T(4,128)(2,1)S(1)} %get-tuple-element.53), channel_id=1, source_target_pairs={{0,4},{4,8},{8,12},{1,5},{5,9},{9,13},{2,6},{6,10},{10,14},{3,7},{... | collective-permute-start | bytes 73736 | tf_op jit(solution)/shard_map/ppermute | solution.py:17
  243.1 4.2 %collective-permute-done.21 = bf16[3,1,32,128]{3,0,2,1:T(4,128)(2,1)S(1)} collective-permute-done((bf16[3,1,32,128]{3,0,2,1:T(4,128)(2,1)S(1)}, bf16[3,1,32,128]{3,0,2,1:T(4,128)(2,1)S(1)}, u32[]{:S(2)}, u32[]{:S(2)}) %collective-permute-start.21) | collective-permute-done | bytes 24608 | tf_op jit(solution)/shard_map/ppermute | solution.py:19
  247.4 3.4 %collective-permute-start.22 = (bf16[3,6,1,128]{3,0,2,1:T(4,128)(2,1)S(1)}, bf16[3,6,1,128]{3,0,2,1:T(4,128)(2,1)S(1)}, u32[]{:S(2)}, u32[]{:S(2)}) collective-permute-start(bf16[3,6,1,128]{3,0,2,1:T(4,128)(2,1)S(1)} %get-tuple-element.45), channel_id=1, source_target_pairs={{0,2},{1,3},{4,6},{5,7},{8,10},{9,11},{12,14},{13,15},{16,18},{17,... | collective-permute-start | bytes 13832 | tf_op jit(solution)/shard_map/ppermute | solution.py:17
  252.4 37.5 %psum.71 = f32[3,8,3,3,3]{1,4,3,2,0:T(4,128)} all-reduce(f32[3,8,3,3,3]{1,4,3,2,0:T(4,128)S(1)} %copy.170), channel_id=1, replica_groups=mesh['crops'=2,'xy'=4,'gz'=2,'lab'=2] {'xy','gz'}, use_global_device_ids=true, to_apply=%region_17.18 | all-reduce | flops 648 | bytes 5184 | tf_op jit(solution)/shard_map/psum | solution.py:167
  (366 shorter events, 66.9 us)
Async XLA Ops:
  7.2 55.5 %all-reduce.14.cloned.1.call-start = ((), (), s32[]{:S(2)}) async-start(), calls=%async_computation | async-start | bytes 262144 | tf_op jit(solution)/shard_map/psum | solution.py:65
  8.4 14.6 %collective-permute-start.1 = (bf16[8,1,32,128]{3,0,2,1:T(8,128)(2,1)S(1)}, bf16[8,1,32,128]{3,0,2,1:T(8,128)(2,1)S(1)}, u32[]{:S(2)}, u32[]{:S(2)}) collective-permute-start(bf16[8,1,32,128]{3,0,2,1:T(8,128)(2,1)S(1)} %get-tuple-element.41), channel_id=1, source_target_pairs={{4,0},{8,4},{12,8},{5,1},{9,5},{13,9},{6,2},{10,6},{14,10},{7,3},{... | collective-permute-start | bytes 196616 | tf_op jit(solution)/shard_map/ppermute | solution.py:19
  9.7 13.1 %collective-permute-start = (bf16[8,1,32,128]{3,0,2,1:T(8,128)(2,1)S(1)}, bf16[8,1,32,128]{3,0,2,1:T(8,128)(2,1)S(1)}, u32[]{:S(2)}, u32[]{:S(2)}) collective-permute-start(bf16[8,1,32,128]{3,0,2,1:T(8,128)(2,1)S(1)} %get-tuple-element.42), channel_id=1, source_target_pairs={{0,4},{4,8},{8,12},{1,5},{5,9},{9,13},{2,6},{6,10},{10,14},{3,7},{... | collective-permute-start | bytes 196616 | tf_op jit(solution)/shard_map/ppermute | solution.py:17
  16.2 11.6 %collective-permute-start.4 = (bf16[4,1,32,128]{3,2,1,0:T(8,128)(2,1)S(1)}, bf16[4,1,32,128]{3,2,1,0:T(8,128)(2,1)S(1)}, u32[]{:S(2)}, u32[]{:S(2)}) collective-permute-start(bf16[4,1,32,128]{3,2,1,0:T(8,128)(2,1)S(1)} %get-tuple-element.59), channel_id=1, source_target_pairs={{0,4},{4,8},{8,12},{1,5},{5,9},{9,13},{2,6},{6,10},{10,14},{3,7},{... | collective-permute-start | bytes 98312 | tf_op jit(solution)/shard_map/ppermute | solution.py:17
  20.3 7.5 %collective-permute-start.5 = (bf16[4,1,32,128]{3,2,1,0:T(8,128)(2,1)S(1)}, bf16[4,1,32,128]{3,2,1,0:T(8,128)(2,1)S(1)}, u32[]{:S(2)}, u32[]{:S(2)}) collective-permute-start(bf16[4,1,32,128]{3,2,1,0:T(8,128)(2,1)S(1)} %get-tuple-element.60), channel_id=1, source_target_pairs={{4,0},{8,4},{12,8},{5,1},{9,5},{13,9},{6,2},{10,6},{14,10},{7,3},{... | collective-permute-start | bytes 98312 | tf_op jit(solution)/shard_map/ppermute | solution.py:19
  23.1 10.6 %collective-permute-start.2 = (bf16[8,6,1,128]{3,0,2,1:T(8,128)(2,1)S(1)}, bf16[8,6,1,128]{3,0,2,1:T(8,128)(2,1)S(1)}, u32[]{:S(2)}, u32[]{:S(2)}) collective-permute-start(bf16[8,6,1,128]{3,0,2,1:T(8,128)(2,1)S(1)} %get-tuple-element.30), channel_id=1, source_target_pairs={{0,2},{1,3},{4,6},{5,7},{8,10},{9,11},{12,14},{13,15},{16,18},{17,... | collective-permute-start | bytes 36872 | tf_op jit(solution)/shard_map/ppermute | solution.py:17
  26.5 7.2 %collective-permute-start.3 = (bf16[8,6,1,128]{3,0,2,1:T(8,128)(2,1)S(1)}, bf16[8,6,1,128]{3,0,2,1:T(8,128)(2,1)S(1)}, u32[]{:S(2)}, u32[]{:S(2)}) collective-permute-start(bf16[8,6,1,128]{3,0,2,1:T(8,128)(2,1)S(1)} %get-tuple-element.31), channel_id=1, source_target_pairs={{2,0},{3,1},{6,4},{7,5},{10,8},{11,9},{14,12},{15,13},{18,16},{19,... | collective-permute-start | bytes 36872 | tf_op jit(solution)/shard_map/ppermute | solution.py:19
  27.8 14.4 %collective-permute-start.6 = (bf16[4,6,1,128]{3,2,1,0:T(2,128)(2,1)S(1)}, bf16[4,6,1,128]{3,2,1,0:T(2,128)(2,1)S(1)}, u32[]{:S(2)}, u32[]{:S(2)}) collective-permute-start(bf16[4,6,1,128]{3,2,1,0:T(2,128)(2,1)S(1)} %get-tuple-element.51), channel_id=1, source_target_pairs={{0,2},{1,3},{4,6},{5,7},{8,10},{9,11},{12,14},{13,15},{16,18},{17,... | collective-permute-start | bytes 18440 | tf_op jit(solution)/shard_map/ppermute | solution.py:17
  32.4 9.8 %collective-permute-start.7 = (bf16[4,6,1,128]{3,2,1,0:T(2,128)(2,1)S(1)}, bf16[4,6,1,128]{3,2,1,0:T(2,128)(2,1)S(1)}, u32[]{:S(2)}, u32[]{:S(2)}) collective-permute-start(bf16[4,6,1,128]{3,2,1,0:T(2,128)(2,1)S(1)} %get-tuple-element.52), channel_id=1, source_target_pairs={{2,0},{3,1},{6,4},{7,5},{10,8},{11,9},{14,12},{15,13},{18,16},{19,... | collective-permute-start | bytes 18440 | tf_op jit(solution)/shard_map/ppermute | solution.py:19
  42.2 186.2 %all-reduce.16.cloned.1.call-start = ((), (), s32[]{:S(2)}) async-start(), calls=%async_computation.1 | async-start | bytes 524288 | tf_op jit(solution)/shard_map/psum | solution.py:139
  64.4 7.6 %collective-permute-start.9 = (f32[4,1,128]{2,0,1:T(4,128)S(1)}, f32[4,1,128]{2,0,1:T(4,128)S(1)}, u32[]{:S(2)}, u32[]{:S(2)}) collective-permute-start(f32[4,1,128]{2,0,1:T(4,128)S(1)} %bitcast.468), channel_id=1, source_target_pairs={{0,2},{1,3},{4,6},{5,7},{8,10},{9,11},{12,14},{13,15},{16,18},{17,... | collective-permute-start | bytes 6152 | tf_op jit(solution)/shard_map/ppermute | solution.py:29
  68.4 4.8 %collective-permute-start.8 = (f32[1,32,128]{2,1,0:T(8,128)S(1)}, f32[1,32,128]{2,1,0:T(8,128)S(1)}, u32[]{:S(2)}, u32[]{:S(2)}) collective-permute-start(f32[1,32,128]{2,1,0:T(8,128)S(1)} %bitcast.466), channel_id=1, source_target_pairs={{0,4},{4,8},{8,12},{1,5},{5,9},{9,13},{2,6},{6,10},{10,14},{3,7},{... | collective-permute-start | bytes 49160 | tf_op jit(solution)/shard_map/ppermute | solution.py:29
  113.3 5.8 %collective-permute-start.11 = (bf16[4,1,32,128]{3,2,1,0:T(8,128)(2,1)S(1)}, bf16[4,1,32,128]{3,2,1,0:T(8,128)(2,1)S(1)}, u32[]{:S(2)}, u32[]{:S(2)}) collective-permute-start(bf16[4,1,32,128]{3,2,1,0:T(8,128)(2,1)S(1)} %get-tuple-element.58), channel_id=1, source_target_pairs={{4,0},{8,4},{12,8},{5,1},{9,5},{13,9},{6,2},{10,6},{14,10},{7,3},{... | collective-permute-start | bytes 98312 | tf_op jit(solution)/shard_map/ppermute | solution.py:19
  119.1 5.3 %collective-permute-start.12 = (bf16[4,6,1,128]{3,2,1,0:T(2,128)(2,1)S(1)}, bf16[4,6,1,128]{3,2,1,0:T(2,128)(2,1)S(1)}, u32[]{:S(2)}, u32[]{:S(2)}) collective-permute-start(bf16[4,6,1,128]{3,2,1,0:T(2,128)(2,1)S(1)} %get-tuple-element.49), channel_id=1, source_target_pairs={{0,2},{1,3},{4,6},{5,7},{8,10},{9,11},{12,14},{13,15},{16,18},{17,... | collective-permute-start | bytes 18440 | tf_op jit(solution)/shard_map/ppermute | solution.py:17
  122.9 5.6 %collective-permute-start.13 = (bf16[4,6,1,128]{3,2,1,0:T(2,128)(2,1)S(1)}, bf16[4,6,1,128]{3,2,1,0:T(2,128)(2,1)S(1)}, u32[]{:S(2)}, u32[]{:S(2)}) collective-permute-start(bf16[4,6,1,128]{3,2,1,0:T(2,128)(2,1)S(1)} %get-tuple-element.50), channel_id=1, source_target_pairs={{2,0},{3,1},{6,4},{7,5},{10,8},{11,9},{14,12},{15,13},{18,16},{19,... | collective-permute-start | bytes 18440 | tf_op jit(solution)/shard_map/ppermute | solution.py:19
  170.1 5.8 %collective-permute-start.15 = (bf16[4,1,32,128]{3,2,1,0:T(8,128)(2,1)S(1)}, bf16[4,1,32,128]{3,2,1,0:T(8,128)(2,1)S(1)}, u32[]{:S(2)}, u32[]{:S(2)}) collective-permute-start(bf16[4,1,32,128]{3,2,1,0:T(8,128)(2,1)S(1)} %get-tuple-element.56), channel_id=1, source_target_pairs={{4,0},{8,4},{12,8},{5,1},{9,5},{13,9},{6,2},{10,6},{14,10},{7,3},{... | collective-permute-start | bytes 98312 | tf_op jit(solution)/shard_map/ppermute | solution.py:19
  176.0 3.5 %collective-permute-start.16 = (bf16[4,6,1,128]{3,2,1,0:T(2,128)(2,1)S(1)}, bf16[4,6,1,128]{3,2,1,0:T(2,128)(2,1)S(1)}, u32[]{:S(2)}, u32[]{:S(2)}) collective-permute-start(bf16[4,6,1,128]{3,2,1,0:T(2,128)(2,1)S(1)} %get-tuple-element.47), channel_id=1, source_target_pairs={{0,2},{1,3},{4,6},{5,7},{8,10},{9,11},{12,14},{13,15},{16,18},{17,... | collective-permute-start | bytes 18440 | tf_op jit(solution)/shard_map/ppermute | solution.py:17
  177.9 5.6 %collective-permute-start.17 = (bf16[4,6,1,128]{3,2,1,0:T(2,128)(2,1)S(1)}, bf16[4,6,1,128]{3,2,1,0:T(2,128)(2,1)S(1)}, u32[]{:S(2)}, u32[]{:S(2)}) collective-permute-start(bf16[4,6,1,128]{3,2,1,0:T(2,128)(2,1)S(1)} %get-tuple-element.48), channel_id=1, source_target_pairs={{2,0},{3,1},{6,4},{7,5},{10,8},{11,9},{14,12},{15,13},{18,16},{19,... | collective-permute-start | bytes 18440 | tf_op jit(solution)/shard_map/ppermute | solution.py:19
  201.7 7.5 %collective-permute-start.19 = (f32[8,4,1,128]{3,2,1,0:T(1,128)S(1)}, f32[8,4,1,128]{3,2,1,0:T(1,128)S(1)}, u32[]{:S(2)}, u32[]{:S(2)}) collective-permute-start(f32[8,4,1,128]{3,2,1,0:T(1,128)S(1)} %fusion.176), channel_id=1, source_target_pairs={{2,0},{3,1},{6,4},{7,5},{10,8},{11,9},{14,12},{15,13},{18,16},{19,... | collective-permute-start | bytes 49160 | tf_op jit(solution)/shard_map/ppermute | solution.py:29
  203.0 6.2 %collective-permute-start.18 = (bf16[8,1,32,128]{3,2,1,0:T(8,128)(2,1)S(1)}, bf16[8,1,32,128]{3,2,1,0:T(8,128)(2,1)S(1)}, u32[]{:S(2)}, u32[]{:S(2)}) collective-permute-start(bf16[8,1,32,128]{3,2,1,0:T(8,128)(2,1)S(1)} %fusion.141), channel_id=1, source_target_pairs={{4,0},{8,4},{12,8},{5,1},{9,5},{13,9},{6,2},{10,6},{14,10},{7,3},{... | collective-permute-start | bytes 196616 | tf_op jit(solution)/shard_map/ppermute | solution.py:29
  237.9 5.3 %collective-permute-start.20 = (bf16[3,1,32,128]{3,0,2,1:T(4,128)(2,1)S(1)}, bf16[3,1,32,128]{3,0,2,1:T(4,128)(2,1)S(1)}, u32[]{:S(2)}, u32[]{:S(2)}) collective-permute-start(bf16[3,1,32,128]{3,0,2,1:T(4,128)(2,1)S(1)} %get-tuple-element.53), channel_id=1, source_target_pairs={{0,4},{4,8},{8,12},{1,5},{5,9},{9,13},{2,6},{6,10},{10,14},{3,7},{... | collective-permute-start | bytes 73736 | tf_op jit(solution)/shard_map/ppermute | solution.py:17
  241.5 5.8 %collective-permute-start.21 = (bf16[3,1,32,128]{3,0,2,1:T(4,128)(2,1)S(1)}, bf16[3,1,32,128]{3,0,2,1:T(4,128)(2,1)S(1)}, u32[]{:S(2)}, u32[]{:S(2)}) collective-permute-start(bf16[3,1,32,128]{3,0,2,1:T(4,128)(2,1)S(1)} %get-tuple-element.54), channel_id=1, source_target_pairs={{4,0},{8,4},{12,8},{5,1},{9,5},{13,9},{6,2},{10,6},{14,10},{7,3},{... | collective-permute-start | bytes 73736 | tf_op jit(solution)/shard_map/ppermute | solution.py:19
  247.4 42.6 %collective-permute-start.22 = (bf16[3,6,1,128]{3,0,2,1:T(4,128)(2,1)S(1)}, bf16[3,6,1,128]{3,0,2,1:T(4,128)(2,1)S(1)}, u32[]{:S(2)}, u32[]{:S(2)}) collective-permute-start(bf16[3,6,1,128]{3,0,2,1:T(4,128)(2,1)S(1)} %get-tuple-element.45), channel_id=1, source_target_pairs={{0,2},{1,3},{4,6},{5,7},{8,10},{9,11},{12,14},{13,15},{16,18},{17,... | collective-permute-start | bytes 13832 | tf_op jit(solution)/shard_map/ppermute | solution.py:17
  250.7 39.2 %collective-permute-start.23 = (bf16[3,6,1,128]{3,0,2,1:T(4,128)(2,1)S(1)}, bf16[3,6,1,128]{3,0,2,1:T(4,128)(2,1)S(1)}, u32[]{:S(2)}, u32[]{:S(2)}) collective-permute-start(bf16[3,6,1,128]{3,0,2,1:T(4,128)(2,1)S(1)} %get-tuple-element.46), channel_id=1, source_target_pairs={{2,0},{3,1},{6,4},{7,5},{10,8},{11,9},{14,12},{15,13},{18,16},{19,... | collective-permute-start | bytes 13832 | tf_op jit(solution)/shard_map/ppermute | solution.py:19
  (90 other events, 802.6 us)
Sparse Core Ops, SparseCore 0:
  42.3 20.3 all-reduce.13
  210.8 17.5 all-reduce.15
where the time goes:
time: 313 us; the launch traced here: 312 us
  blocking collectives  128 us (41%)
  waiting for transfers between devices  65.5 us (21%)
  starting transfers between devices  55.7 us (18%)
  matrix products  23.8 us (8%)
  between operations  15.9 us (5%)
  local copies, waits for them, and re-layouts  11.5 us (4%)
  other arithmetic  11.3 us (4%)
    psum x3, blocking collectives, squares(): lax.psum(jnp.sum(remainder_grid * remainder_grid, axis=(1, 2, 3)), ('xy',...  56.4 us
    psum x1, blocking collectives, local(): grad_filter = lax.psum(filter_part, ('xy', 'gz'))  37.5 us
    psum x2, blocking collectives, local(): lax.psum(jnp.sum(direction * picture_pixels_flat, axis=(1, 2, 3)), ('xy',...  34.5 us
    ppermute x10, starting transfers between devices, with_halo(): lax.ppermute(tail, axis, [(i, (i + 1) % count) for i in range(ends)])  32.9 us
    ppermute x10, waiting for transfers between devices, with_halo(): lax.ppermute(head, axis, [((i + 1) % count, i) for i in range(ends)])  20.9 us
    psum x1, waiting for transfers between devices, local(): lax.psum(correlate(own_filt, own_wide, rows_x, rows_z, rows_y).astype(jnp...  20.3 us
    psum x1, waiting for transfers between devices, local(): edge_grad = lax.psum(jnp.stack(partial_grads), 'lab')  17.7 us
    ppermute x10, starting transfers between devices, with_halo(): lax.ppermute(head, axis, [((i + 1) % count, i) for i in range(ends)])  12.9 us
  transfers between devices with their start and end apart: 26, of which 11 were waited for; matrix products, arithmetic and copies ran while one was open for 4% of the time, Pallas kernels for 0%

commit v1 on v0

v1 whole, which is shorter than its diff:
```python
import jax
import jax.numpy as jnp
from jax import lax
from jax.sharding import PartitionSpec as P

HALO = 4
SEED = 64.0
SPREAD = 6.3


def pair_routes(count, phase):
    route = []
    for low in range(phase, count - 1, 2):
        route += [(low, low + 1), (low + 1, low)]
    return route


def swap(block, axis, phase):
    return lax.ppermute(block, axis, pair_routes(lax.axis_size(axis), phase))


def neighbours(upward, downward, axis):
    even = lax.axis_index(axis) % 2 == 0
    first = swap(jnp.where(even, upward, downward), axis, 0)
    if lax.axis_size(axis) > 2:
        second = swap(jnp.where(even, downward, upward), axis, 1)
    else:
        second = jnp.zeros_like(first)
    return jnp.where(even, first, second), jnp.where(even, second, first)


def shared_neighbours(upward, downward, axis):
    count = lax.axis_size(axis)
    lab_count = lax.axis_size("lab")
    route = [
        (src * lab_count + lab, dst * lab_count + lab)
        for lab in range(lab_count)
        for src, dst in pair_routes(count, lab % 2)
    ]
    up = (lax.axis_index(axis) + lax.axis_index("lab")) % 2 == 0
    mine = lax.ppermute(jnp.where(up, upward, downward), (axis, "lab"), route)
    other = lax.ppermute(mine, "lab", [(0, 1), (1, 0)])
    return jnp.where(up, mine, other), jnp.where(up, other, mine)


def offsets():
    return [(i, j, k) for i in range(3) for j in range(3) for k in range(3)]


def total(part, axes):
    count = 1
    for axis in axes:
        count *= lax.axis_size(axis)
    copies = jnp.broadcast_to(part[None], (count,) + part.shape)
    return jnp.sum(lax.all_to_all(copies, axes, 0, 0), axis=0)


def up(field, dim):
    return jnp.roll(field, -1, dim)


def down(field, dim):
    return jnp.roll(field, 1, dim)


def wrap(own, above, below, dim):
    return jnp.concatenate([own, above, below], axis=dim)


def local(image, filt, planted, likelihoods, loss_slope):
    channels = image.shape[0]
    labels, rows_x, rows_z, rows_y = likelihoods.shape
    lab = lax.axis_index("lab")
    colour_count = labels * lax.axis_size("lab")
    bf16, f32 = jnp.bfloat16, jnp.float32
    own_filt = lax.dynamic_slice_in_dim(filt, lab * channels, channels, 1)
    free = (planted >= colour_count)[None]
    colours = lab * labels + jnp.arange(labels, dtype=jnp.int32)
    member = (planted[None] == colours[:, None, None, None]).astype(f32)
    full = free.astype(f32) * likelihoods + member
    rhs = jnp.where(free, loss_slope, SEED)

    def grow(own, width, axis, dim):
        size = own.shape[dim]
        last = lax.slice_in_dim(own, size - width, size, axis=dim)
        first = lax.slice_in_dim(own, 0, width, axis=dim)
        return last, first

    def exchange(fields, axis, dim):
        shapes, ups, downs = [], [], []
        for own, width in fields:
            last, first = grow(own.astype(bf16), width, axis, dim)
            shapes.append(last.shape)
            ups.append(last.reshape(-1, rows_y))
            downs.append(first.reshape(-1, rows_y))
        above, below = neighbours(jnp.concatenate(ups), jnp.concatenate(downs), axis)
        out, at = [], 0
        for (own, width), shape in zip(fields, shapes):
            rows = 1
            for n in shape[:-1]:
                rows *= n
            out.append(
                wrap(
                    own,
                    above[at : at + rows].reshape(shape).astype(own.dtype),
                    below[at : at + rows].reshape(shape).astype(own.dtype),
                    dim,
                )
            )
            at += rows
        return out

    image_z, rhs_z, full_z = exchange([(image, 1), (rhs, HALO), (full, 2)], "gz", 2)
    image_w, rhs_w, full_w = exchange([(image_z, 1), (rhs_z, HALO), (full_z, 2)], "xy", 1)

    def window(field, i, j, k):
        shifted = jnp.roll(field, (1 - i, 1 - j), (1, 2))[:, :rows_x, :rows_z]
        padded = jnp.pad(shifted, ((0, 0), (0, 0), (0, 0), (1, 1)))
        return padded[..., k : k + rows_y]

    part = jnp.zeros((3, rows_x, rows_z, rows_y), f32)
    for i, j, k in offsets():
        part = part + jnp.einsum(
            "dc,cxzy->dxzy", own_filt[:, :, i, j, k], window(image_w, i, j, k), preferred_element_type=f32
        )
    logits = part + lax.ppermute(part, "lab", [(0, 1), (1, 0)])

    last, first = grow(logits.astype(bf16), HALO, "gz", 2)
    above, below = neighbours(last, first, "gz")
    logits_z = wrap(logits, above.astype(f32), below.astype(f32), 2)
    last, first = grow(logits_z.astype(bf16), HALO, "xy", 1)
    above, below = shared_neighbours(last, first, "xy")
    logits_w = wrap(logits_z, above.astype(f32), below.astype(f32), 1)

    def place(rows, axis):
        i = jnp.arange(rows + 2 * HALO, dtype=jnp.int32)
        i = jnp.where(i < rows + HALO, i, i - rows - 2 * HALO)
        return i + lax.axis_index(axis) * rows, rows * lax.axis_size(axis)

    at_x, size_x = place(rows_x, "xy")
    at_z, size_z = place(rows_z, "gz")
    at_y = jnp.arange(rows_y, dtype=jnp.int32)
    in_x, in_z = (at_x >= 0) & (at_x < size_x), (at_z >= 0) & (at_z < size_z)
    next_x, next_z = (at_x >= 0) & (at_x < size_x - 1), (at_z >= 0) & (at_z < size_z - 1)
    next_y = at_y < rows_y - 1
    valid = jnp.stack(
        [
            next_x[:, None, None] & in_z[None, :, None] & jnp.ones((1, 1, rows_y), bool),
            in_x[:, None, None] & next_z[None, :, None] & jnp.ones((1, 1, rows_y), bool),
            in_x[:, None, None] & in_z[None, :, None] & next_y[None, None, :],
        ]
    ).astype(f32)
    squashed = jax.nn.sigmoid(logits_w)
    weight = (0.05 + squashed) * valid
    free_w = (rhs_w < SEED / 2).astype(f32)
    v0 = rhs_w * free_w
    fw = free_w[0]

    def operate(v):
        out = 0.0
        for d in range(3):
            flow = weight[d] * (v - up(v, d + 1))
            out = out + flow - down(flow, d + 1)
        return fw * out

    v1 = operate(v0) * (1.0 / SPREAD) - v0
    v2 = 2.0 * (operate(v1) * (1.0 / SPREAD) - v1) - v0
    av2 = operate(v2)

    def dot(a, b):
        return jnp.sum((a * b)[:, :rows_x, :rows_z], axis=(1, 2, 3))

    dots = jnp.stack([dot(v0, v0), dot(v0, v1), dot(v1, v1), dot(v1, v2), dot(v2, v2), dot(v2, av2)])
    dots = jnp.pad(dots, ((0, 2), (0, 128 - labels)))
    g00, g01, g11, g12, g22, k22 = total(dots, ("xy", "gz"))[:6, :labels]
    g02 = 2.0 * g11 - g00
    k00 = SPREAD * (g00 + g01)
    k01 = SPREAD * (g01 + g11)
    k02 = SPREAD * (g02 + g12)
    k11 = SPREAD * (g11 + 0.5 * (g12 + g01))
    k12 = SPREAD * (g12 + 0.5 * (g22 + g02))
    alpha = g00 / k00
    c0 = alpha
    r0 = 1.0 - alpha * SPREAD
    r1 = -alpha * SPREAD
    rr = r0 * r0 * g00 + 2.0 * r0 * r1 * g01 + r1 * r1 * g11
    beta = rr / g00
    p0, p1 = r0 + beta, r1
    alpha = rr / (p0 * p0 * k00 + 2.0 * p0 * p1 * k01 + p1 * p1 * k11)
    c0, c1 = c0 + alpha * p0, alpha * p1
    r0 = r0 - alpha * SPREAD * (p0 + 0.5 * p1)
    r1 = r1 - alpha * SPREAD * (p0 + p1)
    r2 = -alpha * SPREAD * 0.5 * p1
    rr_next = (
        r0 * r0 * g00 + r1 * r1 * g11 + r2 * r2 * g22 + 2.0 * (r0 * r1 * g01 + r0 * r2 * g02 + r1 * r2 * g12)
    )
    beta = rr_next / rr
    p0, p1, p2 = r0 + beta * p0, r1 + beta * p1, r2
    alpha = rr_next / (
        p0 * p0 * k00 + p1 * p1 * k11 + p2 * p2 * k22 + 2.0 * (p0 * p1 * k01 + p0 * p2 * k02 + p1 * p2 * k12)
    )
    c0, c1, c2 = c0 + alpha * p0, c1 + alpha * p1, alpha * p2
    spread = lambda c: c[:, None, None, None]
    lam = spread(c0) * v0 + spread(c1) * v1 + spread(c2) * v2

    def ring(field, dim, rows, width):
        size = field.shape[dim]
        return jnp.concatenate(
            [
                lax.slice_in_dim(field, 0, rows + width, axis=dim),
                lax.slice_in_dim(field, size - width, size, axis=dim),
            ],
            axis=dim,
        )

    def narrow(field, width):
        return ring(ring(field, 1, rows_x, width), 2, rows_z, width)

    lam = narrow(lam, 2)
    parts = []
    for d in range(3):
        parts.append(-jnp.sum((lam - up(lam, d + 1)) * (full_w - up(full_w, d + 1)), axis=0))
    edge = jnp.stack(parts)
    edge = edge + lax.ppermute(edge, "lab", [(0, 1), (1, 0)])
    s = narrow(squashed, 2)
    logit_grad = (edge * s * (1.0 - s) * narrow(valid, 2)).astype(bf16)

    grad_image = jnp.zeros((channels, rows_x, rows_z, rows_y), f32)
    terms = []
    own_grad = logit_grad[:, :rows_x, :rows_z]
    for i, j, k in offsets():
        grad_image = grad_image + jnp.einsum(
            "dc,dxzy->cxzy",
            own_filt[:, :, i, j, k],
            window(logit_grad, 2 - i, 2 - j, 2 - k),
            preferred_element_type=f32,
        )
        terms.append(
            jnp.einsum("dxzy,cxzy->dc", own_grad, window(image_w, i, j, k), preferred_element_type=f32)
        )
    part = jnp.stack(terms, axis=-1).reshape(3 * channels, 27)
    part = jnp.pad(part, ((0, 0), (0, 128 - 27)))
    grad_filter = total(part, ("xy", "gz"))[:, :27].reshape(3, channels, 3, 3, 3)
    return grad_image.astype(bf16), grad_filter


def solution(mesh):
    return jax.shard_map(
        local,
        mesh=mesh,
        in_specs=(
            P("lab", ("crops", "xy"), "gz", None),
            P(),
            P(("crops", "xy"), "gz", None),
            P("lab", ("crops", "xy"), "gz", None),
            P("lab", ("crops", "xy"), "gz", None),
        ),
        out_specs=(P("lab", ("crops", "xy"), "gz", None), P("crops", "lab", None, None, None)),
        check_vma=False,
    )
```

time: 313 us -> 139 us (0.44)
  blocking collectives: 128 us -> 0 us
  waiting for transfers between devices: 65.5 us -> 10.4 us
  local copies, waits for them, and re-layouts: 11.5 us -> 57.9 us
  starting transfers between devices: 55.7 us -> 21.4 us
  between operations: 15.9 us -> 2.84 us
  other arithmetic: 11.3 us -> 19.9 us
    psum x6 -> x0, blocking collectives: 128 us -> none  [the longest x3 56.4 us: squares(): lax.psum(jnp.sum(remainder_grid * remainder_grid, axis=(1, 2, 3)), ('xy',...]
    ppermute x24 -> x8, starting transfers between devices: 55.6 us -> 12.6 us  [the longest x1 6.68 us: shared_neighbours(): mine = lax.ppermute(jnp.where(up, upward, downward), (axis, 'lab'), route)]
    psum x2 -> x0, waiting for transfers between devices: 38.1 us -> none  [the longest x1 20.3 us: local(): lax.psum(correlate(own_filt, own_wide, rows_x, rows_z, rows_y).astype(jnp...]
    unnamed x181 -> x250, local copies, waits for them, and re-layouts: 9.6 us -> 36.9 us
    ppermute x24 -> x8, waiting for transfers between devices: 27.4 us -> 7.54 us  [the longest x4 4.79 us: swap(): return lax.ppermute(block, axis, pair_routes(lax.axis_size(axis), phase))]
    slice x16 -> x70, local copies, waits for them, and re-layouts: 1.58 us -> 13.6 us  [the longest x23 8.11 us: up(): return jnp.roll(field, -1, dim)]
    all_to_all x0 -> x2, starting transfers between devices: none -> 8.86 us  [total(): return jnp.sum(lax.all_to_all(copies, axes, 0, 0), axis=0)]
    another operation x3 -> x32, local copies, waits for them, and re-layouts: 0.25 us -> 4.04 us  [the longest x28 2.33 us: local(): part = jnp.stack(terms, axis=-1).reshape(3 * channels, 27)]
  transfers between devices with their start and end apart: 26 -> 10, of which waited for: 11 -> 4; matrix products, arithmetic and copies ran while one was open for 4% -> 19% of each run, Pallas kernels for 0% -> 0%
where the time goes in v1:
time: 139 us; the launch traced here: 137 us
  local copies, waits for them, and re-layouts  57.9 us (42%)
  matrix products  24.5 us (18%)
  starting transfers between devices  21.4 us (15%)
  other arithmetic  19.9 us (14%)
  waiting for transfers between devices  10.4 us (7%)
  between operations  2.84 us (2%)
    unnamed x250, local copies, waits for them, and re-layouts  36.9 us
    all_to_all x2, starting transfers between devices, total(): return jnp.sum(lax.all_to_all(copies, axes, 0, 0), axis=0)  8.86 us
    dot_general x27, matrix products, local(): jnp.einsum('dxzy,cxzy->dc', own_grad, window(image_w, i, j, k), preferred...  8.82 us
    dot_general x27, matrix products, local(): jnp.einsum('dc,dxzy->cxzy', own_filt[:, :, i, j, k], window(logit_grad, 2...  8.75 us
    slice x23, local copies, waits for them, and re-layouts, up(): return jnp.roll(field, -1, dim)  8.11 us
    dot_general x27, matrix products, local(): jnp.einsum('dc,cxzy->dxzy', own_filt[:, :, i, j, k], window(image_w, i, j...  6.97 us
    ppermute x1, starting transfers between devices, shared_neighbours(): mine = lax.ppermute(jnp.where(up, upward, downward), (axis, 'lab'), route)  6.68 us
    ppermute x4, starting transfers between devices, swap(): return lax.ppermute(block, axis, pair_routes(lax.axis_size(axis), phase))  5.75 us
  transfers between devices with their start and end apart: 10, of which 4 were waited for; matrix products, arithmetic and copies ran while one was open for 19% of the time, Pallas kernels for 0%

profile of v1, /device:TPU:0, one launch (start us, length us, event | category | flops | bytes accessed | tf_op | source)
XLA Modules:
  0.0 137.0 jit_solution(10271058351359451493)
XLA Ops:
  0.7 0.9 fusion.276
  1.6 1.2 fusion.274
  3.0 3.0 %collective-permute-start = (bf16[128,128]{1,0:T(8,128)(2,1)S(1)}, bf16[128,128]{1,0:T(8,128)(2,1)S(1)}, u32[]{:S(2)}, u32[]{:S(2)}) collective-permute-start(bf16[128,128]{1,0:T(8,128)(2,1)S(1)} %maximum_select_fusion), channel_id=1, source_target_pairs={{0,2},{2,0},{1,3},{3,1},{4,6},{6,4},{5,7},{7,5},{8,10},{10,8},{9,1... | collective-permute-start | bytes 98312 | tf_op jit(solution)/shard_map/ppermute | solution.py:19
  6.9 1.8 %broadcast_and_fusion = pred[1,12,40,128]{3,0,2,1:T(4,128)(4,1)} fusion(pred[128]{0:T(512)(128)(4,1)S(1)} %iota_compare_fusion.1, pred[12,40]{1,0:T(8,128)(4,1)S(1)} %get-tuple-element.121), kind=kLoop, calls=%fused_computation.192 | loop fusion | flops 61440 | bytes 62048 | tf_op jit(solution)/shard_map/and | solution.py:150
  9.8 1.6 %collective-permute-start.1 = (bf16[1200,128]{1,0:T(8,128)(2,1)S(1)}, bf16[1200,128]{1,0:T(8,128)(2,1)S(1)}, u32[]{:S(2)}, u32[]{:S(2)}) collective-permute-start(bf16[1200,128]{1,0:T(8,128)(2,1)S(1)} %get-tuple-element.48), channel_id=1, source_target_pairs={{0,4},{4,0},{8,12},{12,8},{1,5},{5,1},{9,13},{13,9},{2,6},{6,2},{1... | collective-permute-start | bytes 921608 | tf_op jit(solution)/shard_map/ppermute | solution.py:19
  13.8 4.8 %collective-permute-done.1 = bf16[1200,128]{1,0:T(8,128)(2,1)S(1)} collective-permute-done((bf16[1200,128]{1,0:T(8,128)(2,1)S(1)}, bf16[1200,128]{1,0:T(8,128)(2,1)S(1)}, u32[]{:S(2)}, u32[]{:S(2)}) %collective-permute-start.1) | collective-permute-done | bytes 307232 | tf_op jit(solution)/shard_map/ppermute | solution.py:19
  36.4 1.2 collective-permute-done.3
  39.8 1.3 slice.1255
  41.8 6.7 %collective-permute-start.5 = (bf16[3,4,40,128]{3,0,2,1:T(4,128)(2,1)S(1)}, bf16[3,4,40,128]{3,0,2,1:T(4,128)(2,1)S(1)}, u32[]{:S(2)}, u32[]{:S(2)}) collective-permute-start(bf16[3,4,40,128]{3,0,2,1:T(4,128)(2,1)S(1)} %maximum_convert_fusion.1), channel_id=1, source_target_pairs={{0,4},{4,0},{8,12},{12,8},{5,9},{9,5},{2,6},{6,2},{10,14},{14,10},... | collective-permute-start | bytes 368648 | tf_op jit(solution)/shard_map/ppermute | solution.py:41
  48.5 0.9 slice_convert_fusion.1
  50.1 1.5 %collective-permute-done.5 = bf16[3,4,40,128]{3,0,2,1:T(4,128)(2,1)S(1)} collective-permute-done((bf16[3,4,40,128]{3,0,2,1:T(4,128)(2,1)S(1)}, bf16[3,4,40,128]{3,0,2,1:T(4,128)(2,1)S(1)}, u32[]{:S(2)}, u32[]{:S(2)}) %collective-permute-start.5) | collective-permute-done | bytes 122912 | tf_op jit(solution)/shard_map/ppermute | solution.py:41
  51.6 0.9 slice_convert_fusion
  55.5 2.3 %add_select_fusion = (f32[3,12,40,128]{3,0,2,1:T(4,128)S(1)}, f32[3,12,40,128]{3,0,2,1:T(4,128)}) fusion(pred[1,12,40,128]{3,0,2,1:T(4,128)(4,1)S(1)} %copy-done.46, pred[1,12,40,128]{3,0,2,1:T(4,128)(4,1)S(1)} %stack.123, pred[1,12,40,128]{3,0,2,1:T(4,128)(4,1)S(1)} %stack.122, f32[3,4,40,128]{3,0,2,1:T(4,128)S(1)} %get-tuple-element.57, ...), kind=kLoop, calls=%fused_computation.129 | loop fusion | flops 2027520 | bytes 2396160 | tf_op jit(solution)/shard_map/mul | solution.py:154
  59.4 1.1 copy-done.1
  69.0 5.2 %all-to-all-start = ((f32[8,8,128]{2,1,0:T(8,128)}), f32[8,8,128]{2,1,0:T(8,128)}, u32[]{:S(2)}, u32[]{:S(2)}) async-start(f32[8,8,128]{2,1,0:T(8,128)} %broadcast_in_dim.24), calls=%async_computation | async-start | bytes 65536 | tf_op jit(solution)/shard_map/all_to_all | solution.py:55
  74.2 1.2 pad_maximum_fusion.3
  75.4 1.0 slice.1310
  77.0 1.1 slice.1316
  78.2 2.8 %all-to-all-done = f32[8,8,128]{2,1,0:T(8,128)} async-done(((f32[8,8,128]{2,1,0:T(8,128)}), f32[8,8,128]{2,1,0:T(8,128)}, u32[]{:S(2)}, u32[]{:S(2)}) %all-to-all-start) | async-done | bytes 32800 | tf_op jit(solution)/shard_map/all_to_all | solution.py:55
  82.8 0.9 slice-done.4
  88.6 0.9 fusion.267
  89.7 1.0 copy-done.31
  91.0 0.8 fusion.43
  109.9 3.6 %all-to-all-start.1 = ((f32[8,24,128]{2,1,0:T(8,128)}), f32[8,24,128]{2,1,0:T(8,128)S(1)}, u32[]{:S(2)}, u32[]{:S(2)}) async-start(f32[8,24,128]{2,1,0:T(8,128)} %broadcast_in_dim.25), calls=%async_computation.1 | async-start | bytes 196608 | tf_op jit(solution)/shard_map/all_to_all | solution.py:55
  (521 shorter events, 86.4 us)
Async XLA Ops:
  3.0 5.7 %collective-permute-start = (bf16[128,128]{1,0:T(8,128)(2,1)S(1)}, bf16[128,128]{1,0:T(8,128)(2,1)S(1)}, u32[]{:S(2)}, u32[]{:S(2)}) collective-permute-start(bf16[128,128]{1,0:T(8,128)(2,1)S(1)} %maximum_select_fusion), channel_id=1, source_target_pairs={{0,2},{2,0},{1,3},{3,1},{4,6},{6,4},{5,7},{7,5},{8,10},{10,8},{9,1... | collective-permute-start | bytes 98312 | tf_op jit(solution)/shard_map/ppermute | solution.py:19
  6.2 26.4 %copy-start.9 = (bf16[8,4,32,128]{3,0,2,1:T(8,128)(2,1)}, bf16[8,4,32,128]{3,0,2,1:T(8,128)(2,1)S(1)}, u32[]{:S(2)}) copy-start(bf16[8,4,32,128]{3,0,2,1:T(8,128)(2,1)S(1)} %get-tuple-element.71) | copy-start | bytes 786436
  9.5 26.8 %copy-start.32 = (f32[4,4,4,128]{3,2,1,0:T(4,128)}, f32[4,4,4,128]{3,2,1,0:T(4,128)S(1)}, u32[]{:S(2)}) copy-start(f32[4,4,4,128]{3,2,1,0:T(4,128)S(1)} %convert.10) | copy-start | bytes 98308
  9.5 26.8 %copy-start.36 = (f32[4,4,4,128]{3,2,1,0:T(4,128)}, f32[4,4,4,128]{3,2,1,0:T(4,128)S(1)}, u32[]{:S(2)}) copy-start(f32[4,4,4,128]{3,2,1,0:T(4,128)S(1)} %convert.11) | copy-start | bytes 98308
  9.8 8.8 %collective-permute-start.1 = (bf16[1200,128]{1,0:T(8,128)(2,1)S(1)}, bf16[1200,128]{1,0:T(8,128)(2,1)S(1)}, u32[]{:S(2)}, u32[]{:S(2)}) collective-permute-start(bf16[1200,128]{1,0:T(8,128)(2,1)S(1)} %get-tuple-element.48), channel_id=1, source_target_pairs={{0,4},{4,0},{8,12},{12,8},{1,5},{5,1},{9,13},{13,9},{2,6},{6,2},{1... | collective-permute-start | bytes 921608 | tf_op jit(solution)/shard_map/ppermute | solution.py:19
  11.4 7.2 %collective-permute-start.2 = (bf16[1200,128]{1,0:T(8,128)(2,1)S(1)}, bf16[1200,128]{1,0:T(8,128)(2,1)S(1)}, u32[]{:S(2)}, u32[]{:S(2)}) collective-permute-start(bf16[1200,128]{1,0:T(8,128)(2,1)S(1)} %get-tuple-element.49), channel_id=1, source_target_pairs={{4,8},{8,4},{5,9},{9,5},{6,10},{10,6},{7,11},{11,7},{20,24},{24,20... | collective-permute-start | bytes 921608 | tf_op jit(solution)/shard_map/ppermute | solution.py:19
  13.0 20.6 %copy-start.84 = (bf16[3,8,1,1,1]{1,4,3,2,0:T(2,128)(2,1)}, bf16[3,8,1,1,1]{1,4,3,2,0:T(2,128)(2,1)S(1)}, u32[]{:S(2)}) copy-start(bf16[3,8,1,1,1]{1,4,3,2,0:T(2,128)(2,1)S(1)} %get-tuple-element.95) | copy-start | bytes 148
  13.0 20.9 %copy-start.82 = (bf16[3,8,1,1,1]{1,4,3,2,0:T(2,128)(2,1)}, bf16[3,8,1,1,1]{1,4,3,2,0:T(2,128)(2,1)S(1)}, u32[]{:S(2)}) copy-start(bf16[3,8,1,1,1]{1,4,3,2,0:T(2,128)(2,1)S(1)} %get-tuple-element.94) | copy-start | bytes 148
  13.0 21.1 %copy-start.80 = (bf16[3,8,1,1,1]{1,4,3,2,0:T(2,128)(2,1)}, bf16[3,8,1,1,1]{1,4,3,2,0:T(2,128)(2,1)S(1)}, u32[]{:S(2)}) copy-start(bf16[3,8,1,1,1]{1,4,3,2,0:T(2,128)(2,1)S(1)} %get-tuple-element.93) | copy-start | bytes 148
  13.0 21.4 %copy-start.78 = (bf16[3,8,1,1,1]{1,4,3,2,0:T(2,128)(2,1)}, bf16[3,8,1,1,1]{1,4,3,2,0:T(2,128)(2,1)S(1)}, u32[]{:S(2)}) copy-start(bf16[3,8,1,1,1]{1,4,3,2,0:T(2,128)(2,1)S(1)} %get-tuple-element.92) | copy-start | bytes 148
  13.0 21.7 %copy-start.76 = (bf16[3,8,1,1,1]{1,4,3,2,0:T(2,128)(2,1)}, bf16[3,8,1,1,1]{1,4,3,2,0:T(2,128)(2,1)S(1)}, u32[]{:S(2)}) copy-start(bf16[3,8,1,1,1]{1,4,3,2,0:T(2,128)(2,1)S(1)} %get-tuple-element.91) | copy-start | bytes 148
  13.0 21.9 %copy-start.74 = (bf16[3,8,1,1,1]{1,4,3,2,0:T(2,128)(2,1)}, bf16[3,8,1,1,1]{1,4,3,2,0:T(2,128)(2,1)S(1)}, u32[]{:S(2)}) copy-start(bf16[3,8,1,1,1]{1,4,3,2,0:T(2,128)(2,1)S(1)} %get-tuple-element.90) | copy-start | bytes 148
  13.1 22.2 %copy-start.72 = (bf16[3,8,1,1,1]{1,4,3,2,0:T(2,128)(2,1)}, bf16[3,8,1,1,1]{1,4,3,2,0:T(2,128)(2,1)S(1)}, u32[]{:S(2)}) copy-start(bf16[3,8,1,1,1]{1,4,3,2,0:T(2,128)(2,1)S(1)} %get-tuple-element.89) | copy-start | bytes 148
  13.1 22.5 %copy-start.70 = (bf16[3,8,1,1,1]{1,4,3,2,0:T(2,128)(2,1)}, bf16[3,8,1,1,1]{1,4,3,2,0:T(2,128)(2,1)S(1)}, u32[]{:S(2)}) copy-start(bf16[3,8,1,1,1]{1,4,3,2,0:T(2,128)(2,1)S(1)} %get-tuple-element.88) | copy-start | bytes 148
  13.1 22.7 %copy-start.68 = (bf16[3,8,1,1,1]{1,4,3,2,0:T(2,128)(2,1)}, bf16[3,8,1,1,1]{1,4,3,2,0:T(2,128)(2,1)S(1)}, u32[]{:S(2)}) copy-start(bf16[3,8,1,1,1]{1,4,3,2,0:T(2,128)(2,1)S(1)} %get-tuple-element.87) | copy-start | bytes 148
  36.1 1.6 %collective-permute-start.3 = (f32[3,4,32,128]{3,0,2,1:T(4,128)S(1)}, f32[3,4,32,128]{3,0,2,1:T(4,128)S(1)}, u32[]{:S(2)}, u32[]{:S(2)}) collective-permute-start(f32[3,4,32,128]{3,0,2,1:T(4,128)S(1)} %convolution_add_fusion.26), channel_id=1, source_target_pairs={{0,1},{1,0},{2,3},{3,2},{4,5},{5,4},{6,7},{7,6},{8,9},{9,8},{10,11... | collective-permute-start | bytes 589832 | tf_op jit(solution)/shard_map/ppermute | solution.py:126
  36.2 25.2 %copy-start.2 = (f32[4,4,40,128]{3,2,1,0:T(8,128)}, f32[4,4,40,128]{3,2,1,0:T(8,128)S(1)}, u32[]{:S(2)}) copy-start(f32[4,4,40,128]{3,2,1,0:T(8,128)S(1)} %convert.15) | copy-start | bytes 983044
  37.8 3.9 %collective-permute-start.4 = (bf16[3,4,4,128]{3,0,2,1:T(4,128)(2,1)S(1)}, bf16[3,4,4,128]{3,0,2,1:T(4,128)(2,1)S(1)}, u32[]{:S(2)}, u32[]{:S(2)}) collective-permute-start(bf16[3,4,4,128]{3,0,2,1:T(4,128)(2,1)S(1)} %slice_select_fusion), channel_id=1, source_target_pairs={{0,2},{2,0},{1,3},{3,1},{4,6},{6,4},{5,7},{7,5},{8,10},{10,8},{9,1... | collective-permute-start | bytes 36872 | tf_op jit(solution)/shard_map/ppermute | solution.py:19
  41.8 9.8 %collective-permute-start.5 = (bf16[3,4,40,128]{3,0,2,1:T(4,128)(2,1)S(1)}, bf16[3,4,40,128]{3,0,2,1:T(4,128)(2,1)S(1)}, u32[]{:S(2)}, u32[]{:S(2)}) collective-permute-start(bf16[3,4,40,128]{3,0,2,1:T(4,128)(2,1)S(1)} %maximum_convert_fusion.1), channel_id=1, source_target_pairs={{0,4},{4,0},{8,12},{12,8},{5,9},{9,5},{2,6},{6,2},{10,14},{14,10},... | collective-permute-start | bytes 368648 | tf_op jit(solution)/shard_map/ppermute | solution.py:41
  51.6 1.6 %collective-permute-start.6 = (bf16[3,4,40,128]{3,0,2,1:T(4,128)(2,1)S(1)}, bf16[3,4,40,128]{3,0,2,1:T(4,128)(2,1)S(1)}, u32[]{:S(2)}, u32[]{:S(2)}) collective-permute-start(bf16[3,4,40,128]{3,0,2,1:T(4,128)(2,1)S(1)} %collective-permute-done.5), channel_id=1, source_target_pairs={{0,1},{1,0},{2,3},{3,2},{4,5},{5,4},{6,7},{7,6},{8,9},{9,8},{10,11... | collective-permute-start | bytes 368648 | tf_op jit(solution)/shard_map/ppermute | solution.py:42
  69.0 12.0 %all-to-all-start = ((f32[8,8,128]{2,1,0:T(8,128)}), f32[8,8,128]{2,1,0:T(8,128)}, u32[]{:S(2)}, u32[]{:S(2)}) async-start(f32[8,8,128]{2,1,0:T(8,128)} %broadcast_in_dim.24), calls=%async_computation | async-start | bytes 65536 | tf_op jit(solution)/shard_map/all_to_all | solution.py:55
  87.6 3.4 %collective-permute-start.7 = (f32[3,8,36,128]{3,1,2,0:T(8,128)S(1)}, f32[3,8,36,128]{3,1,2,0:T(8,128)S(1)}, u32[]{:S(2)}, u32[]{:S(2)}) collective-permute-start(f32[3,8,36,128]{3,1,2,0:T(8,128)S(1)} %copy.112), channel_id=1, source_target_pairs={{0,1},{1,0},{2,3},{3,2},{4,5},{5,4},{6,7},{7,6},{8,9},{9,8},{10,11... | collective-permute-start | bytes 1327112 | tf_op jit(solution)/shard_map/ppermute | solution.py:224
  91.9 32.3 %copy-start.4 = (bf16[3,8,36,128]{3,0,2,1:T(4,128)(2,1)}, bf16[3,8,36,128]{3,0,2,1:T(4,128)(2,1)S(1)}, u32[]{:S(2)}) copy-start(bf16[3,8,36,128]{3,0,2,1:T(4,128)(2,1)S(1)} %fusion.43) | copy-start | bytes 663556
  109.9 26.3 %all-to-all-start.1 = ((f32[8,24,128]{2,1,0:T(8,128)}), f32[8,24,128]{2,1,0:T(8,128)S(1)}, u32[]{:S(2)}, u32[]{:S(2)}) async-start(f32[8,24,128]{2,1,0:T(8,128)} %broadcast_in_dim.25), calls=%async_computation.1 | async-start | bytes 196608 | tf_op jit(solution)/shard_map/all_to_all | solution.py:55
  (114 other events, 311.3 us)

commit v2 on v1

v2 whole, which is shorter than its diff:
```python
import functools

import jax
import jax.numpy as jnp
from jax import lax
from jax.experimental import pallas as pl
from jax.experimental.pallas import tpu as pltpu
from jax.sharding import PartitionSpec as P

HALO = 4
SEED = 64.0
SPREAD = 6.3
TILE = 8
LANES = 128
BF16, F32 = jnp.bfloat16, jnp.float32
EVEN_X, EVEN_Z, FIRST_X, FIRST_Z, COLOUR, UP = range(6)


def pair_routes(count, phase):
    route = []
    for low in range(phase, count - 1, 2):
        route += [(low, low + 1), (low + 1, low)]
    return route


def swap(block, axis, phase):
    return lax.ppermute(block, axis, pair_routes(lax.axis_size(axis), phase))


def lab_swap(block):
    return lax.ppermute(block, "lab", [(0, 1), (1, 0)])


def split_swap(block, axis):
    labs = lax.axis_size("lab")
    route = [
        (src * labs + lab, dst * labs + lab)
        for lab in range(labs)
        for src, dst in pair_routes(lax.axis_size(axis), lab % 2)
    ]
    return lax.ppermute(block, (axis, "lab"), route)


def everyones(part, axes):
    count = 1
    for axis in axes:
        count *= lax.axis_size(axis)
    return lax.all_to_all(jnp.broadcast_to(part[None], (count,) + part.shape), axes, 0, 0)


def call(kernel, outs, *ins, scratch=(), flops=1_000_000, name=None):
    specs = [pl.BlockSpec(memory_space=pltpu.SMEM)]
    specs += [pl.BlockSpec(memory_space=pltpu.VMEM)] * (len(ins) - 1)
    bytes_moved = sum(a.size * a.dtype.itemsize for a in ins)
    return pl.pallas_call(
        kernel,
        out_shape=outs,
        in_specs=specs,
        out_specs=jax.tree.map(lambda _: pl.BlockSpec(memory_space=pltpu.VMEM), outs),
        scratch_shapes=list(scratch),
        compiler_params=pltpu.CompilerParams(vmem_limit_bytes=40 * 2**20),
        cost_estimate=pl.CostEstimate(flops=flops, bytes_accessed=bytes_moved, transcendentals=0),
        name=name,
    )(*ins)


def shaped(shape, dtype):
    return jax.ShapeDtypeStruct(shape, dtype)


def rows_iota(rows=TILE):
    return lax.broadcasted_iota(jnp.int32, (rows, LANES), 0)


def lanes_iota(rows=TILE):
    return lax.broadcasted_iota(jnp.int32, (rows, LANES), 1)


def fields(planted, likelihood, slope, colours, colour):
    free = planted >= colours
    member = jnp.where(planted == colour, 1.0, 0.0)
    return jnp.where(free, slope, SEED), jnp.where(free, likelihood, member)


def pack_z(colours, flip, info, image, planted, likelihoods, slope, out):
    labels, rows_x, rows_z, _ = likelihoods.shape
    even = info[EVEN_Z] != flip
    place = (rows_iota() + jnp.where(even, 0, 4)) & 7
    last, first = slice(rows_z - TILE, rows_z), slice(0, TILE)

    def at_end(ref, *lead):
        return jnp.where(even, ref[(*lead, last)].astype(ref.dtype), ref[(*lead, first)])

    def channel(c, x):
        return jnp.where(even, image[c, x, last].astype(F32), image[c, x, first].astype(F32))

    def turned(tile, for_even, for_odd):
        return jnp.where(even, pltpu.roll(tile, for_even, 0), pltpu.roll(tile, for_odd, 0))

    for x in range(rows_x):
        seeds = at_end(planted, x)
        for l in range(labels):
            rhs, full = fields(seeds, at_end(likelihoods, l, x), at_end(slope, l, x), colours, info[COLOUR] + l)
            first_channel = turned(channel(2 * l, x), 3, 6)
            second_channel = turned(channel(2 * l + 1, x), 4, 7)
            rest = jnp.where(place == 2, first_channel, second_channel)
            rest = jnp.where(place < 2, turned(full, 2, 4), rest)
            out[x, l] = jnp.where(place >= 4, rhs, rest).astype(BF16)


def sides(even, first, second):
    if second is None:
        return jnp.where(even, first, 0.0), jnp.where(even, 0.0, first)
    return jnp.where(even, first, second), jnp.where(even, second, first)


def assemble_z(colours, two, info, *refs):
    first_z = refs[0]
    second_z = refs[1] if two else None
    image, planted, likelihoods, slope, rhs_out, full_out, image_out, send_a, send_b = refs[1 + two :]
    labels, rows_x, rows_z, _ = likelihoods.shape
    channels = image.shape[0]
    upper = rows_iota() < 4
    for x in range(rows_x):
        for l in range(labels):
            rhs, full = fields(planted[x], likelihoods[l, x], slope[l, x], colours, info[COLOUR] + l)
            above, below = sides(
                info[EVEN_Z] == 1,
                first_z[x, l].astype(F32),
                second_z[x, l].astype(F32) if two else None,
            )
            rhs = jnp.concatenate([rhs, jnp.where(upper, above, below)], axis=0)
            full_tile = jnp.where(upper, pltpu.roll(above, 4, 0), pltpu.roll(below, 6, 0))
            rhs_out[l, x] = rhs
            full_out[l, x] = jnp.concatenate([full, full_tile], axis=0)
            plane = channels + l * rows_x + x
            send_a[plane] = rhs.astype(BF16)
            send_b[plane] = rhs.astype(BF16)
            for c, up, down in ((2 * l, 2, 5), (2 * l + 1, 1, 4)):
                tile = jnp.where(upper, pltpu.roll(above, up, 0), pltpu.roll(below, down, 0))
                image_out[c, x] = jnp.concatenate([image[c, x].astype(F32), tile], axis=0).astype(BF16)
    even = info[EVEN_X] == 1
    high, low = jnp.where(even, rows_x - 1, 0), jnp.where(even, 0, rows_x - 1)
    for c in range(channels):
        send_a[c] = image_out[c, high]
        send_b[c] = image_out[c, low]
    high, low = jnp.where(even, rows_x - 2, 0), jnp.where(even, 0, rows_x - 2)
    for l in range(labels):
        for r in range(2):
            plane = channels + labels * rows_x + 2 * l + r
            send_a[plane] = full_out[l, high + r].astype(BF16)
            send_b[plane] = full_out[l, low + r].astype(BF16)


def band(half, j, o, transposed=False):
    z, lane = rows_iota(), lanes_iota()
    other = lane & 7
    at = (z + 1 - other - 8 * o) if transposed else (other + 8 * o - z + 1)
    mask = at == j
    if half is not None:
        mask = mask & ((lane >> 6) == half)
    return mask


def bands(o, transposed=False):
    if o == 0:
        return (0, 1, 2)
    return (0,) if (o < 0) != transposed else (2,)


def spread_filter(info, first, second, one, two, wide_out, back_out):
    wide = jnp.dot(first[...], one[...], preferred_element_type=F32)
    back = jnp.dot(second[...], two[...], preferred_element_type=F32)
    zero = jnp.zeros((TILE, LANES), F32)
    for o in (-1, 0, 1):
        masks = {(h, j): band(h, j, o) for h in range(2) for j in bands(o)}
        for kd in range(9):
            for pair in range(2):
                for block in range(3):
                    tiles = []
                    for x in (2 * pair, 2 * pair + 1):
                        tile = zero
                        for i in range(3):
                            if (x + i) // 2 == block:
                                for j in bands(o):
                                    row = kd * 9 + i * 3 + j
                                    value = jnp.broadcast_to(wide[row : row + 1], (TILE, LANES))
                                    tile = jnp.where(masks[(x + i) % 2, j], value, tile)
                        tiles.append(tile)
                    at = (kd * 4 + 2 * pair) * TILE
                    wide_out[o + 1, at : at + 16, block * LANES : (block + 1) * LANES] = jnp.concatenate(
                        tiles, axis=0
                    ).astype(BF16)
        masks = {j: band(None, j, o, True) for j in bands(o, True)}
        for c in range(8):
            for pair in range(2):
                for block in range(6):
                    tiles = []
                    for x in (2 * pair, 2 * pair + 1):
                        tile = zero
                        i = x + 2 - block
                        if 0 <= i < 3:
                            for j in bands(o, True):
                                row = c * 9 + i * 3 + j
                                value = jnp.broadcast_to(back[row : row + 1], (TILE, LANES))
                                tile = jnp.where(masks[j], value, tile)
                        tiles.append(tile)
                    at = (c * 4 + 2 * pair) * TILE
                    back_out[o + 1, at : at + 16, block * LANES : (block + 1) * LANES] = jnp.concatenate(
                        tiles, axis=0
                    ).astype(BF16)


def tile_rows(t):
    at = (4 if t < 0 else t) * TILE
    return slice(at, at + TILE)


def convolve(info, image, first, second, matrix, part, stack, sums):
    channels, rows_x = image.shape[0], image.shape[1]
    even = info[EVEN_X] == 1
    for xp in range(rows_x + 2):
        for c in range(0, channels, 2):
            planes = []
            for ch in (c, c + 1):
                if 0 < xp <= rows_x:
                    planes.append(image[ch, xp - 1].astype(F32))
                else:
                    above, below = sides(even, first[ch].astype(F32), second[ch].astype(F32))
                    planes.append(below if xp == 0 else above)
            at = (xp * channels + c) * TILE
            for t in range(-1, 5):
                both = jnp.concatenate([plane[tile_rows(t)] for plane in planes], axis=0)
                stack[at : at + 16, (t + 1) * LANES : (t + 2) * LANES] = both.astype(BF16)
    total = jnp.dot(matrix[0], stack[:, 0:512], preferred_element_type=F32)
    total = total + jnp.dot(matrix[1], stack[:, 128:640], preferred_element_type=F32)
    sums[...] = total + jnp.dot(matrix[2], stack[:, 256:768], preferred_element_type=F32)
    lane = lanes_iota()
    for d in range(3):
        for x in range(rows_x):
            for t in range(4):
                cols = slice(t * LANES, (t + 1) * LANES)

                def piece(k):
                    at = ((k * 3 + d) * rows_x + x) * TILE
                    return sums[at : at + TILE, cols]

                before = jnp.where(lane > 0, pltpu.roll(piece(0), 1, 1), 0.0)
                after = jnp.where(lane < LANES - 1, pltpu.roll(piece(2), LANES - 1, 1), 0.0)
                part[d, x, tile_rows(t)] = piece(1) + before + after


def add_parts(two, info, part, other, logits, send_a, *send_b):
    rows_x, rows_z = part.shape[1], part.shape[2]
    even = info[EVEN_Z] == 1
    for d in range(3):
        for x in range(rows_x):
            total = part[d, x] + other[d, x]
            logits[d, x] = total
            first, last = total[:TILE], total[rows_z - TILE :]
            send_a[d, x] = jnp.where(even, last, first).astype(BF16)
            if two:
                send_b[0][d, x] = jnp.where(even, first, last).astype(BF16)


def extend_logits(two, info, logits, first, *refs):
    second = refs[0] if two else None
    out = refs[-1]
    upper = rows_iota() < 4
    for d in range(3):
        for x in range(logits.shape[1]):
            above, below = sides(
                info[EVEN_Z] == 1, first[d, x].astype(F32), second[d, x].astype(F32) if two else None
            )
            tile = jnp.where(upper, above, below)
            out[d, x] = jnp.concatenate([logits[d, x], tile], axis=0).astype(BF16)


def up(plane, dim):
    return pltpu.roll(plane, plane.shape[dim] - 1, dim)


def down(plane, dim):
    return pltpu.roll(plane, 1, dim)


def krylov(
    size_x, size_z, info, logits, own, mine, other, rhs, first, second, v0, v1, v2, slope_out, dots, weight, free
):
    labels, rows_x, rows, _ = rhs.shape
    rows_z = rows - TILE
    channels = 2 * labels
    is_up, even = info[UP] == 1, info[EVEN_X] == 1
    z = rows_iota(rows)
    z = info[FIRST_Z] + jnp.where(z < rows_z + HALO, z, z - rows)
    inside_z = (z >= 0) & (z < size_z)
    in_z = jnp.where(inside_z, 1.0, 0.0)
    next_z = jnp.where(inside_z & (z < size_z - 1), 1.0, 0.0)
    in_zy = jnp.where(lanes_iota(rows) < LANES - 1, in_z, 0.0)
    for at in range(rows_x + 2 * HALO):
        x = at - HALO
        place = info[FIRST_X] + x
        inside = (place >= 0) & (place < size_x)
        in_x = jnp.where(inside, 1.0, 0.0)
        next_x = jnp.where(inside & (place < size_x - 1), 1.0, 0.0)
        for d in range(3):
            if 0 <= x < rows_x:
                plane = jnp.concatenate([logits[d, x], own[d, x, rows_z:].astype(F32)], axis=0)
            elif x < 0:
                plane = jnp.where(is_up, other[d, x + HALO].astype(F32), mine[d, x + HALO].astype(F32))
            else:
                plane = jnp.where(is_up, mine[d, x - rows_x].astype(F32), other[d, x - rows_x].astype(F32))
            squashed = 1.0 / (1.0 + jnp.exp(-plane))
            valid = (in_z * next_x, next_z * in_x, in_zy * in_x)[d]
            weight[d, at] = (0.05 + squashed) * valid
            if -1 <= x <= rows_x:
                slope_out[d, x + 1] = squashed * (1.0 - squashed) * valid
        for l in range(labels):
            if 0 <= x < rows_x:
                plane = rhs[l, x]
            else:
                index = channels + l * rows_x + (x + HALO if x < 0 else x - rows_x)
                above, below = sides(even, first[index].astype(F32), second[index].astype(F32))
                plane = below if x < 0 else above
            open_cell = plane < SEED / 2
            v0[l, at] = jnp.where(open_cell, plane, 0.0)
            if l == 0:
                free[at] = jnp.where(open_cell, 1.0, 0.0)

    def label(l, carry):
        def operate(v, start, stop):
            flow_before = weight[0, start - 1] * (v[l, start - 1] - v[l, start])
            for at in range(start, stop):
                here = v[l, at]
                flow = weight[0, at] * (here - v[l, at + 1])
                flow_z = weight[1, at] * (here - up(here, 0))
                flow_y = weight[2, at] * (here - up(here, 1))
                result = flow - flow_before + (flow_z - down(flow_z, 0)) + (flow_y - down(flow_y, 1))
                yield at, here, free[at] * result
                flow_before = flow

        for at, here, result in operate(v0, 1, rows_x + 2 * HALO - 1):
            v1[l, at] = result * (1.0 / SPREAD) - here
        for at, here, result in operate(v1, 2, rows_x + 2 * HALO - 2):
            v2[l, at] = result * (2.0 / SPREAD) - 2.0 * here - v0[l, at]
        sums = [jnp.zeros((TILE, LANES), F32)] * 6
        for at, here, result in operate(v2, HALO, HALO + rows_x):
            a, b = v0[l, at], v1[l, at]
            for n, product in enumerate((a * a, a * b, b * b, b * here, here * here, here * result)):
                for t in range(rows_z // TILE):
                    sums[n] = sums[n] + product[tile_rows(t)]
        for n in range(6):
            dots[pl.ds(n * labels + l, 1), :] = jnp.sum(sums[n], axis=0, keepdims=True)
        return carry

    lax.fori_loop(0, labels, label, 0)


def steps(g00, g01, g11, g12, g22, k22):
    g02 = 2.0 * g11 - g00
    k00 = SPREAD * (g00 + g01)
    k01 = SPREAD * (g01 + g11)
    k02 = SPREAD * (g02 + g12)
    k11 = SPREAD * (g11 + 0.5 * (g12 + g01))
    k12 = SPREAD * (g12 + 0.5 * (g22 + g02))
    alpha = g00 / k00
    c0 = alpha
    r0 = 1.0 - alpha * SPREAD
    r1 = -alpha * SPREAD
    rr = r0 * r0 * g00 + 2.0 * r0 * r1 * g01 + r1 * r1 * g11
    beta = rr / g00
    p0, p1 = r0 + beta, r1
    alpha = rr / (p0 * p0 * k00 + 2.0 * p0 * p1 * k01 + p1 * p1 * k11)
    c0, c1 = c0 + alpha * p0, alpha * p1
    r0 = r0 - alpha * SPREAD * (p0 + 0.5 * p1)
    r1 = r1 - alpha * SPREAD * (p0 + p1)
    r2 = -alpha * SPREAD * 0.5 * p1
    rr_next = r0 * r0 * g00 + r1 * r1 * g11 + r2 * r2 * g22
    rr_next = rr_next + 2.0 * (r0 * r1 * g01 + r0 * r2 * g02 + r1 * r2 * g12)
    beta = rr_next / rr
    p0, p1, p2 = r0 + beta * p0, r1 + beta * p1, r2
    curve = p0 * p0 * k00 + p1 * p1 * k11 + p2 * p2 * k22
    curve = curve + 2.0 * (p0 * p1 * k01 + p0 * p2 * k02 + p1 * p2 * k12)
    alpha = rr_next / curve
    return c0 + alpha * p0, c1 + alpha * p1, alpha * p2


def edges(info, parts, v0, v1, v2, full, first, second, out, lam, field):
    labels, rows_x, rows, _ = full.shape
    even = info[EVEN_X] == 1
    total = jnp.sum(parts[...], axis=0)
    total = jnp.broadcast_to(jnp.sum(total, axis=1, keepdims=True), total.shape)
    grams = []
    for t in range(3):
        tile = total[tile_rows(t)]
        grams += [tile, pltpu.roll(tile, 4, 0)]
    c0, c1, c2 = steps(*grams)
    for l in range(labels):
        s0, s1, s2 = (jnp.broadcast_to(c[l : l + 1], (rows, LANES)) for c in (c0, c1, c2))
        for at in range(rows_x + 3):
            source = at + HALO - 1
            lam[l, at] = s0 * v0[l, source] + s1 * v1[l, source] + s2 * v2[l, source]
            x = at - 1
            if 0 <= x < rows_x:
                plane = full[l, x]
            else:
                index = 2 * labels + labels * rows_x + 2 * l + (1 if x < 0 else x - rows_x)
                above, below = sides(even, first[index].astype(F32), second[index].astype(F32))
                plane = below if x < 0 else above
            field[l, at] = plane
    for at in range(rows_x + 2):
        sums = [jnp.zeros((rows, LANES), F32)] * 3
        for l in range(labels):
            a, b = lam[l, at], field[l, at]
            sums[0] = sums[0] - (a - lam[l, at + 1]) * (b - field[l, at + 1])
            sums[1] = sums[1] - (a - up(a, 0)) * (b - up(b, 0))
            sums[2] = sums[2] - (a - up(a, 1)) * (b - up(b, 1))
        for d in range(3):
            out[d, at] = sums[d]


def filter_sums(info, edge, other, slope, stack, one, grads, out, products, rows_out):
    rows_x = edge.shape[1] - 2
    lane = lanes_iota(edge.shape[2])
    for xp in range(rows_x + 2):
        shifted = [[], [], []]
        for d in range(3):
            plane = ((edge[d, xp] + other[d, xp]) * slope[d, xp]).astype(BF16).astype(F32)
            shifted[0].append(jnp.where(lane < LANES - 1, up(plane, 1), 0.0))
            shifted[1].append(plane)
            shifted[2].append(jnp.where(lane > 0, down(plane, 1), 0.0))
        planes = shifted[0] + shifted[1] + shifted[2]
        planes += [jnp.zeros_like(planes[0])] * 7
        for pair in range(8):
            at = (xp * 16 + 2 * pair) * TILE
            for t in range(-1, 5):
                both = jnp.concatenate([plane[tile_rows(t)] for plane in planes[2 * pair : 2 * pair + 2]], axis=0)
                grads[at : at + 16, (t + 1) * LANES : (t + 2) * LANES] = both.astype(BF16)
    own = grads[LANES : LANES * (rows_x + 1), LANES : 5 * LANES]
    for o in range(3):
        products[o] = lax.dot_general(
            own, stack[:, o * LANES : (o + 4) * LANES], (((1,), (1,)), ((), ())), preferred_element_type=F32
        )
    rows_out[...] = jnp.zeros_like(rows_out)
    masks = {(h, j, o): band(h, j, o) for o in (-1, 0, 1) for h in range(2) for j in bands(o)}
    for kd in range(9):
        k, d = kd // 3, kd % 3
        for i in range(3):
            for j in range(3):
                total = jnp.zeros((TILE, LANES), F32)
                for o in (-1, 0, 1):
                    if j in bands(o):
                        for x in range(rows_x):
                            at = (x * 16 + kd) * TILE
                            col = (x + i) // 2 * LANES
                            piece = products[o + 1, at : at + TILE, col : col + LANES]
                            total = total + jnp.where(masks[(x + i) % 2, j, o], piece, 0.0)
                row = i * 9 + j * 3 + k
                rows_out[d, row : row + 1] = jnp.sum(total, axis=0, keepdims=True)
    for d in range(3):
        out[d * TILE : (d + 1) * TILE] = lax.dot_general(
            one[...],
            rows_out[d],
            (((1,), (1,)), ((), ())),
            precision=lax.Precision.HIGHEST,
            preferred_element_type=F32,
        )


def image_sums(info, grads, matrix, out, sums):
    total = jnp.dot(matrix[0], grads[:, 0:512], preferred_element_type=F32)
    total = total + jnp.dot(matrix[1], grads[:, 128:640], preferred_element_type=F32)
    sums[...] = total + jnp.dot(matrix[2], grads[:, 256:768], preferred_element_type=F32)
    channels, rows_x, rows_z, _ = out.shape
    for c in range(channels):
        for x in range(rows_x):
            at = (c * rows_x + x) * TILE
            for t in range(0, rows_z // TILE, 2):
                both = [sums[at : at + TILE, s * LANES : (s + 1) * LANES] for s in (t, t + 1)]
                out[c, x, t * TILE : (t + 2) * TILE] = jnp.concatenate(both, axis=0).astype(BF16)


def local(image, filt, planted, likelihoods, slope):
    channels = image.shape[0]
    labels, rows_x, rows_z, rows_y = likelihoods.shape
    if (channels, labels, rows_x, rows_z, rows_y) != (8, 4, HALO, 4 * TILE, LANES):
        raise ValueError("brick size")
    lab, xy, gz = lax.axis_index("lab"), lax.axis_index("xy"), lax.axis_index("gz")
    colours = labels * lax.axis_size("lab")
    size_x, size_z = rows_x * lax.axis_size("xy"), rows_z * lax.axis_size("gz")
    rows = rows_z + TILE
    two = lax.axis_size("gz") > 2
    info = jnp.stack(
        [1 - xy % 2, 1 - gz % 2, xy * rows_x, gz * rows_z, lab * labels, 1 - (xy + lab) % 2]
    ).astype(jnp.int32)

    inputs = (image, planted, likelihoods, slope)
    faces = []
    for phase in range(1 + two):
        block = call(
            functools.partial(pack_z, colours, phase),
            shaped((rows_x, labels, TILE, LANES), BF16),
            info,
            *inputs,
            name="pack_z",
        )
        faces.append(swap(block, "gz", phase))
    planes = channels + labels * rows_x + 2 * labels
    rhs, full, wide_image, send_a, send_b = call(
        functools.partial(assemble_z, colours, two),
        [
            shaped((labels, rows_x, rows, LANES), F32),
            shaped((labels, rows_x, rows, LANES), F32),
            shaped((channels, rows_x, rows, LANES), BF16),
            shaped((planes, rows, LANES), BF16),
            shaped((planes, rows, LANES), BF16),
        ],
        info,
        *faces,
        *inputs,
        name="assemble_z",
    )
    first = swap(send_a, "xy", 0)
    second = swap(send_b, "xy", 1)

    own_filt = lax.dynamic_slice_in_dim(filt, lab * channels, channels, 1)
    lines = jnp.transpose(own_filt, (4, 0, 2, 3, 1)).reshape(81, channels)
    lines = jnp.pad(lines, ((0, 7), (0, LANES - channels)))
    backs = jnp.transpose(own_filt, (1, 2, 3, 4, 0)).reshape(72, 9)
    backs = jnp.pad(backs, ((0, 0), (0, LANES - 9)))
    lane = jnp.arange(LANES, dtype=jnp.int32)
    by_channel = ((lane[None] >> 3) & 7) == lane[:, None]
    by_edge = (lane[None] >> 3) == lane[:, None]
    matrix, back_matrix = call(
        spread_filter,
        [shaped((3, 288, 384), BF16), shaped((3, 256, 768), BF16)],
        info,
        lines,
        backs,
        by_channel.astype(BF16),
        by_edge.astype(BF16),
        flops=10_000_000,
        name="spread_filter",
    )
    part, stack = call(
        convolve,
        [shaped((3, rows_x, rows_z, LANES), F32), shaped((384, 768), BF16)],
        info,
        wide_image,
        first,
        second,
        matrix,
        scratch=[pltpu.VMEM((288, 512), F32)],
        name="convolve",
    )
    faces_shape = shaped((3, rows_x, TILE, LANES), BF16)
    logits, *sends = call(
        functools.partial(add_parts, two),
        [shaped(part.shape, F32)] + [faces_shape] * (1 + two),
        info,
        part,
        lab_swap(part),
        name="add_parts",
    )
    faces = [swap(block, "gz", phase) for phase, block in enumerate(sends)]
    own = call(
        functools.partial(extend_logits, two),
        shaped((3, rows_x, rows, LANES), BF16),
        info,
        logits,
        *faces,
        name="extend_logits",
    )
    mine = split_swap(own, "xy")
    other = lab_swap(mine)
    extended = (labels, rows_x + 2 * HALO, rows, LANES)
    ring = shaped((3, rows_x + 2, rows, LANES), F32)
    v0, v1, v2, squash_slope, dots = call(
        functools.partial(krylov, size_x, size_z),
        [shaped(extended, F32)] * 3 + [ring, shaped((6 * labels, LANES), F32)],
        info,
        logits,
        own,
        mine,
        other,
        rhs,
        first,
        second,
        scratch=[
            pltpu.VMEM((3,) + extended[1:], F32),
            pltpu.VMEM(extended[1:], F32),
        ],
        name="krylov",
    )
    edge = call(
        edges,
        ring,
        info,
        everyones(dots, ("xy", "gz")),
        v0,
        v1,
        v2,
        full,
        first,
        second,
        scratch=[pltpu.VMEM((labels, rows_x + 3, rows, LANES), F32)] * 2,
        name="edges",
    )
    grads, sums = call(
        filter_sums,
        [shaped((768, 768), BF16), shaped((3 * TILE, LANES), F32)],
        info,
        edge,
        lab_swap(edge),
        squash_slope,
        stack,
        by_channel[:TILE].astype(F32),
        scratch=[pltpu.VMEM((3, 512, 384), F32), pltpu.VMEM((3, LANES, LANES), F32)],
        name="filter_sums",
    )
    grad_image = call(
        image_sums,
        shaped(image.shape, BF16),
        info,
        grads,
        back_matrix,
        scratch=[pltpu.VMEM((256, 512), F32)],
        flops=10_000_000,
        name="image_sums",
    )
    grad_filter = jnp.sum(everyones(sums, ("xy", "gz")), axis=0)
    return grad_image, grad_filter[:, :27].reshape(3, channels, 3, 3, 3)


def solution(mesh):
    return jax.shard_map(
        local,
        mesh=mesh,
        in_specs=(
            P("lab", ("crops", "xy"), "gz", None),
            P(),
            P(("crops", "xy"), "gz", None),
            P("lab", ("crops", "xy"), "gz", None),
            P("lab", ("crops", "xy"), "gz", None),
        ),
        out_specs=(P("lab", ("crops", "xy"), "gz", None), P("crops", "lab", None, None, None)),
        check_vma=False,
    )
```

time: 139 us -> 70.9 us (0.51); the launches traced: 137 us -> 70.5 us
  local copies, waits for them, and re-layouts: 57.9 us -> 6.55 us
  matrix products: 24.5 us -> 0 us
  other arithmetic: 19.9 us -> 0.05 us
  Pallas kernels: 0 us -> 13 us
  blocking collectives: 0 us -> 12.3 us
  waiting for transfers between devices: 10.4 us -> 20 us
  starting transfers between devices: 21.4 us -> 17.7 us
  between operations: 2.84 us -> 0.86 us
    unnamed x250 -> x17, local copies, waits for them, and re-layouts: 36.9 us -> 4.34 us
    dot_general x81 -> x0, matrix products: 24.5 us -> none  [the longest x27 8.82 us: local(): jnp.einsum('dxzy,cxzy->dc', own_grad, window(image_w, i, j, k), preferred...]
    slice x70 -> x1, local copies, waits for them, and re-layouts: 13.6 us -> 0.08 us  [local(): return (grad_image, grad_filter[:, :27].reshape(3, channels, 3, 3, 3))]
    pallas_call x0 -> x10, Pallas kernels: none -> 13 us  [call(): pl.pallas_call(kernel, out_shape=outs, in_specs=specs, out_specs=jax.tree...]
    all_to_all x0 -> x1, blocking collectives: none -> 12.3 us  [everyones(): lax.all_to_all(jnp.broadcast_to(part[None], (count,) + part.shape), axes,...]
    convert_element_type x18 -> x1, other arithmetic: 6.07 us -> 0.01 us  [local(): by_channel[:TILE].astype(F32)]
    all_to_all x2 -> x1, starting transfers between devices: 8.86 us -> 3.36 us  [everyones(): lax.all_to_all(jnp.broadcast_to(part[None], (count,) + part.shape), axes,...]
    ppermute x4, waiting for transfers between devices: 2.75 us -> 7.27 us  [the longest x3 4.42 us: lab_swap(): return lax.ppermute(block, 'lab', [(0, 1), (1, 0)])]
  transfers between devices with their start and end apart: 10 -> 9, of which waited for: 4 -> 8; matrix products, arithmetic and copies ran while one was open for 19% -> 2% of each run, Pallas kernels for 0% -> 4%
where the time goes in v2:
time: 70.9 us; the launch traced here: 70.5 us
  waiting for transfers between devices  20 us (28%)
  starting transfers between devices  17.7 us (25%)
  Pallas kernels  13 us (18%)
  blocking collectives  12.3 us (17%)
  local copies, waits for them, and re-layouts  6.55 us (9%)
  between operations  0.86 us (1%)
    pallas_call x10, Pallas kernels, call(): pl.pallas_call(kernel, out_shape=outs, in_specs=specs, out_specs=jax.tree...  13 us
    all_to_all x1, blocking collectives, everyones(): lax.all_to_all(jnp.broadcast_to(part[None], (count,) + part.shape), axes,...  12.3 us
    ppermute x4, waiting for transfers between devices, swap(): return lax.ppermute(block, axis, pair_routes(lax.axis_size(axis), phase))  7.66 us
    ppermute x4, starting transfers between devices, swap(): return lax.ppermute(block, axis, pair_routes(lax.axis_size(axis), phase))  7.56 us
    ppermute x1, starting transfers between devices, split_swap(): return lax.ppermute(block, (axis, 'lab'), route)  6.67 us
    all_to_all x1, waiting for transfers between devices, everyones(): lax.all_to_all(jnp.broadcast_to(part[None], (count,) + part.shape), axes,...  5.04 us
    ppermute x3, waiting for transfers between devices, lab_swap(): return lax.ppermute(block, 'lab', [(0, 1), (1, 0)])  4.42 us
    unnamed x17, local copies, waits for them, and re-layouts  4.34 us
  transfers between devices with their start and end apart: 9, of which 8 were waited for; matrix products, arithmetic and copies ran while one was open for 2% of the time, Pallas kernels for 4%

profile of v2, /device:TPU:0, one launch (start us, length us, event | category | flops | bytes accessed | tf_op | source)
XLA Modules:
  0.0 70.5 jit_solution(14045724432851887298)
XLA Ops:
  0.8 1.0 %copy-done = bf16[8,4,32,128]{3,2,1,0:T(8,128)(2,1)S(1)} copy-done((bf16[8,4,32,128]{3,2,1,0:T(8,128)(2,1)S(1)}, bf16[8,4,32,128]{3,2,1,0:T(8,128)(2,1)}, u32[]{:S(2)}) %copy-start) | copy-done | bytes 262168
  1.7 0.9 %copy-done.2 = f32[4,4,32,128]{3,2,1,0:T(8,128)S(1)} copy-done((f32[4,4,32,128]{3,2,1,0:T(8,128)S(1)}, f32[4,4,32,128]{3,2,1,0:T(8,128)}, u32[]{:S(2)}) %copy-start.2) | copy-done | bytes 262168
  2.7 0.9 %copy-done.4 = f32[4,4,32,128]{3,2,1,0:T(8,128)S(1)} copy-done((f32[4,4,32,128]{3,2,1,0:T(8,128)S(1)}, f32[4,4,32,128]{3,2,1,0:T(8,128)}, u32[]{:S(2)}) %copy-start.4) | copy-done | bytes 262168
  3.6 0.8 %copy-done.6 = s32[4,32,128]{2,1,0:T(8,128)S(1)} copy-done((s32[4,32,128]{2,1,0:T(8,128)S(1)}, s32[4,32,128]{2,1,0:T(8,128)}, u32[]{:S(2)}) %copy-start.6) | copy-done | bytes 65560
  5.1 3.0 %collective-permute-start = (bf16[4,4,8,128]{3,2,1,0:T(8,128)(2,1)S(1)}, bf16[4,4,8,128]{3,2,1,0:T(8,128)(2,1)S(1)}, u32[]{:S(2)}, u32[]{:S(2)}) collective-permute-start(bf16[4,4,8,128]{3,2,1,0:T(8,128)(2,1)S(1)} %pack_z.1), channel_id=1, source_target_pairs={{0,2},{2,0},{1,3},{3,1},{4,6},{6,4},{5,7},{7,5},{8,10},{10,8},{9,1... | collective-permute-start | bytes 98312 | tf_op jit(solution)/shard_map/ppermute | solution.py:27
  8.1 0.8 %dynamic-slice_bitcast_fusion = (bf16[8,3,3,3,3]{0,3,2,1,4:T(4,128)(2,1)S(1)}, bf16[3,3,3,3,8]{4,0,3,2,1:T(4,128)(2,1)S(1)}) fusion(bf16[3,16,3,3,3]{1,4,3,2,0:T(4,128)(2,1)} %param.6, s32[]{:T(128)S(6)} %select_n.21), kind=kLoop, calls=%fused_computation.3 | loop fusion | bytes 3892 | tf_op jit(solution)/shard_map/transpose | solution.py:529
  10.7 2.2 %collective-permute-start.1 = (bf16[32,40,128]{2,1,0:T(8,128)(2,1)S(1)}, bf16[32,40,128]{2,1,0:T(8,128)(2,1)S(1)}, u32[]{:S(2)}, u32[]{:S(2)}) collective-permute-start(bf16[32,40,128]{2,1,0:T(8,128)(2,1)S(1)} %get-tuple-element.21), channel_id=1, source_target_pairs={{0,4},{4,0},{8,12},{12,8},{1,5},{5,1},{9,13},{13,9},{2,6},{6,2},{1... | collective-permute-start | bytes 983048 | tf_op jit(solution)/shard_map/ppermute | solution.py:27
  13.6 0.9 %spread_filter.1 = (bf16[3,288,384]{2,1,0:T(8,128)(2,1)S(1)}, bf16[3,256,768]{2,1,0:T(8,128)(2,1)S(1)}) custom-call(s32[6]{0:T(128)S(1)} %stack.27.info, bf16[88,128]{1,0:T(8,128)(2,1)S(1)} %pad.8.first, bf16[72,128]{1,0:T(8,128)(2,1)S(1)} %pad.9.second, bf16[128,128]{1,0:T(8,128)(2,1)S(1)} %get-tuple-element.45.one, bf16[128,128]{1,0:T(8,128)(2,1)S(1)} %get-tuple-element.46.two), custom_call_target="tpu_custom_call" | custom-call | flops 10000000 | bytes 106520 | tf_op jit(solution)/shard_map/spread_filter/pallas_call | solution.py:55
  14.5 4.9 %collective-permute-done.1.first = bf16[32,40,128]{2,1,0:T(8,128)(2,1)S(1)} collective-permute-done((bf16[32,40,128]{2,1,0:T(8,128)(2,1)S(1)}, bf16[32,40,128]{2,1,0:T(8,128)(2,1)S(1)}, u32[]{:S(2)}, u32[]{:S(2)}) %collective-permute-start.1) | collective-permute-done | bytes 327712 | tf_op jit(solution)/shard_map/ppermute | solution.py:27
  19.4 1.3 %convolve.1 = (f32[3,4,32,128]{3,2,1,0:T(8,128)S(1)}, bf16[384,768]{1,0:T(8,128)(2,1)S(1)}) custom-call(s32[6]{0:T(128)S(1)} %stack.27.info, bf16[8,4,40,128]{3,2,1,0:T(8,128)(2,1)S(1)} %get-tuple-element.20.image, bf16[32,40,128]{2,1,0:T(8,128)(2,1)S(1)} %collective-permute-done.1.first, bf16[32,40,128]{2,1,0:T(8,128)(2,1)S(1)} %collective-permute-done.2.second, ...), custom_call_target="tpu_custom_call" | custom-call | flops 1000000 | bytes 1646616 | tf_op jit(solution)/shard_map/convolve/pallas_call | solution.py:55
  20.9 1.4 %collective-permute-done.3.other = f32[3,4,32,128]{3,2,1,0:T(8,128)S(1)} collective-permute-done((f32[3,4,32,128]{3,2,1,0:T(8,128)S(1)}, f32[3,4,32,128]{3,2,1,0:T(8,128)S(1)}, u32[]{:S(2)}, u32[]{:S(2)}) %collective-permute-start.3) | collective-permute-done | bytes 196640 | tf_op jit(solution)/shard_map/ppermute | solution.py:31
  22.9 1.7 %collective-permute-start.4 = (bf16[3,4,8,128]{3,2,1,0:T(8,128)(2,1)S(1)}, bf16[3,4,8,128]{3,2,1,0:T(8,128)(2,1)S(1)}, u32[]{:S(2)}, u32[]{:S(2)}) collective-permute-start(bf16[3,4,8,128]{3,2,1,0:T(8,128)(2,1)S(1)} %get-tuple-element.26), channel_id=1, source_target_pairs={{0,2},{2,0},{1,3},{3,1},{4,6},{6,4},{5,7},{7,5},{8,10},{10,8},{9,1... | collective-permute-start | bytes 73736 | tf_op jit(solution)/shard_map/ppermute | solution.py:27
  24.6 2.2 %collective-permute-done.4.first = bf16[3,4,8,128]{3,2,1,0:T(8,128)(2,1)S(1)} collective-permute-done((bf16[3,4,8,128]{3,2,1,0:T(8,128)(2,1)S(1)}, bf16[3,4,8,128]{3,2,1,0:T(8,128)(2,1)S(1)}, u32[]{:S(2)}, u32[]{:S(2)}) %collective-permute-start.4) | collective-permute-done | bytes 24608 | tf_op jit(solution)/shard_map/ppermute | solution.py:27
  27.3 6.7 %collective-permute-start.5 = (bf16[3,4,40,128]{3,2,1,0:T(8,128)(2,1)S(1)}, bf16[3,4,40,128]{3,2,1,0:T(8,128)(2,1)S(1)}, u32[]{:S(2)}, u32[]{:S(2)}) collective-permute-start(bf16[3,4,40,128]{3,2,1,0:T(8,128)(2,1)S(1)} %extend_logits.1.own), channel_id=1, source_target_pairs={{0,4},{4,0},{8,12},{12,8},{5,9},{9,5},{2,6},{6,2},{10,14},{14,10},... | collective-permute-start | bytes 368648 | tf_op jit(solution)/shard_map/ppermute | solution.py:41
  34.0 2.8 %collective-permute-done.5.mine = bf16[3,4,40,128]{3,2,1,0:T(8,128)(2,1)S(1)} collective-permute-done((bf16[3,4,40,128]{3,2,1,0:T(8,128)(2,1)S(1)}, bf16[3,4,40,128]{3,2,1,0:T(8,128)(2,1)S(1)}, u32[]{:S(2)}, u32[]{:S(2)}) %collective-permute-start.5) | collective-permute-done | bytes 122912 | tf_op jit(solution)/shard_map/ppermute | solution.py:41
  36.8 1.3 %collective-permute-done.6.other = bf16[3,4,40,128]{3,2,1,0:T(8,128)(2,1)S(1)} collective-permute-done((bf16[3,4,40,128]{3,2,1,0:T(8,128)(2,1)S(1)}, bf16[3,4,40,128]{3,2,1,0:T(8,128)(2,1)S(1)}, u32[]{:S(2)}, u32[]{:S(2)}) %collective-permute-start.6) | collective-permute-done | bytes 122912 | tf_op jit(solution)/shard_map/ppermute | solution.py:31
  38.2 2.9 %krylov.1 = (f32[4,12,40,128]{3,2,1,0:T(8,128)S(1)}, f32[4,12,40,128]{3,2,1,0:T(8,128)S(1)}, f32[4,12,40,128]{3,2,1,0:T(8,128)S(1)}, f32[3,6,40,128]{3,2,1,0:T(8,128)S(1)}, f32[24,128]{1,0:T(8,128)S(1)}) custom-call(s32[6]{0:T(128)S(1)} %stack.27.info, f32[3,4,32,128]{3,2,1,0:T(8,128)S(1)} %get-tuple-element.25.logits, ...), custom_call_target="tpu_custom_call" | custom-call | flops 1000000 | bytes 1548312 | tf_op jit(solution)/shard_map/krylov/pallas_call | solution.py:55
  41.1 12.3 %all_to_all.10.parts = f32[8,24,128]{2,1,0:T(8,128)S(1)} all-to-all(f32[8,24,128]{2,1,0:T(8,128)S(1)} %broadcast_in_dim.4), channel_id=1, replica_groups=mesh['crops'=2,'xy'=4,'gz'=2,'lab'=2] {'xy','gz'}, dimensions={0} | all-to-all | bytes 196608 | tf_op jit(solution)/shard_map/all_to_all | solution.py:48
  53.4 1.2 %edges.1.edge = f32[3,6,40,128]{3,2,1,0:T(8,128)S(1)} custom-call(s32[6]{0:T(128)S(1)} %stack.27.info, f32[8,24,128]{2,1,0:T(8,128)S(1)} %all_to_all.10.parts, f32[4,12,40,128]{3,2,1,0:T(8,128)S(1)} %get-tuple-element.29.v0, f32[4,12,40,128]{3,2,1,0:T(8,128)S(1)} %get-tuple-element.30.v1, f32[4,12,40,128]{3,2,1,0:T(8,128)S(1)} %get-tuple-element.31.v2, ...), custom_call_target="tpu_custom_call" | custom-call | flops 1000000 | bytes 4030488 | tf_op jit(solution)/shard_map/edges/pallas_call | solution.py:55
  54.7 1.7 %collective-permute-done.7.other = f32[3,6,40,128]{3,2,1,0:T(8,128)S(1)} collective-permute-done((f32[3,6,40,128]{3,2,1,0:T(8,128)S(1)}, f32[3,6,40,128]{3,2,1,0:T(8,128)S(1)}, u32[]{:S(2)}, u32[]{:S(2)}) %collective-permute-start.7) | collective-permute-done | bytes 368672 | tf_op jit(solution)/shard_map/ppermute | solution.py:31
  56.4 2.2 %filter_sums.1 = (bf16[768,768]{1,0:T(8,128)(2,1)S(1)}, f32[24,128]{1,0:T(8,128)S(1)}) custom-call(s32[6]{0:T(128)S(1)} %stack.27.info, f32[3,6,40,128]{3,2,1,0:T(8,128)S(1)} %edges.1.edge, f32[3,6,40,128]{3,2,1,0:T(8,128)S(1)} %collective-permute-done.7.other, f32[3,6,40,128]{3,2,1,0:T(8,128)S(1)} %get-tuple-element.33.slope, ...), custom_call_target="tpu_custom_call" | custom-call | flops 1000000 | bytes 1699864 | tf_op jit(solution)/shard_map/filter_sums/pallas_call | solution.py:55
  59.2 3.4 %all-to-all-start.1 = ((f32[8,24,128]{2,1,0:T(8,128)}), f32[8,24,128]{2,1,0:T(8,128)S(1)}, u32[]{:S(2)}, u32[]{:S(2)}) async-start(f32[8,24,128]{2,1,0:T(8,128)} %broadcast_in_dim.5), calls=%async_computation.1 | async-start | bytes 196608 | tf_op jit(solution)/shard_map/all_to_all | solution.py:48
  62.6 2.0 %image_sums.1 = bf16[8,4,32,128]{3,2,1,0:T(8,128)(2,1)} custom-call(s32[6]{0:T(128)S(1)} %stack.27.info, bf16[768,768]{1,0:T(8,128)(2,1)S(1)} %get-tuple-element.35.grads, bf16[3,256,768]{2,1,0:T(8,128)(2,1)S(1)} %get-tuple-element.36.matrix), custom_call_target="tpu_custom_call" | custom-call | flops 10000000 | bytes 2359320 | tf_op jit(solution)/shard_map/image_sums/pallas_call | solution.py:55
  64.6 5.0 %all-to-all-done.1 = f32[8,24,128]{2,1,0:T(8,128)S(1)} async-done(((f32[8,24,128]{2,1,0:T(8,128)}), f32[8,24,128]{2,1,0:T(8,128)S(1)}, u32[]{:S(2)}, u32[]{:S(2)}) %all-to-all-start.1) | async-done | bytes 98336 | tf_op jit(solution)/shard_map/all_to_all | solution.py:48
  (39 shorter events, 5.9 us)
Async XLA Ops:
  0.6 9.3 %copy-start.7 = (s32[4,32,128]{2,1,0:T(8,128)S(1)}, s32[4,32,128]{2,1,0:T(8,128)}, u32[]{:S(2)}) copy-start(s32[4,32,128]{2,1,0:T(8,128)} %refs_2_.1) | copy-start | bytes 196612
  0.8 1.0 %copy-start = (bf16[8,4,32,128]{3,2,1,0:T(8,128)(2,1)S(1)}, bf16[8,4,32,128]{3,2,1,0:T(8,128)(2,1)}, u32[]{:S(2)}) copy-start(bf16[8,4,32,128]{3,2,1,0:T(8,128)(2,1)} %refs_1_.1) | copy-start | bytes 786436
  1.7 0.9 %copy-start.2 = (f32[4,4,32,128]{3,2,1,0:T(8,128)S(1)}, f32[4,4,32,128]{3,2,1,0:T(8,128)}, u32[]{:S(2)}) copy-start(f32[4,4,32,128]{3,2,1,0:T(8,128)} %refs_3_.1) | copy-start | bytes 786436
  2.7 0.9 %copy-start.4 = (f32[4,4,32,128]{3,2,1,0:T(8,128)S(1)}, f32[4,4,32,128]{3,2,1,0:T(8,128)}, u32[]{:S(2)}) copy-start(f32[4,4,32,128]{3,2,1,0:T(8,128)} %refs_4_.1) | copy-start | bytes 786436
  3.6 0.8 %copy-start.6 = (s32[4,32,128]{2,1,0:T(8,128)S(1)}, s32[4,32,128]{2,1,0:T(8,128)}, u32[]{:S(2)}) copy-start(s32[4,32,128]{2,1,0:T(8,128)} %refs_2_.1) | copy-start | bytes 196612
  4.4 5.5 %copy-start.1 = (bf16[8,4,32,128]{3,2,1,0:T(8,128)(2,1)S(1)}, bf16[8,4,32,128]{3,2,1,0:T(8,128)(2,1)}, u32[]{:S(2)}) copy-start(bf16[8,4,32,128]{3,2,1,0:T(8,128)(2,1)} %refs_1_.1) | copy-start | bytes 786436
  4.5 5.5 %copy-start.3 = (f32[4,4,32,128]{3,2,1,0:T(8,128)S(1)}, f32[4,4,32,128]{3,2,1,0:T(8,128)}, u32[]{:S(2)}) copy-start(f32[4,4,32,128]{3,2,1,0:T(8,128)} %refs_3_.1) | copy-start | bytes 786436
  4.5 5.5 %copy-start.5 = (f32[4,4,32,128]{3,2,1,0:T(8,128)S(1)}, f32[4,4,32,128]{3,2,1,0:T(8,128)}, u32[]{:S(2)}) copy-start(f32[4,4,32,128]{3,2,1,0:T(8,128)} %refs_4_.1) | copy-start | bytes 786436
  5.1 4.9 %collective-permute-start = (bf16[4,4,8,128]{3,2,1,0:T(8,128)(2,1)S(1)}, bf16[4,4,8,128]{3,2,1,0:T(8,128)(2,1)S(1)}, u32[]{:S(2)}, u32[]{:S(2)}) collective-permute-start(bf16[4,4,8,128]{3,2,1,0:T(8,128)(2,1)S(1)} %pack_z.1), channel_id=1, source_target_pairs={{0,2},{2,0},{1,3},{3,1},{4,6},{6,4},{5,7},{7,5},{8,10},{10,8},{9,1... | collective-permute-start | bytes 98312 | tf_op jit(solution)/shard_map/ppermute | solution.py:27
  10.7 8.7 %collective-permute-start.1 = (bf16[32,40,128]{2,1,0:T(8,128)(2,1)S(1)}, bf16[32,40,128]{2,1,0:T(8,128)(2,1)S(1)}, u32[]{:S(2)}, u32[]{:S(2)}) collective-permute-start(bf16[32,40,128]{2,1,0:T(8,128)(2,1)S(1)} %get-tuple-element.21), channel_id=1, source_target_pairs={{0,4},{4,0},{8,12},{12,8},{1,5},{5,1},{9,13},{13,9},{2,6},{6,2},{1... | collective-permute-start | bytes 983048 | tf_op jit(solution)/shard_map/ppermute | solution.py:27
  12.9 6.6 %collective-permute-start.2 = (bf16[32,40,128]{2,1,0:T(8,128)(2,1)S(1)}, bf16[32,40,128]{2,1,0:T(8,128)(2,1)S(1)}, u32[]{:S(2)}, u32[]{:S(2)}) collective-permute-start(bf16[32,40,128]{2,1,0:T(8,128)(2,1)S(1)} %get-tuple-element.22), channel_id=1, source_target_pairs={{4,8},{8,4},{5,9},{9,5},{6,10},{10,6},{7,11},{11,7},{20,24},{24,20... | collective-permute-start | bytes 983048 | tf_op jit(solution)/shard_map/ppermute | solution.py:27
  20.8 1.5 %collective-permute-start.3 = (f32[3,4,32,128]{3,2,1,0:T(8,128)S(1)}, f32[3,4,32,128]{3,2,1,0:T(8,128)S(1)}, u32[]{:S(2)}, u32[]{:S(2)}) collective-permute-start(f32[3,4,32,128]{3,2,1,0:T(8,128)S(1)} %get-tuple-element.24.part), channel_id=1, source_target_pairs={{0,1},{1,0},{2,3},{3,2},{4,5},{5,4},{6,7},{7,6},{8,9},{9,8},{10,11... | collective-permute-start | bytes 589832 | tf_op jit(solution)/shard_map/ppermute | solution.py:31
  22.9 3.9 %collective-permute-start.4 = (bf16[3,4,8,128]{3,2,1,0:T(8,128)(2,1)S(1)}, bf16[3,4,8,128]{3,2,1,0:T(8,128)(2,1)S(1)}, u32[]{:S(2)}, u32[]{:S(2)}) collective-permute-start(bf16[3,4,8,128]{3,2,1,0:T(8,128)(2,1)S(1)} %get-tuple-element.26), channel_id=1, source_target_pairs={{0,2},{2,0},{1,3},{3,1},{4,6},{6,4},{5,7},{7,5},{8,10},{10,8},{9,1... | collective-permute-start | bytes 73736 | tf_op jit(solution)/shard_map/ppermute | solution.py:27
  27.3 9.5 %collective-permute-start.5 = (bf16[3,4,40,128]{3,2,1,0:T(8,128)(2,1)S(1)}, bf16[3,4,40,128]{3,2,1,0:T(8,128)(2,1)S(1)}, u32[]{:S(2)}, u32[]{:S(2)}) collective-permute-start(bf16[3,4,40,128]{3,2,1,0:T(8,128)(2,1)S(1)} %extend_logits.1.own), channel_id=1, source_target_pairs={{0,4},{4,0},{8,12},{12,8},{5,9},{9,5},{2,6},{6,2},{10,14},{14,10},... | collective-permute-start | bytes 368648 | tf_op jit(solution)/shard_map/ppermute | solution.py:41
  36.8 1.3 %collective-permute-start.6 = (bf16[3,4,40,128]{3,2,1,0:T(8,128)(2,1)S(1)}, bf16[3,4,40,128]{3,2,1,0:T(8,128)(2,1)S(1)}, u32[]{:S(2)}, u32[]{:S(2)}) collective-permute-start(bf16[3,4,40,128]{3,2,1,0:T(8,128)(2,1)S(1)} %collective-permute-done.5.mine), channel_id=1, source_target_pairs={{0,1},{1,0},{2,3},{3,2},{4,5},{5,4},{6,7},{7,6},{8,9},{9,8},{10,11... | collective-permute-start | bytes 368648 | tf_op jit(solution)/shard_map/ppermute | solution.py:31
  54.6 1.8 %collective-permute-start.7 = (f32[3,6,40,128]{3,2,1,0:T(8,128)S(1)}, f32[3,6,40,128]{3,2,1,0:T(8,128)S(1)}, u32[]{:S(2)}, u32[]{:S(2)}) collective-permute-start(f32[3,6,40,128]{3,2,1,0:T(8,128)S(1)} %edges.1.edge), channel_id=1, source_target_pairs={{0,1},{1,0},{2,3},{3,2},{4,5},{5,4},{6,7},{7,6},{8,9},{9,8},{10,11... | collective-permute-start | bytes 1105928 | tf_op jit(solution)/shard_map/ppermute | solution.py:31
  59.2 10.4 %all-to-all-start.1 = ((f32[8,24,128]{2,1,0:T(8,128)}), f32[8,24,128]{2,1,0:T(8,128)S(1)}, u32[]{:S(2)}, u32[]{:S(2)}) async-start(f32[8,24,128]{2,1,0:T(8,128)} %broadcast_in_dim.5), calls=%async_computation.1 | async-start | bytes 196608 | tf_op jit(solution)/shard_map/all_to_all | solution.py:48

commit v3 on v2

--- a/solution.py
+++ b/solution.py
@@ -31,26 +31,42 @@
     return lax.ppermute(block, "lab", [(0, 1), (1, 0)])
 
 
-def split_swap(block, axis):
+def diagonal_swap(block, x_phase, z_phase):
+    along_x = pair_routes(lax.axis_size("xy"), x_phase)
+    along_z = pair_routes(lax.axis_size("gz"), z_phase)
+    count = lax.axis_size("gz")
+    route = [(sx * count + sz, dx * count + dz) for sx, dx in along_x for sz, dz in along_z]
+    return lax.ppermute(block, ("xy", "gz"), route)
+
+
+def split_swap(block):
     labs = lax.axis_size("lab")
     route = [
         (src * labs + lab, dst * labs + lab)
         for lab in range(labs)
-        for src, dst in pair_routes(lax.axis_size(axis), lab % 2)
+        for src, dst in pair_routes(lax.axis_size("xy"), lab % 2)
     ]
-    return lax.ppermute(block, (axis, "lab"), route)
-
-
-def everyones(part, axes):
-    count = 1
-    for axis in axes:
-        count *= lax.axis_size(axis)
-    return lax.all_to_all(jnp.broadcast_to(part[None], (count,) + part.shape), axes, 0, 0)
-
-
-def call(kernel, outs, *ins, scratch=(), flops=1_000_000, name=None):
+    return lax.ppermute(block, ("xy", "lab"), route)
+
+
+def split_diagonal_swap(block, z_phase):
+    labs, count = lax.axis_size("lab"), lax.axis_size("gz")
+    route = [
+        ((sx * count + sz) * labs + lab, (dx * count + dz) * labs + lab)
+        for lab in range(labs)
+        for sx, dx in pair_routes(lax.axis_size("xy"), lab % 2)
+        for sz, dz in pair_routes(count, z_phase)
+    ]
+    return lax.ppermute(block, ("xy", "gz", "lab"), route)
+
+
+def everyones(copies, axes):
+    return lax.all_to_all(copies, axes, 0, 0)
+
+
+def call(kernel, outs, *ins, scratch=(), flops=1_000_000, name=None, space=pltpu.VMEM):
     specs = [pl.BlockSpec(memory_space=pltpu.SMEM)]
-    specs += [pl.BlockSpec(memory_space=pltpu.VMEM)] * (len(ins) - 1)
+    specs += [pl.BlockSpec(memory_space=space)] * (len(ins) - 1)
     bytes_moved = sum(a.size * a.dtype.itemsize for a in ins)
     return pl.pallas_call(
         kernel,
@@ -82,30 +98,56 @@
     return jnp.where(free, slope, SEED), jnp.where(free, likelihood, member)
 
 
-def pack_z(colours, flip, info, image, planted, likelihoods, slope, out):
+def pack(colours, two, info, image_in, planted_in, likelihoods_in, slope_in, image, planted, likelihoods, slope, *refs):
+    faces, (send_a, send_b, sems) = refs[: 1 + two], refs[1 + two :]
+    pairs = ((planted_in, planted), (slope_in, slope), (likelihoods_in, likelihoods), (image_in, image))
+    copies = [pltpu.make_async_copy(src, dst, sems.at[n]) for n, (src, dst) in enumerate(pairs)]
+    for copy in copies:
+        copy.start()
+    for copy in copies:
+        copy.wait()
     labels, rows_x, rows_z, _ = likelihoods.shape
-    even = info[EVEN_Z] != flip
-    place = (rows_iota() + jnp.where(even, 0, 4)) & 7
+    channels = image.shape[0]
     last, first = slice(rows_z - TILE, rows_z), slice(0, TILE)
-
-    def at_end(ref, *lead):
-        return jnp.where(even, ref[(*lead, last)].astype(ref.dtype), ref[(*lead, first)])
-
-    def channel(c, x):
-        return jnp.where(even, image[c, x, last].astype(F32), image[c, x, first].astype(F32))
-
-    def turned(tile, for_even, for_odd):
-        return jnp.where(even, pltpu.roll(tile, for_even, 0), pltpu.roll(tile, for_odd, 0))
-
+    for phase, out in enumerate(faces):
+        even = info[EVEN_Z] != phase
+        place = (rows_iota() + jnp.where(even, 0, 4)) & 7
+
+        def at_end(plane):
+            return jnp.where(even, plane[last], plane[first])
+
+        def channel(c, x):
+            return jnp.where(even, image[c, x, last].astype(F32), image[c, x, first].astype(F32))
+
+        def turned(tile, for_even, for_odd):
+            return jnp.where(even, pltpu.roll(tile, for_even, 0), pltpu.roll(tile, for_odd, 0))
+
+        for x in range(rows_x):
+            seeds = jnp.where(even, planted[x, last], planted[x, first])
+            for l in range(labels):
+                ends = [jnp.where(even, ref[l, x, last], ref[l, x, first]) for ref in (likelihoods, slope)]
+                rhs, full = fields(seeds, *ends, colours, info[COLOUR] + l)
+                first_channel = turned(channel(2 * l, x), 3, 6)
+                second_channel = turned(channel(2 * l + 1, x), 4, 7)
+                rest = jnp.where(place == 2, first_channel, second_channel)
+                rest = jnp.where(place < 2, turned(full, 2, 4), rest)
+                out[x, l] = jnp.where(place >= 4, rhs, rest).astype(BF16)
+    even = info[EVEN_X] == 1
+    high, low = jnp.where(even, rows_x - 1, 0), jnp.where(even, 0, rows_x - 1)
+    for c in range(channels):
+        send_a[c] = image[c, high]
+        send_b[c] = image[c, low]
     for x in range(rows_x):
-        seeds = at_end(planted, x)
         for l in range(labels):
-            rhs, full = fields(seeds, at_end(likelihoods, l, x), at_end(slope, l, x), colours, info[COLOUR] + l)
-            first_channel = turned(channel(2 * l, x), 3, 6)
-            second_channel = turned(channel(2 * l + 1, x), 4, 7)
-            rest = jnp.where(place == 2, first_channel, second_channel)
-            rest = jnp.where(place < 2, turned(full, 2, 4), rest)
-            out[x, l] = jnp.where(place >= 4, rhs, rest).astype(BF16)
+            rhs = jnp.where(planted[x] >= colours, slope[l, x], SEED).astype(BF16)
+            send_a[channels + l * rows_x + x] = rhs
+            send_b[channels + l * rows_x + x] = rhs
+    for l in range(labels):
+        for send, at in ((send_a, high), (send_b, low)):
+            for r in range(2):
+                x = jnp.where(at == 0, 0, rows_x - 2) + r
+                _, full = fields(planted[x], likelihoods[l, x], slope[l, x], colours, info[COLOUR] + l)
+                send[channels + labels * rows_x + 2 * l + r] = full.astype(BF16)
 
 
 def sides(even, first, second):
@@ -114,42 +156,22 @@
     return jnp.where(even, first, second), jnp.where(even, second, first)
 
 
-def assemble_z(colours, two, info, *refs):
-    first_z = refs[0]
-    second_z = refs[1] if two else None
-    image, planted, likelihoods, slope, rhs_out, full_out, image_out, send_a, send_b = refs[1 + two :]
-    labels, rows_x, rows_z, _ = likelihoods.shape
-    channels = image.shape[0]
-    upper = rows_iota() < 4
-    for x in range(rows_x):
-        for l in range(labels):
-            rhs, full = fields(planted[x], likelihoods[l, x], slope[l, x], colours, info[COLOUR] + l)
-            above, below = sides(
-                info[EVEN_Z] == 1,
-                first_z[x, l].astype(F32),
-                second_z[x, l].astype(F32) if two else None,
-            )
-            rhs = jnp.concatenate([rhs, jnp.where(upper, above, below)], axis=0)
-            full_tile = jnp.where(upper, pltpu.roll(above, 4, 0), pltpu.roll(below, 6, 0))
-            rhs_out[l, x] = rhs
-            full_out[l, x] = jnp.concatenate([full, full_tile], axis=0)
-            plane = channels + l * rows_x + x
-            send_a[plane] = rhs.astype(BF16)
-            send_b[plane] = rhs.astype(BF16)
-            for c, up, down in ((2 * l, 2, 5), (2 * l + 1, 1, 4)):
-                tile = jnp.where(upper, pltpu.roll(above, up, 0), pltpu.roll(below, down, 0))
-                image_out[c, x] = jnp.concatenate([image[c, x].astype(F32), tile], axis=0).astype(BF16)
-    even = info[EVEN_X] == 1
-    high, low = jnp.where(even, rows_x - 1, 0), jnp.where(even, 0, rows_x - 1)
-    for c in range(channels):
-        send_a[c] = image_out[c, high]
-        send_b[c] = image_out[c, low]
-    high, low = jnp.where(even, rows_x - 2, 0), jnp.where(even, 0, rows_x - 2)
-    for l in range(labels):
-        for r in range(2):
-            plane = channels + labels * rows_x + 2 * l + r
-            send_a[plane] = full_out[l, high + r].astype(BF16)
-            send_b[plane] = full_out[l, low + r].astype(BF16)
+def ends_z(info, tiles, x, l):
+    both = [ref[x, l].astype(F32) for ref in tiles]
+    return sides(info[EVEN_Z] == 1, both[0], both[1] if len(both) > 1 else None)
+
+
+def rhs_tile(above, below):
+    return jnp.where(rows_iota() < 4, above, below)
+
+
+def full_tile(above, below):
+    return jnp.where(rows_iota() < 4, pltpu.roll(above, 4, 0), pltpu.roll(below, 6, 0))
+
+
+def image_tile(above, below, c):
+    up, down = (2, 5) if c % 2 == 0 else (1, 4)
+    return jnp.where(rows_iota() < 4, pltpu.roll(above, up, 0), pltpu.roll(below, down, 0))
 
 
 def band(half, j, o, transposed=False):
@@ -216,17 +238,28 @@
     return slice(at, at + TILE)
 
 
-def convolve(info, image, first, second, matrix, part, stack, sums):
+def convolve(two, info, image, first, second, *refs):
+    faces, edges_a, edges_b = refs[: 1 + two], refs[1 + two : 2 + 2 * two], refs[2 + 2 * two : 3 + 3 * two]
+    matrix, part, stack, sums = refs[3 + 3 * two :]
     channels, rows_x = image.shape[0], image.shape[1]
     even = info[EVEN_X] == 1
     for xp in range(rows_x + 2):
         for c in range(0, channels, 2):
             planes = []
+            if 0 < xp <= rows_x:
+                ends = [ends_z(info, faces, xp - 1, c // 2)]
+            else:
+                ends = [ends_z(info, tiles, rows_x - 1 if xp == 0 else 0, c // 2) for tiles in (edges_a, edges_b)]
             for ch in (c, c + 1):
+                tiles = [image_tile(*pair, ch) for pair in ends]
                 if 0 < xp <= rows_x:
-                    planes.append(image[ch, xp - 1].astype(F32))
+                    planes.append(jnp.concatenate([image[ch, xp - 1].astype(F32), tiles[0]], axis=0))
                 else:
-                    above, below = sides(even, first[ch].astype(F32), second[ch].astype(F32))
+                    received = [
+                        jnp.concatenate([ref[ch].astype(F32), tile], axis=0)
+                        for ref, tile in zip((first, second), tiles)
+                    ]
+                    above, below = sides(even, *received)
                     planes.append(below if xp == 0 else above)
             at = (xp * channels + c) * TILE
             for t in range(-1, 5):
@@ -250,30 +283,16 @@
                 part[d, x, tile_rows(t)] = piece(1) + before + after
 
 
-def add_parts(two, info, part, other, logits, send_a, *send_b):
+def add_parts(two, info, part, other, logits, brick, *faces):
     rows_x, rows_z = part.shape[1], part.shape[2]
-    even = info[EVEN_Z] == 1
     for d in range(3):
         for x in range(rows_x):
             total = part[d, x] + other[d, x]
             logits[d, x] = total
-            first, last = total[:TILE], total[rows_z - TILE :]
-            send_a[d, x] = jnp.where(even, last, first).astype(BF16)
-            if two:
-                send_b[0][d, x] = jnp.where(even, first, last).astype(BF16)
-
-
-def extend_logits(two, info, logits, first, *refs):
-    second = refs[0] if two else None
-    out = refs[-1]
-    upper = rows_iota() < 4
-    for d in range(3):
-        for x in range(logits.shape[1]):
-            above, below = sides(
-                info[EVEN_Z] == 1, first[d, x].astype(F32), second[d, x].astype(F32) if two else None
-            )
-            tile = jnp.where(upper, above, below)
-            out[d, x] = jnp.concatenate([logits[d, x], tile], axis=0).astype(BF16)
+            brick[d, x] = total.astype(BF16)
+            for phase, face in enumerate(faces):
+                even = info[EVEN_Z] != phase
+                face[d, x] = jnp.where(even, total[rows_z - TILE :], total[:TILE]).astype(BF16)
 
 
 def up(plane, dim):
@@ -284,11 +303,12 @@
     return pltpu.roll(plane, 1, dim)
 
 
-def krylov(
-    size_x, size_z, info, logits, own, mine, other, rhs, first, second, v0, v1, v2, slope_out, dots, weight, free
-):
-    labels, rows_x, rows, _ = rhs.shape
-    rows_z = rows - TILE
+def krylov(colours, size_x, size_z, two, info, planted, slope, logits, mine, other, first, second, *refs):
+    groups = [refs[n * (1 + two) : (n + 1) * (1 + two)] for n in range(6)]
+    faces, mine_edges, other_edges, rhs_faces, edges_a, edges_b = groups
+    v0, v1, v2, slope_out, dots_out, weight, free, dots = refs[6 * (1 + two) :]
+    labels, rows_x, rows_z, _ = slope.shape
+    rows = rows_z + TILE
     channels = 2 * labels
     is_up, even = info[UP] == 1, info[EVEN_X] == 1
     z = rows_iota(rows)
@@ -304,23 +324,33 @@
         in_x = jnp.where(inside, 1.0, 0.0)
         next_x = jnp.where(inside & (place < size_x - 1), 1.0, 0.0)
         for d in range(3):
+            def grown(plane, tiles, source):
+                return jnp.concatenate([plane, rhs_tile(*ends_z(info, tiles, d, source))], axis=0)
+
             if 0 <= x < rows_x:
-                plane = jnp.concatenate([logits[d, x], own[d, x, rows_z:].astype(F32)], axis=0)
-            elif x < 0:
-                plane = jnp.where(is_up, other[d, x + HALO].astype(F32), mine[d, x + HALO].astype(F32))
+                plane = grown(logits[d, x], faces, x)
             else:
-                plane = jnp.where(is_up, mine[d, x - rows_x].astype(F32), other[d, x - rows_x].astype(F32))
+                source = x % rows_x
+                here = grown(mine[d, source].astype(F32), mine_edges, source)
+                there = grown(other[d, source].astype(F32), other_edges, source)
+                plane = jnp.where(is_up, there, here) if x < 0 else jnp.where(is_up, here, there)
             squashed = 1.0 / (1.0 + jnp.exp(-plane))
             valid = (in_z * next_x, next_z * in_x, in_zy * in_x)[d]
             weight[d, at] = (0.05 + squashed) * valid
             if -1 <= x <= rows_x:
                 slope_out[d, x + 1] = squashed * (1.0 - squashed) * valid
         for l in range(labels):
+            source = x % rows_x
             if 0 <= x < rows_x:
-                plane = rhs[l, x]
+                plane = jnp.where(planted[x] >= colours, slope[l, x], SEED)
+                plane = jnp.concatenate([plane, rhs_tile(*ends_z(info, rhs_faces, x, l))], axis=0)
             else:
-                index = channels + l * rows_x + (x + HALO if x < 0 else x - rows_x)
-                above, below = sides(even, first[index].astype(F32), second[index].astype(F32))
+                index = channels + l * rows_x + source
+                received = [
+                    jnp.concatenate([ref[index].astype(F32), rhs_tile(*ends_z(info, tiles, source, l))], axis=0)
+                    for ref, tiles in ((first, edges_a), (second, edges_b))
+                ]
+                above, below = sides(even, *received)
                 plane = below if x < 0 else above
             open_cell = plane < SEED / 2
             v0[l, at] = jnp.where(open_cell, plane, 0.0)
@@ -354,6 +384,8 @@
         return carry
 
     lax.fori_loop(0, labels, label, 0)
+    for n in range(dots_out.shape[0]):
+        dots_out[n] = dots[...]
 
 
 def steps(g00, g01, g11, g12, g22, k22):
@@ -385,8 +417,11 @@
     return c0 + alpha * p0, c1 + alpha * p1, alpha * p2
 
 
-def edges(info, parts, v0, v1, v2, full, first, second, out, lam, field):
-    labels, rows_x, rows, _ = full.shape
+def edges(colours, two, info, parts, v0, v1, v2, planted, likelihoods, first, second, *refs):
+    faces, edges_a, edges_b = refs[: 1 + two], refs[1 + two : 2 + 2 * two], refs[2 + 2 * two : 3 + 3 * two]
+    out, lam, field = refs[3 + 3 * two :]
+    labels, rows_x, rows_z, _ = likelihoods.shape
+    rows = rows_z + TILE
     even = info[EVEN_X] == 1
     total = jnp.sum(parts[...], axis=0)
     total = jnp.broadcast_to(jnp.sum(total, axis=1, keepdims=True), total.shape)
@@ -401,11 +436,18 @@
             source = at + HALO - 1
             lam[l, at] = s0 * v0[l, source] + s1 * v1[l, source] + s2 * v2[l, source]
             x = at - 1
+            source = x % rows_x
             if 0 <= x < rows_x:
-                plane = full[l, x]
+                member = jnp.where(planted[x] == info[COLOUR] + l, 1.0, 0.0)
+                plane = jnp.where(planted[x] >= colours, likelihoods[l, x], member)
+                plane = jnp.concatenate([plane, full_tile(*ends_z(info, faces, x, l))], axis=0)
             else:
-                index = 2 * labels + labels * rows_x + 2 * l + (1 if x < 0 else x - rows_x)
-                above, below = sides(even, first[index].astype(F32), second[index].astype(F32))
+                index = 2 * labels + labels * rows_x + 2 * l + (1 if x < 0 else source)
+                received = [
+                    jnp.concatenate([ref[index].astype(F32), full_tile(*ends_z(info, tiles, source, l))], axis=0)
+                    for ref, tiles in ((first, edges_a), (second, edges_b))
+                ]
+                above, below = sides(even, *received)
                 plane = below if x < 0 else above
             field[l, at] = plane
     for at in range(rows_x + 2):
@@ -458,13 +500,15 @@
                 row = i * 9 + j * 3 + k
                 rows_out[d, row : row + 1] = jnp.sum(total, axis=0, keepdims=True)
     for d in range(3):
-        out[d * TILE : (d + 1) * TILE] = lax.dot_general(
+        sums = lax.dot_general(
             one[...],
             rows_out[d],
             (((1,), (1,)), ((), ())),
             precision=lax.Precision.HIGHEST,
             preferred_element_type=F32,
         )
+        for n in range(out.shape[0]):
+            out[n, d * TILE : (d + 1) * TILE] = sums
 
 
 def image_sums(info, grads, matrix, out, sums):
@@ -490,38 +534,33 @@
     size_x, size_z = rows_x * lax.axis_size("xy"), rows_z * lax.axis_size("gz")
     rows = rows_z + TILE
     two = lax.axis_size("gz") > 2
+    phases = range(1 + two)
+    members = lax.axis_size("xy") * lax.axis_size("gz")
     info = jnp.stack(
         [1 - xy % 2, 1 - gz % 2, xy * rows_x, gz * rows_z, lab * labels, 1 - (xy + lab) % 2]
     ).astype(jnp.int32)
 
+    planes = channels + labels * rows_x + 2 * labels
+    brick = shaped((planes, rows_z, LANES), BF16)
     inputs = (image, planted, likelihoods, slope)
-    faces = []
-    for phase in range(1 + two):
-        block = call(
-            functools.partial(pack_z, colours, phase),
-            shaped((rows_x, labels, TILE, LANES), BF16),
-            info,
-            *inputs,
-            name="pack_z",
-        )
-        faces.append(swap(block, "gz", phase))
-    planes = channels + labels * rows_x + 2 * labels
-    rhs, full, wide_image, send_a, send_b = call(
-        functools.partial(assemble_z, colours, two),
-        [
-            shaped((labels, rows_x, rows, LANES), F32),
-            shaped((labels, rows_x, rows, LANES), F32),
-            shaped((channels, rows_x, rows, LANES), BF16),
-            shaped((planes, rows, LANES), BF16),
-            shaped((planes, rows, LANES), BF16),
-        ],
-        info,
-        *faces,
+    image, planted, likelihoods, slope, *packed = call(
+        functools.partial(pack, colours, two),
+        [shaped(a.shape, a.dtype) for a in inputs]
+        + [shaped((rows_x, labels, TILE, LANES), BF16)] * (1 + two)
+        + [brick, brick],
+        info,
         *inputs,
-        name="assemble_z",
-    )
+        scratch=[pltpu.SemaphoreType.DMA((4,))],
+        name="pack",
+        space=pl.ANY,
+    )
+    send_a, send_b = packed[1 + two :]
+    second = swap(send_b, "xy", 1)
     first = swap(send_a, "xy", 0)
-    second = swap(send_b, "xy", 1)
+    edges_b = [diagonal_swap(packed[phase], 1, phase) for phase in phases]
+    edges_a = [diagonal_swap(packed[phase], 0, phase) for phase in phases]
+    faces = [swap(packed[phase], "gz", phase) for phase in phases]
+    received = (first, second, *faces, *edges_a, *edges_b)
 
     own_filt = lax.dynamic_slice_in_dim(filt, lab * channels, channels, 1)
     lines = jnp.transpose(own_filt, (4, 0, 2, 3, 1)).reshape(81, channels)
@@ -543,72 +582,72 @@
         name="spread_filter",
     )
     part, stack = call(
-        convolve,
+        functools.partial(convolve, two),
         [shaped((3, rows_x, rows_z, LANES), F32), shaped((384, 768), BF16)],
         info,
-        wide_image,
-        first,
-        second,
+        image,
+        *received,
         matrix,
         scratch=[pltpu.VMEM((288, 512), F32)],
         name="convolve",
     )
-    faces_shape = shaped((3, rows_x, TILE, LANES), BF16)
-    logits, *sends = call(
+    logits, own, *sends = call(
         functools.partial(add_parts, two),
-        [shaped(part.shape, F32)] + [faces_shape] * (1 + two),
+        [shaped(part.shape, F32), shaped(part.shape, BF16)]
+        + [shaped((3, rows_x, TILE, LANES), BF16)] * (1 + two),
         info,
         part,
         lab_swap(part),
         name="add_parts",
     )
-    faces = [swap(block, "gz", phase) for phase, block in enumerate(sends)]
-    own = call(
-        functools.partial(extend_logits, two),
-        shaped((3, rows_x, rows, LANES), BF16),
-        info,
-        logits,
-        *faces,
-        name="extend_logits",
-    )
-    mine = split_swap(own, "xy")
+    mine = split_swap(own)
+    mine_edges = [split_diagonal_swap(sends[phase], phase) for phase in phases]
+    logit_faces = [swap(sends[phase], "gz", phase) for phase in phases]
     other = lab_swap(mine)
+    other_edges = [lab_swap(block) for block in mine_edges]
     extended = (labels, rows_x + 2 * HALO, rows, LANES)
     ring = shaped((3, rows_x + 2, rows, LANES), F32)
     v0, v1, v2, squash_slope, dots = call(
-        functools.partial(krylov, size_x, size_z),
-        [shaped(extended, F32)] * 3 + [ring, shaped((6 * labels, LANES), F32)],
-        info,
+        functools.partial(krylov, colours, size_x, size_z, two),
+        [shaped(extended, F32)] * 3 + [ring, shaped((members, 6 * labels, LANES), F32)],
+        info,
+        planted,
+        slope,
         logits,
-        own,
         mine,
         other,
-        rhs,
         first,
         second,
+        *logit_faces,
+        *mine_edges,
+        *other_edges,
+        *faces,
+        *edges_a,
+        *edges_b,
         scratch=[
             pltpu.VMEM((3,) + extended[1:], F32),
             pltpu.VMEM(extended[1:], F32),
+            pltpu.VMEM((6 * labels, LANES), F32),
         ],
         name="krylov",
     )
     edge = call(
-        edges,
+        functools.partial(edges, colours, two),
         ring,
         info,
         everyones(dots, ("xy", "gz")),
         v0,
         v1,
         v2,
-        full,
-        first,
-        second,
+        planted,
+        likelihoods,
+        *received,
         scratch=[pltpu.VMEM((labels, rows_x + 3, rows, LANES), F32)] * 2,
         name="edges",
     )
     grads, sums = call(
         filter_sums,
-        [shaped((768, 768), BF16), shaped((3 * TILE, LANES), F32)],
+        [shaped((768, 768), BF16), shaped((members, 3 * TILE, LANES), F32)],
         info,
         edge,
         lab_swap(edge),

time: 70.9 us -> 72 us (1.016)
  starting transfers between devices: 17.7 us -> 24.1 us
  waiting for transfers between devices: 20 us -> 17.3 us
  blocking collectives: 12.3 us -> 10.5 us
    ppermute x1 -> x4, starting transfers between devices: 6.67 us -> 16.9 us  [the longest x2 7.47 us: diagonal_swap(): return lax.ppermute(block, ('xy', 'gz'), route)]
    ppermute x4, starting transfers between devices: 7.56 us -> 3.71 us  [swap(): return lax.ppermute(block, axis, pair_routes(lax.axis_size(axis), phase))]
    ppermute x4, waiting for transfers between devices: 7.66 us -> 5.38 us  [swap(): return lax.ppermute(block, axis, pair_routes(lax.axis_size(axis), phase))]
    all_to_all x1, blocking collectives: 12.3 us -> 10.5 us  [everyones(): return lax.all_to_all(copies, axes, 0, 0)]
    ppermute x3 -> x4, waiting for transfers between devices: 4.42 us -> 3.11 us  [lab_swap(): return lax.ppermute(block, 'lab', [(0, 1), (1, 0)])]
    ppermute x1 -> x4, waiting for transfers between devices: 2.84 us -> 3.75 us  [the longest x1 2.58 us: split_swap(): return lax.ppermute(block, ('xy', 'lab'), route)]
    pallas_call x10 -> x8, Pallas kernels: 13 us -> 12.8 us  [call(): pl.pallas_call(kernel, out_shape=outs, in_specs=specs, out_specs=jax.tree...]
    unnamed x17 -> x9, local copies, waits for them, and re-layouts: 4.34 us -> 4.33 us
  transfers between devices with their start and end apart: 9 -> 13, of which waited for: 8 -> 7; matrix products, arithmetic and copies ran while one was open for 2% -> 2% of each run, Pallas kernels for 4% -> 4%
where the time goes in v3:
time: 72 us; the launch traced here: 71.5 us
  starting transfers between devices  24.1 us (33%)
  waiting for transfers between devices  17.3 us (24%)
  Pallas kernels  12.8 us (18%)
  blocking collectives  10.5 us (15%)
  local copies, waits for them, and re-layouts  5.89 us (8%)
  between operations  0.86 us (1%)
    pallas_call x8, Pallas kernels, call(): pl.pallas_call(kernel, out_shape=outs, in_specs=specs, out_specs=jax.tree...  12.8 us
    all_to_all x1, blocking collectives, everyones(): return lax.all_to_all(copies, axes, 0, 0)  10.5 us
    ppermute x2, starting transfers between devices, diagonal_swap(): return lax.ppermute(block, ('xy', 'gz'), route)  7.47 us
    ppermute x1, starting transfers between devices, split_swap(): return lax.ppermute(block, ('xy', 'lab'), route)  5.53 us
    ppermute x4, waiting for transfers between devices, swap(): return lax.ppermute(block, axis, pair_routes(lax.axis_size(axis), phase))  5.38 us
    all_to_all x1, waiting for transfers between devices, everyones(): return lax.all_to_all(copies, axes, 0, 0)  5.04 us
    unnamed x9, local copies, waits for them, and re-layouts  4.33 us
    ppermute x1, starting transfers between devices, split_diagonal_swap(): return lax.ppermute(block, ('xy', 'gz', 'lab'), route)  3.89 us
  transfers between devices with their start and end apart: 13, of which 7 were waited for; matrix products, arithmetic and copies ran while one was open for 2% of the time, Pallas kernels for 4%

profile of v3, /device:TPU:0, one launch (start us, length us, event | category | flops | bytes accessed | tf_op | source)
XLA Modules:
  0.0 71.5 jit_solution(4535098815514925597)
XLA Ops:
  0.7 1.0 %copy-done = bf16[8,4,32,128]{3,2,1,0:T(8,128)(2,1)S(1)} copy-done((bf16[8,4,32,128]{3,2,1,0:T(8,128)(2,1)S(1)}, bf16[8,4,32,128]{3,2,1,0:T(8,128)(2,1)}, u32[]{:S(2)}) %copy-start) | copy-done | bytes 262168
  1.7 0.9 %copy-done.1 = f32[4,4,32,128]{3,2,1,0:T(8,128)S(1)} copy-done((f32[4,4,32,128]{3,2,1,0:T(8,128)S(1)}, f32[4,4,32,128]{3,2,1,0:T(8,128)}, u32[]{:S(2)}) %copy-start.1) | copy-done | bytes 262168
  2.6 0.9 %copy-done.2 = f32[4,4,32,128]{3,2,1,0:T(8,128)S(1)} copy-done((f32[4,4,32,128]{3,2,1,0:T(8,128)S(1)}, f32[4,4,32,128]{3,2,1,0:T(8,128)}, u32[]{:S(2)}) %copy-start.2) | copy-done | bytes 262168
  3.6 0.8 %copy-done.3 = s32[4,32,128]{2,1,0:T(8,128)S(1)} copy-done((s32[4,32,128]{2,1,0:T(8,128)S(1)}, s32[4,32,128]{2,1,0:T(8,128)}, u32[]{:S(2)}) %copy-start.3) | copy-done | bytes 65560
  6.0 6.8 %collective-permute-start.3 = (bf16[4,4,8,128]{3,2,1,0:T(8,128)(2,1)S(1)}, bf16[4,4,8,128]{3,2,1,0:T(8,128)(2,1)S(1)}, u32[]{:S(2)}, u32[]{:S(2)}) collective-permute-start(bf16[4,4,8,128]{3,2,1,0:T(8,128)(2,1)S(1)} %get-tuple-element.28), channel_id=1, source_target_pairs={{0,6},{2,4},{4,2},{6,0},{8,14},{10,12},{12,10},{14,8},{1,7},{3,5},... | collective-permute-start | bytes 98312 | tf_op jit(solution)/shard_map/ppermute | solution.py:39
  12.8 1.5 %collective-permute-start.2 = (bf16[4,4,8,128]{3,2,1,0:T(8,128)(2,1)S(1)}, bf16[4,4,8,128]{3,2,1,0:T(8,128)(2,1)S(1)}, u32[]{:S(2)}, u32[]{:S(2)}) collective-permute-start(bf16[4,4,8,128]{3,2,1,0:T(8,128)(2,1)S(1)} %get-tuple-element.28), channel_id=1, source_target_pairs={{0,2},{2,0},{1,3},{3,1},{4,6},{6,4},{5,7},{7,5},{8,10},{10,8},{9,1... | collective-permute-start | bytes 98312 | tf_op jit(solution)/shard_map/ppermute | solution.py:27
  16.3 0.9 %spread_filter.1 = (bf16[3,288,384]{2,1,0:T(8,128)(2,1)S(1)}, bf16[3,256,768]{2,1,0:T(8,128)(2,1)S(1)}) custom-call(s32[6]{0:T(128)S(1)} %stack.27.info, bf16[88,128]{1,0:T(8,128)(2,1)S(1)} %pad.8.first, bf16[72,128]{1,0:T(8,128)(2,1)S(1)} %pad.9.second, bf16[128,128]{1,0:T(8,128)(2,1)S(1)} %get-tuple-element.51.one, bf16[128,128]{1,0:T(8,128)(2,1)S(1)} %get-tuple-element.52.two), custom_call_target="tpu_custom_call" | custom-call | flops 10000000 | bytes 106520 | tf_op jit(solution)/shard_map/spread_filter/pallas_call | solution.py:71
  17.3 4.2 %collective-permute-done.first = bf16[32,32,128]{2,1,0:T(8,128)(2,1)S(1)} collective-permute-done((bf16[32,32,128]{2,1,0:T(8,128)(2,1)S(1)}, bf16[32,32,128]{2,1,0:T(8,128)(2,1)S(1)}, u32[]{:S(2)}, u32[]{:S(2)}) %collective-permute-start) | collective-permute-done | bytes 262176 | tf_op jit(solution)/shard_map/ppermute | solution.py:27
  21.5 1.4 %convolve.1 = (f32[3,4,32,128]{3,2,1,0:T(8,128)S(1)}, bf16[384,768]{1,0:T(8,128)(2,1)S(1)}) custom-call(s32[6]{0:T(128)S(1)} %stack.27.info, bf16[8,4,32,128]{3,2,1,0:T(8,128)(2,1)S(1)} %get-tuple-element.25.image, bf16[32,32,128]{2,1,0:T(8,128)(2,1)S(1)} %collective-permute-done.first, bf16[32,32,128]{2,1,0:T(8,128)(2,1)S(1)} %collective-permute-done.1.second, ...), custom_call_target="tpu_custom_call" | custom-call | flops 1000000 | bytes 1548312 | tf_op jit(solution)/shard_map/convolve/pallas_call | solution.py:71
  22.9 1.4 %collective-permute-done.5.other = f32[3,4,32,128]{3,2,1,0:T(8,128)S(1)} collective-permute-done((f32[3,4,32,128]{3,2,1,0:T(8,128)S(1)}, f32[3,4,32,128]{3,2,1,0:T(8,128)S(1)}, u32[]{:S(2)}, u32[]{:S(2)}) %collective-permute-start.5) | collective-permute-done | bytes 196640 | tf_op jit(solution)/shard_map/ppermute | solution.py:31
  24.9 5.5 %collective-permute-start.6 = (bf16[3,4,32,128]{3,2,1,0:T(8,128)(2,1)S(1)}, bf16[3,4,32,128]{3,2,1,0:T(8,128)(2,1)S(1)}, u32[]{:S(2)}, u32[]{:S(2)}) collective-permute-start(bf16[3,4,32,128]{3,2,1,0:T(8,128)(2,1)S(1)} %get-tuple-element.32), channel_id=1, source_target_pairs={{0,4},{4,0},{8,12},{12,8},{5,9},{9,5},{2,6},{6,2},{10,14},{14,10},... | collective-permute-start | bytes 294920 | tf_op jit(solution)/shard_map/ppermute | solution.py:49
  30.4 2.6 %collective-permute-done.6.mine = bf16[3,4,32,128]{3,2,1,0:T(8,128)(2,1)S(1)} collective-permute-done((bf16[3,4,32,128]{3,2,1,0:T(8,128)(2,1)S(1)}, bf16[3,4,32,128]{3,2,1,0:T(8,128)(2,1)S(1)}, u32[]{:S(2)}, u32[]{:S(2)}) %collective-permute-start.6) | collective-permute-done | bytes 98336 | tf_op jit(solution)/shard_map/ppermute | solution.py:49
  33.0 3.9 %collective-permute-start.9 = (bf16[3,4,8,128]{3,2,1,0:T(8,128)(2,1)S(1)}, bf16[3,4,8,128]{3,2,1,0:T(8,128)(2,1)S(1)}, u32[]{:S(2)}, u32[]{:S(2)}) collective-permute-start(bf16[3,4,8,128]{3,2,1,0:T(8,128)(2,1)S(1)} %get-tuple-element.33), channel_id=1, source_target_pairs={{0,6},{2,4},{4,2},{6,0},{8,14},{10,12},{12,10},{14,8},{5,11},{7,9}... | collective-permute-start | bytes 73736 | tf_op jit(solution)/shard_map/ppermute | solution.py:60
  36.9 1.6 %collective-permute-start.8 = (bf16[3,4,8,128]{3,2,1,0:T(8,128)(2,1)S(1)}, bf16[3,4,8,128]{3,2,1,0:T(8,128)(2,1)S(1)}, u32[]{:S(2)}, u32[]{:S(2)}) collective-permute-start(bf16[3,4,8,128]{3,2,1,0:T(8,128)(2,1)S(1)} %get-tuple-element.33), channel_id=1, source_target_pairs={{0,2},{2,0},{1,3},{3,1},{4,6},{6,4},{5,7},{7,5},{8,10},{10,8},{9,1... | collective-permute-start | bytes 73736 | tf_op jit(solution)/shard_map/ppermute | solution.py:27
  38.5 1.2 %collective-permute-done.9.refs_1_ = bf16[3,4,8,128]{3,2,1,0:T(8,128)(2,1)S(1)} collective-permute-done((bf16[3,4,8,128]{3,2,1,0:T(8,128)(2,1)S(1)}, bf16[3,4,8,128]{3,2,1,0:T(8,128)(2,1)S(1)}, u32[]{:S(2)}, u32[]{:S(2)}) %collective-permute-start.9) | collective-permute-done | bytes 24608 | tf_op jit(solution)/shard_map/ppermute | solution.py:60
  39.6 1.2 %collective-permute-done.8.refs_0_ = bf16[3,4,8,128]{3,2,1,0:T(8,128)(2,1)S(1)} collective-permute-done((bf16[3,4,8,128]{3,2,1,0:T(8,128)(2,1)S(1)}, bf16[3,4,8,128]{3,2,1,0:T(8,128)(2,1)S(1)}, u32[]{:S(2)}, u32[]{:S(2)}) %collective-permute-start.8) | collective-permute-done | bytes 24608 | tf_op jit(solution)/shard_map/ppermute | solution.py:27
  40.8 3.1 %krylov.1 = (f32[4,12,40,128]{3,2,1,0:T(8,128)S(1)}, f32[4,12,40,128]{3,2,1,0:T(8,128)S(1)}, f32[4,12,40,128]{3,2,1,0:T(8,128)S(1)}, f32[3,6,40,128]{3,2,1,0:T(8,128)S(1)}, f32[8,24,128]{2,1,0:T(8,128)S(1)}) custom-call(s32[6]{0:T(128)S(1)} %stack.27.info, s32[4,32,128]{2,1,0:T(8,128)S(1)} %get-tuple-element.23.planted, ...), custom_call_target="tpu_custom_call" | custom-call | flops 1000000 | bytes 1417240 | tf_op jit(solution)/shard_map/krylov/pallas_call | solution.py:71
  43.9 10.5 %all_to_all.10.parts = f32[8,24,128]{2,1,0:T(8,128)S(1)} all-to-all(f32[8,24,128]{2,1,0:T(8,128)S(1)} %get-tuple-element.34), channel_id=1, replica_groups=mesh['crops'=2,'xy'=4,'gz'=2,'lab'=2] {'xy','gz'}, dimensions={0} | all-to-all | bytes 196608 | tf_op jit(solution)/shard_map/all_to_all | solution.py:64
  54.4 1.2 %edges.1.edge = f32[3,6,40,128]{3,2,1,0:T(8,128)S(1)} custom-call(s32[6]{0:T(128)S(1)} %stack.27.info, f32[8,24,128]{2,1,0:T(8,128)S(1)} %all_to_all.10.parts, f32[4,12,40,128]{3,2,1,0:T(8,128)S(1)} %get-tuple-element.35.v0, f32[4,12,40,128]{3,2,1,0:T(8,128)S(1)} %get-tuple-element.36.v1, f32[4,12,40,128]{3,2,1,0:T(8,128)S(1)} %get-tuple-element.37.v2, ...), custom_call_target="tpu_custom_call" | custom-call | flops 1000000 | bytes 3997720 | tf_op jit(solution)/shard_map/edges/pallas_call | solution.py:71
  55.7 1.7 %collective-permute-done.11.other = f32[3,6,40,128]{3,2,1,0:T(8,128)S(1)} collective-permute-done((f32[3,6,40,128]{3,2,1,0:T(8,128)S(1)}, f32[3,6,40,128]{3,2,1,0:T(8,128)S(1)}, u32[]{:S(2)}, u32[]{:S(2)}) %collective-permute-start.11) | collective-permute-done | bytes 368672 | tf_op jit(solution)/shard_map/ppermute | solution.py:31
  57.3 2.9 %filter_sums.1 = (bf16[768,768]{1,0:T(8,128)(2,1)S(1)}, f32[8,24,128]{2,1,0:T(8,128)}) custom-call(s32[6]{0:T(128)S(1)} %stack.27.info, f32[3,6,40,128]{3,2,1,0:T(8,128)S(1)} %edges.1.edge, f32[3,6,40,128]{3,2,1,0:T(8,128)S(1)} %collective-permute-done.11.other, f32[3,6,40,128]{3,2,1,0:T(8,128)S(1)} %get-tuple-element.39.slope, ...), custom_call_target="tpu_custom_call" | custom-call | flops 1000000 | bytes 1699864 | tf_op jit(solution)/shard_map/filter_sums/pallas_call | solution.py:71
  60.2 3.4 %all-to-all-start.1 = ((f32[8,24,128]{2,1,0:T(8,128)}), f32[8,24,128]{2,1,0:T(8,128)S(1)}, u32[]{:S(2)}, u32[]{:S(2)}) async-start(f32[8,24,128]{2,1,0:T(8,128)} %get-tuple-element.43), calls=%async_computation.1 | async-start | bytes 196608 | tf_op jit(solution)/shard_map/all_to_all | solution.py:64
  63.6 2.0 %image_sums.1 = bf16[8,4,32,128]{3,2,1,0:T(8,128)(2,1)} custom-call(s32[6]{0:T(128)S(1)} %stack.27.info, bf16[768,768]{1,0:T(8,128)(2,1)S(1)} %get-tuple-element.41.grads, bf16[3,256,768]{2,1,0:T(8,128)(2,1)S(1)} %get-tuple-element.42.matrix), custom_call_target="tpu_custom_call" | custom-call | flops 10000000 | bytes 2359320 | tf_op jit(solution)/shard_map/image_sums/pallas_call | solution.py:71
  65.6 5.0 %all-to-all-done.1 = f32[8,24,128]{2,1,0:T(8,128)S(1)} async-done(((f32[8,24,128]{2,1,0:T(8,128)}), f32[8,24,128]{2,1,0:T(8,128)S(1)}, u32[]{:S(2)}, u32[]{:S(2)}) %all-to-all-start.1) | async-done | bytes 98336 | tf_op jit(solution)/shard_map/all_to_all | solution.py:64
  (35 shorter events, 5.2 us)
Async XLA Ops:
  0.7 1.0 %copy-start = (bf16[8,4,32,128]{3,2,1,0:T(8,128)(2,1)S(1)}, bf16[8,4,32,128]{3,2,1,0:T(8,128)(2,1)}, u32[]{:S(2)}) copy-start(bf16[8,4,32,128]{3,2,1,0:T(8,128)(2,1)} %image_in.1) | copy-start | bytes 786436
  1.7 0.9 %copy-start.1 = (f32[4,4,32,128]{3,2,1,0:T(8,128)S(1)}, f32[4,4,32,128]{3,2,1,0:T(8,128)}, u32[]{:S(2)}) copy-start(f32[4,4,32,128]{3,2,1,0:T(8,128)} %likelihoods_in.1) | copy-start | bytes 786436
  2.6 0.9 %copy-start.2 = (f32[4,4,32,128]{3,2,1,0:T(8,128)S(1)}, f32[4,4,32,128]{3,2,1,0:T(8,128)}, u32[]{:S(2)}) copy-start(f32[4,4,32,128]{3,2,1,0:T(8,128)} %slope_in.1) | copy-start | bytes 786436
  3.6 0.8 %copy-start.3 = (s32[4,32,128]{2,1,0:T(8,128)S(1)}, s32[4,32,128]{2,1,0:T(8,128)}, u32[]{:S(2)}) copy-start(s32[4,32,128]{2,1,0:T(8,128)} %planted_in.1) | copy-start | bytes 196612
  5.3 11.9 %collective-permute-start.4 = (bf16[4,4,8,128]{3,2,1,0:T(8,128)(2,1)S(1)}, bf16[4,4,8,128]{3,2,1,0:T(8,128)(2,1)S(1)}, u32[]{:S(2)}, u32[]{:S(2)}) collective-permute-start(bf16[4,4,8,128]{3,2,1,0:T(8,128)(2,1)S(1)} %get-tuple-element.28), channel_id=1, source_target_pairs={{4,10},{6,8},{8,6},{10,4},{5,11},{7,9},{9,7},{11,5},{20,26},{22,24... | collective-permute-start | bytes 98312 | tf_op jit(solution)/shard_map/ppermute | solution.py:39
  6.0 11.3 %collective-permute-start.3 = (bf16[4,4,8,128]{3,2,1,0:T(8,128)(2,1)S(1)}, bf16[4,4,8,128]{3,2,1,0:T(8,128)(2,1)S(1)}, u32[]{:S(2)}, u32[]{:S(2)}) collective-permute-start(bf16[4,4,8,128]{3,2,1,0:T(8,128)(2,1)S(1)} %get-tuple-element.28), channel_id=1, source_target_pairs={{0,6},{2,4},{4,2},{6,0},{8,14},{10,12},{12,10},{14,8},{1,7},{3,5},... | collective-permute-start | bytes 98312 | tf_op jit(solution)/shard_map/ppermute | solution.py:39
  12.8 4.5 %collective-permute-start.2 = (bf16[4,4,8,128]{3,2,1,0:T(8,128)(2,1)S(1)}, bf16[4,4,8,128]{3,2,1,0:T(8,128)(2,1)S(1)}, u32[]{:S(2)}, u32[]{:S(2)}) collective-permute-start(bf16[4,4,8,128]{3,2,1,0:T(8,128)(2,1)S(1)} %get-tuple-element.28), channel_id=1, source_target_pairs={{0,2},{2,0},{1,3},{3,1},{4,6},{6,4},{5,7},{7,5},{8,10},{10,8},{9,1... | collective-permute-start | bytes 98312 | tf_op jit(solution)/shard_map/ppermute | solution.py:27
  14.3 7.2 %collective-permute-start = (bf16[32,32,128]{2,1,0:T(8,128)(2,1)S(1)}, bf16[32,32,128]{2,1,0:T(8,128)(2,1)S(1)}, u32[]{:S(2)}, u32[]{:S(2)}) collective-permute-start(bf16[32,32,128]{2,1,0:T(8,128)(2,1)S(1)} %get-tuple-element.26), channel_id=1, source_target_pairs={{0,4},{4,0},{8,12},{12,8},{1,5},{5,1},{9,13},{13,9},{2,6},{6,2},{1... | collective-permute-start | bytes 786440 | tf_op jit(solution)/shard_map/ppermute | solution.py:27
  14.3 7.2 %collective-permute-start.1 = (bf16[32,32,128]{2,1,0:T(8,128)(2,1)S(1)}, bf16[32,32,128]{2,1,0:T(8,128)(2,1)S(1)}, u32[]{:S(2)}, u32[]{:S(2)}) collective-permute-start(bf16[32,32,128]{2,1,0:T(8,128)(2,1)S(1)} %get-tuple-element.27), channel_id=1, source_target_pairs={{4,8},{8,4},{5,9},{9,5},{6,10},{10,6},{7,11},{11,7},{20,24},{24,20... | collective-permute-start | bytes 786440 | tf_op jit(solution)/shard_map/ppermute | solution.py:27
  22.8 1.5 %collective-permute-start.5 = (f32[3,4,32,128]{3,2,1,0:T(8,128)S(1)}, f32[3,4,32,128]{3,2,1,0:T(8,128)S(1)}, u32[]{:S(2)}, u32[]{:S(2)}) collective-permute-start(f32[3,4,32,128]{3,2,1,0:T(8,128)S(1)} %get-tuple-element.30.part), channel_id=1, source_target_pairs={{0,1},{1,0},{2,3},{3,2},{4,5},{5,4},{6,7},{7,6},{8,9},{9,8},{10,11... | collective-permute-start | bytes 589832 | tf_op jit(solution)/shard_map/ppermute | solution.py:31
  24.9 8.1 %collective-permute-start.6 = (bf16[3,4,32,128]{3,2,1,0:T(8,128)(2,1)S(1)}, bf16[3,4,32,128]{3,2,1,0:T(8,128)(2,1)S(1)}, u32[]{:S(2)}, u32[]{:S(2)}) collective-permute-start(bf16[3,4,32,128]{3,2,1,0:T(8,128)(2,1)S(1)} %get-tuple-element.32), channel_id=1, source_target_pairs={{0,4},{4,0},{8,12},{12,8},{5,9},{9,5},{2,6},{6,2},{10,14},{14,10},... | collective-permute-start | bytes 294920 | tf_op jit(solution)/shard_map/ppermute | solution.py:49
  33.0 7.8 %collective-permute-start.7 = (bf16[3,4,32,128]{3,2,1,0:T(8,128)(2,1)S(1)}, bf16[3,4,32,128]{3,2,1,0:T(8,128)(2,1)S(1)}, u32[]{:S(2)}, u32[]{:S(2)}) collective-permute-start(bf16[3,4,32,128]{3,2,1,0:T(8,128)(2,1)S(1)} %collective-permute-done.6.mine), channel_id=1, source_target_pairs={{0,1},{1,0},{2,3},{3,2},{4,5},{5,4},{6,7},{7,6},{8,9},{9,8},{10,11... | collective-permute-start | bytes 294920 | tf_op jit(solution)/shard_map/ppermute | solution.py:31
  33.0 6.6 %collective-permute-start.9 = (bf16[3,4,8,128]{3,2,1,0:T(8,128)(2,1)S(1)}, bf16[3,4,8,128]{3,2,1,0:T(8,128)(2,1)S(1)}, u32[]{:S(2)}, u32[]{:S(2)}) collective-permute-start(bf16[3,4,8,128]{3,2,1,0:T(8,128)(2,1)S(1)} %get-tuple-element.33), channel_id=1, source_target_pairs={{0,6},{2,4},{4,2},{6,0},{8,14},{10,12},{12,10},{14,8},{5,11},{7,9}... | collective-permute-start | bytes 73736 | tf_op jit(solution)/shard_map/ppermute | solution.py:60
  36.9 3.9 %collective-permute-start.8 = (bf16[3,4,8,128]{3,2,1,0:T(8,128)(2,1)S(1)}, bf16[3,4,8,128]{3,2,1,0:T(8,128)(2,1)S(1)}, u32[]{:S(2)}, u32[]{:S(2)}) collective-permute-start(bf16[3,4,8,128]{3,2,1,0:T(8,128)(2,1)S(1)} %get-tuple-element.33), channel_id=1, source_target_pairs={{0,2},{2,0},{1,3},{3,1},{4,6},{6,4},{5,7},{7,5},{8,10},{10,8},{9,1... | collective-permute-start | bytes 73736 | tf_op jit(solution)/shard_map/ppermute | solution.py:27
  39.6 1.2 %collective-permute-start.10 = (bf16[3,4,8,128]{3,2,1,0:T(8,128)(2,1)S(1)}, bf16[3,4,8,128]{3,2,1,0:T(8,128)(2,1)S(1)}, u32[]{:S(2)}, u32[]{:S(2)}) collective-permute-start(bf16[3,4,8,128]{3,2,1,0:T(8,128)(2,1)S(1)} %collective-permute-done.9.refs_1_), channel_id=1, source_target_pairs={{0,1},{1,0},{2,3},{3,2},{4,5},{5,4},{6,7},{7,6},{8,9},{9,8},{10,11... | collective-permute-start | bytes 73736 | tf_op jit(solution)/shard_map/ppermute | solution.py:31
  55.6 1.8 %collective-permute-start.11 = (f32[3,6,40,128]{3,2,1,0:T(8,128)S(1)}, f32[3,6,40,128]{3,2,1,0:T(8,128)S(1)}, u32[]{:S(2)}, u32[]{:S(2)}) collective-permute-start(f32[3,6,40,128]{3,2,1,0:T(8,128)S(1)} %edges.1.edge), channel_id=1, source_target_pairs={{0,1},{1,0},{2,3},{3,2},{4,5},{5,4},{6,7},{7,6},{8,9},{9,8},{10,11... | collective-permute-start | bytes 1105928 | tf_op jit(solution)/shard_map/ppermute | solution.py:31
  60.2 10.4 %all-to-all-start.1 = ((f32[8,24,128]{2,1,0:T(8,128)}), f32[8,24,128]{2,1,0:T(8,128)S(1)}, u32[]{:S(2)}, u32[]{:S(2)}) async-start(f32[8,24,128]{2,1,0:T(8,128)} %get-tuple-element.43), calls=%async_computation.1 | async-start | bytes 196608 | tf_op jit(solution)/shard_map/all_to_all | solution.py:64

commit v4 on v3

--- a/solution.py
+++ b/solution.py
@@ -13,18 +13,20 @@
 TILE = 8
 LANES = 128
 BF16, F32 = jnp.bfloat16, jnp.float32
-EVEN_X, EVEN_Z, FIRST_X, FIRST_Z, COLOUR, UP = range(6)
-
-
-def pair_routes(count, phase):
+EVEN_X, EVEN_Z, FIRST_X, FIRST_Z, COLOUR, UP, PREV_X, NEXT_X, PREV_Z, NEXT_Z = range(10)
+
+
+def pair_routes(count, phase, closed=False):
     route = []
     for low in range(phase, count - 1, 2):
         route += [(low, low + 1), (low + 1, low)]
+    if closed and phase == 1 and count % 2 == 0:
+        route += [(count - 1, 0), (0, count - 1)]
     return route
 
 
-def swap(block, axis, phase):
-    return lax.ppermute(block, axis, pair_routes(lax.axis_size(axis), phase))
+def swap(block, axis, phase, closed=False):
+    return lax.ppermute(block, axis, pair_routes(lax.axis_size(axis), phase, closed))
 
 
 def lab_swap(block):
@@ -32,8 +34,8 @@
 
 
 def diagonal_swap(block, x_phase, z_phase):
-    along_x = pair_routes(lax.axis_size("xy"), x_phase)
-    along_z = pair_routes(lax.axis_size("gz"), z_phase)
+    along_x = pair_routes(lax.axis_size("xy"), x_phase, True)
+    along_z = pair_routes(lax.axis_size("gz"), z_phase, True)
     count = lax.axis_size("gz")
     route = [(sx * count + sz, dx * count + dz) for sx, dx in along_x for sz, dz in along_z]
     return lax.ppermute(block, ("xy", "gz"), route)
@@ -44,7 +46,7 @@
     route = [
         (src * labs + lab, dst * labs + lab)
         for lab in range(labs)
-        for src, dst in pair_routes(lax.axis_size("xy"), lab % 2)
+        for src, dst in pair_routes(lax.axis_size("xy"), lab % 2, True)
     ]
     return lax.ppermute(block, ("xy", "lab"), route)
 
@@ -54,8 +56,8 @@
     route = [
         ((sx * count + sz) * labs + lab, (dx * count + dz) * labs + lab)
         for lab in range(labs)
-        for sx, dx in pair_routes(lax.axis_size("xy"), lab % 2)
-        for sz, dz in pair_routes(count, z_phase)
+        for sx, dx in pair_routes(lax.axis_size("xy"), lab % 2, True)
+        for sz, dz in pair_routes(count, z_phase, True)
     ]
     return lax.ppermute(block, ("xy", "gz", "lab"), route)
 
@@ -104,17 +106,32 @@
     copies = [pltpu.make_async_copy(src, dst, sems.at[n]) for n, (src, dst) in enumerate(pairs)]
     for copy in copies:
         copy.start()
-    for copy in copies:
-        copy.wait()
     labels, rows_x, rows_z, _ = likelihoods.shape
     channels = image.shape[0]
     last, first = slice(rows_z - TILE, rows_z), slice(0, TILE)
+    even = info[EVEN_X] == 1
+    high, low = jnp.where(even, rows_x - 1, 0), jnp.where(even, 0, rows_x - 1)
+    copies[0].wait()
+    copies[1].wait()
+    for x in range(rows_x):
+        for l in range(labels):
+            rhs = jnp.where(planted[x] >= colours, slope[l, x], SEED).astype(BF16)
+            send_a[channels + l * rows_x + x] = rhs
+            send_b[channels + l * rows_x + x] = rhs
+    copies[2].wait()
+    for l in range(labels):
+        for send, at in ((send_a, high), (send_b, low)):
+            for r in range(2):
+                x = jnp.where(at == 0, 0, rows_x - 2) + r
+                _, full = fields(planted[x], likelihoods[l, x], slope[l, x], colours, info[COLOUR] + l)
+                send[channels + labels * rows_x + 2 * l + r] = full.astype(BF16)
+    copies[3].wait()
+    for c in range(channels):
+        send_a[c] = image[c, high]
+        send_b[c] = image[c, low]
     for phase, out in enumerate(faces):
         even = info[EVEN_Z] != phase
         place = (rows_iota() + jnp.where(even, 0, 4)) & 7
-
-        def at_end(plane):
-            return jnp.where(even, plane[last], plane[first])
 
         def channel(c, x):
             return jnp.where(even, image[c, x, last].astype(F32), image[c, x, first].astype(F32))
@@ -132,22 +149,6 @@
                 rest = jnp.where(place == 2, first_channel, second_channel)
                 rest = jnp.where(place < 2, turned(full, 2, 4), rest)
                 out[x, l] = jnp.where(place >= 4, rhs, rest).astype(BF16)
-    even = info[EVEN_X] == 1
-    high, low = jnp.where(even, rows_x - 1, 0), jnp.where(even, 0, rows_x - 1)
-    for c in range(channels):
-        send_a[c] = image[c, high]
-        send_b[c] = image[c, low]
-    for x in range(rows_x):
-        for l in range(labels):
-            rhs = jnp.where(planted[x] >= colours, slope[l, x], SEED).astype(BF16)
-            send_a[channels + l * rows_x + x] = rhs
-            send_b[channels + l * rows_x + x] = rhs
-    for l in range(labels):
-        for send, at in ((send_a, high), (send_b, low)):
-            for r in range(2):
-                x = jnp.where(at == 0, 0, rows_x - 2) + r
-                _, full = fields(planted[x], likelihoods[l, x], slope[l, x], colours, info[COLOUR] + l)
-                send[channels + labels * rows_x + 2 * l + r] = full.astype(BF16)
 
 
 def sides(even, first, second):
@@ -169,8 +170,10 @@
     return jnp.where(rows_iota() < 4, pltpu.roll(above, 4, 0), pltpu.roll(below, 6, 0))
 
 
-def image_tile(above, below, c):
+def image_tile(info, above, below, c):
     up, down = (2, 5) if c % 2 == 0 else (1, 4)
+    above = jnp.where(info[NEXT_Z] == 1, above, 0.0)
+    below = jnp.where(info[PREV_Z] == 1, below, 0.0)
     return jnp.where(rows_iota() < 4, pltpu.roll(above, up, 0), pltpu.roll(below, down, 0))
 
 
@@ -251,7 +254,7 @@
             else:
                 ends = [ends_z(info, tiles, rows_x - 1 if xp == 0 else 0, c // 2) for tiles in (edges_a, edges_b)]
             for ch in (c, c + 1):
-                tiles = [image_tile(*pair, ch) for pair in ends]
+                tiles = [image_tile(info, *pair, ch) for pair in ends]
                 if 0 < xp <= rows_x:
                     planes.append(jnp.concatenate([image[ch, xp - 1].astype(F32), tiles[0]], axis=0))
                 else:
@@ -260,7 +263,8 @@
                         for ref, tile in zip((first, second), tiles)
                     ]
                     above, below = sides(even, *received)
-                    planes.append(below if xp == 0 else above)
+                    plane, exists = (below, PREV_X) if xp == 0 else (above, NEXT_X)
+                    planes.append(jnp.where(info[exists] == 1, plane, 0.0))
             at = (xp * channels + c) * TILE
             for t in range(-1, 5):
                 both = jnp.concatenate([plane[tile_rows(t)] for plane in planes], axis=0)
@@ -384,8 +388,14 @@
         return carry
 
     lax.fori_loop(0, labels, label, 0)
+    total = jnp.sum(dots[...], axis=1, keepdims=True)
+    tile = jnp.zeros((TILE, LANES), F32)
+    for n in range(6):
+        column = total[tile_rows(n // 2)]
+        column = jnp.broadcast_to(column, (TILE, LANES))
+        tile = jnp.where(lanes_iota() == n, pltpu.roll(column, 4, 0) if n % 2 else column, tile)
     for n in range(dots_out.shape[0]):
-        dots_out[n] = dots[...]
+        dots_out[n] = tile
 
 
 def steps(g00, g01, g11, g12, g22, k22):
@@ -424,11 +434,7 @@
     rows = rows_z + TILE
     even = info[EVEN_X] == 1
     total = jnp.sum(parts[...], axis=0)
-    total = jnp.broadcast_to(jnp.sum(total, axis=1, keepdims=True), total.shape)
-    grams = []
-    for t in range(3):
-        tile = total[tile_rows(t)]
-        grams += [tile, pltpu.roll(tile, 4, 0)]
+    grams = [jnp.broadcast_to(total[:, n : n + 1], (TILE, LANES)) for n in range(6)]
     c0, c1, c2 = steps(*grams)
     for l in range(labels):
         s0, s1, s2 = (jnp.broadcast_to(c[l : l + 1], (rows, LANES)) for c in (c0, c1, c2))
@@ -497,18 +503,17 @@
                             col = (x + i) // 2 * LANES
                             piece = products[o + 1, at : at + TILE, col : col + LANES]
                             total = total + jnp.where(masks[(x + i) % 2, j, o], piece, 0.0)
-                row = i * 9 + j * 3 + k
-                rows_out[d, row : row + 1] = jnp.sum(total, axis=0, keepdims=True)
-    for d in range(3):
-        sums = lax.dot_general(
-            one[...],
-            rows_out[d],
-            (((1,), (1,)), ((), ())),
-            precision=lax.Precision.HIGHEST,
-            preferred_element_type=F32,
-        )
-        for n in range(out.shape[0]):
-            out[n, d * TILE : (d + 1) * TILE] = sums
+                row = d * 27 + i * 9 + j * 3 + k
+                rows_out[row : row + 1] = jnp.sum(total, axis=0, keepdims=True)
+    sums = lax.dot_general(
+        one[...],
+        rows_out[...],
+        (((1,), (1,)), ((), ())),
+        precision=lax.Precision.HIGHEST,
+        preferred_element_type=F32,
+    )
+    for n in range(out.shape[0]):
+        out[n] = sums
 
 
 def image_sums(info, grads, matrix, out, sums):
@@ -537,12 +542,23 @@
     phases = range(1 + two)
     members = lax.axis_size("xy") * lax.axis_size("gz")
     info = jnp.stack(
-        [1 - xy % 2, 1 - gz % 2, xy * rows_x, gz * rows_z, lab * labels, 1 - (xy + lab) % 2]
+        [
+            1 - xy % 2,
+            1 - gz % 2,
+            xy * rows_x,
+            gz * rows_z,
+            lab * labels,
+            1 - (xy + lab) % 2,
+            jnp.minimum(xy, 1),
+            jnp.minimum(lax.axis_size("xy") - 1 - xy, 1),
+            jnp.minimum(gz, 1),
+            jnp.minimum(lax.axis_size("gz") - 1 - gz, 1),
+        ]
     ).astype(jnp.int32)
 
+    inputs = (image, planted, likelihoods, slope)
     planes = channels + labels * rows_x + 2 * labels
     brick = shaped((planes, rows_z, LANES), BF16)
-    inputs = (image, planted, likelihoods, slope)
     image, planted, likelihoods, slope, *packed = call(
         functools.partial(pack, colours, two),
         [shaped(a.shape, a.dtype) for a in inputs]
@@ -552,14 +568,14 @@
         *inputs,
         scratch=[pltpu.SemaphoreType.DMA((4,))],
         name="pack",
-        space=pl.ANY,
+        space=pltpu.HBM,
     )
     send_a, send_b = packed[1 + two :]
+    faces = [swap(packed[phase], "gz", phase, True) for phase in phases]
+    edges_a = [diagonal_swap(packed[phase], 0, phase) for phase in phases]
+    edges_b = [diagonal_swap(packed[phase], 1, phase) for phase in phases]
     second = swap(send_b, "xy", 1)
     first = swap(send_a, "xy", 0)
-    edges_b = [diagonal_swap(packed[phase], 1, phase) for phase in phases]
-    edges_a = [diagonal_swap(packed[phase], 0, phase) for phase in phases]
-    faces = [swap(packed[phase], "gz", phase) for phase in phases]
     received = (first, second, *faces, *edges_a, *edges_b)
 
     own_filt = lax.dynamic_slice_in_dim(filt, lab * channels, channels, 1)
@@ -602,14 +618,15 @@
     )
     mine = split_swap(own)
     mine_edges = [split_diagonal_swap(sends[phase], phase) for phase in phases]
-    logit_faces = [swap(sends[phase], "gz", phase) for phase in phases]
+    logit_faces = [swap(sends[phase], "gz", phase, True) for phase in phases]
+    mine, mine_edges, logit_faces = lax.optimization_barrier((mine, mine_edges, logit_faces))
     other = lab_swap(mine)
     other_edges = [lab_swap(block) for block in mine_edges]
     extended = (labels, rows_x + 2 * HALO, rows, LANES)
     ring = shaped((3, rows_x + 2, rows, LANES), F32)
     v0, v1, v2, squash_slope, dots = call(
         functools.partial(krylov, colours, size_x, size_z, two),
-        [shaped(extended, F32)] * 3 + [ring, shaped((members, 6 * labels, LANES), F32)],
+        [shaped(extended, F32)] * 3 + [ring, shaped((members, TILE, LANES), F32)],
         info,
         planted,
         slope,
@@ -647,14 +664,14 @@
     )
     grads, sums = call(
         filter_sums,
-        [shaped((768, 768), BF16), shaped((members, 3 * TILE, LANES), F32)],
+        [shaped((768, 768), BF16), shaped((members, TILE, LANES), F32)],
         info,
         edge,
         lab_swap(edge),
         squash_slope,
         stack,
         by_channel[:TILE].astype(F32),
-        scratch=[pltpu.VMEM((3, 512, 384), F32), pltpu.VMEM((3, LANES, LANES), F32)],
+        scratch=[pltpu.VMEM((3, 512, 384), F32), pltpu.VMEM((LANES, LANES), F32)],
         name="filter_sums",
     )
     grad_image = call(
@@ -668,7 +685,8 @@
         name="image_sums",
     )
     grad_filter = jnp.sum(everyones(sums, ("xy", "gz")), axis=0)
-    return grad_image, grad_filter[:, :27].reshape(3, channels, 3, 3, 3)
+    grad_filter = grad_filter[:, :81].reshape(channels, 3, 27)
+    return grad_image, jnp.transpose(grad_filter, (1, 0, 2)).reshape(3, channels, 3, 3, 3)
 
 
 def solution(mesh):

time: 72 us -> 64 us (0.89)
  starting transfers between devices: 24.1 us -> 19.1 us
  waiting for transfers between devices: 17.3 us -> 15.1 us
    ppermute x1, starting transfers between devices: 3.89 us -> 0.98 us  [split_diagonal_swap(): return lax.ppermute(block, ('xy', 'gz', 'lab'), route)]
    ppermute x1, waiting for transfers between devices: 2.58 us -> 0.01 us  [split_swap(): return lax.ppermute(block, ('xy', 'lab'), route)]
    ppermute x1, starting transfers between devices: 5.53 us -> 3.34 us  [split_swap(): return lax.ppermute(block, ('xy', 'lab'), route)]
    ppermute x2, starting transfers between devices: 7.47 us -> 6.04 us  [diagonal_swap(): return lax.ppermute(block, ('xy', 'gz'), route)]
    ppermute x4, starting transfers between devices: 3.71 us -> 4.71 us  [swap(): lax.ppermute(block, axis, pair_routes(lax.axis_size(axis), phase, closed))]
    ppermute x4, waiting for transfers between devices: 3.11 us -> 3.94 us  [lab_swap(): return lax.ppermute(block, 'lab', [(0, 1), (1, 0)])]
    unnamed x9 -> x8, local copies, waits for them, and re-layouts: 4.33 us -> 3.69 us
  transfers between devices with their start and end apart: 13 -> 13, of which waited for: 7 -> 7; matrix products, arithmetic and copies ran while one was open for 2% -> 2% of each run, Pallas kernels for 4% -> 5%
where the time goes in v4:
time: 64 us; the launch traced here: 63.6 us
  starting transfers between devices  19.1 us (30%)
  waiting for transfers between devices  15.1 us (24%)
  Pallas kernels  12.6 us (20%)
  blocking collectives  9.96 us (16%)
  local copies, waits for them, and re-layouts  5.92 us (9%)
  between operations  0.83 us (1%)
    pallas_call x8, Pallas kernels, call(): pl.pallas_call(kernel, out_shape=outs, in_specs=specs, out_specs=jax.tree...  12.6 us
    all_to_all x1, blocking collectives, everyones(): return lax.all_to_all(copies, axes, 0, 0)  9.96 us
    ppermute x2, starting transfers between devices, diagonal_swap(): return lax.ppermute(block, ('xy', 'gz'), route)  6.04 us
    ppermute x4, waiting for transfers between devices, swap(): lax.ppermute(block, axis, pair_routes(lax.axis_size(axis), phase, closed))  5.35 us
    ppermute x4, starting transfers between devices, swap(): lax.ppermute(block, axis, pair_routes(lax.axis_size(axis), phase, closed))  4.71 us
    all_to_all x1, waiting for transfers between devices, everyones(): return lax.all_to_all(copies, axes, 0, 0)  4.6 us
    ppermute x4, waiting for transfers between devices, lab_swap(): return lax.ppermute(block, 'lab', [(0, 1), (1, 0)])  3.94 us
    unnamed x8, local copies, waits for them, and re-layouts  3.69 us
  transfers between devices with their start and end apart: 13, of which 7 were waited for; matrix products, arithmetic and copies ran while one was open for 2% of the time, Pallas kernels for 5%

profile of v4, /device:TPU:0, one launch (start us, length us, event | category | flops | bytes accessed | tf_op | source)
XLA Modules:
  0.0 63.6 jit_solution(7617499499079373526)
XLA Ops:
  0.8 1.0 %copy-done = bf16[8,4,32,128]{3,2,1,0:T(8,128)(2,1)S(1)} copy-done((bf16[8,4,32,128]{3,2,1,0:T(8,128)(2,1)S(1)}, bf16[8,4,32,128]{3,2,1,0:T(8,128)(2,1)}, u32[]{:S(2)}) %copy-start) | copy-done | bytes 262168
  1.7 0.9 %copy-done.1 = f32[4,4,32,128]{3,2,1,0:T(8,128)S(1)} copy-done((f32[4,4,32,128]{3,2,1,0:T(8,128)S(1)}, f32[4,4,32,128]{3,2,1,0:T(8,128)}, u32[]{:S(2)}) %copy-start.1) | copy-done | bytes 262168
  2.7 0.9 %copy-done.2 = f32[4,4,32,128]{3,2,1,0:T(8,128)S(1)} copy-done((f32[4,4,32,128]{3,2,1,0:T(8,128)S(1)}, f32[4,4,32,128]{3,2,1,0:T(8,128)}, u32[]{:S(2)}) %copy-start.2) | copy-done | bytes 262168
  4.5 0.9 %pack.1 = (bf16[8,4,32,128]{3,2,1,0:T(8,128)(2,1)S(1)}, s32[4,32,128]{2,1,0:T(8,128)S(1)}, f32[4,4,32,128]{3,2,1,0:T(8,128)S(1)}, f32[4,4,32,128]{3,2,1,0:T(8,12...) custom-call(s32[10]{0:T(128)S(1)} %stack.43.info, ...), custom_call_target="tpu_custom_call" | custom-call | flops 1000000 | bytes 852008 | tf_op jit(solution)/shard_map/pack/pallas_call | solution.py:73
  5.3 6.0 %collective-permute-start.4 = (bf16[4,4,8,128]{3,2,1,0:T(8,128)(2,1)S(1)}, bf16[4,4,8,128]{3,2,1,0:T(8,128)(2,1)S(1)}, u32[]{:S(2)}, u32[]{:S(2)}) collective-permute-start(bf16[4,4,8,128]{3,2,1,0:T(8,128)(2,1)S(1)} %get-tuple-element.31), channel_id=1, source_target_pairs={{4,10},{6,8},{8,6},{10,4},{12,2},{14,0},{0,14},{2,12},{5,11},{7,9}... | collective-permute-start | bytes 98312 | tf_op jit(solution)/shard_map/ppermute | solution.py:41
  11.4 1.0 %collective-permute-start.2 = (bf16[4,4,8,128]{3,2,1,0:T(8,128)(2,1)S(1)}, bf16[4,4,8,128]{3,2,1,0:T(8,128)(2,1)S(1)}, u32[]{:S(2)}, u32[]{:S(2)}) collective-permute-start(bf16[4,4,8,128]{3,2,1,0:T(8,128)(2,1)S(1)} %get-tuple-element.31), channel_id=1, source_target_pairs={{0,2},{2,0},{1,3},{3,1},{4,6},{6,4},{5,7},{7,5},{8,10},{10,8},{9,1... | collective-permute-start | bytes 98312 | tf_op jit(solution)/shard_map/ppermute | solution.py:29
  12.4 2.5 %collective-permute-start = (bf16[32,32,128]{2,1,0:T(8,128)(2,1)S(1)}, bf16[32,32,128]{2,1,0:T(8,128)(2,1)S(1)}, u32[]{:S(2)}, u32[]{:S(2)}) collective-permute-start(bf16[32,32,128]{2,1,0:T(8,128)(2,1)S(1)} %get-tuple-element.29), channel_id=1, source_target_pairs={{0,4},{4,0},{8,12},{12,8},{1,5},{5,1},{9,13},{13,9},{2,6},{6,2},{1... | collective-permute-start | bytes 786440 | tf_op jit(solution)/shard_map/ppermute | solution.py:29
  16.9 0.9 %spread_filter.1 = (bf16[3,288,384]{2,1,0:T(8,128)(2,1)S(1)}, bf16[3,256,768]{2,1,0:T(8,128)(2,1)S(1)}) custom-call(s32[10]{0:T(128)S(1)} %stack.43.info, bf16[88,128]{1,0:T(8,128)(2,1)S(1)} %pad.8.first, bf16[72,128]{1,0:T(8,128)(2,1)S(1)} %pad.9.second, bf16[128,128]{1,0:T(8,128)(2,1)S(1)} %get-tuple-element.53.one, bf16[128,128]{1,0:T(8,128)(2,1)S(1)} %get-tuple-element.54.two), custom_call_target="tpu_custom_call" | custom-call | flops 10000000 | bytes 106536 | tf_op jit(solution)/shard_map/spread_filter/pallas_call | solution.py:73
  17.8 2.8 %collective-permute-done.first = bf16[32,32,128]{2,1,0:T(8,128)(2,1)S(1)} collective-permute-done((bf16[32,32,128]{2,1,0:T(8,128)(2,1)S(1)}, bf16[32,32,128]{2,1,0:T(8,128)(2,1)S(1)}, u32[]{:S(2)}, u32[]{:S(2)}) %collective-permute-start) | collective-permute-done | bytes 262176 | tf_op jit(solution)/shard_map/ppermute | solution.py:29
  20.7 1.4 %convolve.1 = (f32[3,4,32,128]{3,2,1,0:T(8,128)S(1)}, bf16[384,768]{1,0:T(8,128)(2,1)S(1)}) custom-call(s32[10]{0:T(128)S(1)} %stack.43.info, bf16[8,4,32,128]{3,2,1,0:T(8,128)(2,1)S(1)} %get-tuple-element.28.image, bf16[32,32,128]{2,1,0:T(8,128)(2,1)S(1)} %collective-permute-done.first, bf16[32,32,128]{2,1,0:T(8,128)(2,1)S(1)} %collective-permute-done.1.second, ...), custom_call_target="tpu_custom_call" | custom-call | flops 1000000 | bytes 1548328 | tf_op jit(solution)/shard_map/convolve/pallas_call | solution.py:73
  22.1 1.4 %collective-permute-done.5.other = f32[3,4,32,128]{3,2,1,0:T(8,128)S(1)} collective-permute-done((f32[3,4,32,128]{3,2,1,0:T(8,128)S(1)}, f32[3,4,32,128]{3,2,1,0:T(8,128)S(1)}, u32[]{:S(2)}, u32[]{:S(2)}) %collective-permute-start.5) | collective-permute-done | bytes 196640 | tf_op jit(solution)/shard_map/ppermute | solution.py:33
  24.1 3.3 %collective-permute-start.6 = (bf16[3,4,32,128]{3,2,1,0:T(8,128)(2,1)S(1)}, bf16[3,4,32,128]{3,2,1,0:T(8,128)(2,1)S(1)}, u32[]{:S(2)}, u32[]{:S(2)}) collective-permute-start(bf16[3,4,32,128]{3,2,1,0:T(8,128)(2,1)S(1)} %get-tuple-element.35), channel_id=1, source_target_pairs={{0,4},{4,0},{8,12},{12,8},{5,9},{9,5},{13,1},{1,13},{2,6},{6,2},{1... | collective-permute-start | bytes 294920 | tf_op jit(solution)/shard_map/ppermute | solution.py:51
  28.0 1.0 %collective-permute-start.7 = (bf16[3,4,8,128]{3,2,1,0:T(8,128)(2,1)S(1)}, bf16[3,4,8,128]{3,2,1,0:T(8,128)(2,1)S(1)}, u32[]{:S(2)}, u32[]{:S(2)}) collective-permute-start(bf16[3,4,8,128]{3,2,1,0:T(8,128)(2,1)S(1)} %get-tuple-element.36), channel_id=1, source_target_pairs={{0,6},{2,4},{4,2},{6,0},{8,14},{10,12},{12,10},{14,8},{5,11},{7,9}... | collective-permute-start | bytes 73736 | tf_op jit(solution)/shard_map/ppermute | solution.py:62
  29.0 2.5 %collective-permute-done.8.refs_0_ = bf16[3,4,8,128]{3,2,1,0:T(8,128)(2,1)S(1)} collective-permute-done((bf16[3,4,8,128]{3,2,1,0:T(8,128)(2,1)S(1)}, bf16[3,4,8,128]{3,2,1,0:T(8,128)(2,1)S(1)}, u32[]{:S(2)}, u32[]{:S(2)}) %collective-permute-start.8) | collective-permute-done | bytes 24608 | tf_op jit(solution)/shard_map/ppermute | solution.py:29
  31.5 1.2 %collective-permute-done.7.refs_1_ = bf16[3,4,8,128]{3,2,1,0:T(8,128)(2,1)S(1)} collective-permute-done((bf16[3,4,8,128]{3,2,1,0:T(8,128)(2,1)S(1)}, bf16[3,4,8,128]{3,2,1,0:T(8,128)(2,1)S(1)}, u32[]{:S(2)}, u32[]{:S(2)}) %collective-permute-start.7) | collective-permute-done | bytes 24608 | tf_op jit(solution)/shard_map/ppermute | solution.py:62
  33.2 0.8 %collective-permute-done.10.refs_2_ = bf16[3,4,8,128]{3,2,1,0:T(8,128)(2,1)S(1)} collective-permute-done((bf16[3,4,8,128]{3,2,1,0:T(8,128)(2,1)S(1)}, bf16[3,4,8,128]{3,2,1,0:T(8,128)(2,1)S(1)}, u32[]{:S(2)}, u32[]{:S(2)}) %collective-permute-start.10) | collective-permute-done | bytes 24608 | tf_op jit(solution)/shard_map/ppermute | solution.py:33
  34.1 3.2 %krylov.1 = (f32[4,12,40,128]{3,2,1,0:T(8,128)S(1)}, f32[4,12,40,128]{3,2,1,0:T(8,128)S(1)}, f32[4,12,40,128]{3,2,1,0:T(8,128)S(1)}, f32[3,6,40,128]{3,2,1,0:T(8,128)S(1)}, f32[8,8,128]{2,1,0:T(8,128)S(1)}) custom-call(s32[10]{0:T(128)S(1)} %stack.43.info, s32[4,32,128]{2,1,0:T(8,128)S(1)} %get-tuple-element.26.planted, ...), custom_call_target="tpu_custom_call" | custom-call | flops 1000000 | bytes 1417256 | tf_op jit(solution)/shard_map/krylov/pallas_call | solution.py:73
  37.3 10.0 %all_to_all.10.parts = f32[8,8,128]{2,1,0:T(8,128)S(1)} all-to-all(f32[8,8,128]{2,1,0:T(8,128)S(1)} %get-tuple-element.40), channel_id=1, replica_groups=mesh['crops'=2,'xy'=4,'gz'=2,'lab'=2] {'xy','gz'}, dimensions={0} | all-to-all | bytes 65536 | tf_op jit(solution)/shard_map/all_to_all | solution.py:66
  47.2 1.2 %edges.1.edge = f32[3,6,40,128]{3,2,1,0:T(8,128)S(1)} custom-call(s32[10]{0:T(128)S(1)} %stack.43.info, f32[8,8,128]{2,1,0:T(8,128)S(1)} %all_to_all.10.parts, f32[4,12,40,128]{3,2,1,0:T(8,128)S(1)} %get-tuple-element.41.v0, f32[4,12,40,128]{3,2,1,0:T(8,128)S(1)} %get-tuple-element.42.v1, f32[4,12,40,128]{3,2,1,0:T(8,128)S(1)} %get-tuple-element.43.v2, ...), custom_call_target="tpu_custom_call" | custom-call | flops 1000000 | bytes 3932200 | tf_op jit(solution)/shard_map/edges/pallas_call | solution.py:73
  48.5 1.7 %collective-permute-done.11.other = f32[3,6,40,128]{3,2,1,0:T(8,128)S(1)} collective-permute-done((f32[3,6,40,128]{3,2,1,0:T(8,128)S(1)}, f32[3,6,40,128]{3,2,1,0:T(8,128)S(1)}, u32[]{:S(2)}, u32[]{:S(2)}) %collective-permute-start.11) | collective-permute-done | bytes 368672 | tf_op jit(solution)/shard_map/ppermute | solution.py:33
  50.1 2.6 %filter_sums.1 = (bf16[768,768]{1,0:T(8,128)(2,1)S(1)}, f32[8,8,128]{2,1,0:T(8,128)}) custom-call(s32[10]{0:T(128)S(1)} %stack.43.info, f32[3,6,40,128]{3,2,1,0:T(8,128)S(1)} %edges.1.edge, f32[3,6,40,128]{3,2,1,0:T(8,128)S(1)} %collective-permute-done.11.other, f32[3,6,40,128]{3,2,1,0:T(8,128)S(1)} %get-tuple-element.45.slope, ...), custom_call_target="tpu_custom_call" | custom-call | flops 1000000 | bytes 1699880 | tf_op jit(solution)/shard_map/filter_sums/pallas_call | solution.py:73
  52.8 3.3 %all-to-all-start.1 = ((f32[8,8,128]{2,1,0:T(8,128)}), f32[8,8,128]{2,1,0:T(8,128)S(1)}, u32[]{:S(2)}, u32[]{:S(2)}) async-start(f32[8,8,128]{2,1,0:T(8,128)} %get-tuple-element.49), calls=%async_computation.1 | async-start | bytes 65536 | tf_op jit(solution)/shard_map/all_to_all | solution.py:66
  56.1 2.0 %image_sums.1 = bf16[8,4,32,128]{3,2,1,0:T(8,128)(2,1)} custom-call(s32[10]{0:T(128)S(1)} %stack.43.info, bf16[768,768]{1,0:T(8,128)(2,1)S(1)} %get-tuple-element.47.grads, bf16[3,256,768]{2,1,0:T(8,128)(2,1)S(1)} %get-tuple-element.48.matrix), custom_call_target="tpu_custom_call" | custom-call | flops 10000000 | bytes 2359336 | tf_op jit(solution)/shard_map/image_sums/pallas_call | solution.py:73
  58.1 4.6 %all-to-all-done.1 = f32[8,8,128]{2,1,0:T(8,128)S(1)} async-done(((f32[8,8,128]{2,1,0:T(8,128)}), f32[8,8,128]{2,1,0:T(8,128)S(1)}, u32[]{:S(2)}, u32[]{:S(2)}) %all-to-all-start.1) | async-done | bytes 32800 | tf_op jit(solution)/shard_map/all_to_all | solution.py:66
  (35 shorter events, 5.6 us)
Async XLA Ops:
  0.8 1.0 %copy-start = (bf16[8,4,32,128]{3,2,1,0:T(8,128)(2,1)S(1)}, bf16[8,4,32,128]{3,2,1,0:T(8,128)(2,1)}, u32[]{:S(2)}) copy-start(bf16[8,4,32,128]{3,2,1,0:T(8,128)(2,1)} %image_in.1) | copy-start | bytes 786436
  1.7 0.9 %copy-start.1 = (f32[4,4,32,128]{3,2,1,0:T(8,128)S(1)}, f32[4,4,32,128]{3,2,1,0:T(8,128)}, u32[]{:S(2)}) copy-start(f32[4,4,32,128]{3,2,1,0:T(8,128)} %likelihoods_in.1) | copy-start | bytes 786436
  2.7 0.9 %copy-start.2 = (f32[4,4,32,128]{3,2,1,0:T(8,128)S(1)}, f32[4,4,32,128]{3,2,1,0:T(8,128)}, u32[]{:S(2)}) copy-start(f32[4,4,32,128]{3,2,1,0:T(8,128)} %slope_in.1) | copy-start | bytes 786436
  3.6 0.8 %copy-start.3 = (s32[4,32,128]{2,1,0:T(8,128)S(1)}, s32[4,32,128]{2,1,0:T(8,128)}, u32[]{:S(2)}) copy-start(s32[4,32,128]{2,1,0:T(8,128)} %planted_in.1) | copy-start | bytes 196612
  5.3 12.5 %collective-permute-start.4 = (bf16[4,4,8,128]{3,2,1,0:T(8,128)(2,1)S(1)}, bf16[4,4,8,128]{3,2,1,0:T(8,128)(2,1)S(1)}, u32[]{:S(2)}, u32[]{:S(2)}) collective-permute-start(bf16[4,4,8,128]{3,2,1,0:T(8,128)(2,1)S(1)} %get-tuple-element.31), channel_id=1, source_target_pairs={{4,10},{6,8},{8,6},{10,4},{12,2},{14,0},{0,14},{2,12},{5,11},{7,9}... | collective-permute-start | bytes 98312 | tf_op jit(solution)/shard_map/ppermute | solution.py:41
  11.4 6.5 %collective-permute-start.3 = (bf16[4,4,8,128]{3,2,1,0:T(8,128)(2,1)S(1)}, bf16[4,4,8,128]{3,2,1,0:T(8,128)(2,1)S(1)}, u32[]{:S(2)}, u32[]{:S(2)}) collective-permute-start(bf16[4,4,8,128]{3,2,1,0:T(8,128)(2,1)S(1)} %get-tuple-element.31), channel_id=1, source_target_pairs={{0,6},{2,4},{4,2},{6,0},{8,14},{10,12},{12,10},{14,8},{1,7},{3,5},... | collective-permute-start | bytes 98312 | tf_op jit(solution)/shard_map/ppermute | solution.py:41
  11.4 6.5 %collective-permute-start.2 = (bf16[4,4,8,128]{3,2,1,0:T(8,128)(2,1)S(1)}, bf16[4,4,8,128]{3,2,1,0:T(8,128)(2,1)S(1)}, u32[]{:S(2)}, u32[]{:S(2)}) collective-permute-start(bf16[4,4,8,128]{3,2,1,0:T(8,128)(2,1)S(1)} %get-tuple-element.31), channel_id=1, source_target_pairs={{0,2},{2,0},{1,3},{3,1},{4,6},{6,4},{5,7},{7,5},{8,10},{10,8},{9,1... | collective-permute-start | bytes 98312 | tf_op jit(solution)/shard_map/ppermute | solution.py:29
  12.4 8.3 %collective-permute-start = (bf16[32,32,128]{2,1,0:T(8,128)(2,1)S(1)}, bf16[32,32,128]{2,1,0:T(8,128)(2,1)S(1)}, u32[]{:S(2)}, u32[]{:S(2)}) collective-permute-start(bf16[32,32,128]{2,1,0:T(8,128)(2,1)S(1)} %get-tuple-element.29), channel_id=1, source_target_pairs={{0,4},{4,0},{8,12},{12,8},{1,5},{5,1},{9,13},{13,9},{2,6},{6,2},{1... | collective-permute-start | bytes 786440 | tf_op jit(solution)/shard_map/ppermute | solution.py:29
  14.8 5.8 %collective-permute-start.1 = (bf16[32,32,128]{2,1,0:T(8,128)(2,1)S(1)}, bf16[32,32,128]{2,1,0:T(8,128)(2,1)S(1)}, u32[]{:S(2)}, u32[]{:S(2)}) collective-permute-start(bf16[32,32,128]{2,1,0:T(8,128)(2,1)S(1)} %get-tuple-element.30), channel_id=1, source_target_pairs={{4,8},{8,4},{5,9},{9,5},{6,10},{10,6},{7,11},{11,7},{20,24},{24,20... | collective-permute-start | bytes 786440 | tf_op jit(solution)/shard_map/ppermute | solution.py:29
  22.0 1.5 %collective-permute-start.5 = (f32[3,4,32,128]{3,2,1,0:T(8,128)S(1)}, f32[3,4,32,128]{3,2,1,0:T(8,128)S(1)}, u32[]{:S(2)}, u32[]{:S(2)}) collective-permute-start(f32[3,4,32,128]{3,2,1,0:T(8,128)S(1)} %get-tuple-element.33.part), channel_id=1, source_target_pairs={{0,1},{1,0},{2,3},{3,2},{4,5},{5,4},{6,7},{7,6},{8,9},{9,8},{10,11... | collective-permute-start | bytes 589832 | tf_op jit(solution)/shard_map/ppermute | solution.py:33
  24.1 8.6 %collective-permute-start.6 = (bf16[3,4,32,128]{3,2,1,0:T(8,128)(2,1)S(1)}, bf16[3,4,32,128]{3,2,1,0:T(8,128)(2,1)S(1)}, u32[]{:S(2)}, u32[]{:S(2)}) collective-permute-start(bf16[3,4,32,128]{3,2,1,0:T(8,128)(2,1)S(1)} %get-tuple-element.35), channel_id=1, source_target_pairs={{0,4},{4,0},{8,12},{12,8},{5,9},{9,5},{13,1},{1,13},{2,6},{6,2},{1... | collective-permute-start | bytes 294920 | tf_op jit(solution)/shard_map/ppermute | solution.py:51
  27.4 4.1 %collective-permute-start.8 = (bf16[3,4,8,128]{3,2,1,0:T(8,128)(2,1)S(1)}, bf16[3,4,8,128]{3,2,1,0:T(8,128)(2,1)S(1)}, u32[]{:S(2)}, u32[]{:S(2)}) collective-permute-start(bf16[3,4,8,128]{3,2,1,0:T(8,128)(2,1)S(1)} %get-tuple-element.36), channel_id=1, source_target_pairs={{0,2},{2,0},{1,3},{3,1},{4,6},{6,4},{5,7},{7,5},{8,10},{10,8},{9,1... | collective-permute-start | bytes 73736 | tf_op jit(solution)/shard_map/ppermute | solution.py:29
  28.0 4.7 %collective-permute-start.7 = (bf16[3,4,8,128]{3,2,1,0:T(8,128)(2,1)S(1)}, bf16[3,4,8,128]{3,2,1,0:T(8,128)(2,1)S(1)}, u32[]{:S(2)}, u32[]{:S(2)}) collective-permute-start(bf16[3,4,8,128]{3,2,1,0:T(8,128)(2,1)S(1)} %get-tuple-element.36), channel_id=1, source_target_pairs={{0,6},{2,4},{4,2},{6,0},{8,14},{10,12},{12,10},{14,8},{5,11},{7,9}... | collective-permute-start | bytes 73736 | tf_op jit(solution)/shard_map/ppermute | solution.py:62
  32.7 1.4 %collective-permute-start.9 = (bf16[3,4,32,128]{3,2,1,0:T(8,128)(2,1)S(1)}, bf16[3,4,32,128]{3,2,1,0:T(8,128)(2,1)S(1)}, u32[]{:S(2)}, u32[]{:S(2)}) collective-permute-start(bf16[3,4,32,128]{3,2,1,0:T(8,128)(2,1)S(1)} %collective-permute-done.6.mine), channel_id=1, source_target_pairs={{0,1},{1,0},{2,3},{3,2},{4,5},{5,4},{6,7},{7,6},{8,9},{9,8},{10,11... | collective-permute-start | bytes 294920 | tf_op jit(solution)/shard_map/ppermute | solution.py:33
  32.7 1.4 %collective-permute-start.10 = (bf16[3,4,8,128]{3,2,1,0:T(8,128)(2,1)S(1)}, bf16[3,4,8,128]{3,2,1,0:T(8,128)(2,1)S(1)}, u32[]{:S(2)}, u32[]{:S(2)}) collective-permute-start(bf16[3,4,8,128]{3,2,1,0:T(8,128)(2,1)S(1)} %collective-permute-done.7.refs_1_), channel_id=1, source_target_pairs={{0,1},{1,0},{2,3},{3,2},{4,5},{5,4},{6,7},{7,6},{8,9},{9,8},{10,11... | collective-permute-start | bytes 73736 | tf_op jit(solution)/shard_map/ppermute | solution.py:33
  48.4 1.8 %collective-permute-start.11 = (f32[3,6,40,128]{3,2,1,0:T(8,128)S(1)}, f32[3,6,40,128]{3,2,1,0:T(8,128)S(1)}, u32[]{:S(2)}, u32[]{:S(2)}) collective-permute-start(f32[3,6,40,128]{3,2,1,0:T(8,128)S(1)} %edges.1.edge), channel_id=1, source_target_pairs={{0,1},{1,0},{2,3},{3,2},{4,5},{5,4},{6,7},{7,6},{8,9},{9,8},{10,11... | collective-permute-start | bytes 1105928 | tf_op jit(solution)/shard_map/ppermute | solution.py:33
  52.8 10.0 %all-to-all-start.1 = ((f32[8,8,128]{2,1,0:T(8,128)}), f32[8,8,128]{2,1,0:T(8,128)S(1)}, u32[]{:S(2)}, u32[]{:S(2)}) async-start(f32[8,8,128]{2,1,0:T(8,128)} %get-tuple-element.49), calls=%async_computation.1 | async-start | bytes 65536 | tf_op jit(solution)/shard_map/all_to_all | solution.py:66

commit v5 on v4

--- a/solution.py
+++ b/solution.py
@@ -100,12 +100,36 @@
     return jnp.where(free, slope, SEED), jnp.where(free, likelihood, member)
 
 
-def pack(colours, two, info, image_in, planted_in, likelihoods_in, slope_in, image, planted, likelihoods, slope, *refs):
-    faces, (send_a, send_b, sems) = refs[: 1 + two], refs[1 + two :]
-    pairs = ((planted_in, planted), (slope_in, slope), (likelihoods_in, likelihoods), (image_in, image))
+def pack(
+    colours,
+    two,
+    info,
+    filt_in,
+    image_in,
+    planted_in,
+    likelihoods_in,
+    slope_in,
+    wide_out,
+    back_out,
+    image,
+    planted,
+    likelihoods,
+    slope,
+    *refs,
+):
+    faces, (send_a, send_b, filt, taps, sems) = refs[: 1 + two], refs[1 + two :]
+    pairs = (
+        (planted_in, planted),
+        (slope_in, slope),
+        (likelihoods_in, likelihoods),
+        (image_in, image),
+        (filt_in, filt),
+    )
     copies = [pltpu.make_async_copy(src, dst, sems.at[n]) for n, (src, dst) in enumerate(pairs)]
-    for copy in copies:
+    for copy in reversed(copies):
         copy.start()
+    copies[4].wait()
+    spread_filter(info, filt, taps, wide_out, back_out)
     labels, rows_x, rows_z, _ = likelihoods.shape
     channels = image.shape[0]
     last, first = slice(rows_z - TILE, rows_z), slice(0, TILE)
@@ -193,9 +217,28 @@
     return (0,) if (o < 0) != transposed else (2,)
 
 
-def spread_filter(info, first, second, one, two, wide_out, back_out):
-    wide = jnp.dot(first[...], one[...], preferred_element_type=F32)
-    back = jnp.dot(second[...], two[...], preferred_element_type=F32)
+def spread_filter(info, filt, taps, wide_out, back_out):
+    taps[...] = jnp.zeros_like(taps)
+    for d in range(3):
+        for i in range(3):
+            for j in range(3):
+                at = (d * 9 + i * 3 + j) * 4
+                taps[at : at + 3, : filt.shape[-1]] = filt[d, i, j].astype(F32)
+    lane = lanes_iota(LANES)
+    channel = rows_iota(LANES) - 2 * info[COLOUR]
+    all_taps = taps[...].astype(BF16)
+    by_channel = jnp.where(channel == ((lane >> 3) & 7), 1.0, 0.0).astype(BF16)
+    own = jnp.dot(
+        all_taps, jnp.where(channel == lane, 1.0, 0.0).astype(BF16), preferred_element_type=F32
+    ).astype(BF16)
+    wide = jnp.dot(all_taps, by_channel, preferred_element_type=F32)
+    tap, edge = rows_iota(taps.shape[0]), lanes_iota(taps.shape[0]) >> 3
+    shift = jnp.where(edge >= 3, 1, 0) + jnp.where(edge >= 6, 1, 0)
+    first_tap = jnp.where(edge < 9, (edge - 3 * shift) * 36 + shift, -LANES)
+    places = [jnp.where(tap == first_tap + 4 * ij, 1.0, 0.0).astype(BF16) for ij in range(9)]
+    back = [
+        lax.dot_general(own, place, (((0,), (0,)), ((), ())), preferred_element_type=F32) for place in places
+    ]
     zero = jnp.zeros((TILE, LANES), F32)
     for o in (-1, 0, 1):
         masks = {(h, j): band(h, j, o) for h in range(2) for j in bands(o)}
@@ -208,7 +251,7 @@
                         for i in range(3):
                             if (x + i) // 2 == block:
                                 for j in bands(o):
-                                    row = kd * 9 + i * 3 + j
+                                    row = (kd % 3 * 9 + i * 3 + j) * 4 + kd // 3
                                     value = jnp.broadcast_to(wide[row : row + 1], (TILE, LANES))
                                     tile = jnp.where(masks[(x + i) % 2, j], value, tile)
                         tiles.append(tile)
@@ -226,8 +269,7 @@
                         i = x + 2 - block
                         if 0 <= i < 3:
                             for j in bands(o, True):
-                                row = c * 9 + i * 3 + j
-                                value = jnp.broadcast_to(back[row : row + 1], (TILE, LANES))
+                                value = jnp.broadcast_to(back[i * 3 + j][c : c + 1], (TILE, LANES))
                                 tile = jnp.where(masks[j], value, tile)
                         tiles.append(tile)
                     at = (c * 4 + 2 * pair) * TILE
@@ -467,7 +509,7 @@
             out[d, at] = sums[d]
 
 
-def filter_sums(info, edge, other, slope, stack, one, grads, out, products, rows_out):
+def filter_sums(info, edge, other, slope, stack, grads, out, products, rows_out):
     rows_x = edge.shape[1] - 2
     lane = lanes_iota(edge.shape[2])
     for xp in range(rows_x + 2):
@@ -506,7 +548,7 @@
                 row = d * 27 + i * 9 + j * 3 + k
                 rows_out[row : row + 1] = jnp.sum(total, axis=0, keepdims=True)
     sums = lax.dot_general(
-        one[...],
+        jnp.where(((lanes_iota() >> 3) & 7) == rows_iota(), 1.0, 0.0),
         rows_out[...],
         (((1,), (1,)), ((), ())),
         precision=lax.Precision.HIGHEST,
@@ -559,14 +601,20 @@
     inputs = (image, planted, likelihoods, slope)
     planes = channels + labels * rows_x + 2 * labels
     brick = shaped((planes, rows_z, LANES), BF16)
-    image, planted, likelihoods, slope, *packed = call(
+    taps = jnp.transpose(filt, (0, 2, 3, 4, 1))
+    matrix, back_matrix, image, planted, likelihoods, slope, *packed = call(
         functools.partial(pack, colours, two),
-        [shaped(a.shape, a.dtype) for a in inputs]
+        [shaped((3, 288, 384), BF16), shaped((3, 256, 768), BF16)]
+        + [shaped(a.shape, a.dtype) for a in inputs]
         + [shaped((rows_x, labels, TILE, LANES), BF16)] * (1 + two)
         + [brick, brick],
         info,
-        *inputs,
-        scratch=[pltpu.SemaphoreType.DMA((4,))],
+        *(pltpu.with_memory_space_constraint(a, pltpu.HBM) for a in (taps, *inputs)),
+        scratch=[
+            pltpu.VMEM(taps.shape, BF16),
+            pltpu.VMEM((112, LANES), F32),
+            pltpu.SemaphoreType.DMA((5,)),
+        ],
         name="pack",
         space=pltpu.HBM,
     )
@@ -578,25 +626,6 @@
     first = swap(send_a, "xy", 0)
     received = (first, second, *faces, *edges_a, *edges_b)
 
-    own_filt = lax.dynamic_slice_in_dim(filt, lab * channels, channels, 1)
-    lines = jnp.transpose(own_filt, (4, 0, 2, 3, 1)).reshape(81, channels)
-    lines = jnp.pad(lines, ((0, 7), (0, LANES - channels)))
-    backs = jnp.transpose(own_filt, (1, 2, 3, 4, 0)).reshape(72, 9)
-    backs = jnp.pad(backs, ((0, 0), (0, LANES - 9)))
-    lane = jnp.arange(LANES, dtype=jnp.int32)
-    by_channel = ((lane[None] >> 3) & 7) == lane[:, None]
-    by_edge = (lane[None] >> 3) == lane[:, None]
-    matrix, back_matrix = call(
-        spread_filter,
-        [shaped((3, 288, 384), BF16), shaped((3, 256, 768), BF16)],
-        info,
-        lines,
-        backs,
-        by_channel.astype(BF16),
-        by_edge.astype(BF16),
-        flops=10_000_000,
-        name="spread_filter",
-    )
     part, stack = call(
         functools.partial(convolve, two),
         [shaped((3, rows_x, rows_z, LANES), F32), shaped((384, 768), BF16)],
@@ -670,7 +699,6 @@
         lab_swap(edge),
         squash_slope,
         stack,
-        by_channel[:TILE].astype(F32),
         scratch=[pltpu.VMEM((3, 512, 384), F32), pltpu.VMEM((LANES, LANES), F32)],
         name="filter_sums",
     )

time: 64 us -> 60.6 us (0.947)
  local copies, waits for them, and re-layouts: 5.92 us -> 0.93 us
  blocking collectives: 9.96 us -> 10.7 us
    unnamed x8 -> x0, local copies, waits for them, and re-layouts: 3.69 us -> none
    ppermute x4, waiting for transfers between devices: 5.35 us -> 2.29 us  [swap(): lax.ppermute(block, axis, pair_routes(lax.axis_size(axis), phase, closed))]
    ppermute x2, waiting for transfers between devices: 0.01 us -> 3.06 us  [diagonal_swap(): return lax.ppermute(block, ('xy', 'gz'), route)]
    ppermute x4, starting transfers between devices: 4.71 us -> 5.69 us  [swap(): lax.ppermute(block, axis, pair_routes(lax.axis_size(axis), phase, closed))]
    transpose x2 -> x0, local copies, waits for them, and re-layouts: 0.85 us -> none  [the longest x1 0.84 us: local(): backs = jnp.transpose(own_filt, (1, 2, 3, 4, 0)).reshape(72, 9)]
    all_to_all x1, blocking collectives: 9.96 us -> 10.7 us  [everyones(): return lax.all_to_all(copies, axes, 0, 0)]
    pallas_call x8 -> x7, Pallas kernels: 12.6 us -> 12.9 us  [call(): pl.pallas_call(kernel, out_shape=outs, in_specs=specs, out_specs=jax.tree...]
  transfers between devices with their start and end apart: 13 -> 13, of which waited for: 7 -> 7; matrix products, arithmetic and copies ran while one was open for 2% -> 0% of each run, Pallas kernels for 5% -> 3%
where the time goes in v5:
time: 60.6 us; the launch traced here: 60.3 us
  starting transfers between devices  19.3 us (32%)
  waiting for transfers between devices  15.7 us (26%)
  Pallas kernels  12.9 us (21%)
  blocking collectives  10.7 us (18%)
  local copies, waits for them, and re-layouts  0.93 us (2%)
  between operations  0.74 us (1%)
    pallas_call x7, Pallas kernels, call(): pl.pallas_call(kernel, out_shape=outs, in_specs=specs, out_specs=jax.tree...  12.9 us
    all_to_all x1, blocking collectives, everyones(): return lax.all_to_all(copies, axes, 0, 0)  10.7 us
    ppermute x4, starting transfers between devices, swap(): lax.ppermute(block, axis, pair_routes(lax.axis_size(axis), phase, closed))  5.69 us
    ppermute x2, starting transfers between devices, diagonal_swap(): return lax.ppermute(block, ('xy', 'gz'), route)  5.45 us
    all_to_all x1, waiting for transfers between devices, everyones(): return lax.all_to_all(copies, axes, 0, 0)  4.6 us
    ppermute x4, waiting for transfers between devices, lab_swap(): return lax.ppermute(block, 'lab', [(0, 1), (1, 0)])  4.3 us
    all_to_all x1, starting transfers between devices, everyones(): return lax.all_to_all(copies, axes, 0, 0)  3.34 us
    ppermute x2, waiting for transfers between devices, diagonal_swap(): return lax.ppermute(block, ('xy', 'gz'), route)  3.06 us
  transfers between devices with their start and end apart: 13, of which 7 were waited for; matrix products, arithmetic and copies ran while one was open for 0% of the time, Pallas kernels for 3%

profile of v5, /device:TPU:0, one launch (start us, length us, event | category | flops | bytes accessed | tf_op | source)
XLA Modules:
  0.0 60.3 jit_solution(15893126083736157870)
XLA Ops:
  0.8 2.1 %pack.1 = (bf16[3,288,384]{2,1,0:T(8,128)(2,1)S(1)}, bf16[3,256,768]{2,1,0:T(8,128)(2,1)S(1)}, bf16[8,4,32,128]{3,2,1,0:T(8,128)(2,1)S(1)}, s32[4,32,128]{2,1,0:...) custom-call(s32[10]{0:T(128)S(1)} %stack.43.info, ...), custom_call_target="tpu_custom_call" | custom-call | flops 1000000 | bytes 854600 | tf_op jit(solution)/shard_map/pack/pallas_call | solution.py:73
  2.8 3.1 %collective-permute-start = (bf16[32,32,128]{2,1,0:T(8,128)(2,1)S(1)}, bf16[32,32,128]{2,1,0:T(8,128)(2,1)S(1)}, u32[]{:S(2)}, u32[]{:S(2)}) collective-permute-start(bf16[32,32,128]{2,1,0:T(8,128)(2,1)S(1)} %get-tuple-element.29), channel_id=1, source_target_pairs={{0,4},{4,0},{8,12},{12,8},{1,5},{5,1},{9,13},{13,9},{2,6},{6,2},{1... | collective-permute-start | bytes 786440 | tf_op jit(solution)/shard_map/ppermute | solution.py:29
  5.9 0.7 %collective-permute-start.1 = (bf16[32,32,128]{2,1,0:T(8,128)(2,1)S(1)}, bf16[32,32,128]{2,1,0:T(8,128)(2,1)S(1)}, u32[]{:S(2)}, u32[]{:S(2)}) collective-permute-start(bf16[32,32,128]{2,1,0:T(8,128)(2,1)S(1)} %get-tuple-element.30), channel_id=1, source_target_pairs={{4,8},{8,4},{5,9},{9,5},{6,10},{10,6},{7,11},{11,7},{20,24},{24,20... | collective-permute-start | bytes 786440 | tf_op jit(solution)/shard_map/ppermute | solution.py:29
  6.6 3.5 %collective-permute-start.4 = (bf16[4,4,8,128]{3,2,1,0:T(8,128)(2,1)S(1)}, bf16[4,4,8,128]{3,2,1,0:T(8,128)(2,1)S(1)}, u32[]{:S(2)}, u32[]{:S(2)}) collective-permute-start(bf16[4,4,8,128]{3,2,1,0:T(8,128)(2,1)S(1)} %get-tuple-element.31), channel_id=1, source_target_pairs={{4,10},{6,8},{8,6},{10,4},{12,2},{14,0},{0,14},{2,12},{5,11},{7,9}... | collective-permute-start | bytes 98312 | tf_op jit(solution)/shard_map/ppermute | solution.py:41
  10.1 2.0 %collective-permute-start.3 = (bf16[4,4,8,128]{3,2,1,0:T(8,128)(2,1)S(1)}, bf16[4,4,8,128]{3,2,1,0:T(8,128)(2,1)S(1)}, u32[]{:S(2)}, u32[]{:S(2)}) collective-permute-start(bf16[4,4,8,128]{3,2,1,0:T(8,128)(2,1)S(1)} %get-tuple-element.31), channel_id=1, source_target_pairs={{0,6},{2,4},{4,2},{6,0},{8,14},{10,12},{12,10},{14,8},{1,7},{3,5},... | collective-permute-start | bytes 98312 | tf_op jit(solution)/shard_map/ppermute | solution.py:41
  12.0 1.4 %collective-permute-start.2 = (bf16[4,4,8,128]{3,2,1,0:T(8,128)(2,1)S(1)}, bf16[4,4,8,128]{3,2,1,0:T(8,128)(2,1)S(1)}, u32[]{:S(2)}, u32[]{:S(2)}) collective-permute-start(bf16[4,4,8,128]{3,2,1,0:T(8,128)(2,1)S(1)} %get-tuple-element.31), channel_id=1, source_target_pairs={{0,2},{2,0},{1,3},{3,1},{4,6},{6,4},{5,7},{7,5},{8,10},{10,8},{9,1... | collective-permute-start | bytes 98312 | tf_op jit(solution)/shard_map/ppermute | solution.py:29
  13.4 3.1 %collective-permute-done.4.refs_2_.refs_5_ = bf16[4,4,8,128]{3,2,1,0:T(8,128)(2,1)S(1)} collective-permute-done((bf16[4,4,8,128]{3,2,1,0:T(8,128)(2,1)S(1)}, bf16[4,4,8,128]{3,2,1,0:T(8,128)(2,1)S(1)}, u32[]{:S(2)}, u32[]{:S(2)}) %collective-permute-start.4) | collective-permute-done | bytes 32800 | tf_op jit(solution)/shard_map/ppermute | solution.py:41
  16.5 1.4 %convolve.1 = (f32[3,4,32,128]{3,2,1,0:T(8,128)S(1)}, bf16[384,768]{1,0:T(8,128)(2,1)S(1)}) custom-call(s32[10]{0:T(128)S(1)} %stack.43.info, bf16[8,4,32,128]{3,2,1,0:T(8,128)(2,1)S(1)} %get-tuple-element.28.image, bf16[32,32,128]{2,1,0:T(8,128)(2,1)S(1)} %collective-permute-done.first, bf16[32,32,128]{2,1,0:T(8,128)(2,1)S(1)} %collective-permute-done.1.second, ...), custom_call_target="tpu_custom_call" | custom-call | flops 1000000 | bytes 1548328 | tf_op jit(solution)/shard_map/convolve/pallas_call | solution.py:73
  18.0 1.4 %collective-permute-done.5.other = f32[3,4,32,128]{3,2,1,0:T(8,128)S(1)} collective-permute-done((f32[3,4,32,128]{3,2,1,0:T(8,128)S(1)}, f32[3,4,32,128]{3,2,1,0:T(8,128)S(1)}, u32[]{:S(2)}, u32[]{:S(2)}) %collective-permute-start.5) | collective-permute-done | bytes 196640 | tf_op jit(solution)/shard_map/ppermute | solution.py:33
  20.0 2.9 %collective-permute-start.6 = (bf16[3,4,32,128]{3,2,1,0:T(8,128)(2,1)S(1)}, bf16[3,4,32,128]{3,2,1,0:T(8,128)(2,1)S(1)}, u32[]{:S(2)}, u32[]{:S(2)}) collective-permute-start(bf16[3,4,32,128]{3,2,1,0:T(8,128)(2,1)S(1)} %get-tuple-element.35), channel_id=1, source_target_pairs={{0,4},{4,0},{8,12},{12,8},{5,9},{9,5},{13,1},{1,13},{2,6},{6,2},{1... | collective-permute-start | bytes 294920 | tf_op jit(solution)/shard_map/ppermute | solution.py:51
  23.4 1.0 %collective-permute-start.7 = (bf16[3,4,8,128]{3,2,1,0:T(8,128)(2,1)S(1)}, bf16[3,4,8,128]{3,2,1,0:T(8,128)(2,1)S(1)}, u32[]{:S(2)}, u32[]{:S(2)}) collective-permute-start(bf16[3,4,8,128]{3,2,1,0:T(8,128)(2,1)S(1)} %get-tuple-element.36), channel_id=1, source_target_pairs={{0,6},{2,4},{4,2},{6,0},{8,14},{10,12},{12,10},{14,8},{5,11},{7,9}... | collective-permute-start | bytes 73736 | tf_op jit(solution)/shard_map/ppermute | solution.py:62
  24.4 2.3 %collective-permute-done.8.refs_0_ = bf16[3,4,8,128]{3,2,1,0:T(8,128)(2,1)S(1)} collective-permute-done((bf16[3,4,8,128]{3,2,1,0:T(8,128)(2,1)S(1)}, bf16[3,4,8,128]{3,2,1,0:T(8,128)(2,1)S(1)}, u32[]{:S(2)}, u32[]{:S(2)}) %collective-permute-start.8) | collective-permute-done | bytes 24608 | tf_op jit(solution)/shard_map/ppermute | solution.py:29
  26.7 1.4 %collective-permute-done.7.refs_1_ = bf16[3,4,8,128]{3,2,1,0:T(8,128)(2,1)S(1)} collective-permute-done((bf16[3,4,8,128]{3,2,1,0:T(8,128)(2,1)S(1)}, bf16[3,4,8,128]{3,2,1,0:T(8,128)(2,1)S(1)}, u32[]{:S(2)}, u32[]{:S(2)}) %collective-permute-start.7) | collective-permute-done | bytes 24608 | tf_op jit(solution)/shard_map/ppermute | solution.py:62
  28.1 0.8 %collective-permute-start.9 = (bf16[3,4,32,128]{3,2,1,0:T(8,128)(2,1)S(1)}, bf16[3,4,32,128]{3,2,1,0:T(8,128)(2,1)S(1)}, u32[]{:S(2)}, u32[]{:S(2)}) collective-permute-start(bf16[3,4,32,128]{3,2,1,0:T(8,128)(2,1)S(1)} %collective-permute-done.6.mine), channel_id=1, source_target_pairs={{0,1},{1,0},{2,3},{3,2},{4,5},{5,4},{6,7},{7,6},{8,9},{9,8},{10,11... | collective-permute-start | bytes 294920 | tf_op jit(solution)/shard_map/ppermute | solution.py:33
  28.9 1.2 %collective-permute-done.10.refs_2_ = bf16[3,4,8,128]{3,2,1,0:T(8,128)(2,1)S(1)} collective-permute-done((bf16[3,4,8,128]{3,2,1,0:T(8,128)(2,1)S(1)}, bf16[3,4,8,128]{3,2,1,0:T(8,128)(2,1)S(1)}, u32[]{:S(2)}, u32[]{:S(2)}) %collective-permute-start.10) | collective-permute-done | bytes 24608 | tf_op jit(solution)/shard_map/ppermute | solution.py:33
  30.1 3.2 %krylov.1 = (f32[4,12,40,128]{3,2,1,0:T(8,128)S(1)}, f32[4,12,40,128]{3,2,1,0:T(8,128)S(1)}, f32[4,12,40,128]{3,2,1,0:T(8,128)S(1)}, f32[3,6,40,128]{3,2,1,0:T(8,128)S(1)}, f32[8,8,128]{2,1,0:T(8,128)S(1)}) custom-call(s32[10]{0:T(128)S(1)} %stack.43.info, s32[4,32,128]{2,1,0:T(8,128)S(1)} %get-tuple-element.26.planted, ...), custom_call_target="tpu_custom_call" | custom-call | flops 1000000 | bytes 1417256 | tf_op jit(solution)/shard_map/krylov/pallas_call | solution.py:73
  33.2 10.7 %all_to_all.10.parts = f32[8,8,128]{2,1,0:T(8,128)S(1)} all-to-all(f32[8,8,128]{2,1,0:T(8,128)S(1)} %get-tuple-element.40), channel_id=1, replica_groups=mesh['crops'=2,'xy'=4,'gz'=2,'lab'=2] {'xy','gz'}, dimensions={0} | all-to-all | bytes 65536 | tf_op jit(solution)/shard_map/all_to_all | solution.py:66
  43.9 1.2 %edges.1.edge = f32[3,6,40,128]{3,2,1,0:T(8,128)S(1)} custom-call(s32[10]{0:T(128)S(1)} %stack.43.info, f32[8,8,128]{2,1,0:T(8,128)S(1)} %all_to_all.10.parts, f32[4,12,40,128]{3,2,1,0:T(8,128)S(1)} %get-tuple-element.41.v0, f32[4,12,40,128]{3,2,1,0:T(8,128)S(1)} %get-tuple-element.42.v1, f32[4,12,40,128]{3,2,1,0:T(8,128)S(1)} %get-tuple-element.43.v2, ...), custom_call_target="tpu_custom_call" | custom-call | flops 1000000 | bytes 3932200 | tf_op jit(solution)/shard_map/edges/pallas_call | solution.py:73
  45.2 1.7 %collective-permute-done.11.other = f32[3,6,40,128]{3,2,1,0:T(8,128)S(1)} collective-permute-done((f32[3,6,40,128]{3,2,1,0:T(8,128)S(1)}, f32[3,6,40,128]{3,2,1,0:T(8,128)S(1)}, u32[]{:S(2)}, u32[]{:S(2)}) %collective-permute-start.11) | collective-permute-done | bytes 368672 | tf_op jit(solution)/shard_map/ppermute | solution.py:33
  46.9 2.6 %filter_sums.1 = (bf16[768,768]{1,0:T(8,128)(2,1)S(1)}, f32[8,8,128]{2,1,0:T(8,128)}) custom-call(s32[10]{0:T(128)S(1)} %stack.43.info, f32[3,6,40,128]{3,2,1,0:T(8,128)S(1)} %edges.1.edge, f32[3,6,40,128]{3,2,1,0:T(8,128)S(1)} %collective-permute-done.11.other, f32[3,6,40,128]{3,2,1,0:T(8,128)S(1)} %get-tuple-element.45.slope, ...), custom_call_target="tpu_custom_call" | custom-call | flops 1000000 | bytes 1695784 | tf_op jit(solution)/shard_map/filter_sums/pallas_call | solution.py:73
  49.5 3.3 %all-to-all-start.1 = ((f32[8,8,128]{2,1,0:T(8,128)}), f32[8,8,128]{2,1,0:T(8,128)S(1)}, u32[]{:S(2)}, u32[]{:S(2)}) async-start(f32[8,8,128]{2,1,0:T(8,128)} %get-tuple-element.49), calls=%async_computation.1 | async-start | bytes 65536 | tf_op jit(solution)/shard_map/all_to_all | solution.py:66
  52.8 2.0 %image_sums.1 = bf16[8,4,32,128]{3,2,1,0:T(8,128)(2,1)} custom-call(s32[10]{0:T(128)S(1)} %stack.43.info, bf16[768,768]{1,0:T(8,128)(2,1)S(1)} %get-tuple-element.47.grads, bf16[3,256,768]{2,1,0:T(8,128)(2,1)S(1)} %get-tuple-element.48.matrix), custom_call_target="tpu_custom_call" | custom-call | flops 10000000 | bytes 2359336 | tf_op jit(solution)/shard_map/image_sums/pallas_call | solution.py:73
  54.8 4.6 %all-to-all-done.1 = f32[8,8,128]{2,1,0:T(8,128)S(1)} async-done(((f32[8,8,128]{2,1,0:T(8,128)}), f32[8,8,128]{2,1,0:T(8,128)S(1)}, u32[]{:S(2)}, u32[]{:S(2)}) %all-to-all-start.1) | async-done | bytes 32800 | tf_op jit(solution)/shard_map/all_to_all | solution.py:66
  59.6 0.7 %reshape.11 = f32[3,8,3,3,3]{1,4,3,2,0:T(4,128)} reshape(f32[3,8,27]{1,2,0:T(8,128)S(1)} %copy.7) | data formatting | bytes 5184 | tf_op jit(solution)/shard_map/reshape | solution.py:717
  (15 shorter events, 1.5 us)
Async XLA Ops:
  2.8 13.7 %collective-permute-start = (bf16[32,32,128]{2,1,0:T(8,128)(2,1)S(1)}, bf16[32,32,128]{2,1,0:T(8,128)(2,1)S(1)}, u32[]{:S(2)}, u32[]{:S(2)}) collective-permute-start(bf16[32,32,128]{2,1,0:T(8,128)(2,1)S(1)} %get-tuple-element.29), channel_id=1, source_target_pairs={{0,4},{4,0},{8,12},{12,8},{1,5},{5,1},{9,13},{13,9},{2,6},{6,2},{1... | collective-permute-start | bytes 786440 | tf_op jit(solution)/shard_map/ppermute | solution.py:29
  5.9 10.6 %collective-permute-start.1 = (bf16[32,32,128]{2,1,0:T(8,128)(2,1)S(1)}, bf16[32,32,128]{2,1,0:T(8,128)(2,1)S(1)}, u32[]{:S(2)}, u32[]{:S(2)}) collective-permute-start(bf16[32,32,128]{2,1,0:T(8,128)(2,1)S(1)} %get-tuple-element.30), channel_id=1, source_target_pairs={{4,8},{8,4},{5,9},{9,5},{6,10},{10,6},{7,11},{11,7},{20,24},{24,20... | collective-permute-start | bytes 786440 | tf_op jit(solution)/shard_map/ppermute | solution.py:29
  6.6 9.9 %collective-permute-start.4 = (bf16[4,4,8,128]{3,2,1,0:T(8,128)(2,1)S(1)}, bf16[4,4,8,128]{3,2,1,0:T(8,128)(2,1)S(1)}, u32[]{:S(2)}, u32[]{:S(2)}) collective-permute-start(bf16[4,4,8,128]{3,2,1,0:T(8,128)(2,1)S(1)} %get-tuple-element.31), channel_id=1, source_target_pairs={{4,10},{6,8},{8,6},{10,4},{12,2},{14,0},{0,14},{2,12},{5,11},{7,9}... | collective-permute-start | bytes 98312 | tf_op jit(solution)/shard_map/ppermute | solution.py:41
  10.1 6.4 %collective-permute-start.3 = (bf16[4,4,8,128]{3,2,1,0:T(8,128)(2,1)S(1)}, bf16[4,4,8,128]{3,2,1,0:T(8,128)(2,1)S(1)}, u32[]{:S(2)}, u32[]{:S(2)}) collective-permute-start(bf16[4,4,8,128]{3,2,1,0:T(8,128)(2,1)S(1)} %get-tuple-element.31), channel_id=1, source_target_pairs={{0,6},{2,4},{4,2},{6,0},{8,14},{10,12},{12,10},{14,8},{1,7},{3,5},... | collective-permute-start | bytes 98312 | tf_op jit(solution)/shard_map/ppermute | solution.py:41
  12.0 4.5 %collective-permute-start.2 = (bf16[4,4,8,128]{3,2,1,0:T(8,128)(2,1)S(1)}, bf16[4,4,8,128]{3,2,1,0:T(8,128)(2,1)S(1)}, u32[]{:S(2)}, u32[]{:S(2)}) collective-permute-start(bf16[4,4,8,128]{3,2,1,0:T(8,128)(2,1)S(1)} %get-tuple-element.31), channel_id=1, source_target_pairs={{0,2},{2,0},{1,3},{3,1},{4,6},{6,4},{5,7},{7,5},{8,10},{10,8},{9,1... | collective-permute-start | bytes 98312 | tf_op jit(solution)/shard_map/ppermute | solution.py:29
  17.9 1.5 %collective-permute-start.5 = (f32[3,4,32,128]{3,2,1,0:T(8,128)S(1)}, f32[3,4,32,128]{3,2,1,0:T(8,128)S(1)}, u32[]{:S(2)}, u32[]{:S(2)}) collective-permute-start(f32[3,4,32,128]{3,2,1,0:T(8,128)S(1)} %get-tuple-element.33.part), channel_id=1, source_target_pairs={{0,1},{1,0},{2,3},{3,2},{4,5},{5,4},{6,7},{7,6},{8,9},{9,8},{10,11... | collective-permute-start | bytes 589832 | tf_op jit(solution)/shard_map/ppermute | solution.py:33
  20.0 8.1 %collective-permute-start.6 = (bf16[3,4,32,128]{3,2,1,0:T(8,128)(2,1)S(1)}, bf16[3,4,32,128]{3,2,1,0:T(8,128)(2,1)S(1)}, u32[]{:S(2)}, u32[]{:S(2)}) collective-permute-start(bf16[3,4,32,128]{3,2,1,0:T(8,128)(2,1)S(1)} %get-tuple-element.35), channel_id=1, source_target_pairs={{0,4},{4,0},{8,12},{12,8},{5,9},{9,5},{13,1},{1,13},{2,6},{6,2},{1... | collective-permute-start | bytes 294920 | tf_op jit(solution)/shard_map/ppermute | solution.py:51
  22.8 3.8 %collective-permute-start.8 = (bf16[3,4,8,128]{3,2,1,0:T(8,128)(2,1)S(1)}, bf16[3,4,8,128]{3,2,1,0:T(8,128)(2,1)S(1)}, u32[]{:S(2)}, u32[]{:S(2)}) collective-permute-start(bf16[3,4,8,128]{3,2,1,0:T(8,128)(2,1)S(1)} %get-tuple-element.36), channel_id=1, source_target_pairs={{0,2},{2,0},{1,3},{3,1},{4,6},{6,4},{5,7},{7,5},{8,10},{10,8},{9,1... | collective-permute-start | bytes 73736 | tf_op jit(solution)/shard_map/ppermute | solution.py:29
  23.4 4.7 %collective-permute-start.7 = (bf16[3,4,8,128]{3,2,1,0:T(8,128)(2,1)S(1)}, bf16[3,4,8,128]{3,2,1,0:T(8,128)(2,1)S(1)}, u32[]{:S(2)}, u32[]{:S(2)}) collective-permute-start(bf16[3,4,8,128]{3,2,1,0:T(8,128)(2,1)S(1)} %get-tuple-element.36), channel_id=1, source_target_pairs={{0,6},{2,4},{4,2},{6,0},{8,14},{10,12},{12,10},{14,8},{5,11},{7,9}... | collective-permute-start | bytes 73736 | tf_op jit(solution)/shard_map/ppermute | solution.py:62
  28.1 2.0 %collective-permute-start.9 = (bf16[3,4,32,128]{3,2,1,0:T(8,128)(2,1)S(1)}, bf16[3,4,32,128]{3,2,1,0:T(8,128)(2,1)S(1)}, u32[]{:S(2)}, u32[]{:S(2)}) collective-permute-start(bf16[3,4,32,128]{3,2,1,0:T(8,128)(2,1)S(1)} %collective-permute-done.6.mine), channel_id=1, source_target_pairs={{0,1},{1,0},{2,3},{3,2},{4,5},{5,4},{6,7},{7,6},{8,9},{9,8},{10,11... | collective-permute-start | bytes 294920 | tf_op jit(solution)/shard_map/ppermute | solution.py:33
  28.9 1.2 %collective-permute-start.10 = (bf16[3,4,8,128]{3,2,1,0:T(8,128)(2,1)S(1)}, bf16[3,4,8,128]{3,2,1,0:T(8,128)(2,1)S(1)}, u32[]{:S(2)}, u32[]{:S(2)}) collective-permute-start(bf16[3,4,8,128]{3,2,1,0:T(8,128)(2,1)S(1)} %collective-permute-done.7.refs_1_), channel_id=1, source_target_pairs={{0,1},{1,0},{2,3},{3,2},{4,5},{5,4},{6,7},{7,6},{8,9},{9,8},{10,11... | collective-permute-start | bytes 73736 | tf_op jit(solution)/shard_map/ppermute | solution.py:33
  45.1 1.8 %collective-permute-start.11 = (f32[3,6,40,128]{3,2,1,0:T(8,128)S(1)}, f32[3,6,40,128]{3,2,1,0:T(8,128)S(1)}, u32[]{:S(2)}, u32[]{:S(2)}) collective-permute-start(f32[3,6,40,128]{3,2,1,0:T(8,128)S(1)} %edges.1.edge), channel_id=1, source_target_pairs={{0,1},{1,0},{2,3},{3,2},{4,5},{5,4},{6,7},{7,6},{8,9},{9,8},{10,11... | collective-permute-start | bytes 1105928 | tf_op jit(solution)/shard_map/ppermute | solution.py:33
  49.5 10.0 %all-to-all-start.1 = ((f32[8,8,128]{2,1,0:T(8,128)}), f32[8,8,128]{2,1,0:T(8,128)S(1)}, u32[]{:S(2)}, u32[]{:S(2)}) async-start(f32[8,8,128]{2,1,0:T(8,128)} %get-tuple-element.49), calls=%async_computation.1 | async-start | bytes 65536 | tf_op jit(solution)/shard_map/all_to_all | solution.py:66

commit v6 on v5

--- a/solution.py
+++ b/solution.py
@@ -240,8 +240,9 @@
         lax.dot_general(own, place, (((0,), (0,)), ((), ())), preferred_element_type=F32) for place in places
     ]
     zero = jnp.zeros((TILE, LANES), F32)
-    for o in (-1, 0, 1):
-        masks = {(h, j): band(h, j, o) for h in range(2) for j in bands(o)}
+    for at_out, distances in enumerate(((0,), (-1, 1))):
+        cases = [(o, j) for o in distances for j in bands(o)]
+        masks = {(h, j): band(h, j, o) for h in range(2) for o, j in cases}
         for kd in range(9):
             for pair in range(2):
                 for block in range(3):
@@ -250,16 +251,17 @@
                         tile = zero
                         for i in range(3):
                             if (x + i) // 2 == block:
-                                for j in bands(o):
+                                for _, j in cases:
                                     row = (kd % 3 * 9 + i * 3 + j) * 4 + kd // 3
                                     value = jnp.broadcast_to(wide[row : row + 1], (TILE, LANES))
                                     tile = jnp.where(masks[(x + i) % 2, j], value, tile)
                         tiles.append(tile)
                     at = (kd * 4 + 2 * pair) * TILE
-                    wide_out[o + 1, at : at + 16, block * LANES : (block + 1) * LANES] = jnp.concatenate(
+                    wide_out[at_out, at : at + 16, block * LANES : (block + 1) * LANES] = jnp.concatenate(
                         tiles, axis=0
                     ).astype(BF16)
-        masks = {j: band(None, j, o, True) for j in bands(o, True)}
+        cases = [(o, j) for o in distances for j in bands(o, True)]
+        masks = {j: band(None, j, o, True) for o, j in cases}
         for c in range(8):
             for pair in range(2):
                 for block in range(6):
@@ -268,14 +270,23 @@
                         tile = zero
                         i = x + 2 - block
                         if 0 <= i < 3:
-                            for j in bands(o, True):
+                            for _, j in cases:
                                 value = jnp.broadcast_to(back[i * 3 + j][c : c + 1], (TILE, LANES))
                                 tile = jnp.where(masks[j], value, tile)
                         tiles.append(tile)
                     at = (c * 4 + 2 * pair) * TILE
-                    back_out[o + 1, at : at + 16, block * LANES : (block + 1) * LANES] = jnp.concatenate(
+                    back_out[at_out, at : at + 16, block * LANES : (block + 1) * LANES] = jnp.concatenate(
                         tiles, axis=0
                     ).astype(BF16)
+
+
+def store_tiles(out, at, planes):
+    for t in range(4):
+        both = jnp.concatenate([plane[tile_rows(t)] for plane in planes], axis=0)
+        out[at : at + 16, t * LANES : (t + 1) * LANES] = both.astype(BF16)
+        both = [jnp.where(rows_iota() < 4, plane[tile_rows(t + 1)], plane[tile_rows(t - 1)]) for plane in planes]
+        both = jnp.concatenate(both, axis=0)
+        out[at : at + 16, (t + 4) * LANES : (t + 5) * LANES] = both.astype(BF16)
 
 
 def tile_rows(t):
@@ -308,12 +319,9 @@
                     plane, exists = (below, PREV_X) if xp == 0 else (above, NEXT_X)
                     planes.append(jnp.where(info[exists] == 1, plane, 0.0))
             at = (xp * channels + c) * TILE
-            for t in range(-1, 5):
-                both = jnp.concatenate([plane[tile_rows(t)] for plane in planes], axis=0)
-                stack[at : at + 16, (t + 1) * LANES : (t + 2) * LANES] = both.astype(BF16)
-    total = jnp.dot(matrix[0], stack[:, 0:512], preferred_element_type=F32)
-    total = total + jnp.dot(matrix[1], stack[:, 128:640], preferred_element_type=F32)
-    sums[...] = total + jnp.dot(matrix[2], stack[:, 256:768], preferred_element_type=F32)
+            store_tiles(stack, at, planes)
+    total = jnp.dot(matrix[0], stack[:, :512], preferred_element_type=F32)
+    sums[...] = total + jnp.dot(matrix[1], stack[:, 512:], preferred_element_type=F32)
     lane = lanes_iota()
     for d in range(3):
         for x in range(rows_x):
@@ -349,14 +357,45 @@
     return pltpu.roll(plane, 1, dim)
 
 
-def krylov(colours, size_x, size_z, two, info, planted, slope, logits, mine, other, first, second, *refs):
-    groups = [refs[n * (1 + two) : (n + 1) * (1 + two)] for n in range(6)]
-    faces, mine_edges, other_edges, rhs_faces, edges_a, edges_b = groups
-    v0, v1, v2, slope_out, dots_out, weight, free, dots = refs[6 * (1 + two) :]
-    labels, rows_x, rows_z, _ = slope.shape
-    rows = rows_z + TILE
+def prepare(colours, two, info, planted, slope, likelihoods, first, second, *refs):
+    faces, edges_a, edges_b = refs[: 1 + two], refs[1 + two : 2 + 2 * two], refs[2 + 2 * two : 3 + 3 * two]
+    v0, free, field = refs[3 + 3 * two :]
+    labels, rows_x, _, _ = slope.shape
     channels = 2 * labels
-    is_up, even = info[UP] == 1, info[EVEN_X] == 1
+    even = info[EVEN_X] == 1
+
+    def grown(index, source, l, tile):
+        received = [
+            jnp.concatenate([ref[index].astype(F32), tile(*ends_z(info, tiles, source, l))], axis=0)
+            for ref, tiles in ((first, edges_a), (second, edges_b))
+        ]
+        return sides(even, *received)
+
+    for x in range(rows_x):
+        for l in range(labels):
+            ends = ends_z(info, faces, x, l)
+            rhs, full = fields(planted[x], likelihoods[l, x], slope[l, x], colours, info[COLOUR] + l)
+            rhs = jnp.concatenate([rhs, rhs_tile(*ends)], axis=0)
+            field[l, x + 1] = jnp.concatenate([full, full_tile(*ends)], axis=0)
+            above, below = grown(channels + l * rows_x + x, x, l, rhs_tile)
+            for at, plane in ((x + HALO, rhs), (x, below), (x + HALO + rows_x, above)):
+                open_cell = plane < SEED / 2
+                v0[l, at] = jnp.where(open_cell, plane, 0.0)
+                if l == 0:
+                    free[at] = jnp.where(open_cell, 1.0, 0.0)
+    for l in range(labels):
+        base = 2 * labels + labels * rows_x + 2 * l
+        field[l, 0] = grown(base + 1, rows_x - 1, l, full_tile)[1]
+        for r in range(2):
+            field[l, rows_x + 1 + r] = grown(base + r, r, l, full_tile)[0]
+
+
+def krylov(size_x, size_z, two, info, v0, free, logits, mine, other, *refs):
+    faces, mine_edges, other_edges = (refs[n * (1 + two) : (n + 1) * (1 + two)] for n in range(3))
+    v1, v2, slope_out, dots_out, weight, dots = refs[3 * (1 + two) :]
+    labels, _, rows, _ = v0.shape
+    rows_x, rows_z = logits.shape[1:3]
+    is_up = info[UP] == 1
     z = rows_iota(rows)
     z = info[FIRST_Z] + jnp.where(z < rows_z + HALO, z, z - rows)
     inside_z = (z >= 0) & (z < size_z)
@@ -385,23 +424,6 @@
             weight[d, at] = (0.05 + squashed) * valid
             if -1 <= x <= rows_x:
                 slope_out[d, x + 1] = squashed * (1.0 - squashed) * valid
-        for l in range(labels):
-            source = x % rows_x
-            if 0 <= x < rows_x:
-                plane = jnp.where(planted[x] >= colours, slope[l, x], SEED)
-                plane = jnp.concatenate([plane, rhs_tile(*ends_z(info, rhs_faces, x, l))], axis=0)
-            else:
-                index = channels + l * rows_x + source
-                received = [
-                    jnp.concatenate([ref[index].astype(F32), rhs_tile(*ends_z(info, tiles, source, l))], axis=0)
-                    for ref, tiles in ((first, edges_a), (second, edges_b))
-                ]
-                above, below = sides(even, *received)
-                plane = below if x < 0 else above
-            open_cell = plane < SEED / 2
-            v0[l, at] = jnp.where(open_cell, plane, 0.0)
-            if l == 0:
-                free[at] = jnp.where(open_cell, 1.0, 0.0)
 
     def label(l, carry):
         def operate(v, start, stop):
@@ -469,12 +491,9 @@
     return c0 + alpha * p0, c1 + alpha * p1, alpha * p2
 
 
-def edges(colours, two, info, parts, v0, v1, v2, planted, likelihoods, first, second, *refs):
-    faces, edges_a, edges_b = refs[: 1 + two], refs[1 + two : 2 + 2 * two], refs[2 + 2 * two : 3 + 3 * two]
-    out, lam, field = refs[3 + 3 * two :]
-    labels, rows_x, rows_z, _ = likelihoods.shape
-    rows = rows_z + TILE
-    even = info[EVEN_X] == 1
+def edges(info, parts, v0, v1, v2, field, out, lam):
+    labels, _, rows, _ = v0.shape
+    rows_x = out.shape[1] - 2
     total = jnp.sum(parts[...], axis=0)
     grams = [jnp.broadcast_to(total[:, n : n + 1], (TILE, LANES)) for n in range(6)]
     c0, c1, c2 = steps(*grams)
@@ -483,21 +502,6 @@
         for at in range(rows_x + 3):
             source = at + HALO - 1
             lam[l, at] = s0 * v0[l, source] + s1 * v1[l, source] + s2 * v2[l, source]
-            x = at - 1
-            source = x % rows_x
-            if 0 <= x < rows_x:
-                member = jnp.where(planted[x] == info[COLOUR] + l, 1.0, 0.0)
-                plane = jnp.where(planted[x] >= colours, likelihoods[l, x], member)
-                plane = jnp.concatenate([plane, full_tile(*ends_z(info, faces, x, l))], axis=0)
-            else:
-                index = 2 * labels + labels * rows_x + 2 * l + (1 if x < 0 else source)
-                received = [
-                    jnp.concatenate([ref[index].astype(F32), full_tile(*ends_z(info, tiles, source, l))], axis=0)
-                    for ref, tiles in ((first, edges_a), (second, edges_b))
-                ]
-                above, below = sides(even, *received)
-                plane = below if x < 0 else above
-            field[l, at] = plane
     for at in range(rows_x + 2):
         sums = [jnp.zeros((rows, LANES), F32)] * 3
         for l in range(labels):
@@ -523,13 +527,11 @@
         planes += [jnp.zeros_like(planes[0])] * 7
         for pair in range(8):
             at = (xp * 16 + 2 * pair) * TILE
-            for t in range(-1, 5):
-                both = jnp.concatenate([plane[tile_rows(t)] for plane in planes[2 * pair : 2 * pair + 2]], axis=0)
-                grads[at : at + 16, (t + 1) * LANES : (t + 2) * LANES] = both.astype(BF16)
-    own = grads[LANES : LANES * (rows_x + 1), LANES : 5 * LANES]
-    for o in range(3):
-        products[o] = lax.dot_general(
-            own, stack[:, o * LANES : (o + 4) * LANES], (((1,), (1,)), ((), ())), preferred_element_type=F32
+            store_tiles(grads, at, planes[2 * pair : 2 * pair + 2])
+    own = grads[LANES : LANES * (rows_x + 1), : 4 * LANES]
+    for n in range(2):
+        products[n] = lax.dot_general(
+            own, stack[:, 512 * n : 512 * (n + 1)], (((1,), (1,)), ((), ())), preferred_element_type=F32
         )
     rows_out[...] = jnp.zeros_like(rows_out)
     masks = {(h, j, o): band(h, j, o) for o in (-1, 0, 1) for h in range(2) for j in bands(o)}
@@ -543,7 +545,7 @@
                         for x in range(rows_x):
                             at = (x * 16 + kd) * TILE
                             col = (x + i) // 2 * LANES
-                            piece = products[o + 1, at : at + TILE, col : col + LANES]
+                            piece = products[abs(o), at : at + TILE, col : col + LANES]
                             total = total + jnp.where(masks[(x + i) % 2, j, o], piece, 0.0)
                 row = d * 27 + i * 9 + j * 3 + k
                 rows_out[row : row + 1] = jnp.sum(total, axis=0, keepdims=True)
@@ -559,9 +561,8 @@
 
 
 def image_sums(info, grads, matrix, out, sums):
-    total = jnp.dot(matrix[0], grads[:, 0:512], preferred_element_type=F32)
-    total = total + jnp.dot(matrix[1], grads[:, 128:640], preferred_element_type=F32)
-    sums[...] = total + jnp.dot(matrix[2], grads[:, 256:768], preferred_element_type=F32)
+    total = jnp.dot(matrix[0], grads[:, :512], preferred_element_type=F32)
+    sums[...] = total + jnp.dot(matrix[1], grads[:, 512:], preferred_element_type=F32)
     channels, rows_x, rows_z, _ = out.shape
     for c in range(channels):
         for x in range(rows_x):
@@ -604,7 +605,7 @@
     taps = jnp.transpose(filt, (0, 2, 3, 4, 1))
     matrix, back_matrix, image, planted, likelihoods, slope, *packed = call(
         functools.partial(pack, colours, two),
-        [shaped((3, 288, 384), BF16), shaped((3, 256, 768), BF16)]
+        [shaped((2, 288, 384), BF16), shaped((2, 256, 768), BF16)]
         + [shaped(a.shape, a.dtype) for a in inputs]
         + [shaped((rows_x, labels, TILE, LANES), BF16)] * (1 + two)
         + [brick, brick],
@@ -628,7 +629,7 @@
 
     part, stack = call(
         functools.partial(convolve, two),
-        [shaped((3, rows_x, rows_z, LANES), F32), shaped((384, 768), BF16)],
+        [shaped((3, rows_x, rows_z, LANES), F32), shaped((384, 1024), BF16)],
         info,
         image,
         *received,
@@ -653,53 +654,52 @@
     other_edges = [lab_swap(block) for block in mine_edges]
     extended = (labels, rows_x + 2 * HALO, rows, LANES)
     ring = shaped((3, rows_x + 2, rows, LANES), F32)
-    v0, v1, v2, squash_slope, dots = call(
-        functools.partial(krylov, colours, size_x, size_z, two),
-        [shaped(extended, F32)] * 3 + [ring, shaped((members, TILE, LANES), F32)],
+    v0, free, field = call(
+        functools.partial(prepare, colours, two),
+        [shaped(extended, F32), shaped(extended[1:], F32), shaped((labels, rows_x + 3, rows, LANES), F32)],
         info,
         planted,
         slope,
+        likelihoods,
+        *received,
+        name="prepare",
+    )
+    v1, v2, squash_slope, dots = call(
+        functools.partial(krylov, size_x, size_z, two),
+        [shaped(extended, F32)] * 2 + [ring, shaped((members, TILE, LANES), F32)],
+        info,
+        v0,
+        free,
         logits,
         mine,
         other,
-        first,
-        second,
         *logit_faces,
         *mine_edges,
         *other_edges,
-        *faces,
-        *edges_a,
-        *edges_b,
-        scratch=[
-            pltpu.VMEM((3,) + extended[1:], F32),
-            pltpu.VMEM(extended[1:], F32),
-            pltpu.VMEM((6 * labels, LANES), F32),
-        ],
+        scratch=[pltpu.VMEM((3,) + extended[1:], F32), pltpu.VMEM((6 * labels, LANES), F32)],
         name="krylov",
     )
     edge = call(
-        functools.partial(edges, colours, two),
+        edges,
         ring,
         info,
         everyones(dots, ("xy", "gz")),
         v0,
         v1,
         v2,
-        planted,
-        likelihoods,
-        *received,
-        scratch=[pltpu.VMEM((labels, rows_x + 3, rows, LANES), F32)] * 2,
+        field,
+        scratch=[pltpu.VMEM((labels, rows_x + 3, rows, LANES), F32)],
         name="edges",
     )
     grads, sums = call(
         filter_sums,
-        [shaped((768, 768), BF16), shaped((members, TILE, LANES), F32)],
+        [shaped((768, 1024), BF16), shaped((members, TILE, LANES), F32)],
         info,
         edge,
         lab_swap(edge),
         squash_slope,
         stack,
-        scratch=[pltpu.VMEM((3, 512, 384), F32), pltpu.VMEM((LANES, LANES), F32)],
+        scratch=[pltpu.VMEM((2, 512, 384), F32), pltpu.VMEM((LANES, LANES), F32)],
         name="filter_sums",
     )
     grad_image = call(

time: 60.6 us -> 60.1 us (level)
    ppermute x4, waiting for transfers between devices: 4.3 us -> 3.53 us  [lab_swap(): return lax.ppermute(block, 'lab', [(0, 1), (1, 0)])]
    pallas_call x7 -> x8, Pallas kernels: 12.9 us -> 13.1 us  [call(): pl.pallas_call(kernel, out_shape=outs, in_specs=specs, out_specs=jax.tree...]
  transfers between devices with their start and end apart: 13 -> 13, of which waited for: 7 -> 7; matrix products, arithmetic and copies ran while one was open for 0% -> 0% of each run, Pallas kernels for 3% -> 4%
where the time goes in v6:
time: 60.1 us; the launch traced here: 59.9 us
  starting transfers between devices  19.3 us (32%)
  waiting for transfers between devices  15.1 us (25%)
  Pallas kernels  13.1 us (22%)
  blocking collectives  10.7 us (18%)
  local copies, waits for them, and re-layouts  0.93 us (2%)
  between operations  0.76 us (1%)
    pallas_call x8, Pallas kernels, call(): pl.pallas_call(kernel, out_shape=outs, in_specs=specs, out_specs=jax.tree...  13.1 us
    all_to_all x1, blocking collectives, everyones(): return lax.all_to_all(copies, axes, 0, 0)  10.7 us
    ppermute x4, starting transfers between devices, swap(): lax.ppermute(block, axis, pair_routes(lax.axis_size(axis), phase, closed))  5.69 us
    ppermute x2, starting transfers between devices, diagonal_swap(): return lax.ppermute(block, ('xy', 'gz'), route)  5.45 us
    all_to_all x1, waiting for transfers between devices, everyones(): return lax.all_to_all(copies, axes, 0, 0)  4.8 us
    ppermute x4, waiting for transfers between devices, lab_swap(): return lax.ppermute(block, 'lab', [(0, 1), (1, 0)])  3.53 us
    all_to_all x1, starting transfers between devices, everyones(): return lax.all_to_all(copies, axes, 0, 0)  3.34 us
    ppermute x2, waiting for transfers between devices, diagonal_swap(): return lax.ppermute(block, ('xy', 'gz'), route)  3.06 us
  transfers between devices with their start and end apart: 13, of which 7 were waited for; matrix products, arithmetic and copies ran while one was open for 0% of the time, Pallas kernels for 4%

profile of v6, /device:TPU:0, one launch (start us, length us, event | category | flops | bytes accessed | tf_op | source)
XLA Modules:
  0.0 59.9 jit_solution(6925816537478305175)
XLA Ops:
  0.8 2.0 %pack.1 = (bf16[2,288,384]{2,1,0:T(8,128)(2,1)S(1)}, bf16[2,256,768]{2,1,0:T(8,128)(2,1)S(1)}, bf16[8,4,32,128]{3,2,1,0:T(8,128)(2,1)S(1)}, s32[4,32,128]{2,1,0:...) custom-call(s32[10]{0:T(128)S(1)} %stack.43.info, ...), custom_call_target="tpu_custom_call" | custom-call | flops 1000000 | bytes 854600 | tf_op jit(solution)/shard_map/pack/pallas_call | solution.py:73
  2.8 3.1 %collective-permute-start = (bf16[32,32,128]{2,1,0:T(8,128)(2,1)S(1)}, bf16[32,32,128]{2,1,0:T(8,128)(2,1)S(1)}, u32[]{:S(2)}, u32[]{:S(2)}) collective-permute-start(bf16[32,32,128]{2,1,0:T(8,128)(2,1)S(1)} %get-tuple-element.31), channel_id=1, source_target_pairs={{0,4},{4,0},{8,12},{12,8},{1,5},{5,1},{9,13},{13,9},{2,6},{6,2},{1... | collective-permute-start | bytes 786440 | tf_op jit(solution)/shard_map/ppermute | solution.py:29
  5.9 0.7 %collective-permute-start.1 = (bf16[32,32,128]{2,1,0:T(8,128)(2,1)S(1)}, bf16[32,32,128]{2,1,0:T(8,128)(2,1)S(1)}, u32[]{:S(2)}, u32[]{:S(2)}) collective-permute-start(bf16[32,32,128]{2,1,0:T(8,128)(2,1)S(1)} %get-tuple-element.32), channel_id=1, source_target_pairs={{4,8},{8,4},{5,9},{9,5},{6,10},{10,6},{7,11},{11,7},{20,24},{24,20... | collective-permute-start | bytes 786440 | tf_op jit(solution)/shard_map/ppermute | solution.py:29
  6.5 3.5 %collective-permute-start.4 = (bf16[4,4,8,128]{3,2,1,0:T(8,128)(2,1)S(1)}, bf16[4,4,8,128]{3,2,1,0:T(8,128)(2,1)S(1)}, u32[]{:S(2)}, u32[]{:S(2)}) collective-permute-start(bf16[4,4,8,128]{3,2,1,0:T(8,128)(2,1)S(1)} %get-tuple-element.33), channel_id=1, source_target_pairs={{4,10},{6,8},{8,6},{10,4},{12,2},{14,0},{0,14},{2,12},{5,11},{7,9}... | collective-permute-start | bytes 98312 | tf_op jit(solution)/shard_map/ppermute | solution.py:41
  10.0 2.0 %collective-permute-start.3 = (bf16[4,4,8,128]{3,2,1,0:T(8,128)(2,1)S(1)}, bf16[4,4,8,128]{3,2,1,0:T(8,128)(2,1)S(1)}, u32[]{:S(2)}, u32[]{:S(2)}) collective-permute-start(bf16[4,4,8,128]{3,2,1,0:T(8,128)(2,1)S(1)} %get-tuple-element.33), channel_id=1, source_target_pairs={{0,6},{2,4},{4,2},{6,0},{8,14},{10,12},{12,10},{14,8},{1,7},{3,5},... | collective-permute-start | bytes 98312 | tf_op jit(solution)/shard_map/ppermute | solution.py:41
  12.0 1.4 %collective-permute-start.2 = (bf16[4,4,8,128]{3,2,1,0:T(8,128)(2,1)S(1)}, bf16[4,4,8,128]{3,2,1,0:T(8,128)(2,1)S(1)}, u32[]{:S(2)}, u32[]{:S(2)}) collective-permute-start(bf16[4,4,8,128]{3,2,1,0:T(8,128)(2,1)S(1)} %get-tuple-element.33), channel_id=1, source_target_pairs={{0,2},{2,0},{1,3},{3,1},{4,6},{6,4},{5,7},{7,5},{8,10},{10,8},{9,1... | collective-permute-start | bytes 98312 | tf_op jit(solution)/shard_map/ppermute | solution.py:29
  13.4 3.1 %collective-permute-done.4.refs_2_ = bf16[4,4,8,128]{3,2,1,0:T(8,128)(2,1)S(1)} collective-permute-done((bf16[4,4,8,128]{3,2,1,0:T(8,128)(2,1)S(1)}, bf16[4,4,8,128]{3,2,1,0:T(8,128)(2,1)S(1)}, u32[]{:S(2)}, u32[]{:S(2)}) %collective-permute-start.4) | collective-permute-done | bytes 32800 | tf_op jit(solution)/shard_map/ppermute | solution.py:41
  16.5 1.3 %convolve.1 = (f32[3,4,32,128]{3,2,1,0:T(8,128)S(1)}, bf16[384,1024]{1,0:T(8,128)(2,1)S(1)}) custom-call(s32[10]{0:T(128)S(1)} %stack.43.info, bf16[8,4,32,128]{3,2,1,0:T(8,128)(2,1)S(1)} %get-tuple-element.36.image, bf16[32,32,128]{2,1,0:T(8,128)(2,1)S(1)} %collective-permute-done.first, bf16[32,32,128]{2,1,0:T(8,128)(2,1)S(1)} %collective-permute-done.1.second, ...), custom_call_target="tpu_custom_call" | custom-call | flops 1000000 | bytes 1327144 | tf_op jit(solution)/shard_map/convolve/pallas_call | solution.py:73
  17.8 1.4 %collective-permute-done.5.other = f32[3,4,32,128]{3,2,1,0:T(8,128)S(1)} collective-permute-done((f32[3,4,32,128]{3,2,1,0:T(8,128)S(1)}, f32[3,4,32,128]{3,2,1,0:T(8,128)S(1)}, u32[]{:S(2)}, u32[]{:S(2)}) %collective-permute-start.5) | collective-permute-done | bytes 196640 | tf_op jit(solution)/shard_map/ppermute | solution.py:33
  19.8 2.9 %collective-permute-start.6 = (bf16[3,4,32,128]{3,2,1,0:T(8,128)(2,1)S(1)}, bf16[3,4,32,128]{3,2,1,0:T(8,128)(2,1)S(1)}, u32[]{:S(2)}, u32[]{:S(2)}) collective-permute-start(bf16[3,4,32,128]{3,2,1,0:T(8,128)(2,1)S(1)} %get-tuple-element.40), channel_id=1, source_target_pairs={{0,4},{4,0},{8,12},{12,8},{5,9},{9,5},{13,1},{1,13},{2,6},{6,2},{1... | collective-permute-start | bytes 294920 | tf_op jit(solution)/shard_map/ppermute | solution.py:51
  23.3 1.0 %collective-permute-start.7 = (bf16[3,4,8,128]{3,2,1,0:T(8,128)(2,1)S(1)}, bf16[3,4,8,128]{3,2,1,0:T(8,128)(2,1)S(1)}, u32[]{:S(2)}, u32[]{:S(2)}) collective-permute-start(bf16[3,4,8,128]{3,2,1,0:T(8,128)(2,1)S(1)} %get-tuple-element.41), channel_id=1, source_target_pairs={{0,6},{2,4},{4,2},{6,0},{8,14},{10,12},{12,10},{14,8},{5,11},{7,9}... | collective-permute-start | bytes 73736 | tf_op jit(solution)/shard_map/ppermute | solution.py:62
  24.3 2.3 %collective-permute-done.8.refs_0_ = bf16[3,4,8,128]{3,2,1,0:T(8,128)(2,1)S(1)} collective-permute-done((bf16[3,4,8,128]{3,2,1,0:T(8,128)(2,1)S(1)}, bf16[3,4,8,128]{3,2,1,0:T(8,128)(2,1)S(1)}, u32[]{:S(2)}, u32[]{:S(2)}) %collective-permute-start.8) | collective-permute-done | bytes 24608 | tf_op jit(solution)/shard_map/ppermute | solution.py:29
  26.6 1.4 %collective-permute-done.7.refs_1_ = bf16[3,4,8,128]{3,2,1,0:T(8,128)(2,1)S(1)} collective-permute-done((bf16[3,4,8,128]{3,2,1,0:T(8,128)(2,1)S(1)}, bf16[3,4,8,128]{3,2,1,0:T(8,128)(2,1)S(1)}, u32[]{:S(2)}, u32[]{:S(2)}) %collective-permute-start.7) | collective-permute-done | bytes 24608 | tf_op jit(solution)/shard_map/ppermute | solution.py:62
  28.0 0.8 %collective-permute-start.9 = (bf16[3,4,32,128]{3,2,1,0:T(8,128)(2,1)S(1)}, bf16[3,4,32,128]{3,2,1,0:T(8,128)(2,1)S(1)}, u32[]{:S(2)}, u32[]{:S(2)}) collective-permute-start(bf16[3,4,32,128]{3,2,1,0:T(8,128)(2,1)S(1)} %collective-permute-done.6.mine), channel_id=1, source_target_pairs={{0,1},{1,0},{2,3},{3,2},{4,5},{5,4},{6,7},{7,6},{8,9},{9,8},{10,11... | collective-permute-start | bytes 294920 | tf_op jit(solution)/shard_map/ppermute | solution.py:33
  28.8 0.8 %prepare.1 = (f32[4,12,40,128]{3,2,1,0:T(8,128)S(1)}, f32[12,40,128]{2,1,0:T(8,128)S(1)}, f32[4,7,40,128]{3,2,1,0:T(8,128)S(1)}) custom-call(s32[10]{0:T(128)S(1)} %stack.43.info, s32[4,32,128]{2,1,0:T(8,128)S(1)} %get-tuple-element.28.planted, f32[4,4,32,128]{3,2,1,0:T(8,128)S(1)} %get-tuple-element.29.slope, ...), custom_call_target="tpu_custom_call" | custom-call | flops 1000000 | bytes 1212456 | tf_op jit(solution)/shard_map/prepare/pallas_call | solution.py:73
  30.0 3.0 %krylov.1 = (f32[4,12,40,128]{3,2,1,0:T(8,128)S(1)}, f32[4,12,40,128]{3,2,1,0:T(8,128)S(1)}, f32[3,6,40,128]{3,2,1,0:T(8,128)S(1)}, f32[8,8,128]{2,1,0:T(8,128)S(1)}) custom-call(s32[10]{0:T(128)S(1)} %stack.43.info, f32[4,12,40,128]{3,2,1,0:T(8,128)S(1)} %get-tuple-element.34.v0, f32[12,40,128]{2,1,0:T(8,128)S(1)} %get-tuple-element.35.free, ...), custom_call_target="tpu_custom_call" | custom-call | flops 1000000 | bytes 1695784 | tf_op jit(solution)/shard_map/krylov/pallas_call | solution.py:73
  33.0 10.7 %all_to_all.10.parts = f32[8,8,128]{2,1,0:T(8,128)S(1)} all-to-all(f32[8,8,128]{2,1,0:T(8,128)S(1)} %get-tuple-element.45), channel_id=1, replica_groups=mesh['crops'=2,'xy'=4,'gz'=2,'lab'=2] {'xy','gz'}, dimensions={0} | all-to-all | bytes 65536 | tf_op jit(solution)/shard_map/all_to_all | solution.py:66
  43.7 1.2 %edges.1.edge = f32[3,6,40,128]{3,2,1,0:T(8,128)S(1)} custom-call(s32[10]{0:T(128)S(1)} %stack.43.info, f32[8,8,128]{2,1,0:T(8,128)S(1)} %all_to_all.10.parts, f32[4,12,40,128]{3,2,1,0:T(8,128)S(1)} %get-tuple-element.34.v0, f32[4,12,40,128]{3,2,1,0:T(8,128)S(1)} %get-tuple-element.46.v1, f32[4,12,40,128]{3,2,1,0:T(8,128)S(1)} %get-tuple-element.47.v2, ...), custom_call_target="tpu_custom_call" | custom-call | flops 1000000 | bytes 3555368 | tf_op jit(solution)/shard_map/edges/pallas_call | solution.py:73
  44.9 1.7 %collective-permute-done.11.other = f32[3,6,40,128]{3,2,1,0:T(8,128)S(1)} collective-permute-done((f32[3,6,40,128]{3,2,1,0:T(8,128)S(1)}, f32[3,6,40,128]{3,2,1,0:T(8,128)S(1)}, u32[]{:S(2)}, u32[]{:S(2)}) %collective-permute-start.11) | collective-permute-done | bytes 368672 | tf_op jit(solution)/shard_map/ppermute | solution.py:33
  46.6 2.5 %filter_sums.1 = (bf16[768,1024]{1,0:T(8,128)(2,1)S(1)}, f32[8,8,128]{2,1,0:T(8,128)}) custom-call(s32[10]{0:T(128)S(1)} %stack.43.info, f32[3,6,40,128]{3,2,1,0:T(8,128)S(1)} %edges.1.edge, f32[3,6,40,128]{3,2,1,0:T(8,128)S(1)} %collective-permute-done.11.other, f32[3,6,40,128]{3,2,1,0:T(8,128)S(1)} %get-tuple-element.49.slope, ...), custom_call_target="tpu_custom_call" | custom-call | flops 1000000 | bytes 1892392 | tf_op jit(solution)/shard_map/filter_sums/pallas_call | solution.py:73
  49.0 3.3 %all-to-all-start.1 = ((f32[8,8,128]{2,1,0:T(8,128)}), f32[8,8,128]{2,1,0:T(8,128)S(1)}, u32[]{:S(2)}, u32[]{:S(2)}) async-start(f32[8,8,128]{2,1,0:T(8,128)} %get-tuple-element.53), calls=%async_computation.1 | async-start | bytes 65536 | tf_op jit(solution)/shard_map/all_to_all | solution.py:66
  52.4 1.8 %image_sums.1 = bf16[8,4,32,128]{3,2,1,0:T(8,128)(2,1)} custom-call(s32[10]{0:T(128)S(1)} %stack.43.info, bf16[768,1024]{1,0:T(8,128)(2,1)S(1)} %get-tuple-element.51.grads, bf16[2,256,768]{2,1,0:T(8,128)(2,1)S(1)} %get-tuple-element.52.matrix), custom_call_target="tpu_custom_call" | custom-call | flops 10000000 | bytes 2359336 | tf_op jit(solution)/shard_map/image_sums/pallas_call | solution.py:73
  54.2 4.8 %all-to-all-done.1 = f32[8,8,128]{2,1,0:T(8,128)S(1)} async-done(((f32[8,8,128]{2,1,0:T(8,128)}), f32[8,8,128]{2,1,0:T(8,128)S(1)}, u32[]{:S(2)}, u32[]{:S(2)}) %all-to-all-start.1) | async-done | bytes 32800 | tf_op jit(solution)/shard_map/all_to_all | solution.py:66
  59.2 0.7 %reshape.11 = f32[3,8,3,3,3]{1,4,3,2,0:T(4,128)} reshape(f32[3,8,27]{1,2,0:T(8,128)S(1)} %copy.7) | data formatting | bytes 5184 | tf_op jit(solution)/shard_map/reshape | solution.py:717
  (16 shorter events, 2.0 us)
Async XLA Ops:
  2.8 13.7 %collective-permute-start = (bf16[32,32,128]{2,1,0:T(8,128)(2,1)S(1)}, bf16[32,32,128]{2,1,0:T(8,128)(2,1)S(1)}, u32[]{:S(2)}, u32[]{:S(2)}) collective-permute-start(bf16[32,32,128]{2,1,0:T(8,128)(2,1)S(1)} %get-tuple-element.31), channel_id=1, source_target_pairs={{0,4},{4,0},{8,12},{12,8},{1,5},{5,1},{9,13},{13,9},{2,6},{6,2},{1... | collective-permute-start | bytes 786440 | tf_op jit(solution)/shard_map/ppermute | solution.py:29
  5.9 10.6 %collective-permute-start.1 = (bf16[32,32,128]{2,1,0:T(8,128)(2,1)S(1)}, bf16[32,32,128]{2,1,0:T(8,128)(2,1)S(1)}, u32[]{:S(2)}, u32[]{:S(2)}) collective-permute-start(bf16[32,32,128]{2,1,0:T(8,128)(2,1)S(1)} %get-tuple-element.32), channel_id=1, source_target_pairs={{4,8},{8,4},{5,9},{9,5},{6,10},{10,6},{7,11},{11,7},{20,24},{24,20... | collective-permute-start | bytes 786440 | tf_op jit(solution)/shard_map/ppermute | solution.py:29
  6.5 9.9 %collective-permute-start.4 = (bf16[4,4,8,128]{3,2,1,0:T(8,128)(2,1)S(1)}, bf16[4,4,8,128]{3,2,1,0:T(8,128)(2,1)S(1)}, u32[]{:S(2)}, u32[]{:S(2)}) collective-permute-start(bf16[4,4,8,128]{3,2,1,0:T(8,128)(2,1)S(1)} %get-tuple-element.33), channel_id=1, source_target_pairs={{4,10},{6,8},{8,6},{10,4},{12,2},{14,0},{0,14},{2,12},{5,11},{7,9}... | collective-permute-start | bytes 98312 | tf_op jit(solution)/shard_map/ppermute | solution.py:41
  10.0 6.4 %collective-permute-start.3 = (bf16[4,4,8,128]{3,2,1,0:T(8,128)(2,1)S(1)}, bf16[4,4,8,128]{3,2,1,0:T(8,128)(2,1)S(1)}, u32[]{:S(2)}, u32[]{:S(2)}) collective-permute-start(bf16[4,4,8,128]{3,2,1,0:T(8,128)(2,1)S(1)} %get-tuple-element.33), channel_id=1, source_target_pairs={{0,6},{2,4},{4,2},{6,0},{8,14},{10,12},{12,10},{14,8},{1,7},{3,5},... | collective-permute-start | bytes 98312 | tf_op jit(solution)/shard_map/ppermute | solution.py:41
  12.0 4.5 %collective-permute-start.2 = (bf16[4,4,8,128]{3,2,1,0:T(8,128)(2,1)S(1)}, bf16[4,4,8,128]{3,2,1,0:T(8,128)(2,1)S(1)}, u32[]{:S(2)}, u32[]{:S(2)}) collective-permute-start(bf16[4,4,8,128]{3,2,1,0:T(8,128)(2,1)S(1)} %get-tuple-element.33), channel_id=1, source_target_pairs={{0,2},{2,0},{1,3},{3,1},{4,6},{6,4},{5,7},{7,5},{8,10},{10,8},{9,1... | collective-permute-start | bytes 98312 | tf_op jit(solution)/shard_map/ppermute | solution.py:29
  17.8 1.5 %collective-permute-start.5 = (f32[3,4,32,128]{3,2,1,0:T(8,128)S(1)}, f32[3,4,32,128]{3,2,1,0:T(8,128)S(1)}, u32[]{:S(2)}, u32[]{:S(2)}) collective-permute-start(f32[3,4,32,128]{3,2,1,0:T(8,128)S(1)} %get-tuple-element.38.part), channel_id=1, source_target_pairs={{0,1},{1,0},{2,3},{3,2},{4,5},{5,4},{6,7},{7,6},{8,9},{9,8},{10,11... | collective-permute-start | bytes 589832 | tf_op jit(solution)/shard_map/ppermute | solution.py:33
  19.8 8.1 %collective-permute-start.6 = (bf16[3,4,32,128]{3,2,1,0:T(8,128)(2,1)S(1)}, bf16[3,4,32,128]{3,2,1,0:T(8,128)(2,1)S(1)}, u32[]{:S(2)}, u32[]{:S(2)}) collective-permute-start(bf16[3,4,32,128]{3,2,1,0:T(8,128)(2,1)S(1)} %get-tuple-element.40), channel_id=1, source_target_pairs={{0,4},{4,0},{8,12},{12,8},{5,9},{9,5},{13,1},{1,13},{2,6},{6,2},{1... | collective-permute-start | bytes 294920 | tf_op jit(solution)/shard_map/ppermute | solution.py:51
  22.7 3.8 %collective-permute-start.8 = (bf16[3,4,8,128]{3,2,1,0:T(8,128)(2,1)S(1)}, bf16[3,4,8,128]{3,2,1,0:T(8,128)(2,1)S(1)}, u32[]{:S(2)}, u32[]{:S(2)}) collective-permute-start(bf16[3,4,8,128]{3,2,1,0:T(8,128)(2,1)S(1)} %get-tuple-element.41), channel_id=1, source_target_pairs={{0,2},{2,0},{1,3},{3,1},{4,6},{6,4},{5,7},{7,5},{8,10},{10,8},{9,1... | collective-permute-start | bytes 73736 | tf_op jit(solution)/shard_map/ppermute | solution.py:29
  23.3 4.7 %collective-permute-start.7 = (bf16[3,4,8,128]{3,2,1,0:T(8,128)(2,1)S(1)}, bf16[3,4,8,128]{3,2,1,0:T(8,128)(2,1)S(1)}, u32[]{:S(2)}, u32[]{:S(2)}) collective-permute-start(bf16[3,4,8,128]{3,2,1,0:T(8,128)(2,1)S(1)} %get-tuple-element.41), channel_id=1, source_target_pairs={{0,6},{2,4},{4,2},{6,0},{8,14},{10,12},{12,10},{14,8},{5,11},{7,9}... | collective-permute-start | bytes 73736 | tf_op jit(solution)/shard_map/ppermute | solution.py:62
  28.0 2.0 %collective-permute-start.9 = (bf16[3,4,32,128]{3,2,1,0:T(8,128)(2,1)S(1)}, bf16[3,4,32,128]{3,2,1,0:T(8,128)(2,1)S(1)}, u32[]{:S(2)}, u32[]{:S(2)}) collective-permute-start(bf16[3,4,32,128]{3,2,1,0:T(8,128)(2,1)S(1)} %collective-permute-done.6.mine), channel_id=1, source_target_pairs={{0,1},{1,0},{2,3},{3,2},{4,5},{5,4},{6,7},{7,6},{8,9},{9,8},{10,11... | collective-permute-start | bytes 294920 | tf_op jit(solution)/shard_map/ppermute | solution.py:33
  28.8 1.2 %collective-permute-start.10 = (bf16[3,4,8,128]{3,2,1,0:T(8,128)(2,1)S(1)}, bf16[3,4,8,128]{3,2,1,0:T(8,128)(2,1)S(1)}, u32[]{:S(2)}, u32[]{:S(2)}) collective-permute-start(bf16[3,4,8,128]{3,2,1,0:T(8,128)(2,1)S(1)} %collective-permute-done.7.refs_1_), channel_id=1, source_target_pairs={{0,1},{1,0},{2,3},{3,2},{4,5},{5,4},{6,7},{7,6},{8,9},{9,8},{10,11... | collective-permute-start | bytes 73736 | tf_op jit(solution)/shard_map/ppermute | solution.py:33
  44.8 1.8 %collective-permute-start.11 = (f32[3,6,40,128]{3,2,1,0:T(8,128)S(1)}, f32[3,6,40,128]{3,2,1,0:T(8,128)S(1)}, u32[]{:S(2)}, u32[]{:S(2)}) collective-permute-start(f32[3,6,40,128]{3,2,1,0:T(8,128)S(1)} %edges.1.edge), channel_id=1, source_target_pairs={{0,1},{1,0},{2,3},{3,2},{4,5},{5,4},{6,7},{7,6},{8,9},{9,8},{10,11... | collective-permute-start | bytes 1105928 | tf_op jit(solution)/shard_map/ppermute | solution.py:33
  49.0 10.0 %all-to-all-start.1 = ((f32[8,8,128]{2,1,0:T(8,128)}), f32[8,8,128]{2,1,0:T(8,128)S(1)}, u32[]{:S(2)}, u32[]{:S(2)}) async-start(f32[8,8,128]{2,1,0:T(8,128)} %get-tuple-element.53), calls=%async_computation.1 | async-start | bytes 65536 | tf_op jit(solution)/shard_map/all_to_all | solution.py:66

commit v7 on v6

--- a/solution.py
+++ b/solution.py
@@ -16,50 +16,85 @@
 EVEN_X, EVEN_Z, FIRST_X, FIRST_Z, COLOUR, UP, PREV_X, NEXT_X, PREV_Z, NEXT_Z = range(10)
 
 
-def pair_routes(count, phase, closed=False):
-    route = []
-    for low in range(phase, count - 1, 2):
-        route += [(low, low + 1), (low + 1, low)]
-    if closed and phase == 1 and count % 2 == 0:
-        route += [(count - 1, 0), (0, count - 1)]
-    return route
-
-
-def swap(block, axis, phase, closed=False):
-    return lax.ppermute(block, axis, pair_routes(lax.axis_size(axis), phase, closed))
+SWAP_AXES = ("xy", "gz", "lab")
+
+
+def mate(place, phase, count):
+    other = place + 1 if (place - phase) % 2 == 0 else place - 1
+    return other if phase <= min(place, other) and max(place, other) < count else None
+
+
+def swap(block, partner):
+    sizes = [lax.axis_size(axis) for axis in SWAP_AXES]
+    devices = [(x, z, lab) for x in range(sizes[0]) for z in range(sizes[1]) for lab in range(sizes[2])]
+    pairs = {}
+    for device in devices:
+        if partner(*device) is not None:
+            pairs[device] = partner(*device)
+    for other_of in (lambda x, z, lab: (x, z, lab ^ 1), lambda x, z, lab: (x, z ^ 1, lab)):
+        for device in devices:
+            other = other_of(*device)
+            if device not in pairs and other in devices and other not in pairs:
+                pairs[device], pairs[other] = other, device
+
+    def flat(x, z, lab):
+        return (x * sizes[1] + z) * sizes[2] + lab
+
+    return lax.ppermute(block, SWAP_AXES, [(flat(*src), flat(*dst)) for src, dst in sorted(pairs.items())])
+
+
+def x_swap(block, phase):
+    count = lax.axis_size("xy")
+
+    def partner(x, z, lab):
+        other = mate(x, phase, count)
+        return None if other is None else (other, z, lab)
+
+    return swap(block, partner)
+
+
+def z_swap(block, phase):
+    count = lax.axis_size("gz")
+
+    def partner(x, z, lab):
+        other = mate(z, phase, count)
+        return None if other is None else (x, other, lab)
+
+    return swap(block, partner)
+
+
+def diagonal_swap(block, x_phase, z_phase):
+    counts = lax.axis_size("xy"), lax.axis_size("gz")
+
+    def partner(x, z, lab):
+        others = mate(x, x_phase, counts[0]), mate(z, z_phase, counts[1])
+        return None if None in others else (*others, lab)
+
+    return swap(block, partner)
 
 
 def lab_swap(block):
     return lax.ppermute(block, "lab", [(0, 1), (1, 0)])
 
 
-def diagonal_swap(block, x_phase, z_phase):
-    along_x = pair_routes(lax.axis_size("xy"), x_phase, True)
-    along_z = pair_routes(lax.axis_size("gz"), z_phase, True)
-    count = lax.axis_size("gz")
-    route = [(sx * count + sz, dx * count + dz) for sx, dx in along_x for sz, dz in along_z]
-    return lax.ppermute(block, ("xy", "gz"), route)
-
-
 def split_swap(block):
-    labs = lax.axis_size("lab")
-    route = [
-        (src * labs + lab, dst * labs + lab)
-        for lab in range(labs)
-        for src, dst in pair_routes(lax.axis_size("xy"), lab % 2, True)
-    ]
-    return lax.ppermute(block, ("xy", "lab"), route)
+    count = lax.axis_size("xy")
+
+    def partner(x, z, lab):
+        other = mate(x, lab % 2, count)
+        return None if other is None else (other, z, lab)
+
+    return swap(block, partner)
 
 
 def split_diagonal_swap(block, z_phase):
-    labs, count = lax.axis_size("lab"), lax.axis_size("gz")
-    route = [
-        ((sx * count + sz) * labs + lab, (dx * count + dz) * labs + lab)
-        for lab in range(labs)
-        for sx, dx in pair_routes(lax.axis_size("xy"), lab % 2, True)
-        for sz, dz in pair_routes(count, z_phase, True)
-    ]
-    return lax.ppermute(block, ("xy", "gz", "lab"), route)
+    counts = lax.axis_size("xy"), lax.axis_size("gz")
+
+    def partner(x, z, lab):
+        others = mate(x, lab % 2, counts[0]), mate(z, z_phase, counts[1])
+        return None if None in others else (*others, lab)
+
+    return swap(block, partner)
 
 
 def everyones(copies, axes):
@@ -620,11 +655,11 @@
         space=pltpu.HBM,
     )
     send_a, send_b = packed[1 + two :]
-    faces = [swap(packed[phase], "gz", phase, True) for phase in phases]
+    faces = [z_swap(packed[phase], phase) for phase in phases]
     edges_a = [diagonal_swap(packed[phase], 0, phase) for phase in phases]
     edges_b = [diagonal_swap(packed[phase], 1, phase) for phase in phases]
-    second = swap(send_b, "xy", 1)
-    first = swap(send_a, "xy", 0)
+    second = x_swap(send_b, 1)
+    first = x_swap(send_a, 0)
     received = (first, second, *faces, *edges_a, *edges_b)
 
     part, stack = call(
@@ -648,7 +683,7 @@
     )
     mine = split_swap(own)
     mine_edges = [split_diagonal_swap(sends[phase], phase) for phase in phases]
-    logit_faces = [swap(sends[phase], "gz", phase, True) for phase in phases]
+    logit_faces = [z_swap(sends[phase], phase) for phase in phases]
     mine, mine_edges, logit_faces = lax.optimization_barrier((mine, mine_edges, logit_faces))
     other = lab_swap(mine)
     other_edges = [lab_swap(block) for block in mine_edges]

time: 60.1 us -> 57.5 us (0.957)
  starting transfers between devices: 19.3 us -> 16.7 us
    ppermute x8, starting transfers between devices: 15 us -> 12.7 us  [swap(): lax.ppermute(block, SWAP_AXES, [(flat(*src), flat(*dst)) for src, dst in...]
    all_to_all x1, blocking collectives: 10.7 us -> 11.3 us  [everyones(): return lax.all_to_all(copies, axes, 0, 0)]
  transfers between devices with their start and end apart: 13 -> 13, of which waited for: 7 -> 8; matrix products, arithmetic and copies ran while one was open for 0% -> 0% of each run, Pallas kernels for 4% -> 4%
where the time goes in v7:
time: 57.5 us; the launch traced here: 57.3 us
  starting transfers between devices  16.7 us (29%)
  waiting for transfers between devices  14.5 us (25%)
  Pallas kernels  13.1 us (23%)
  blocking collectives  11.3 us (20%)
  local copies, waits for them, and re-layouts  0.93 us (2%)
  between operations  0.74 us (1%)
    pallas_call x8, Pallas kernels, call(): pl.pallas_call(kernel, out_shape=outs, in_specs=specs, out_specs=jax.tree...  13.1 us
    ppermute x8, starting transfers between devices, swap(): lax.ppermute(block, SWAP_AXES, [(flat(*src), flat(*dst)) for src, dst in...  12.7 us
    all_to_all x1, blocking collectives, everyones(): return lax.all_to_all(copies, axes, 0, 0)  11.3 us
    ppermute x8, waiting for transfers between devices, swap(): lax.ppermute(block, SWAP_AXES, [(flat(*src), flat(*dst)) for src, dst in...  6.53 us
    all_to_all x1, waiting for transfers between devices, everyones(): return lax.all_to_all(copies, axes, 0, 0)  4.8 us
    all_to_all x1, starting transfers between devices, everyones(): return lax.all_to_all(copies, axes, 0, 0)  3.34 us
    ppermute x4, waiting for transfers between devices, lab_swap(): return lax.ppermute(block, 'lab', [(0, 1), (1, 0)])  3.19 us
  transfers between devices with their start and end apart: 13, of which 8 were waited for; matrix products, arithmetic and copies ran while one was open for 0% of the time, Pallas kernels for 4%

profile of v7, /device:TPU:0, one launch (start us, length us, event | category | flops | bytes accessed | tf_op | source)
XLA Modules:
  0.0 57.3 jit_solution(17061516359969310498)
XLA Ops:
  0.8 2.0 %pack.1 = (bf16[2,288,384]{2,1,0:T(8,128)(2,1)S(1)}, bf16[2,256,768]{2,1,0:T(8,128)(2,1)S(1)}, bf16[8,4,32,128]{3,2,1,0:T(8,128)(2,1)S(1)}, s32[4,32,128]{2,1,0:...) custom-call(s32[10]{0:T(128)S(1)} %stack.43.info, ...), custom_call_target="tpu_custom_call" | custom-call | flops 1000000 | bytes 854600 | tf_op jit(solution)/shard_map/pack/pallas_call | solution.py:108
  2.8 3.1 %collective-permute-start = (bf16[32,32,128]{2,1,0:T(8,128)(2,1)S(1)}, bf16[32,32,128]{2,1,0:T(8,128)(2,1)S(1)}, u32[]{:S(2)}, u32[]{:S(2)}) collective-permute-start(bf16[32,32,128]{2,1,0:T(8,128)(2,1)S(1)} %get-tuple-element.31), channel_id=1, source_target_pairs={{0,4},{1,5},{2,6},{3,7},{4,0},{5,1},{6,2},{7,3},{8,12},{9,13},{10,... | collective-permute-start | bytes 786440 | tf_op jit(solution)/shard_map/ppermute | solution.py:43
  6.4 3.6 %collective-permute-start.3 = (bf16[4,4,8,128]{3,2,1,0:T(8,128)(2,1)S(1)}, bf16[4,4,8,128]{3,2,1,0:T(8,128)(2,1)S(1)}, u32[]{:S(2)}, u32[]{:S(2)}) collective-permute-start(bf16[4,4,8,128]{3,2,1,0:T(8,128)(2,1)S(1)} %get-tuple-element.33), channel_id=1, source_target_pairs={{0,6},{1,7},{2,4},{3,5},{4,2},{5,3},{6,0},{7,1},{8,14},{9,15},{10,... | collective-permute-start | bytes 98312 | tf_op jit(solution)/shard_map/ppermute | solution.py:43
  10.0 1.5 %collective-permute-start.2 = (bf16[4,4,8,128]{3,2,1,0:T(8,128)(2,1)S(1)}, bf16[4,4,8,128]{3,2,1,0:T(8,128)(2,1)S(1)}, u32[]{:S(2)}, u32[]{:S(2)}) collective-permute-start(bf16[4,4,8,128]{3,2,1,0:T(8,128)(2,1)S(1)} %get-tuple-element.33), channel_id=1, source_target_pairs={{0,2},{1,3},{2,0},{3,1},{4,6},{5,7},{6,4},{7,5},{8,10},{9,11},{10,... | collective-permute-start | bytes 98312 | tf_op jit(solution)/shard_map/ppermute | solution.py:43
  11.4 2.7 %collective-permute-done.3.refs_1_ = bf16[4,4,8,128]{3,2,1,0:T(8,128)(2,1)S(1)} collective-permute-done((bf16[4,4,8,128]{3,2,1,0:T(8,128)(2,1)S(1)}, bf16[4,4,8,128]{3,2,1,0:T(8,128)(2,1)S(1)}, u32[]{:S(2)}, u32[]{:S(2)}) %collective-permute-start.3) | collective-permute-done | bytes 32800 | tf_op jit(solution)/shard_map/ppermute | solution.py:43
  14.2 1.3 %convolve.1 = (f32[3,4,32,128]{3,2,1,0:T(8,128)S(1)}, bf16[384,1024]{1,0:T(8,128)(2,1)S(1)}) custom-call(s32[10]{0:T(128)S(1)} %stack.43.info, bf16[8,4,32,128]{3,2,1,0:T(8,128)(2,1)S(1)} %get-tuple-element.36.image, bf16[32,32,128]{2,1,0:T(8,128)(2,1)S(1)} %collective-permute-done.first, bf16[32,32,128]{2,1,0:T(8,128)(2,1)S(1)} %collective-permute-done.1.second, ...), custom_call_target="tpu_custom_call" | custom-call | flops 1000000 | bytes 1327144 | tf_op jit(solution)/shard_map/convolve/pallas_call | solution.py:108
  15.6 1.4 %collective-permute-done.5.other = f32[3,4,32,128]{3,2,1,0:T(8,128)S(1)} collective-permute-done((f32[3,4,32,128]{3,2,1,0:T(8,128)S(1)}, f32[3,4,32,128]{3,2,1,0:T(8,128)S(1)}, u32[]{:S(2)}, u32[]{:S(2)}) %collective-permute-start.5) | collective-permute-done | bytes 196640 | tf_op jit(solution)/shard_map/ppermute | solution.py:77
  17.0 0.6 add_parts.1
  17.6 2.5 %collective-permute-start.6 = (bf16[3,4,32,128]{3,2,1,0:T(8,128)(2,1)S(1)}, bf16[3,4,32,128]{3,2,1,0:T(8,128)(2,1)S(1)}, u32[]{:S(2)}, u32[]{:S(2)}) collective-permute-start(bf16[3,4,32,128]{3,2,1,0:T(8,128)(2,1)S(1)} %get-tuple-element.40), channel_id=1, source_target_pairs={{0,4},{1,3},{2,6},{3,1},{4,0},{5,9},{6,2},{7,11},{8,12},{9,5},{10,... | collective-permute-start | bytes 294920 | tf_op jit(solution)/shard_map/ppermute | solution.py:43
  20.1 0.5 collective-permute-start.8
  20.7 1.0 %collective-permute-start.7 = (bf16[3,4,8,128]{3,2,1,0:T(8,128)(2,1)S(1)}, bf16[3,4,8,128]{3,2,1,0:T(8,128)(2,1)S(1)}, u32[]{:S(2)}, u32[]{:S(2)}) collective-permute-start(bf16[3,4,8,128]{3,2,1,0:T(8,128)(2,1)S(1)} %get-tuple-element.41), channel_id=1, source_target_pairs={{0,6},{1,3},{2,4},{3,1},{4,2},{5,11},{6,0},{7,9},{8,14},{9,7},{10,... | collective-permute-start | bytes 73736 | tf_op jit(solution)/shard_map/ppermute | solution.py:43
  21.7 2.3 %collective-permute-done.8.refs_0_ = bf16[3,4,8,128]{3,2,1,0:T(8,128)(2,1)S(1)} collective-permute-done((bf16[3,4,8,128]{3,2,1,0:T(8,128)(2,1)S(1)}, bf16[3,4,8,128]{3,2,1,0:T(8,128)(2,1)S(1)}, u32[]{:S(2)}, u32[]{:S(2)}) %collective-permute-start.8) | collective-permute-done | bytes 24608 | tf_op jit(solution)/shard_map/ppermute | solution.py:43
  24.0 1.4 %collective-permute-done.7.refs_1_ = bf16[3,4,8,128]{3,2,1,0:T(8,128)(2,1)S(1)} collective-permute-done((bf16[3,4,8,128]{3,2,1,0:T(8,128)(2,1)S(1)}, bf16[3,4,8,128]{3,2,1,0:T(8,128)(2,1)S(1)}, u32[]{:S(2)}, u32[]{:S(2)}) %collective-permute-start.7) | collective-permute-done | bytes 24608 | tf_op jit(solution)/shard_map/ppermute | solution.py:43
  25.4 0.5 collective-permute-start.10
  25.9 0.8 %prepare.1 = (f32[4,12,40,128]{3,2,1,0:T(8,128)S(1)}, f32[12,40,128]{2,1,0:T(8,128)S(1)}, f32[4,7,40,128]{3,2,1,0:T(8,128)S(1)}) custom-call(s32[10]{0:T(128)S(1)} %stack.43.info, s32[4,32,128]{2,1,0:T(8,128)S(1)} %get-tuple-element.28.planted, f32[4,4,32,128]{3,2,1,0:T(8,128)S(1)} %get-tuple-element.29.slope, ...), custom_call_target="tpu_custom_call" | custom-call | flops 1000000 | bytes 1212456 | tf_op jit(solution)/shard_map/prepare/pallas_call | solution.py:108
  26.8 3.0 %krylov.1 = (f32[4,12,40,128]{3,2,1,0:T(8,128)S(1)}, f32[4,12,40,128]{3,2,1,0:T(8,128)S(1)}, f32[3,6,40,128]{3,2,1,0:T(8,128)S(1)}, f32[8,8,128]{2,1,0:T(8,128)S(1)}) custom-call(s32[10]{0:T(128)S(1)} %stack.43.info, f32[4,12,40,128]{3,2,1,0:T(8,128)S(1)} %get-tuple-element.34.v0, f32[12,40,128]{2,1,0:T(8,128)S(1)} %get-tuple-element.35.free, ...), custom_call_target="tpu_custom_call" | custom-call | flops 1000000 | bytes 1695784 | tf_op jit(solution)/shard_map/krylov/pallas_call | solution.py:108
  29.8 11.3 %all_to_all.10.parts = f32[8,8,128]{2,1,0:T(8,128)S(1)} all-to-all(f32[8,8,128]{2,1,0:T(8,128)S(1)} %get-tuple-element.45), channel_id=1, replica_groups=mesh['crops'=2,'xy'=4,'gz'=2,'lab'=2] {'xy','gz'}, dimensions={0} | all-to-all | bytes 65536 | tf_op jit(solution)/shard_map/all_to_all | solution.py:101
  41.1 1.2 %edges.1.edge = f32[3,6,40,128]{3,2,1,0:T(8,128)S(1)} custom-call(s32[10]{0:T(128)S(1)} %stack.43.info, f32[8,8,128]{2,1,0:T(8,128)S(1)} %all_to_all.10.parts, f32[4,12,40,128]{3,2,1,0:T(8,128)S(1)} %get-tuple-element.34.v0, f32[4,12,40,128]{3,2,1,0:T(8,128)S(1)} %get-tuple-element.46.v1, f32[4,12,40,128]{3,2,1,0:T(8,128)S(1)} %get-tuple-element.47.v2, ...), custom_call_target="tpu_custom_call" | custom-call | flops 1000000 | bytes 3555368 | tf_op jit(solution)/shard_map/edges/pallas_call | solution.py:108
  42.3 1.7 %collective-permute-done.11.other = f32[3,6,40,128]{3,2,1,0:T(8,128)S(1)} collective-permute-done((f32[3,6,40,128]{3,2,1,0:T(8,128)S(1)}, f32[3,6,40,128]{3,2,1,0:T(8,128)S(1)}, u32[]{:S(2)}, u32[]{:S(2)}) %collective-permute-start.11) | collective-permute-done | bytes 368672 | tf_op jit(solution)/shard_map/ppermute | solution.py:77
  44.0 2.5 %filter_sums.1 = (bf16[768,1024]{1,0:T(8,128)(2,1)S(1)}, f32[8,8,128]{2,1,0:T(8,128)}) custom-call(s32[10]{0:T(128)S(1)} %stack.43.info, f32[3,6,40,128]{3,2,1,0:T(8,128)S(1)} %edges.1.edge, f32[3,6,40,128]{3,2,1,0:T(8,128)S(1)} %collective-permute-done.11.other, f32[3,6,40,128]{3,2,1,0:T(8,128)S(1)} %get-tuple-element.49.slope, ...), custom_call_target="tpu_custom_call" | custom-call | flops 1000000 | bytes 1892392 | tf_op jit(solution)/shard_map/filter_sums/pallas_call | solution.py:108
  46.5 3.3 %all-to-all-start.1 = ((f32[8,8,128]{2,1,0:T(8,128)}), f32[8,8,128]{2,1,0:T(8,128)S(1)}, u32[]{:S(2)}, u32[]{:S(2)}) async-start(f32[8,8,128]{2,1,0:T(8,128)} %get-tuple-element.53), calls=%async_computation.1 | async-start | bytes 65536 | tf_op jit(solution)/shard_map/all_to_all | solution.py:101
  49.8 1.8 %image_sums.1 = bf16[8,4,32,128]{3,2,1,0:T(8,128)(2,1)} custom-call(s32[10]{0:T(128)S(1)} %stack.43.info, bf16[768,1024]{1,0:T(8,128)(2,1)S(1)} %get-tuple-element.51.grads, bf16[2,256,768]{2,1,0:T(8,128)(2,1)S(1)} %get-tuple-element.52.matrix), custom_call_target="tpu_custom_call" | custom-call | flops 10000000 | bytes 2359336 | tf_op jit(solution)/shard_map/image_sums/pallas_call | solution.py:108
  51.6 4.8 %all-to-all-done.1 = f32[8,8,128]{2,1,0:T(8,128)S(1)} async-done(((f32[8,8,128]{2,1,0:T(8,128)}), f32[8,8,128]{2,1,0:T(8,128)S(1)}, u32[]{:S(2)}, u32[]{:S(2)}) %all-to-all-start.1) | async-done | bytes 32800 | tf_op jit(solution)/shard_map/all_to_all | solution.py:101
  56.6 0.7 %reshape.11 = f32[3,8,3,3,3]{1,4,3,2,0:T(4,128)} reshape(f32[3,8,27]{1,2,0:T(8,128)S(1)} %copy.7) | data formatting | bytes 5184 | tf_op jit(solution)/shard_map/reshape | solution.py:752
  (16 shorter events, 1.2 us)
Async XLA Ops:
  2.8 11.4 %collective-permute-start = (bf16[32,32,128]{2,1,0:T(8,128)(2,1)S(1)}, bf16[32,32,128]{2,1,0:T(8,128)(2,1)S(1)}, u32[]{:S(2)}, u32[]{:S(2)}) collective-permute-start(bf16[32,32,128]{2,1,0:T(8,128)(2,1)S(1)} %get-tuple-element.31), channel_id=1, source_target_pairs={{0,4},{1,5},{2,6},{3,7},{4,0},{5,1},{6,2},{7,3},{8,12},{9,13},{10,... | collective-permute-start | bytes 786440 | tf_op jit(solution)/shard_map/ppermute | solution.py:43
  5.9 8.4 %collective-permute-start.1 = (bf16[32,32,128]{2,1,0:T(8,128)(2,1)S(1)}, bf16[32,32,128]{2,1,0:T(8,128)(2,1)S(1)}, u32[]{:S(2)}, u32[]{:S(2)}) collective-permute-start(bf16[32,32,128]{2,1,0:T(8,128)(2,1)S(1)} %get-tuple-element.32), channel_id=1, source_target_pairs={{0,1},{1,0},{2,3},{3,2},{4,8},{5,9},{6,10},{7,11},{8,4},{9,5},{10,... | collective-permute-start | bytes 786440 | tf_op jit(solution)/shard_map/ppermute | solution.py:43
  5.9 5.5 %collective-permute-start.4 = (bf16[4,4,8,128]{3,2,1,0:T(8,128)(2,1)S(1)}, bf16[4,4,8,128]{3,2,1,0:T(8,128)(2,1)S(1)}, u32[]{:S(2)}, u32[]{:S(2)}) collective-permute-start(bf16[4,4,8,128]{3,2,1,0:T(8,128)(2,1)S(1)} %get-tuple-element.33), channel_id=1, source_target_pairs={{0,1},{1,0},{2,3},{3,2},{4,10},{5,11},{6,8},{7,9},{8,6},{9,7},{10,... | collective-permute-start | bytes 98312 | tf_op jit(solution)/shard_map/ppermute | solution.py:43
  6.4 7.7 %collective-permute-start.3 = (bf16[4,4,8,128]{3,2,1,0:T(8,128)(2,1)S(1)}, bf16[4,4,8,128]{3,2,1,0:T(8,128)(2,1)S(1)}, u32[]{:S(2)}, u32[]{:S(2)}) collective-permute-start(bf16[4,4,8,128]{3,2,1,0:T(8,128)(2,1)S(1)} %get-tuple-element.33), channel_id=1, source_target_pairs={{0,6},{1,7},{2,4},{3,5},{4,2},{5,3},{6,0},{7,1},{8,14},{9,15},{10,... | collective-permute-start | bytes 98312 | tf_op jit(solution)/shard_map/ppermute | solution.py:43
  10.0 4.3 %collective-permute-start.2 = (bf16[4,4,8,128]{3,2,1,0:T(8,128)(2,1)S(1)}, bf16[4,4,8,128]{3,2,1,0:T(8,128)(2,1)S(1)}, u32[]{:S(2)}, u32[]{:S(2)}) collective-permute-start(bf16[4,4,8,128]{3,2,1,0:T(8,128)(2,1)S(1)} %get-tuple-element.33), channel_id=1, source_target_pairs={{0,2},{1,3},{2,0},{3,1},{4,6},{5,7},{6,4},{7,5},{8,10},{9,11},{10,... | collective-permute-start | bytes 98312 | tf_op jit(solution)/shard_map/ppermute | solution.py:43
  15.5 1.5 %collective-permute-start.5 = (f32[3,4,32,128]{3,2,1,0:T(8,128)S(1)}, f32[3,4,32,128]{3,2,1,0:T(8,128)S(1)}, u32[]{:S(2)}, u32[]{:S(2)}) collective-permute-start(f32[3,4,32,128]{3,2,1,0:T(8,128)S(1)} %get-tuple-element.38.part), channel_id=1, source_target_pairs={{0,1},{1,0},{2,3},{3,2},{4,5},{5,4},{6,7},{7,6},{8,9},{9,8},{10,11... | collective-permute-start | bytes 589832 | tf_op jit(solution)/shard_map/ppermute | solution.py:77
  17.6 7.8 %collective-permute-start.6 = (bf16[3,4,32,128]{3,2,1,0:T(8,128)(2,1)S(1)}, bf16[3,4,32,128]{3,2,1,0:T(8,128)(2,1)S(1)}, u32[]{:S(2)}, u32[]{:S(2)}) collective-permute-start(bf16[3,4,32,128]{3,2,1,0:T(8,128)(2,1)S(1)} %get-tuple-element.40), channel_id=1, source_target_pairs={{0,4},{1,3},{2,6},{3,1},{4,0},{5,9},{6,2},{7,11},{8,12},{9,5},{10,... | collective-permute-start | bytes 294920 | tf_op jit(solution)/shard_map/ppermute | solution.py:43
  20.1 3.8 %collective-permute-start.8 = (bf16[3,4,8,128]{3,2,1,0:T(8,128)(2,1)S(1)}, bf16[3,4,8,128]{3,2,1,0:T(8,128)(2,1)S(1)}, u32[]{:S(2)}, u32[]{:S(2)}) collective-permute-start(bf16[3,4,8,128]{3,2,1,0:T(8,128)(2,1)S(1)} %get-tuple-element.41), channel_id=1, source_target_pairs={{0,2},{1,3},{2,0},{3,1},{4,6},{5,7},{6,4},{7,5},{8,10},{9,11},{10,... | collective-permute-start | bytes 73736 | tf_op jit(solution)/shard_map/ppermute | solution.py:43
  20.7 4.7 %collective-permute-start.7 = (bf16[3,4,8,128]{3,2,1,0:T(8,128)(2,1)S(1)}, bf16[3,4,8,128]{3,2,1,0:T(8,128)(2,1)S(1)}, u32[]{:S(2)}, u32[]{:S(2)}) collective-permute-start(bf16[3,4,8,128]{3,2,1,0:T(8,128)(2,1)S(1)} %get-tuple-element.41), channel_id=1, source_target_pairs={{0,6},{1,3},{2,4},{3,1},{4,2},{5,11},{6,0},{7,9},{8,14},{9,7},{10,... | collective-permute-start | bytes 73736 | tf_op jit(solution)/shard_map/ppermute | solution.py:43
  25.4 1.4 %collective-permute-start.9 = (bf16[3,4,32,128]{3,2,1,0:T(8,128)(2,1)S(1)}, bf16[3,4,32,128]{3,2,1,0:T(8,128)(2,1)S(1)}, u32[]{:S(2)}, u32[]{:S(2)}) collective-permute-start(bf16[3,4,32,128]{3,2,1,0:T(8,128)(2,1)S(1)} %collective-permute-done.6.mine), channel_id=1, source_target_pairs={{0,1},{1,0},{2,3},{3,2},{4,5},{5,4},{6,7},{7,6},{8,9},{9,8},{10,11... | collective-permute-start | bytes 294920 | tf_op jit(solution)/shard_map/ppermute | solution.py:77
  25.4 1.4 %collective-permute-start.10 = (bf16[3,4,8,128]{3,2,1,0:T(8,128)(2,1)S(1)}, bf16[3,4,8,128]{3,2,1,0:T(8,128)(2,1)S(1)}, u32[]{:S(2)}, u32[]{:S(2)}) collective-permute-start(bf16[3,4,8,128]{3,2,1,0:T(8,128)(2,1)S(1)} %collective-permute-done.7.refs_1_), channel_id=1, source_target_pairs={{0,1},{1,0},{2,3},{3,2},{4,5},{5,4},{6,7},{7,6},{8,9},{9,8},{10,11... | collective-permute-start | bytes 73736 | tf_op jit(solution)/shard_map/ppermute | solution.py:77
  42.3 1.8 %collective-permute-start.11 = (f32[3,6,40,128]{3,2,1,0:T(8,128)S(1)}, f32[3,6,40,128]{3,2,1,0:T(8,128)S(1)}, u32[]{:S(2)}, u32[]{:S(2)}) collective-permute-start(f32[3,6,40,128]{3,2,1,0:T(8,128)S(1)} %edges.1.edge), channel_id=1, source_target_pairs={{0,1},{1,0},{2,3},{3,2},{4,5},{5,4},{6,7},{7,6},{8,9},{9,8},{10,11... | collective-permute-start | bytes 1105928 | tf_op jit(solution)/shard_map/ppermute | solution.py:77
  46.5 10.0 %all-to-all-start.1 = ((f32[8,8,128]{2,1,0:T(8,128)}), f32[8,8,128]{2,1,0:T(8,128)S(1)}, u32[]{:S(2)}, u32[]{:S(2)}) async-start(f32[8,8,128]{2,1,0:T(8,128)} %get-tuple-element.53), calls=%async_computation.1 | async-start | bytes 65536 | tf_op jit(solution)/shard_map/all_to_all | solution.py:101

commit v8 on v7

--- a/solution.py
+++ b/solution.py
@@ -437,7 +437,7 @@
     in_z = jnp.where(inside_z, 1.0, 0.0)
     next_z = jnp.where(inside_z & (z < size_z - 1), 1.0, 0.0)
     in_zy = jnp.where(lanes_iota(rows) < LANES - 1, in_z, 0.0)
-    for at in range(rows_x + 2 * HALO):
+    for at in range(1, rows_x + 2 * HALO - 1):
         x = at - HALO
         place = info[FIRST_X] + x
         inside = (place >= 0) & (place < size_x)
@@ -472,9 +472,9 @@
                 yield at, here, free[at] * result
                 flow_before = flow
 
-        for at, here, result in operate(v0, 1, rows_x + 2 * HALO - 1):
+        for at, here, result in operate(v0, 2, rows_x + 2 * HALO - 1):
             v1[l, at] = result * (1.0 / SPREAD) - here
-        for at, here, result in operate(v1, 2, rows_x + 2 * HALO - 2):
+        for at, here, result in operate(v1, 3, rows_x + 2 * HALO - 2):
             v2[l, at] = result * (2.0 / SPREAD) - 2.0 * here - v0[l, at]
         sums = [jnp.zeros((TILE, LANES), F32)] * 6
         for at, here, result in operate(v2, HALO, HALO + rows_x):
@@ -548,25 +548,31 @@
             out[d, at] = sums[d]
 
 
-def filter_sums(info, edge, other, slope, stack, grads, out, products, rows_out):
+def logit_grads(edge, other, slope, xp):
+    lane = lanes_iota(edge.shape[2])
+    shifted = [[], [], []]
+    for d in range(3):
+        plane = ((edge[d, xp] + other[d, xp]) * slope[d, xp]).astype(BF16).astype(F32)
+        shifted[0].append(jnp.where(lane < LANES - 1, up(plane, 1), 0.0))
+        shifted[1].append(plane)
+        shifted[2].append(jnp.where(lane > 0, down(plane, 1), 0.0))
+    return shifted[0] + shifted[1] + shifted[2]
+
+
+def filter_sums(info, edge, other, slope, stack, out, own, products, rows_out):
     rows_x = edge.shape[1] - 2
-    lane = lanes_iota(edge.shape[2])
-    for xp in range(rows_x + 2):
-        shifted = [[], [], []]
-        for d in range(3):
-            plane = ((edge[d, xp] + other[d, xp]) * slope[d, xp]).astype(BF16).astype(F32)
-            shifted[0].append(jnp.where(lane < LANES - 1, up(plane, 1), 0.0))
-            shifted[1].append(plane)
-            shifted[2].append(jnp.where(lane > 0, down(plane, 1), 0.0))
-        planes = shifted[0] + shifted[1] + shifted[2]
-        planes += [jnp.zeros_like(planes[0])] * 7
-        for pair in range(8):
-            at = (xp * 16 + 2 * pair) * TILE
-            store_tiles(grads, at, planes[2 * pair : 2 * pair + 2])
-    own = grads[LANES : LANES * (rows_x + 1), : 4 * LANES]
+    for x in range(rows_x):
+        planes = logit_grads(edge, other, slope, x + 1)
+        planes.append(jnp.zeros_like(planes[0]))
+        for pair in range(5):
+            at = (x * 16 + 2 * pair) * TILE
+            for t in range(4):
+                both = jnp.concatenate([plane[tile_rows(t)] for plane in planes[2 * pair : 2 * pair + 2]], axis=0)
+                own[at : at + 16, t * LANES : (t + 1) * LANES] = both.astype(BF16)
+        own[(x * 16 + 10) * TILE : (x + 1) * 16 * TILE, :] = jnp.zeros((6 * TILE, 4 * LANES), BF16)
     for n in range(2):
         products[n] = lax.dot_general(
-            own, stack[:, 512 * n : 512 * (n + 1)], (((1,), (1,)), ((), ())), preferred_element_type=F32
+            own[...], stack[:, 512 * n : 512 * (n + 1)], (((1,), (1,)), ((), ())), preferred_element_type=F32
         )
     rows_out[...] = jnp.zeros_like(rows_out)
     masks = {(h, j, o): band(h, j, o) for o in (-1, 0, 1) for h in range(2) for j in bands(o)}
@@ -595,7 +601,12 @@
         out[n] = sums
 
 
-def image_sums(info, grads, matrix, out, sums):
+def image_sums(info, edge, other, slope, matrix, out, grads, sums):
+    for xp in range(edge.shape[1]):
+        planes = logit_grads(edge, other, slope, xp)
+        planes += [jnp.zeros_like(planes[0])] * 7
+        for pair in range(8):
+            store_tiles(grads, (xp * 16 + 2 * pair) * TILE, planes[2 * pair : 2 * pair + 2])
     total = jnp.dot(matrix[0], grads[:, :512], preferred_element_type=F32)
     sums[...] = total + jnp.dot(matrix[1], grads[:, 512:], preferred_element_type=F32)
     channels, rows_x, rows_z, _ = out.shape
@@ -726,24 +737,31 @@
         scratch=[pltpu.VMEM((labels, rows_x + 3, rows, LANES), F32)],
         name="edges",
     )
-    grads, sums = call(
+    other_edge = lab_swap(edge)
+    sums = call(
         filter_sums,
-        [shaped((768, 1024), BF16), shaped((members, TILE, LANES), F32)],
+        shaped((members, TILE, LANES), F32),
         info,
         edge,
-        lab_swap(edge),
+        other_edge,
         squash_slope,
         stack,
-        scratch=[pltpu.VMEM((2, 512, 384), F32), pltpu.VMEM((LANES, LANES), F32)],
+        scratch=[
+            pltpu.VMEM((512, 512), BF16),
+            pltpu.VMEM((2, 512, 384), F32),
+            pltpu.VMEM((LANES, LANES), F32),
+        ],
         name="filter_sums",
     )
     grad_image = call(
         image_sums,
         shaped(image.shape, BF16),
         info,
-        grads,
+        edge,
+        other_edge,
+        squash_slope,
         back_matrix,
-        scratch=[pltpu.VMEM((256, 512), F32)],
+        scratch=[pltpu.VMEM((768, 1024), BF16), pltpu.VMEM((256, 512), F32)],
         flops=10_000_000,
         name="image_sums",
     )

time: 57.5 us -> 57.4 us (level)
  transfers between devices with their start and end apart: 13 -> 13, of which waited for: 8 -> 8; matrix products, arithmetic and copies ran while one was open for 0% -> 0% of each run, Pallas kernels for 4% -> 5%
where the time goes in v8:
time: 57.4 us; the launch traced here: 57.2 us
  starting transfers between devices  16.7 us (29%)
  waiting for transfers between devices  14.3 us (25%)
  Pallas kernels  13.1 us (23%)
  blocking collectives  11.3 us (20%)
  local copies, waits for them, and re-layouts  0.93 us (2%)
  between operations  0.74 us (1%)
    pallas_call x8, Pallas kernels, call(): pl.pallas_call(kernel, out_shape=outs, in_specs=specs, out_specs=jax.tree...  13.1 us
    ppermute x8, starting transfers between devices, swap(): lax.ppermute(block, SWAP_AXES, [(flat(*src), flat(*dst)) for src, dst in...  12.7 us
    all_to_all x1, blocking collectives, everyones(): return lax.all_to_all(copies, axes, 0, 0)  11.3 us
    ppermute x8, waiting for transfers between devices, swap(): lax.ppermute(block, SWAP_AXES, [(flat(*src), flat(*dst)) for src, dst in...  6.53 us
    all_to_all x1, waiting for transfers between devices, everyones(): return lax.all_to_all(copies, axes, 0, 0)  4.58 us
    all_to_all x1, starting transfers between devices, everyones(): return lax.all_to_all(copies, axes, 0, 0)  3.34 us
    ppermute x4, waiting for transfers between devices, lab_swap(): return lax.ppermute(block, 'lab', [(0, 1), (1, 0)])  3.19 us
  transfers between devices with their start and end apart: 13, of which 8 were waited for; matrix products, arithmetic and copies ran while one was open for 0% of the time, Pallas kernels for 5%

profile of v8, /device:TPU:0, one launch (start us, length us, event | category | flops | bytes accessed | tf_op | source)
XLA Modules:
  0.0 57.2 jit_solution(10744465688894386882)
XLA Ops:
  0.8 2.0 %pack.1 = (bf16[2,288,384]{2,1,0:T(8,128)(2,1)S(1)}, bf16[2,256,768]{2,1,0:T(8,128)(2,1)S(1)}, bf16[8,4,32,128]{3,2,1,0:T(8,128)(2,1)S(1)}, s32[4,32,128]{2,1,0:...) custom-call(s32[10]{0:T(128)S(1)} %stack.43.info, ...), custom_call_target="tpu_custom_call" | custom-call | flops 1000000 | bytes 854600 | tf_op jit(solution)/shard_map/pack/pallas_call | solution.py:108
  2.8 3.1 %collective-permute-start = (bf16[32,32,128]{2,1,0:T(8,128)(2,1)S(1)}, bf16[32,32,128]{2,1,0:T(8,128)(2,1)S(1)}, u32[]{:S(2)}, u32[]{:S(2)}) collective-permute-start(bf16[32,32,128]{2,1,0:T(8,128)(2,1)S(1)} %get-tuple-element.29), channel_id=1, source_target_pairs={{0,4},{1,5},{2,6},{3,7},{4,0},{5,1},{6,2},{7,3},{8,12},{9,13},{10,... | collective-permute-start | bytes 786440 | tf_op jit(solution)/shard_map/ppermute | solution.py:43
  6.4 3.6 %collective-permute-start.3 = (bf16[4,4,8,128]{3,2,1,0:T(8,128)(2,1)S(1)}, bf16[4,4,8,128]{3,2,1,0:T(8,128)(2,1)S(1)}, u32[]{:S(2)}, u32[]{:S(2)}) collective-permute-start(bf16[4,4,8,128]{3,2,1,0:T(8,128)(2,1)S(1)} %get-tuple-element.31), channel_id=1, source_target_pairs={{0,6},{1,7},{2,4},{3,5},{4,2},{5,3},{6,0},{7,1},{8,14},{9,15},{10,... | collective-permute-start | bytes 98312 | tf_op jit(solution)/shard_map/ppermute | solution.py:43
  10.0 1.5 %collective-permute-start.2 = (bf16[4,4,8,128]{3,2,1,0:T(8,128)(2,1)S(1)}, bf16[4,4,8,128]{3,2,1,0:T(8,128)(2,1)S(1)}, u32[]{:S(2)}, u32[]{:S(2)}) collective-permute-start(bf16[4,4,8,128]{3,2,1,0:T(8,128)(2,1)S(1)} %get-tuple-element.31), channel_id=1, source_target_pairs={{0,2},{1,3},{2,0},{3,1},{4,6},{5,7},{6,4},{7,5},{8,10},{9,11},{10,... | collective-permute-start | bytes 98312 | tf_op jit(solution)/shard_map/ppermute | solution.py:43
  11.4 2.7 %collective-permute-done.3.refs_1_ = bf16[4,4,8,128]{3,2,1,0:T(8,128)(2,1)S(1)} collective-permute-done((bf16[4,4,8,128]{3,2,1,0:T(8,128)(2,1)S(1)}, bf16[4,4,8,128]{3,2,1,0:T(8,128)(2,1)S(1)}, u32[]{:S(2)}, u32[]{:S(2)}) %collective-permute-start.3) | collective-permute-done | bytes 32800 | tf_op jit(solution)/shard_map/ppermute | solution.py:43
  14.2 1.3 %convolve.1 = (f32[3,4,32,128]{3,2,1,0:T(8,128)S(1)}, bf16[384,1024]{1,0:T(8,128)(2,1)S(1)}) custom-call(s32[10]{0:T(128)S(1)} %stack.43.info, bf16[8,4,32,128]{3,2,1,0:T(8,128)(2,1)S(1)} %get-tuple-element.34.image, bf16[32,32,128]{2,1,0:T(8,128)(2,1)S(1)} %collective-permute-done.first, bf16[32,32,128]{2,1,0:T(8,128)(2,1)S(1)} %collective-permute-done.1.second, ...), custom_call_target="tpu_custom_call" | custom-call | flops 1000000 | bytes 1327144 | tf_op jit(solution)/shard_map/convolve/pallas_call | solution.py:108
  15.6 1.4 %collective-permute-done.5.other = f32[3,4,32,128]{3,2,1,0:T(8,128)S(1)} collective-permute-done((f32[3,4,32,128]{3,2,1,0:T(8,128)S(1)}, f32[3,4,32,128]{3,2,1,0:T(8,128)S(1)}, u32[]{:S(2)}, u32[]{:S(2)}) %collective-permute-start.5) | collective-permute-done | bytes 196640 | tf_op jit(solution)/shard_map/ppermute | solution.py:77
  17.0 0.6 add_parts.1
  17.6 2.5 %collective-permute-start.6 = (bf16[3,4,32,128]{3,2,1,0:T(8,128)(2,1)S(1)}, bf16[3,4,32,128]{3,2,1,0:T(8,128)(2,1)S(1)}, u32[]{:S(2)}, u32[]{:S(2)}) collective-permute-start(bf16[3,4,32,128]{3,2,1,0:T(8,128)(2,1)S(1)} %get-tuple-element.38), channel_id=1, source_target_pairs={{0,4},{1,3},{2,6},{3,1},{4,0},{5,9},{6,2},{7,11},{8,12},{9,5},{10,... | collective-permute-start | bytes 294920 | tf_op jit(solution)/shard_map/ppermute | solution.py:43
  20.1 0.5 collective-permute-start.8
  20.7 1.0 %collective-permute-start.7 = (bf16[3,4,8,128]{3,2,1,0:T(8,128)(2,1)S(1)}, bf16[3,4,8,128]{3,2,1,0:T(8,128)(2,1)S(1)}, u32[]{:S(2)}, u32[]{:S(2)}) collective-permute-start(bf16[3,4,8,128]{3,2,1,0:T(8,128)(2,1)S(1)} %get-tuple-element.39), channel_id=1, source_target_pairs={{0,6},{1,3},{2,4},{3,1},{4,2},{5,11},{6,0},{7,9},{8,14},{9,7},{10,... | collective-permute-start | bytes 73736 | tf_op jit(solution)/shard_map/ppermute | solution.py:43
  21.7 2.3 %collective-permute-done.8.refs_0_ = bf16[3,4,8,128]{3,2,1,0:T(8,128)(2,1)S(1)} collective-permute-done((bf16[3,4,8,128]{3,2,1,0:T(8,128)(2,1)S(1)}, bf16[3,4,8,128]{3,2,1,0:T(8,128)(2,1)S(1)}, u32[]{:S(2)}, u32[]{:S(2)}) %collective-permute-start.8) | collective-permute-done | bytes 24608 | tf_op jit(solution)/shard_map/ppermute | solution.py:43
  24.0 1.4 %collective-permute-done.7.refs_1_ = bf16[3,4,8,128]{3,2,1,0:T(8,128)(2,1)S(1)} collective-permute-done((bf16[3,4,8,128]{3,2,1,0:T(8,128)(2,1)S(1)}, bf16[3,4,8,128]{3,2,1,0:T(8,128)(2,1)S(1)}, u32[]{:S(2)}, u32[]{:S(2)}) %collective-permute-start.7) | collective-permute-done | bytes 24608 | tf_op jit(solution)/shard_map/ppermute | solution.py:43
  25.4 0.5 collective-permute-start.10
  25.9 0.8 %prepare.1 = (f32[4,12,40,128]{3,2,1,0:T(8,128)S(1)}, f32[12,40,128]{2,1,0:T(8,128)S(1)}, f32[4,7,40,128]{3,2,1,0:T(8,128)S(1)}) custom-call(s32[10]{0:T(128)S(1)} %stack.43.info, s32[4,32,128]{2,1,0:T(8,128)S(1)} %get-tuple-element.26.planted, f32[4,4,32,128]{3,2,1,0:T(8,128)S(1)} %get-tuple-element.27.slope, ...), custom_call_target="tpu_custom_call" | custom-call | flops 1000000 | bytes 1212456 | tf_op jit(solution)/shard_map/prepare/pallas_call | solution.py:108
  26.8 3.0 %krylov.1 = (f32[4,12,40,128]{3,2,1,0:T(8,128)S(1)}, f32[4,12,40,128]{3,2,1,0:T(8,128)S(1)}, f32[3,6,40,128]{3,2,1,0:T(8,128)S(1)}, f32[8,8,128]{2,1,0:T(8,128)S(1)}) custom-call(s32[10]{0:T(128)S(1)} %stack.43.info, f32[4,12,40,128]{3,2,1,0:T(8,128)S(1)} %get-tuple-element.32.v0, f32[12,40,128]{2,1,0:T(8,128)S(1)} %get-tuple-element.33.free, ...), custom_call_target="tpu_custom_call" | custom-call | flops 1000000 | bytes 1695784 | tf_op jit(solution)/shard_map/krylov/pallas_call | solution.py:108
  29.8 11.3 %all_to_all.10.parts = f32[8,8,128]{2,1,0:T(8,128)S(1)} all-to-all(f32[8,8,128]{2,1,0:T(8,128)S(1)} %get-tuple-element.43), channel_id=1, replica_groups=mesh['crops'=2,'xy'=4,'gz'=2,'lab'=2] {'xy','gz'}, dimensions={0} | all-to-all | bytes 65536 | tf_op jit(solution)/shard_map/all_to_all | solution.py:101
  41.1 1.2 %edges.1.edge = f32[3,6,40,128]{3,2,1,0:T(8,128)S(1)} custom-call(s32[10]{0:T(128)S(1)} %stack.43.info, f32[8,8,128]{2,1,0:T(8,128)S(1)} %all_to_all.10.parts, f32[4,12,40,128]{3,2,1,0:T(8,128)S(1)} %get-tuple-element.32.v0, f32[4,12,40,128]{3,2,1,0:T(8,128)S(1)} %get-tuple-element.44.v1, f32[4,12,40,128]{3,2,1,0:T(8,128)S(1)} %get-tuple-element.45.v2, ...), custom_call_target="tpu_custom_call" | custom-call | flops 1000000 | bytes 3555368 | tf_op jit(solution)/shard_map/edges/pallas_call | solution.py:108
  42.3 1.7 %collective-permute-done.11.other = f32[3,6,40,128]{3,2,1,0:T(8,128)S(1)} collective-permute-done((f32[3,6,40,128]{3,2,1,0:T(8,128)S(1)}, f32[3,6,40,128]{3,2,1,0:T(8,128)S(1)}, u32[]{:S(2)}, u32[]{:S(2)}) %collective-permute-start.11) | collective-permute-done | bytes 368672 | tf_op jit(solution)/shard_map/ppermute | solution.py:77
  44.0 2.3 %filter_sums.1 = f32[8,8,128]{2,1,0:T(8,128)} custom-call(s32[10]{0:T(128)S(1)} %stack.43.info, f32[3,6,40,128]{3,2,1,0:T(8,128)S(1)} %edges.1.edge, f32[3,6,40,128]{3,2,1,0:T(8,128)S(1)} %collective-permute-done.11.other, f32[3,6,40,128]{3,2,1,0:T(8,128)S(1)} %get-tuple-element.47.slope, bf16[384,1024]{1,0:T(8,128)(2,1)S(1)} %get-tuple-element.49.stack), custom_call_target="tpu_custom_call" | custom-call | flops 1000000 | bytes 1892392 | tf_op jit(solution)/shard_map/filter_sums/pallas_call | solution.py:108
  46.3 3.3 %all-to-all-start.1 = ((f32[8,8,128]{2,1,0:T(8,128)}), f32[8,8,128]{2,1,0:T(8,128)S(1)}, u32[]{:S(2)}, u32[]{:S(2)}) async-start(f32[8,8,128]{2,1,0:T(8,128)} %filter_sums.1), calls=%async_computation.1 | async-start | bytes 65536 | tf_op jit(solution)/shard_map/all_to_all | solution.py:101
  49.7 2.0 %image_sums.1 = bf16[8,4,32,128]{3,2,1,0:T(8,128)(2,1)} custom-call(s32[10]{0:T(128)S(1)} %stack.43.info, f32[3,6,40,128]{3,2,1,0:T(8,128)S(1)} %edges.1.edge, f32[3,6,40,128]{3,2,1,0:T(8,128)S(1)} %collective-permute-done.11.other, f32[3,6,40,128]{3,2,1,0:T(8,128)S(1)} %get-tuple-element.47.slope, bf16[2,256,768]{2,1,0:T(8,128)(2,1)S(1)} %get-tuple-element.48.matrix), custom_call_target="tpu_custom_call" | custom-call | flops 10000000 | bytes 1892392 | tf_op jit(solution)/shard_map/image_sums/pallas_call | solution.py:108
  51.7 4.6 %all-to-all-done.1 = f32[8,8,128]{2,1,0:T(8,128)S(1)} async-done(((f32[8,8,128]{2,1,0:T(8,128)}), f32[8,8,128]{2,1,0:T(8,128)S(1)}, u32[]{:S(2)}, u32[]{:S(2)}) %all-to-all-start.1) | async-done | bytes 32800 | tf_op jit(solution)/shard_map/all_to_all | solution.py:101
  56.5 0.7 %reshape.11 = f32[3,8,3,3,3]{1,4,3,2,0:T(4,128)} reshape(f32[3,8,27]{1,2,0:T(8,128)S(1)} %copy.7) | data formatting | bytes 5184 | tf_op jit(solution)/shard_map/reshape | solution.py:770
  (16 shorter events, 1.2 us)
Async XLA Ops:
  2.8 11.4 %collective-permute-start = (bf16[32,32,128]{2,1,0:T(8,128)(2,1)S(1)}, bf16[32,32,128]{2,1,0:T(8,128)(2,1)S(1)}, u32[]{:S(2)}, u32[]{:S(2)}) collective-permute-start(bf16[32,32,128]{2,1,0:T(8,128)(2,1)S(1)} %get-tuple-element.29), channel_id=1, source_target_pairs={{0,4},{1,5},{2,6},{3,7},{4,0},{5,1},{6,2},{7,3},{8,12},{9,13},{10,... | collective-permute-start | bytes 786440 | tf_op jit(solution)/shard_map/ppermute | solution.py:43
  5.9 8.4 %collective-permute-start.1 = (bf16[32,32,128]{2,1,0:T(8,128)(2,1)S(1)}, bf16[32,32,128]{2,1,0:T(8,128)(2,1)S(1)}, u32[]{:S(2)}, u32[]{:S(2)}) collective-permute-start(bf16[32,32,128]{2,1,0:T(8,128)(2,1)S(1)} %get-tuple-element.30), channel_id=1, source_target_pairs={{0,1},{1,0},{2,3},{3,2},{4,8},{5,9},{6,10},{7,11},{8,4},{9,5},{10,... | collective-permute-start | bytes 786440 | tf_op jit(solution)/shard_map/ppermute | solution.py:43
  5.9 5.5 %collective-permute-start.4 = (bf16[4,4,8,128]{3,2,1,0:T(8,128)(2,1)S(1)}, bf16[4,4,8,128]{3,2,1,0:T(8,128)(2,1)S(1)}, u32[]{:S(2)}, u32[]{:S(2)}) collective-permute-start(bf16[4,4,8,128]{3,2,1,0:T(8,128)(2,1)S(1)} %get-tuple-element.31), channel_id=1, source_target_pairs={{0,1},{1,0},{2,3},{3,2},{4,10},{5,11},{6,8},{7,9},{8,6},{9,7},{10,... | collective-permute-start | bytes 98312 | tf_op jit(solution)/shard_map/ppermute | solution.py:43
  6.4 7.7 %collective-permute-start.3 = (bf16[4,4,8,128]{3,2,1,0:T(8,128)(2,1)S(1)}, bf16[4,4,8,128]{3,2,1,0:T(8,128)(2,1)S(1)}, u32[]{:S(2)}, u32[]{:S(2)}) collective-permute-start(bf16[4,4,8,128]{3,2,1,0:T(8,128)(2,1)S(1)} %get-tuple-element.31), channel_id=1, source_target_pairs={{0,6},{1,7},{2,4},{3,5},{4,2},{5,3},{6,0},{7,1},{8,14},{9,15},{10,... | collective-permute-start | bytes 98312 | tf_op jit(solution)/shard_map/ppermute | solution.py:43
  10.0 4.3 %collective-permute-start.2 = (bf16[4,4,8,128]{3,2,1,0:T(8,128)(2,1)S(1)}, bf16[4,4,8,128]{3,2,1,0:T(8,128)(2,1)S(1)}, u32[]{:S(2)}, u32[]{:S(2)}) collective-permute-start(bf16[4,4,8,128]{3,2,1,0:T(8,128)(2,1)S(1)} %get-tuple-element.31), channel_id=1, source_target_pairs={{0,2},{1,3},{2,0},{3,1},{4,6},{5,7},{6,4},{7,5},{8,10},{9,11},{10,... | collective-permute-start | bytes 98312 | tf_op jit(solution)/shard_map/ppermute | solution.py:43
  15.5 1.5 %collective-permute-start.5 = (f32[3,4,32,128]{3,2,1,0:T(8,128)S(1)}, f32[3,4,32,128]{3,2,1,0:T(8,128)S(1)}, u32[]{:S(2)}, u32[]{:S(2)}) collective-permute-start(f32[3,4,32,128]{3,2,1,0:T(8,128)S(1)} %get-tuple-element.36.part), channel_id=1, source_target_pairs={{0,1},{1,0},{2,3},{3,2},{4,5},{5,4},{6,7},{7,6},{8,9},{9,8},{10,11... | collective-permute-start | bytes 589832 | tf_op jit(solution)/shard_map/ppermute | solution.py:77
  17.6 7.8 %collective-permute-start.6 = (bf16[3,4,32,128]{3,2,1,0:T(8,128)(2,1)S(1)}, bf16[3,4,32,128]{3,2,1,0:T(8,128)(2,1)S(1)}, u32[]{:S(2)}, u32[]{:S(2)}) collective-permute-start(bf16[3,4,32,128]{3,2,1,0:T(8,128)(2,1)S(1)} %get-tuple-element.38), channel_id=1, source_target_pairs={{0,4},{1,3},{2,6},{3,1},{4,0},{5,9},{6,2},{7,11},{8,12},{9,5},{10,... | collective-permute-start | bytes 294920 | tf_op jit(solution)/shard_map/ppermute | solution.py:43
  20.1 3.8 %collective-permute-start.8 = (bf16[3,4,8,128]{3,2,1,0:T(8,128)(2,1)S(1)}, bf16[3,4,8,128]{3,2,1,0:T(8,128)(2,1)S(1)}, u32[]{:S(2)}, u32[]{:S(2)}) collective-permute-start(bf16[3,4,8,128]{3,2,1,0:T(8,128)(2,1)S(1)} %get-tuple-element.39), channel_id=1, source_target_pairs={{0,2},{1,3},{2,0},{3,1},{4,6},{5,7},{6,4},{7,5},{8,10},{9,11},{10,... | collective-permute-start | bytes 73736 | tf_op jit(solution)/shard_map/ppermute | solution.py:43
  20.7 4.7 %collective-permute-start.7 = (bf16[3,4,8,128]{3,2,1,0:T(8,128)(2,1)S(1)}, bf16[3,4,8,128]{3,2,1,0:T(8,128)(2,1)S(1)}, u32[]{:S(2)}, u32[]{:S(2)}) collective-permute-start(bf16[3,4,8,128]{3,2,1,0:T(8,128)(2,1)S(1)} %get-tuple-element.39), channel_id=1, source_target_pairs={{0,6},{1,3},{2,4},{3,1},{4,2},{5,11},{6,0},{7,9},{8,14},{9,7},{10,... | collective-permute-start | bytes 73736 | tf_op jit(solution)/shard_map/ppermute | solution.py:43
  25.4 1.4 %collective-permute-start.9 = (bf16[3,4,32,128]{3,2,1,0:T(8,128)(2,1)S(1)}, bf16[3,4,32,128]{3,2,1,0:T(8,128)(2,1)S(1)}, u32[]{:S(2)}, u32[]{:S(2)}) collective-permute-start(bf16[3,4,32,128]{3,2,1,0:T(8,128)(2,1)S(1)} %collective-permute-done.6.mine), channel_id=1, source_target_pairs={{0,1},{1,0},{2,3},{3,2},{4,5},{5,4},{6,7},{7,6},{8,9},{9,8},{10,11... | collective-permute-start | bytes 294920 | tf_op jit(solution)/shard_map/ppermute | solution.py:77
  25.4 1.4 %collective-permute-start.10 = (bf16[3,4,8,128]{3,2,1,0:T(8,128)(2,1)S(1)}, bf16[3,4,8,128]{3,2,1,0:T(8,128)(2,1)S(1)}, u32[]{:S(2)}, u32[]{:S(2)}) collective-permute-start(bf16[3,4,8,128]{3,2,1,0:T(8,128)(2,1)S(1)} %collective-permute-done.7.refs_1_), channel_id=1, source_target_pairs={{0,1},{1,0},{2,3},{3,2},{4,5},{5,4},{6,7},{7,6},{8,9},{9,8},{10,11... | collective-permute-start | bytes 73736 | tf_op jit(solution)/shard_map/ppermute | solution.py:77
  42.3 1.8 %collective-permute-start.11 = (f32[3,6,40,128]{3,2,1,0:T(8,128)S(1)}, f32[3,6,40,128]{3,2,1,0:T(8,128)S(1)}, u32[]{:S(2)}, u32[]{:S(2)}) collective-permute-start(f32[3,6,40,128]{3,2,1,0:T(8,128)S(1)} %edges.1.edge), channel_id=1, source_target_pairs={{0,1},{1,0},{2,3},{3,2},{4,5},{5,4},{6,7},{7,6},{8,9},{9,8},{10,11... | collective-permute-start | bytes 1105928 | tf_op jit(solution)/shard_map/ppermute | solution.py:77
  46.3 10.0 %all-to-all-start.1 = ((f32[8,8,128]{2,1,0:T(8,128)}), f32[8,8,128]{2,1,0:T(8,128)S(1)}, u32[]{:S(2)}, u32[]{:S(2)}) async-start(f32[8,8,128]{2,1,0:T(8,128)} %filter_sums.1), calls=%async_computation.1 | async-start | bytes 65536 | tf_op jit(solution)/shard_map/all_to_all | solution.py:101

commit v9 on v8

--- a/solution.py
+++ b/solution.py
@@ -456,7 +456,10 @@
                 plane = jnp.where(is_up, there, here) if x < 0 else jnp.where(is_up, here, there)
             squashed = 1.0 / (1.0 + jnp.exp(-plane))
             valid = (in_z * next_x, next_z * in_x, in_zy * in_x)[d]
-            weight[d, at] = (0.05 + squashed) * valid
+            edge_weight = (0.05 + squashed) * valid
+            weight[d, at] = edge_weight
+            if d > 0:
+                weight[2 + d, at] = down(edge_weight, d - 1)
             if -1 <= x <= rows_x:
                 slope_out[d, x + 1] = squashed * (1.0 - squashed) * valid
 
@@ -466,9 +469,10 @@
             for at in range(start, stop):
                 here = v[l, at]
                 flow = weight[0, at] * (here - v[l, at + 1])
-                flow_z = weight[1, at] * (here - up(here, 0))
-                flow_y = weight[2, at] * (here - up(here, 1))
-                result = flow - flow_before + (flow_z - down(flow_z, 0)) + (flow_y - down(flow_y, 1))
+                result = flow - flow_before
+                for dim in range(2):
+                    result = result + weight[1 + dim, at] * (here - up(here, dim))
+                    result = result + weight[3 + dim, at] * (here - down(here, dim))
                 yield at, here, free[at] * result
                 flow_before = flow
 
@@ -722,7 +726,7 @@
         *logit_faces,
         *mine_edges,
         *other_edges,
-        scratch=[pltpu.VMEM((3,) + extended[1:], F32), pltpu.VMEM((6 * labels, LANES), F32)],
+        scratch=[pltpu.VMEM((5,) + extended[1:], F32), pltpu.VMEM((6 * labels, LANES), F32)],
         name="krylov",
     )
     edge = call(

time: 57.4 us -> 56.9 us (level)
  no operation moved by 1% of the time
where the time goes in v9:
time: 56.9 us; the launch traced here: 56.6 us
  starting transfers between devices  16.7 us (29%)
  waiting for transfers between devices  14.3 us (25%)
  Pallas kernels  12.6 us (22%)
  blocking collectives  11.3 us (20%)
  local copies, waits for them, and re-layouts  0.93 us (2%)
  between operations  0.74 us (1%)
    ppermute x8, starting transfers between devices, swap(): lax.ppermute(block, SWAP_AXES, [(flat(*src), flat(*dst)) for src, dst in...  12.7 us
    pallas_call x8, Pallas kernels, call(): pl.pallas_call(kernel, out_shape=outs, in_specs=specs, out_specs=jax.tree...  12.6 us
    all_to_all x1, blocking collectives, everyones(): return lax.all_to_all(copies, axes, 0, 0)  11.3 us
    ppermute x8, waiting for transfers between devices, swap(): lax.ppermute(block, SWAP_AXES, [(flat(*src), flat(*dst)) for src, dst in...  6.53 us
    all_to_all x1, waiting for transfers between devices, everyones(): return lax.all_to_all(copies, axes, 0, 0)  4.58 us
    all_to_all x1, starting transfers between devices, everyones(): return lax.all_to_all(copies, axes, 0, 0)  3.34 us
    ppermute x4, waiting for transfers between devices, lab_swap(): return lax.ppermute(block, 'lab', [(0, 1), (1, 0)])  3.19 us
  transfers between devices with their start and end apart: 13, of which 8 were waited for; matrix products, arithmetic and copies ran while one was open for 0% of the time, Pallas kernels for 5%

profile of v9, /device:TPU:0, one launch (start us, length us, event | category | flops | bytes accessed | tf_op | source)
XLA Modules:
  0.0 56.6 jit_solution(2205002180612482354)
XLA Ops:
  0.8 2.0 %pack.1 = (bf16[2,288,384]{2,1,0:T(8,128)(2,1)S(1)}, bf16[2,256,768]{2,1,0:T(8,128)(2,1)S(1)}, bf16[8,4,32,128]{3,2,1,0:T(8,128)(2,1)S(1)}, s32[4,32,128]{2,1,0:...) custom-call(s32[10]{0:T(128)S(1)} %stack.43.info, ...), custom_call_target="tpu_custom_call" | custom-call | flops 1000000 | bytes 854600 | tf_op jit(solution)/shard_map/pack/pallas_call | solution.py:108
  2.8 3.1 %collective-permute-start = (bf16[32,32,128]{2,1,0:T(8,128)(2,1)S(1)}, bf16[32,32,128]{2,1,0:T(8,128)(2,1)S(1)}, u32[]{:S(2)}, u32[]{:S(2)}) collective-permute-start(bf16[32,32,128]{2,1,0:T(8,128)(2,1)S(1)} %get-tuple-element.29), channel_id=1, source_target_pairs={{0,4},{1,5},{2,6},{3,7},{4,0},{5,1},{6,2},{7,3},{8,12},{9,13},{10,... | collective-permute-start | bytes 786440 | tf_op jit(solution)/shard_map/ppermute | solution.py:43
  6.4 3.6 %collective-permute-start.3 = (bf16[4,4,8,128]{3,2,1,0:T(8,128)(2,1)S(1)}, bf16[4,4,8,128]{3,2,1,0:T(8,128)(2,1)S(1)}, u32[]{:S(2)}, u32[]{:S(2)}) collective-permute-start(bf16[4,4,8,128]{3,2,1,0:T(8,128)(2,1)S(1)} %get-tuple-element.31), channel_id=1, source_target_pairs={{0,6},{1,7},{2,4},{3,5},{4,2},{5,3},{6,0},{7,1},{8,14},{9,15},{10,... | collective-permute-start | bytes 98312 | tf_op jit(solution)/shard_map/ppermute | solution.py:43
  10.0 1.5 %collective-permute-start.2 = (bf16[4,4,8,128]{3,2,1,0:T(8,128)(2,1)S(1)}, bf16[4,4,8,128]{3,2,1,0:T(8,128)(2,1)S(1)}, u32[]{:S(2)}, u32[]{:S(2)}) collective-permute-start(bf16[4,4,8,128]{3,2,1,0:T(8,128)(2,1)S(1)} %get-tuple-element.31), channel_id=1, source_target_pairs={{0,2},{1,3},{2,0},{3,1},{4,6},{5,7},{6,4},{7,5},{8,10},{9,11},{10,... | collective-permute-start | bytes 98312 | tf_op jit(solution)/shard_map/ppermute | solution.py:43
  11.4 2.7 %collective-permute-done.3.refs_1_ = bf16[4,4,8,128]{3,2,1,0:T(8,128)(2,1)S(1)} collective-permute-done((bf16[4,4,8,128]{3,2,1,0:T(8,128)(2,1)S(1)}, bf16[4,4,8,128]{3,2,1,0:T(8,128)(2,1)S(1)}, u32[]{:S(2)}, u32[]{:S(2)}) %collective-permute-start.3) | collective-permute-done | bytes 32800 | tf_op jit(solution)/shard_map/ppermute | solution.py:43
  14.2 1.3 %convolve.1 = (f32[3,4,32,128]{3,2,1,0:T(8,128)S(1)}, bf16[384,1024]{1,0:T(8,128)(2,1)S(1)}) custom-call(s32[10]{0:T(128)S(1)} %stack.43.info, bf16[8,4,32,128]{3,2,1,0:T(8,128)(2,1)S(1)} %get-tuple-element.34.image, bf16[32,32,128]{2,1,0:T(8,128)(2,1)S(1)} %collective-permute-done.first, bf16[32,32,128]{2,1,0:T(8,128)(2,1)S(1)} %collective-permute-done.1.second, ...), custom_call_target="tpu_custom_call" | custom-call | flops 1000000 | bytes 1327144 | tf_op jit(solution)/shard_map/convolve/pallas_call | solution.py:108
  15.6 1.4 %collective-permute-done.5.other = f32[3,4,32,128]{3,2,1,0:T(8,128)S(1)} collective-permute-done((f32[3,4,32,128]{3,2,1,0:T(8,128)S(1)}, f32[3,4,32,128]{3,2,1,0:T(8,128)S(1)}, u32[]{:S(2)}, u32[]{:S(2)}) %collective-permute-start.5) | collective-permute-done | bytes 196640 | tf_op jit(solution)/shard_map/ppermute | solution.py:77
  17.0 0.6 %add_parts.1 = (f32[3,4,32,128]{3,2,1,0:T(8,128)S(1)}, bf16[3,4,32,128]{3,2,1,0:T(8,128)(2,1)S(1)}, bf16[3,4,8,128]{3,2,1,0:T(8,128)(2,1)S(1)}) custom-call(s32[10]{0:T(128)S(1)} %stack.43.info, f32[3,4,32,128]{3,2,1,0:T(8,128)S(1)} %get-tuple-element.36.part, f32[3,4,32,128]{3,2,1,0:T(8,128)S(1)} %collective-permute-done.5.other), custom_call_target="tpu_custom_call" | custom-call | flops 1000000 | bytes 393256 | tf_op jit(solution)/shard_map/add_parts/pallas_call | solution.py:108
  17.6 2.5 %collective-permute-start.6 = (bf16[3,4,32,128]{3,2,1,0:T(8,128)(2,1)S(1)}, bf16[3,4,32,128]{3,2,1,0:T(8,128)(2,1)S(1)}, u32[]{:S(2)}, u32[]{:S(2)}) collective-permute-start(bf16[3,4,32,128]{3,2,1,0:T(8,128)(2,1)S(1)} %get-tuple-element.38), channel_id=1, source_target_pairs={{0,4},{1,3},{2,6},{3,1},{4,0},{5,9},{6,2},{7,11},{8,12},{9,5},{10,... | collective-permute-start | bytes 294920 | tf_op jit(solution)/shard_map/ppermute | solution.py:43
  20.1 0.5 collective-permute-start.8
  20.7 1.0 %collective-permute-start.7 = (bf16[3,4,8,128]{3,2,1,0:T(8,128)(2,1)S(1)}, bf16[3,4,8,128]{3,2,1,0:T(8,128)(2,1)S(1)}, u32[]{:S(2)}, u32[]{:S(2)}) collective-permute-start(bf16[3,4,8,128]{3,2,1,0:T(8,128)(2,1)S(1)} %get-tuple-element.39), channel_id=1, source_target_pairs={{0,6},{1,3},{2,4},{3,1},{4,2},{5,11},{6,0},{7,9},{8,14},{9,7},{10,... | collective-permute-start | bytes 73736 | tf_op jit(solution)/shard_map/ppermute | solution.py:43
  21.7 2.3 %collective-permute-done.8.refs_0_ = bf16[3,4,8,128]{3,2,1,0:T(8,128)(2,1)S(1)} collective-permute-done((bf16[3,4,8,128]{3,2,1,0:T(8,128)(2,1)S(1)}, bf16[3,4,8,128]{3,2,1,0:T(8,128)(2,1)S(1)}, u32[]{:S(2)}, u32[]{:S(2)}) %collective-permute-start.8) | collective-permute-done | bytes 24608 | tf_op jit(solution)/shard_map/ppermute | solution.py:43
  24.0 1.4 %collective-permute-done.7.refs_1_ = bf16[3,4,8,128]{3,2,1,0:T(8,128)(2,1)S(1)} collective-permute-done((bf16[3,4,8,128]{3,2,1,0:T(8,128)(2,1)S(1)}, bf16[3,4,8,128]{3,2,1,0:T(8,128)(2,1)S(1)}, u32[]{:S(2)}, u32[]{:S(2)}) %collective-permute-start.7) | collective-permute-done | bytes 24608 | tf_op jit(solution)/shard_map/ppermute | solution.py:43
  25.4 0.5 collective-permute-start.10
  25.9 0.8 %prepare.1 = (f32[4,12,40,128]{3,2,1,0:T(8,128)S(1)}, f32[12,40,128]{2,1,0:T(8,128)S(1)}, f32[4,7,40,128]{3,2,1,0:T(8,128)S(1)}) custom-call(s32[10]{0:T(128)S(1)} %stack.43.info, s32[4,32,128]{2,1,0:T(8,128)S(1)} %get-tuple-element.26.planted, f32[4,4,32,128]{3,2,1,0:T(8,128)S(1)} %get-tuple-element.27.slope, ...), custom_call_target="tpu_custom_call" | custom-call | flops 1000000 | bytes 1212456 | tf_op jit(solution)/shard_map/prepare/pallas_call | solution.py:108
  26.8 2.5 %krylov.1 = (f32[4,12,40,128]{3,2,1,0:T(8,128)S(1)}, f32[4,12,40,128]{3,2,1,0:T(8,128)S(1)}, f32[3,6,40,128]{3,2,1,0:T(8,128)S(1)}, f32[8,8,128]{2,1,0:T(8,128)S(1)}) custom-call(s32[10]{0:T(128)S(1)} %stack.43.info, f32[4,12,40,128]{3,2,1,0:T(8,128)S(1)} %get-tuple-element.32.v0, f32[12,40,128]{2,1,0:T(8,128)S(1)} %get-tuple-element.33.free, ...), custom_call_target="tpu_custom_call" | custom-call | flops 1000000 | bytes 1695784 | tf_op jit(solution)/shard_map/krylov/pallas_call | solution.py:108
  29.2 11.3 %all_to_all.10.parts = f32[8,8,128]{2,1,0:T(8,128)S(1)} all-to-all(f32[8,8,128]{2,1,0:T(8,128)S(1)} %get-tuple-element.43), channel_id=1, replica_groups=mesh['crops'=2,'xy'=4,'gz'=2,'lab'=2] {'xy','gz'}, dimensions={0} | all-to-all | bytes 65536 | tf_op jit(solution)/shard_map/all_to_all | solution.py:101
  40.5 1.2 %edges.1.edge = f32[3,6,40,128]{3,2,1,0:T(8,128)S(1)} custom-call(s32[10]{0:T(128)S(1)} %stack.43.info, f32[8,8,128]{2,1,0:T(8,128)S(1)} %all_to_all.10.parts, f32[4,12,40,128]{3,2,1,0:T(8,128)S(1)} %get-tuple-element.32.v0, f32[4,12,40,128]{3,2,1,0:T(8,128)S(1)} %get-tuple-element.44.v1, f32[4,12,40,128]{3,2,1,0:T(8,128)S(1)} %get-tuple-element.45.v2, ...), custom_call_target="tpu_custom_call" | custom-call | flops 1000000 | bytes 3555368 | tf_op jit(solution)/shard_map/edges/pallas_call | solution.py:108
  41.8 1.7 %collective-permute-done.11.other = f32[3,6,40,128]{3,2,1,0:T(8,128)S(1)} collective-permute-done((f32[3,6,40,128]{3,2,1,0:T(8,128)S(1)}, f32[3,6,40,128]{3,2,1,0:T(8,128)S(1)}, u32[]{:S(2)}, u32[]{:S(2)}) %collective-permute-start.11) | collective-permute-done | bytes 368672 | tf_op jit(solution)/shard_map/ppermute | solution.py:77
  43.5 2.3 %filter_sums.1 = f32[8,8,128]{2,1,0:T(8,128)} custom-call(s32[10]{0:T(128)S(1)} %stack.43.info, f32[3,6,40,128]{3,2,1,0:T(8,128)S(1)} %edges.1.edge, f32[3,6,40,128]{3,2,1,0:T(8,128)S(1)} %collective-permute-done.11.other, f32[3,6,40,128]{3,2,1,0:T(8,128)S(1)} %get-tuple-element.47.slope, bf16[384,1024]{1,0:T(8,128)(2,1)S(1)} %get-tuple-element.49.stack), custom_call_target="tpu_custom_call" | custom-call | flops 1000000 | bytes 1892392 | tf_op jit(solution)/shard_map/filter_sums/pallas_call | solution.py:108
  45.8 3.3 %all-to-all-start.1 = ((f32[8,8,128]{2,1,0:T(8,128)}), f32[8,8,128]{2,1,0:T(8,128)S(1)}, u32[]{:S(2)}, u32[]{:S(2)}) async-start(f32[8,8,128]{2,1,0:T(8,128)} %filter_sums.1), calls=%async_computation.1 | async-start | bytes 65536 | tf_op jit(solution)/shard_map/all_to_all | solution.py:101
  49.1 2.0 %image_sums.1 = bf16[8,4,32,128]{3,2,1,0:T(8,128)(2,1)} custom-call(s32[10]{0:T(128)S(1)} %stack.43.info, f32[3,6,40,128]{3,2,1,0:T(8,128)S(1)} %edges.1.edge, f32[3,6,40,128]{3,2,1,0:T(8,128)S(1)} %collective-permute-done.11.other, f32[3,6,40,128]{3,2,1,0:T(8,128)S(1)} %get-tuple-element.47.slope, bf16[2,256,768]{2,1,0:T(8,128)(2,1)S(1)} %get-tuple-element.48.matrix), custom_call_target="tpu_custom_call" | custom-call | flops 10000000 | bytes 1892392 | tf_op jit(solution)/shard_map/image_sums/pallas_call | solution.py:108
  51.2 4.6 %all-to-all-done.1 = f32[8,8,128]{2,1,0:T(8,128)S(1)} async-done(((f32[8,8,128]{2,1,0:T(8,128)}), f32[8,8,128]{2,1,0:T(8,128)S(1)}, u32[]{:S(2)}, u32[]{:S(2)}) %all-to-all-start.1) | async-done | bytes 32800 | tf_op jit(solution)/shard_map/all_to_all | solution.py:101
  56.0 0.7 %reshape.11 = f32[3,8,3,3,3]{1,4,3,2,0:T(4,128)} reshape(f32[3,8,27]{1,2,0:T(8,128)S(1)} %copy.7) | data formatting | bytes 5184 | tf_op jit(solution)/shard_map/reshape | solution.py:774
  (16 shorter events, 1.2 us)
Async XLA Ops:
  2.8 11.4 %collective-permute-start = (bf16[32,32,128]{2,1,0:T(8,128)(2,1)S(1)}, bf16[32,32,128]{2,1,0:T(8,128)(2,1)S(1)}, u32[]{:S(2)}, u32[]{:S(2)}) collective-permute-start(bf16[32,32,128]{2,1,0:T(8,128)(2,1)S(1)} %get-tuple-element.29), channel_id=1, source_target_pairs={{0,4},{1,5},{2,6},{3,7},{4,0},{5,1},{6,2},{7,3},{8,12},{9,13},{10,... | collective-permute-start | bytes 786440 | tf_op jit(solution)/shard_map/ppermute | solution.py:43
  5.9 8.4 %collective-permute-start.1 = (bf16[32,32,128]{2,1,0:T(8,128)(2,1)S(1)}, bf16[32,32,128]{2,1,0:T(8,128)(2,1)S(1)}, u32[]{:S(2)}, u32[]{:S(2)}) collective-permute-start(bf16[32,32,128]{2,1,0:T(8,128)(2,1)S(1)} %get-tuple-element.30), channel_id=1, source_target_pairs={{0,1},{1,0},{2,3},{3,2},{4,8},{5,9},{6,10},{7,11},{8,4},{9,5},{10,... | collective-permute-start | bytes 786440 | tf_op jit(solution)/shard_map/ppermute | solution.py:43
  5.9 5.5 %collective-permute-start.4 = (bf16[4,4,8,128]{3,2,1,0:T(8,128)(2,1)S(1)}, bf16[4,4,8,128]{3,2,1,0:T(8,128)(2,1)S(1)}, u32[]{:S(2)}, u32[]{:S(2)}) collective-permute-start(bf16[4,4,8,128]{3,2,1,0:T(8,128)(2,1)S(1)} %get-tuple-element.31), channel_id=1, source_target_pairs={{0,1},{1,0},{2,3},{3,2},{4,10},{5,11},{6,8},{7,9},{8,6},{9,7},{10,... | collective-permute-start | bytes 98312 | tf_op jit(solution)/shard_map/ppermute | solution.py:43
  6.4 7.7 %collective-permute-start.3 = (bf16[4,4,8,128]{3,2,1,0:T(8,128)(2,1)S(1)}, bf16[4,4,8,128]{3,2,1,0:T(8,128)(2,1)S(1)}, u32[]{:S(2)}, u32[]{:S(2)}) collective-permute-start(bf16[4,4,8,128]{3,2,1,0:T(8,128)(2,1)S(1)} %get-tuple-element.31), channel_id=1, source_target_pairs={{0,6},{1,7},{2,4},{3,5},{4,2},{5,3},{6,0},{7,1},{8,14},{9,15},{10,... | collective-permute-start | bytes 98312 | tf_op jit(solution)/shard_map/ppermute | solution.py:43
  10.0 4.3 %collective-permute-start.2 = (bf16[4,4,8,128]{3,2,1,0:T(8,128)(2,1)S(1)}, bf16[4,4,8,128]{3,2,1,0:T(8,128)(2,1)S(1)}, u32[]{:S(2)}, u32[]{:S(2)}) collective-permute-start(bf16[4,4,8,128]{3,2,1,0:T(8,128)(2,1)S(1)} %get-tuple-element.31), channel_id=1, source_target_pairs={{0,2},{1,3},{2,0},{3,1},{4,6},{5,7},{6,4},{7,5},{8,10},{9,11},{10,... | collective-permute-start | bytes 98312 | tf_op jit(solution)/shard_map/ppermute | solution.py:43
  15.5 1.5 %collective-permute-start.5 = (f32[3,4,32,128]{3,2,1,0:T(8,128)S(1)}, f32[3,4,32,128]{3,2,1,0:T(8,128)S(1)}, u32[]{:S(2)}, u32[]{:S(2)}) collective-permute-start(f32[3,4,32,128]{3,2,1,0:T(8,128)S(1)} %get-tuple-element.36.part), channel_id=1, source_target_pairs={{0,1},{1,0},{2,3},{3,2},{4,5},{5,4},{6,7},{7,6},{8,9},{9,8},{10,11... | collective-permute-start | bytes 589832 | tf_op jit(solution)/shard_map/ppermute | solution.py:77
  17.6 7.8 %collective-permute-start.6 = (bf16[3,4,32,128]{3,2,1,0:T(8,128)(2,1)S(1)}, bf16[3,4,32,128]{3,2,1,0:T(8,128)(2,1)S(1)}, u32[]{:S(2)}, u32[]{:S(2)}) collective-permute-start(bf16[3,4,32,128]{3,2,1,0:T(8,128)(2,1)S(1)} %get-tuple-element.38), channel_id=1, source_target_pairs={{0,4},{1,3},{2,6},{3,1},{4,0},{5,9},{6,2},{7,11},{8,12},{9,5},{10,... | collective-permute-start | bytes 294920 | tf_op jit(solution)/shard_map/ppermute | solution.py:43
  20.1 3.8 %collective-permute-start.8 = (bf16[3,4,8,128]{3,2,1,0:T(8,128)(2,1)S(1)}, bf16[3,4,8,128]{3,2,1,0:T(8,128)(2,1)S(1)}, u32[]{:S(2)}, u32[]{:S(2)}) collective-permute-start(bf16[3,4,8,128]{3,2,1,0:T(8,128)(2,1)S(1)} %get-tuple-element.39), channel_id=1, source_target_pairs={{0,2},{1,3},{2,0},{3,1},{4,6},{5,7},{6,4},{7,5},{8,10},{9,11},{10,... | collective-permute-start | bytes 73736 | tf_op jit(solution)/shard_map/ppermute | solution.py:43
  20.7 4.7 %collective-permute-start.7 = (bf16[3,4,8,128]{3,2,1,0:T(8,128)(2,1)S(1)}, bf16[3,4,8,128]{3,2,1,0:T(8,128)(2,1)S(1)}, u32[]{:S(2)}, u32[]{:S(2)}) collective-permute-start(bf16[3,4,8,128]{3,2,1,0:T(8,128)(2,1)S(1)} %get-tuple-element.39), channel_id=1, source_target_pairs={{0,6},{1,3},{2,4},{3,1},{4,2},{5,11},{6,0},{7,9},{8,14},{9,7},{10,... | collective-permute-start | bytes 73736 | tf_op jit(solution)/shard_map/ppermute | solution.py:43
  25.4 1.4 %collective-permute-start.9 = (bf16[3,4,32,128]{3,2,1,0:T(8,128)(2,1)S(1)}, bf16[3,4,32,128]{3,2,1,0:T(8,128)(2,1)S(1)}, u32[]{:S(2)}, u32[]{:S(2)}) collective-permute-start(bf16[3,4,32,128]{3,2,1,0:T(8,128)(2,1)S(1)} %collective-permute-done.6.mine), channel_id=1, source_target_pairs={{0,1},{1,0},{2,3},{3,2},{4,5},{5,4},{6,7},{7,6},{8,9},{9,8},{10,11... | collective-permute-start | bytes 294920 | tf_op jit(solution)/shard_map/ppermute | solution.py:77
  25.4 1.4 %collective-permute-start.10 = (bf16[3,4,8,128]{3,2,1,0:T(8,128)(2,1)S(1)}, bf16[3,4,8,128]{3,2,1,0:T(8,128)(2,1)S(1)}, u32[]{:S(2)}, u32[]{:S(2)}) collective-permute-start(bf16[3,4,8,128]{3,2,1,0:T(8,128)(2,1)S(1)} %collective-permute-done.7.refs_1_), channel_id=1, source_target_pairs={{0,1},{1,0},{2,3},{3,2},{4,5},{5,4},{6,7},{7,6},{8,9},{9,8},{10,11... | collective-permute-start | bytes 73736 | tf_op jit(solution)/shard_map/ppermute | solution.py:77
  41.7 1.8 %collective-permute-start.11 = (f32[3,6,40,128]{3,2,1,0:T(8,128)S(1)}, f32[3,6,40,128]{3,2,1,0:T(8,128)S(1)}, u32[]{:S(2)}, u32[]{:S(2)}) collective-permute-start(f32[3,6,40,128]{3,2,1,0:T(8,128)S(1)} %edges.1.edge), channel_id=1, source_target_pairs={{0,1},{1,0},{2,3},{3,2},{4,5},{5,4},{6,7},{7,6},{8,9},{9,8},{10,11... | collective-permute-start | bytes 1105928 | tf_op jit(solution)/shard_map/ppermute | solution.py:77
  45.8 10.0 %all-to-all-start.1 = ((f32[8,8,128]{2,1,0:T(8,128)}), f32[8,8,128]{2,1,0:T(8,128)S(1)}, u32[]{:S(2)}, u32[]{:S(2)}) async-start(f32[8,8,128]{2,1,0:T(8,128)} %filter_sums.1), calls=%async_computation.1 | async-start | bytes 65536 | tf_op jit(solution)/shard_map/all_to_all | solution.py:101

commit v10 on v9

--- a/solution.py
+++ b/solution.py
@@ -369,14 +369,14 @@
 
                 before = jnp.where(lane > 0, pltpu.roll(piece(0), 1, 1), 0.0)
                 after = jnp.where(lane < LANES - 1, pltpu.roll(piece(2), LANES - 1, 1), 0.0)
-                part[d, x, tile_rows(t)] = piece(1) + before + after
+                part[d, x, tile_rows(t)] = (piece(1) + before + after).astype(BF16)
 
 
 def add_parts(two, info, part, other, logits, brick, *faces):
     rows_x, rows_z = part.shape[1], part.shape[2]
     for d in range(3):
         for x in range(rows_x):
-            total = part[d, x] + other[d, x]
+            total = part[d, x].astype(F32) + other[d, x].astype(F32)
             logits[d, x] = total
             brick[d, x] = total.astype(BF16)
             for phase, face in enumerate(faces):
@@ -679,7 +679,7 @@
 
     part, stack = call(
         functools.partial(convolve, two),
-        [shaped((3, rows_x, rows_z, LANES), F32), shaped((384, 1024), BF16)],
+        [shaped((3, rows_x, rows_z, LANES), BF16), shaped((384, 1024), BF16)],
         info,
         image,
         *received,

time: 56.9 us -> 56.7 us (level)
  no operation moved by 1% of the time
where the time goes in v10:
time: 56.7 us; the launch traced here: 56.5 us
  starting transfers between devices  16.7 us (29%)
  waiting for transfers between devices  14.2 us (25%)
  Pallas kernels  12.6 us (22%)
  blocking collectives  11.3 us (20%)
  local copies, waits for them, and re-layouts  0.93 us (2%)
  between operations  0.74 us (1%)
    ppermute x8, starting transfers between devices, swap(): lax.ppermute(block, SWAP_AXES, [(flat(*src), flat(*dst)) for src, dst in...  12.7 us
    pallas_call x8, Pallas kernels, call(): pl.pallas_call(kernel, out_shape=outs, in_specs=specs, out_specs=jax.tree...  12.6 us
    all_to_all x1, blocking collectives, everyones(): return lax.all_to_all(copies, axes, 0, 0)  11.3 us
    ppermute x8, waiting for transfers between devices, swap(): lax.ppermute(block, SWAP_AXES, [(flat(*src), flat(*dst)) for src, dst in...  6.53 us
    all_to_all x1, waiting for transfers between devices, everyones(): return lax.all_to_all(copies, axes, 0, 0)  4.58 us
    all_to_all x1, starting transfers between devices, everyones(): return lax.all_to_all(copies, axes, 0, 0)  3.34 us
    ppermute x4, waiting for transfers between devices, lab_swap(): return lax.ppermute(block, 'lab', [(0, 1), (1, 0)])  3.05 us
  transfers between devices with their start and end apart: 13, of which 8 were waited for; matrix products, arithmetic and copies ran while one was open for 0% of the time, Pallas kernels for 5%

profile of v10, /device:TPU:0, one launch (start us, length us, event | category | flops | bytes accessed | tf_op | source)
XLA Modules:
  0.0 56.5 jit_solution(4075541947859186981)
XLA Ops:
  0.8 2.0 %pack.1 = (bf16[2,288,384]{2,1,0:T(8,128)(2,1)S(1)}, bf16[2,256,768]{2,1,0:T(8,128)(2,1)S(1)}, bf16[8,4,32,128]{3,2,1,0:T(8,128)(2,1)S(1)}, s32[4,32,128]{2,1,0:...) custom-call(s32[10]{0:T(128)S(1)} %stack.43.info, ...), custom_call_target="tpu_custom_call" | custom-call | flops 1000000 | bytes 854600 | tf_op jit(solution)/shard_map/pack/pallas_call | solution.py:108
  2.8 3.1 %collective-permute-start = (bf16[32,32,128]{2,1,0:T(8,128)(2,1)S(1)}, bf16[32,32,128]{2,1,0:T(8,128)(2,1)S(1)}, u32[]{:S(2)}, u32[]{:S(2)}) collective-permute-start(bf16[32,32,128]{2,1,0:T(8,128)(2,1)S(1)} %get-tuple-element.29), channel_id=1, source_target_pairs={{0,4},{1,5},{2,6},{3,7},{4,0},{5,1},{6,2},{7,3},{8,12},{9,13},{10,... | collective-permute-start | bytes 786440 | tf_op jit(solution)/shard_map/ppermute | solution.py:43
  6.4 3.6 %collective-permute-start.3 = (bf16[4,4,8,128]{3,2,1,0:T(8,128)(2,1)S(1)}, bf16[4,4,8,128]{3,2,1,0:T(8,128)(2,1)S(1)}, u32[]{:S(2)}, u32[]{:S(2)}) collective-permute-start(bf16[4,4,8,128]{3,2,1,0:T(8,128)(2,1)S(1)} %get-tuple-element.31), channel_id=1, source_target_pairs={{0,6},{1,7},{2,4},{3,5},{4,2},{5,3},{6,0},{7,1},{8,14},{9,15},{10,... | collective-permute-start | bytes 98312 | tf_op jit(solution)/shard_map/ppermute | solution.py:43
  10.0 1.5 %collective-permute-start.2 = (bf16[4,4,8,128]{3,2,1,0:T(8,128)(2,1)S(1)}, bf16[4,4,8,128]{3,2,1,0:T(8,128)(2,1)S(1)}, u32[]{:S(2)}, u32[]{:S(2)}) collective-permute-start(bf16[4,4,8,128]{3,2,1,0:T(8,128)(2,1)S(1)} %get-tuple-element.31), channel_id=1, source_target_pairs={{0,2},{1,3},{2,0},{3,1},{4,6},{5,7},{6,4},{7,5},{8,10},{9,11},{10,... | collective-permute-start | bytes 98312 | tf_op jit(solution)/shard_map/ppermute | solution.py:43
  11.4 2.7 %collective-permute-done.3.refs_1_ = bf16[4,4,8,128]{3,2,1,0:T(8,128)(2,1)S(1)} collective-permute-done((bf16[4,4,8,128]{3,2,1,0:T(8,128)(2,1)S(1)}, bf16[4,4,8,128]{3,2,1,0:T(8,128)(2,1)S(1)}, u32[]{:S(2)}, u32[]{:S(2)}) %collective-permute-start.3) | collective-permute-done | bytes 32800 | tf_op jit(solution)/shard_map/ppermute | solution.py:43
  14.2 1.3 %convolve.1 = (bf16[3,4,32,128]{3,2,1,0:T(8,128)(2,1)S(1)}, bf16[384,1024]{1,0:T(8,128)(2,1)S(1)}) custom-call(s32[10]{0:T(128)S(1)} %stack.43.info, bf16[8,4,32,128]{3,2,1,0:T(8,128)(2,1)S(1)} %get-tuple-element.34.image, bf16[32,32,128]{2,1,0:T(8,128)(2,1)S(1)} %collective-permute-done.first, bf16[32,32,128]{2,1,0:T(8,128)(2,1)S(1)} %collective-permute-done.1.second, ...), custom_call_target="tpu_custom_call" | custom-call | flops 1000000 | bytes 1327144 | tf_op jit(solution)/shard_map/convolve/pallas_call | solution.py:108
  15.6 1.3 %collective-permute-done.5.other = bf16[3,4,32,128]{3,2,1,0:T(8,128)(2,1)S(1)} collective-permute-done((bf16[3,4,32,128]{3,2,1,0:T(8,128)(2,1)S(1)}, bf16[3,4,32,128]{3,2,1,0:T(8,128)(2,1)S(1)}, u32[]{:S(2)}, u32[]{:S(2)}) %collective-permute-start.5) | collective-permute-done | bytes 98336 | tf_op jit(solution)/shard_map/ppermute | solution.py:77
  16.9 0.6 %add_parts.1 = (f32[3,4,32,128]{3,2,1,0:T(8,128)S(1)}, bf16[3,4,32,128]{3,2,1,0:T(8,128)(2,1)S(1)}, bf16[3,4,8,128]{3,2,1,0:T(8,128)(2,1)S(1)}) custom-call(s32[10]{0:T(128)S(1)} %stack.43.info, bf16[3,4,32,128]{3,2,1,0:T(8,128)(2,1)S(1)} %get-tuple-element.36.part, bf16[3,4,32,128]{3,2,1,0:T(8,128)(2,1)S(1)} %collective-permute-done.5.other), custom_call_target="tpu_custom_call" | custom-call | flops 1000000 | bytes 196648 | tf_op jit(solution)/shard_map/add_parts/pallas_call | solution.py:108
  17.5 2.5 %collective-permute-start.6 = (bf16[3,4,32,128]{3,2,1,0:T(8,128)(2,1)S(1)}, bf16[3,4,32,128]{3,2,1,0:T(8,128)(2,1)S(1)}, u32[]{:S(2)}, u32[]{:S(2)}) collective-permute-start(bf16[3,4,32,128]{3,2,1,0:T(8,128)(2,1)S(1)} %get-tuple-element.38), channel_id=1, source_target_pairs={{0,4},{1,3},{2,6},{3,1},{4,0},{5,9},{6,2},{7,11},{8,12},{9,5},{10,... | collective-permute-start | bytes 294920 | tf_op jit(solution)/shard_map/ppermute | solution.py:43
  20.0 0.5 collective-permute-start.8
  20.5 1.0 %collective-permute-start.7 = (bf16[3,4,8,128]{3,2,1,0:T(8,128)(2,1)S(1)}, bf16[3,4,8,128]{3,2,1,0:T(8,128)(2,1)S(1)}, u32[]{:S(2)}, u32[]{:S(2)}) collective-permute-start(bf16[3,4,8,128]{3,2,1,0:T(8,128)(2,1)S(1)} %get-tuple-element.39), channel_id=1, source_target_pairs={{0,6},{1,3},{2,4},{3,1},{4,2},{5,11},{6,0},{7,9},{8,14},{9,7},{10,... | collective-permute-start | bytes 73736 | tf_op jit(solution)/shard_map/ppermute | solution.py:43
  21.5 2.3 %collective-permute-done.8.refs_0_ = bf16[3,4,8,128]{3,2,1,0:T(8,128)(2,1)S(1)} collective-permute-done((bf16[3,4,8,128]{3,2,1,0:T(8,128)(2,1)S(1)}, bf16[3,4,8,128]{3,2,1,0:T(8,128)(2,1)S(1)}, u32[]{:S(2)}, u32[]{:S(2)}) %collective-permute-start.8) | collective-permute-done | bytes 24608 | tf_op jit(solution)/shard_map/ppermute | solution.py:43
  23.8 1.4 %collective-permute-done.7.refs_1_ = bf16[3,4,8,128]{3,2,1,0:T(8,128)(2,1)S(1)} collective-permute-done((bf16[3,4,8,128]{3,2,1,0:T(8,128)(2,1)S(1)}, bf16[3,4,8,128]{3,2,1,0:T(8,128)(2,1)S(1)}, u32[]{:S(2)}, u32[]{:S(2)}) %collective-permute-start.7) | collective-permute-done | bytes 24608 | tf_op jit(solution)/shard_map/ppermute | solution.py:43
  25.3 0.5 collective-permute-start.10
  25.8 0.8 %prepare.1 = (f32[4,12,40,128]{3,2,1,0:T(8,128)S(1)}, f32[12,40,128]{2,1,0:T(8,128)S(1)}, f32[4,7,40,128]{3,2,1,0:T(8,128)S(1)}) custom-call(s32[10]{0:T(128)S(1)} %stack.43.info, s32[4,32,128]{2,1,0:T(8,128)S(1)} %get-tuple-element.26.planted, f32[4,4,32,128]{3,2,1,0:T(8,128)S(1)} %get-tuple-element.27.slope, ...), custom_call_target="tpu_custom_call" | custom-call | flops 1000000 | bytes 1212456 | tf_op jit(solution)/shard_map/prepare/pallas_call | solution.py:108
  26.6 2.5 %krylov.1 = (f32[4,12,40,128]{3,2,1,0:T(8,128)S(1)}, f32[4,12,40,128]{3,2,1,0:T(8,128)S(1)}, f32[3,6,40,128]{3,2,1,0:T(8,128)S(1)}, f32[8,8,128]{2,1,0:T(8,128)S(1)}) custom-call(s32[10]{0:T(128)S(1)} %stack.43.info, f32[4,12,40,128]{3,2,1,0:T(8,128)S(1)} %get-tuple-element.32.v0, f32[12,40,128]{2,1,0:T(8,128)S(1)} %get-tuple-element.33.free, ...), custom_call_target="tpu_custom_call" | custom-call | flops 1000000 | bytes 1695784 | tf_op jit(solution)/shard_map/krylov/pallas_call | solution.py:108
  29.1 11.3 %all_to_all.10.parts = f32[8,8,128]{2,1,0:T(8,128)S(1)} all-to-all(f32[8,8,128]{2,1,0:T(8,128)S(1)} %get-tuple-element.43), channel_id=1, replica_groups=mesh['crops'=2,'xy'=4,'gz'=2,'lab'=2] {'xy','gz'}, dimensions={0} | all-to-all | bytes 65536 | tf_op jit(solution)/shard_map/all_to_all | solution.py:101
  40.4 1.2 %edges.1.edge = f32[3,6,40,128]{3,2,1,0:T(8,128)S(1)} custom-call(s32[10]{0:T(128)S(1)} %stack.43.info, f32[8,8,128]{2,1,0:T(8,128)S(1)} %all_to_all.10.parts, f32[4,12,40,128]{3,2,1,0:T(8,128)S(1)} %get-tuple-element.32.v0, f32[4,12,40,128]{3,2,1,0:T(8,128)S(1)} %get-tuple-element.44.v1, f32[4,12,40,128]{3,2,1,0:T(8,128)S(1)} %get-tuple-element.45.v2, ...), custom_call_target="tpu_custom_call" | custom-call | flops 1000000 | bytes 3555368 | tf_op jit(solution)/shard_map/edges/pallas_call | solution.py:108
  41.7 1.7 %collective-permute-done.11.other = f32[3,6,40,128]{3,2,1,0:T(8,128)S(1)} collective-permute-done((f32[3,6,40,128]{3,2,1,0:T(8,128)S(1)}, f32[3,6,40,128]{3,2,1,0:T(8,128)S(1)}, u32[]{:S(2)}, u32[]{:S(2)}) %collective-permute-start.11) | collective-permute-done | bytes 368672 | tf_op jit(solution)/shard_map/ppermute | solution.py:77
  43.3 2.3 %filter_sums.1 = f32[8,8,128]{2,1,0:T(8,128)} custom-call(s32[10]{0:T(128)S(1)} %stack.43.info, f32[3,6,40,128]{3,2,1,0:T(8,128)S(1)} %edges.1.edge, f32[3,6,40,128]{3,2,1,0:T(8,128)S(1)} %collective-permute-done.11.other, f32[3,6,40,128]{3,2,1,0:T(8,128)S(1)} %get-tuple-element.47.slope, bf16[384,1024]{1,0:T(8,128)(2,1)S(1)} %get-tuple-element.49.stack), custom_call_target="tpu_custom_call" | custom-call | flops 1000000 | bytes 1892392 | tf_op jit(solution)/shard_map/filter_sums/pallas_call | solution.py:108
  45.7 3.3 %all-to-all-start.1 = ((f32[8,8,128]{2,1,0:T(8,128)}), f32[8,8,128]{2,1,0:T(8,128)S(1)}, u32[]{:S(2)}, u32[]{:S(2)}) async-start(f32[8,8,128]{2,1,0:T(8,128)} %filter_sums.1), calls=%async_computation.1 | async-start | bytes 65536 | tf_op jit(solution)/shard_map/all_to_all | solution.py:101
  49.0 2.0 %image_sums.1 = bf16[8,4,32,128]{3,2,1,0:T(8,128)(2,1)} custom-call(s32[10]{0:T(128)S(1)} %stack.43.info, f32[3,6,40,128]{3,2,1,0:T(8,128)S(1)} %edges.1.edge, f32[3,6,40,128]{3,2,1,0:T(8,128)S(1)} %collective-permute-done.11.other, f32[3,6,40,128]{3,2,1,0:T(8,128)S(1)} %get-tuple-element.47.slope, bf16[2,256,768]{2,1,0:T(8,128)(2,1)S(1)} %get-tuple-element.48.matrix), custom_call_target="tpu_custom_call" | custom-call | flops 10000000 | bytes 1892392 | tf_op jit(solution)/shard_map/image_sums/pallas_call | solution.py:108
  51.0 4.6 %all-to-all-done.1 = f32[8,8,128]{2,1,0:T(8,128)S(1)} async-done(((f32[8,8,128]{2,1,0:T(8,128)}), f32[8,8,128]{2,1,0:T(8,128)S(1)}, u32[]{:S(2)}, u32[]{:S(2)}) %all-to-all-start.1) | async-done | bytes 32800 | tf_op jit(solution)/shard_map/all_to_all | solution.py:101
  55.8 0.7 %reshape.11 = f32[3,8,3,3,3]{1,4,3,2,0:T(4,128)} reshape(f32[3,8,27]{1,2,0:T(8,128)S(1)} %copy.7) | data formatting | bytes 5184 | tf_op jit(solution)/shard_map/reshape | solution.py:774
  (16 shorter events, 1.2 us)
Async XLA Ops:
  2.8 11.4 %collective-permute-start = (bf16[32,32,128]{2,1,0:T(8,128)(2,1)S(1)}, bf16[32,32,128]{2,1,0:T(8,128)(2,1)S(1)}, u32[]{:S(2)}, u32[]{:S(2)}) collective-permute-start(bf16[32,32,128]{2,1,0:T(8,128)(2,1)S(1)} %get-tuple-element.29), channel_id=1, source_target_pairs={{0,4},{1,5},{2,6},{3,7},{4,0},{5,1},{6,2},{7,3},{8,12},{9,13},{10,... | collective-permute-start | bytes 786440 | tf_op jit(solution)/shard_map/ppermute | solution.py:43
  5.9 8.4 %collective-permute-start.1 = (bf16[32,32,128]{2,1,0:T(8,128)(2,1)S(1)}, bf16[32,32,128]{2,1,0:T(8,128)(2,1)S(1)}, u32[]{:S(2)}, u32[]{:S(2)}) collective-permute-start(bf16[32,32,128]{2,1,0:T(8,128)(2,1)S(1)} %get-tuple-element.30), channel_id=1, source_target_pairs={{0,1},{1,0},{2,3},{3,2},{4,8},{5,9},{6,10},{7,11},{8,4},{9,5},{10,... | collective-permute-start | bytes 786440 | tf_op jit(solution)/shard_map/ppermute | solution.py:43
  5.9 5.5 %collective-permute-start.4 = (bf16[4,4,8,128]{3,2,1,0:T(8,128)(2,1)S(1)}, bf16[4,4,8,128]{3,2,1,0:T(8,128)(2,1)S(1)}, u32[]{:S(2)}, u32[]{:S(2)}) collective-permute-start(bf16[4,4,8,128]{3,2,1,0:T(8,128)(2,1)S(1)} %get-tuple-element.31), channel_id=1, source_target_pairs={{0,1},{1,0},{2,3},{3,2},{4,10},{5,11},{6,8},{7,9},{8,6},{9,7},{10,... | collective-permute-start | bytes 98312 | tf_op jit(solution)/shard_map/ppermute | solution.py:43
  6.4 7.7 %collective-permute-start.3 = (bf16[4,4,8,128]{3,2,1,0:T(8,128)(2,1)S(1)}, bf16[4,4,8,128]{3,2,1,0:T(8,128)(2,1)S(1)}, u32[]{:S(2)}, u32[]{:S(2)}) collective-permute-start(bf16[4,4,8,128]{3,2,1,0:T(8,128)(2,1)S(1)} %get-tuple-element.31), channel_id=1, source_target_pairs={{0,6},{1,7},{2,4},{3,5},{4,2},{5,3},{6,0},{7,1},{8,14},{9,15},{10,... | collective-permute-start | bytes 98312 | tf_op jit(solution)/shard_map/ppermute | solution.py:43
  10.0 4.3 %collective-permute-start.2 = (bf16[4,4,8,128]{3,2,1,0:T(8,128)(2,1)S(1)}, bf16[4,4,8,128]{3,2,1,0:T(8,128)(2,1)S(1)}, u32[]{:S(2)}, u32[]{:S(2)}) collective-permute-start(bf16[4,4,8,128]{3,2,1,0:T(8,128)(2,1)S(1)} %get-tuple-element.31), channel_id=1, source_target_pairs={{0,2},{1,3},{2,0},{3,1},{4,6},{5,7},{6,4},{7,5},{8,10},{9,11},{10,... | collective-permute-start | bytes 98312 | tf_op jit(solution)/shard_map/ppermute | solution.py:43
  15.5 1.4 %collective-permute-start.5 = (bf16[3,4,32,128]{3,2,1,0:T(8,128)(2,1)S(1)}, bf16[3,4,32,128]{3,2,1,0:T(8,128)(2,1)S(1)}, u32[]{:S(2)}, u32[]{:S(2)}) collective-permute-start(bf16[3,4,32,128]{3,2,1,0:T(8,128)(2,1)S(1)} %get-tuple-element.36.part), channel_id=1, source_target_pairs={{0,1},{1,0},{2,3},{3,2},{4,5},{5,4},{6,7},{7,6},{8,9},{9,8},{10,11... | collective-permute-start | bytes 294920 | tf_op jit(solution)/shard_map/ppermute | solution.py:77
  17.5 7.8 %collective-permute-start.6 = (bf16[3,4,32,128]{3,2,1,0:T(8,128)(2,1)S(1)}, bf16[3,4,32,128]{3,2,1,0:T(8,128)(2,1)S(1)}, u32[]{:S(2)}, u32[]{:S(2)}) collective-permute-start(bf16[3,4,32,128]{3,2,1,0:T(8,128)(2,1)S(1)} %get-tuple-element.38), channel_id=1, source_target_pairs={{0,4},{1,3},{2,6},{3,1},{4,0},{5,9},{6,2},{7,11},{8,12},{9,5},{10,... | collective-permute-start | bytes 294920 | tf_op jit(solution)/shard_map/ppermute | solution.py:43
  20.0 3.8 %collective-permute-start.8 = (bf16[3,4,8,128]{3,2,1,0:T(8,128)(2,1)S(1)}, bf16[3,4,8,128]{3,2,1,0:T(8,128)(2,1)S(1)}, u32[]{:S(2)}, u32[]{:S(2)}) collective-permute-start(bf16[3,4,8,128]{3,2,1,0:T(8,128)(2,1)S(1)} %get-tuple-element.39), channel_id=1, source_target_pairs={{0,2},{1,3},{2,0},{3,1},{4,6},{5,7},{6,4},{7,5},{8,10},{9,11},{10,... | collective-permute-start | bytes 73736 | tf_op jit(solution)/shard_map/ppermute | solution.py:43
  20.5 4.7 %collective-permute-start.7 = (bf16[3,4,8,128]{3,2,1,0:T(8,128)(2,1)S(1)}, bf16[3,4,8,128]{3,2,1,0:T(8,128)(2,1)S(1)}, u32[]{:S(2)}, u32[]{:S(2)}) collective-permute-start(bf16[3,4,8,128]{3,2,1,0:T(8,128)(2,1)S(1)} %get-tuple-element.39), channel_id=1, source_target_pairs={{0,6},{1,3},{2,4},{3,1},{4,2},{5,11},{6,0},{7,9},{8,14},{9,7},{10,... | collective-permute-start | bytes 73736 | tf_op jit(solution)/shard_map/ppermute | solution.py:43
  25.3 1.4 %collective-permute-start.9 = (bf16[3,4,32,128]{3,2,1,0:T(8,128)(2,1)S(1)}, bf16[3,4,32,128]{3,2,1,0:T(8,128)(2,1)S(1)}, u32[]{:S(2)}, u32[]{:S(2)}) collective-permute-start(bf16[3,4,32,128]{3,2,1,0:T(8,128)(2,1)S(1)} %collective-permute-done.6.mine), channel_id=1, source_target_pairs={{0,1},{1,0},{2,3},{3,2},{4,5},{5,4},{6,7},{7,6},{8,9},{9,8},{10,11... | collective-permute-start | bytes 294920 | tf_op jit(solution)/shard_map/ppermute | solution.py:77
  25.3 1.4 %collective-permute-start.10 = (bf16[3,4,8,128]{3,2,1,0:T(8,128)(2,1)S(1)}, bf16[3,4,8,128]{3,2,1,0:T(8,128)(2,1)S(1)}, u32[]{:S(2)}, u32[]{:S(2)}) collective-permute-start(bf16[3,4,8,128]{3,2,1,0:T(8,128)(2,1)S(1)} %collective-permute-done.7.refs_1_), channel_id=1, source_target_pairs={{0,1},{1,0},{2,3},{3,2},{4,5},{5,4},{6,7},{7,6},{8,9},{9,8},{10,11... | collective-permute-start | bytes 73736 | tf_op jit(solution)/shard_map/ppermute | solution.py:77
  41.6 1.8 %collective-permute-start.11 = (f32[3,6,40,128]{3,2,1,0:T(8,128)S(1)}, f32[3,6,40,128]{3,2,1,0:T(8,128)S(1)}, u32[]{:S(2)}, u32[]{:S(2)}) collective-permute-start(f32[3,6,40,128]{3,2,1,0:T(8,128)S(1)} %edges.1.edge), channel_id=1, source_target_pairs={{0,1},{1,0},{2,3},{3,2},{4,5},{5,4},{6,7},{7,6},{8,9},{9,8},{10,11... | collective-permute-start | bytes 1105928 | tf_op jit(solution)/shard_map/ppermute | solution.py:77
  45.7 10.0 %all-to-all-start.1 = ((f32[8,8,128]{2,1,0:T(8,128)}), f32[8,8,128]{2,1,0:T(8,128)S(1)}, u32[]{:S(2)}, u32[]{:S(2)}) async-start(f32[8,8,128]{2,1,0:T(8,128)} %filter_sums.1), calls=%async_computation.1 | async-start | bytes 65536 | tf_op jit(solution)/shard_map/all_to_all | solution.py:101
